TPU v7x, 32 devices: a whole 2x2x4 slice. The times are simulated.
32 devices in a mesh: groups: 2 (over x), tm: 8 (over z, y), space: 2 (over core).
Axes of the slice: x: 2, y: 2, z: 4, core: 2. Of those that a mesh axis runs over, the one named last changes fastest.
Arguments:
- queries: bfloat16 [16384, 256], P(('groups', 'tm', 'space')), parts along dimension 0, may hold values from -22 to 22, as said below
- key_rows: bfloat16 [16384, 256], P(('groups', 'tm', 'space')), parts along dimension 0, may hold values from -10 to 10
- value_rows: bfloat16 [16384, 256], P(('groups', 'tm', 'space')), parts along dimension 0, may hold values from -6 to 6
- out_grad: bfloat16 [16384, 256], P(('groups', 'tm', 'space')), parts along dimension 0, may hold values from -6 to 6
- block_lists: int32 [32, 8], P('groups'), parts along dimension 0, may hold values from -1 to 31, as said below
Outputs:
- attn_out: bfloat16 [16384, 256], P(('groups', 'tm', 'space')), parts along dimension 0
- grad_queries: bfloat16 [16384, 256], P(('groups', 'tm', 'space')), parts along dimension 0
- grad_keys: bfloat16 [16384, 256], P(('groups', 'tm', 'space')), parts along dimension 0
- grad_values: bfloat16 [16384, 256], P(('groups', 'tm', 'space')), parts along dimension 0
There are 2 independent parts, one for each index of `groups`. A program takes and returns all parts, laid end to end along the dimension named above; each array names one. Nothing has to cross between parts.
Inputs may be any that keep to these rules, and one draw needn't show every extreme that they name: `block_lists`: row r belongs to query slab r. Slots 0 to 3 concern earlier frames and slots 4 to 7 later ones; in each half the first two slots name two different blocks of the frame at distance 1, and the half's slot j >= 2 names one block of the frame at distance 2 ** (j - 1). An entry is frame * 4 + block with block 0 to 3, or -1 exactly where that frame lies outside the video. `queries`: query entries.
All inputs are finite; a program needn't handle non-finite values.
Results may differ from a plain program's by a relative error of at most 0.012.
Values may be sent and summed in bfloat16 or wider, within the bound.
No kernel may reach another device: no remote copies, remote signals or barrier semaphores. Data moves between devices by JAX's collectives and lax.ppermute only.
A program may use at most 128 MiB of HBM per device.

v0:
```python
import math

import jax
import jax.numpy as jnp
from jax import lax
from jax.sharding import PartitionSpec as P

DH = 128
HEADS = 2


def passed_along(value, axis, steps):
    count = lax.axis_size(axis)
    initial, last = (max(0, -steps), min(count, count - steps))
    return lax.ppermute(value, axis, [(source, source + steps) for source in range(initial, last)])


def forward_head(query_h, key_h, value_h, usable, inv_scale):
    scores = jnp.dot(query_h, key_h.T, preferred_element_type=jnp.float32) * inv_scale
    scores = jnp.where(usable[None, :], scores, -jnp.inf)
    row_max = jnp.max(scores, axis=1, keepdims=True)
    raised = jnp.exp(scores - row_max)
    attn_prob = raised / jnp.sum(raised, axis=1, keepdims=True)
    attn_bf = attn_prob.astype(jnp.bfloat16)
    out_head = jnp.dot(attn_bf, value_h, preferred_element_type=jnp.float32).astype(jnp.bfloat16)
    return (attn_prob, attn_bf, out_head)


def backward_head(query_h, key_h, value_h, grad_h, out_head, attn_prob, attn_bf, inv_scale):
    grad_prob = jnp.dot(grad_h, value_h.T, preferred_element_type=jnp.float32)
    row_dot = jnp.sum(
        grad_h.astype(jnp.float32) * out_head.astype(jnp.float32), axis=1, keepdims=True
    )
    grad_score = (attn_prob * (grad_prob - row_dot)).astype(jnp.bfloat16)
    grad_q = (jnp.dot(grad_score, key_h, preferred_element_type=jnp.float32) * inv_scale).astype(
        jnp.bfloat16
    )
    grad_k = jnp.dot(grad_score.T, query_h, preferred_element_type=jnp.float32) * inv_scale
    grad_v = jnp.dot(attn_bf.T, grad_h, preferred_element_type=jnp.float32)
    return (grad_q, grad_k, grad_v)


def split_heads(matrix):
    return matrix.reshape(matrix.shape[0], HEADS, DH).transpose(1, 0, 2)


def merge_heads(stacked):
    return stacked.transpose(1, 0, 2).reshape(stacked.shape[1], HEADS * DH)


def attend_whole(query_s, key_all, value_all, grad_s, usable, inv_scale):

    def per_head(operands):
        query_h, key_h, value_h, grad_h = operands
        attn_prob, attn_bf, out_head = forward_head(query_h, key_h, value_h, usable, inv_scale)
        grad_q, grad_k, grad_v = backward_head(
            query_h, key_h, value_h, grad_h, out_head, attn_prob, attn_bf, inv_scale
        )
        return (out_head, grad_q, grad_k, grad_v)

    results = lax.map(
        per_head,
        (split_heads(query_s), split_heads(key_all), split_heads(value_all), split_heads(grad_s)),
    )
    return tuple((merge_heads(stacked) for stacked in results))


def slot_span(side, level, levels):
    base = side * (levels + 1)
    if level == 0:
        return (base, 2)
    return (base + 1 + level, 1)


def select_blocks(frame_both, local_ids, count, block, width):
    picked = jnp.take(frame_both.reshape(2, 4, block, width), local_ids, axis=1)
    return picked.reshape(2, count * block, width)


def per_device(queries, key_rows, value_rows, out_grad, block_lists):
    s_dev = queries.shape[0]
    width = queries.shape[1]
    n_space = lax.axis_size("space")
    n_tm = lax.axis_size("tm")
    levels = n_tm.bit_length() - 1
    frame_tok = s_dev * n_space
    block = frame_tok // 4
    tm_index = lax.axis_index("tm")
    space_index = lax.axis_index("space")
    my_row = tm_index * n_space + space_index
    my_list = lax.dynamic_index_in_dim(block_lists, my_row, 0, keepdims=False)
    inv_scale = 1.0 / math.sqrt(DH)
    plans = []
    for side in range(2):
        for level in range(levels):
            distance = 1 << level
            shift_by = distance if side == 0 else -distance
            initial_entry, count = slot_span(side, level, levels)
            target = jnp.clip(tm_index + shift_by, 0, n_tm - 1)
            target_list = lax.dynamic_index_in_dim(
                block_lists, target * n_space + space_index, 0, keepdims=False
            )
            local_ids = jnp.clip(
                target_list[initial_entry : initial_entry + count] - tm_index * 4, 0, 3
            )
            own_slots = my_list[initial_entry : initial_entry + count]
            usable_slot = own_slots >= 0
            source_ids = jnp.clip(own_slots - (tm_index - shift_by) * 4, 0, 3)
            plans.append((shift_by, count, local_ids, usable_slot, source_ids))
    usable = jnp.concatenate(
        [jnp.ones((frame_tok,), dtype=bool)] + [jnp.repeat(plan[3], block) for plan in plans]
    )
    own_pair = jnp.stack([key_rows, value_rows])
    frame_both = lax.all_gather(own_pair, "space", axis=1, tiled=True)
    received = []
    for shift_by, count, local_ids, usable_slot, source_ids in plans:
        selected = select_blocks(frame_both, local_ids, count, block, width)
        arrived = passed_along(selected, "tm", shift_by)
        received.append(arrived)
    key_all = jnp.concatenate([frame_both[0]] + [arrived[0] for arrived in received], axis=0)
    value_all = jnp.concatenate([frame_both[1]] + [arrived[1] for arrived in received], axis=0)
    out_s, grad_q, grad_k, grad_v = attend_whole(
        queries, key_all, value_all, out_grad, usable, inv_scale
    )
    accum = jnp.stack([grad_k[:frame_tok], grad_v[:frame_tok]]).reshape(2, 4, block, width)
    offset = frame_tok
    for shift_by, count, local_ids, usable_slot, source_ids in plans:
        span = count * block
        partial_pair = jnp.stack(
            [grad_k[offset : offset + span], grad_v[offset : offset + span]]
        ).astype(jnp.bfloat16)
        returned = passed_along(partial_pair, "tm", -shift_by)
        accum = accum.at[:, local_ids].add(
            returned.astype(jnp.float32).reshape(2, count, block, width)
        )
        offset = offset + span
    summed = lax.psum_scatter(
        accum.reshape(2, frame_tok, width), "space", scatter_dimension=1, tiled=True
    )
    return (out_s, grad_q, summed[0].astype(jnp.bfloat16), summed[1].astype(jnp.bfloat16))


def solution(mesh):
    placed = (
        P(("groups", "tm", "space"), None),
        P(("groups", "tm", "space"), None),
        P(("groups", "tm", "space"), None),
        P(("groups", "tm", "space"), None),
        P("groups", None),
    )
    return jax.shard_map(
        per_device,
        mesh=mesh,
        in_specs=placed,
        out_specs=(
            P(("groups", "tm", "space"), None),
            P(("groups", "tm", "space"), None),
            P(("groups", "tm", "space"), None),
            P(("groups", "tm", "space"), None),
        ),
        check_vma=False,
    )
```

profile of v0, /device:TPU:0, one launch (start us, length us, event | category | flops | bytes accessed | tf_op | source)
XLA Modules:
  0.0 218.2 jit_solution(15380573554906239329)
XLA Ops:
  25.5 5.7 %collective-permute-start = (bf16[2,512,256]{2,1,0:T(8,128)(2,1)}, bf16[2,512,256]{2,1,0:T(8,128)(2,1)}, u32[]{:S(2)}, u32[]{:S(2)}) collective-permute-start(bf16[2,512,256]{2,1,0:T(8,128)(2,1)} %bitcast.19), channel_id=1, source_target_pairs={{0,2},{2,4},{4,6},{6,8},{8,10},{10,12},{12,14},{1,3},{3,5},{5,7},{... | collective-permute-start | bytes 1572872 | tf_op jit(solution)/shard_map/ppermute | solution.py:15
  32.2 3.5 %collective-permute-start.1 = (bf16[2,256,256]{2,1,0:T(8,128)(2,1)}, bf16[2,256,256]{2,1,0:T(8,128)(2,1)}, u32[]{:S(2)}, u32[]{:S(2)}) collective-permute-start(bf16[2,256,256]{2,1,0:T(8,128)(2,1)} %get-tuple-element.201), channel_id=1, source_target_pairs={{0,4},{2,6},{4,8},{6,10},{8,12},{10,14},{1,5},{3,7},{5,9},{7,11},{... | collective-permute-start | bytes 786440 | tf_op jit(solution)/shard_map/ppermute | solution.py:15
  35.7 4.5 %collective-permute-start.2 = (bf16[2,256,256]{2,1,0:T(8,128)(2,1)}, bf16[2,256,256]{2,1,0:T(8,128)(2,1)}, u32[]{:S(2)}, u32[]{:S(2)}) collective-permute-start(bf16[2,256,256]{2,1,0:T(8,128)(2,1)} %get-tuple-element.200), channel_id=1, source_target_pairs={{0,8},{2,10},{4,12},{6,14},{1,9},{3,11},{5,13},{7,15},{16,24},{18,... | collective-permute-start | bytes 786440 | tf_op jit(solution)/shard_map/ppermute | solution.py:15
  47.5 1.7 fusion.52
  49.2 13.3 %collective-permute-done.4 = bf16[2,256,256]{2,1,0:T(8,128)(2,1)S(1)} collective-permute-done((bf16[2,256,256]{2,1,0:T(8,128)(2,1)}, bf16[2,256,256]{2,1,0:T(8,128)(2,1)S(1)}, u32[]{:S(2)}, u32[]{:S(2)}) %collective-permute-start.4) | collective-permute-done | bytes 262176 | tf_op jit(solution)/shard_map/ppermute | solution.py:15
  66.6 6.1 %collective-permute-done.5 = bf16[2,256,256]{2,1,0:T(8,128)(2,1)} collective-permute-done((bf16[2,256,256]{2,1,0:T(8,128)(2,1)}, bf16[2,256,256]{2,1,0:T(8,128)(2,1)}, u32[]{:S(2)}, u32[]{:S(2)}) %collective-permute-start.5) | collective-permute-done | bytes 262176 | tf_op jit(solution)/shard_map/ppermute | solution.py:15
  72.7 1.7 fusion.50
  82.7 1.9 fusion.49
  84.5 1.8 copy.52
  86.3 1.9 fusion.48
  88.2 1.8 copy.56
  90.0 1.8 copy.59
  91.7 1.8 copy.62
  98.6 40.4 %while.21 = (s32[]{:T(128)}, bf16[2,512,128]{1,2,0:T(8,128)(2,1)}, bf16[2,512,128]{2,1,0:T(8,128)(2,1)}, f32[2,3072,128]{1,2,0:T(8,128)}, f32[2,3072,128]{1,2,0:...) while((s32[]{:T(128)}, bf16[2,512,128]{1,2,0:T(8,128)(2,1)}, ...), condition=%wide.region_4.7_spmd, body=%wide.region_0.0_spmd.sunk | while | flops 2441935360 | bytes 148009456 | solution.py:61
  98.8 2.2 %fusion.80 = (f32[512]{0:T(512)S(1)}, f32[512,3072]{1,0:T(8,128)S(1)}) fusion(pred[3072]{0:T(1024)(128)(4,1)S(1)} %get-tuple-element.327, bf16[2,3072,128]{1,2,0:T(8,128)(2,1)S(1)} %get-tuple-element.329, s32[]{:T(128)S(6)} %copy.133, bf16[2,512,128]{1,2,0:T(8,128)(2,1)} %get-tuple-element.328), kind=kOutput, calls=%fused_computation.7.clone.1 | convolution fusion | flops 407371264 | bytes 7215104 | tf_op jit(solution)/shard_map/while/body/eval_jaxpr/dot_general | solution.py:19
  102.5 1.8 fusion.82
  113.7 3.5 %fusion.85 = f32[2,3072,128]{1,2,0:T(8,128)S(1)} fusion(f32[2,3072,128]{1,2,0:T(8,128)S(1)} %copy-done.8, s32[]{:T(128)S(6)} %copy.133, f32[512,3072]{1,0:T(8,128)} %copy-done, bf16[2,512,128]{1,2,0:T(8,128)(2,1)S(1)} %get-tuple-element.331), kind=kOutput, calls=%fused_computation.11.clone.1 | convolution fusion | flops 404226048 | bytes 7996416 | tf_op jit(solution)/shard_map/while/body/eval_jaxpr/dot_general | solution.py:39
  117.2 1.7 copy-done.9
  118.9 2.2 %fusion.80 = (f32[512]{0:T(512)S(1)}, f32[512,3072]{1,0:T(8,128)S(1)}) fusion(pred[3072]{0:T(1024)(128)(4,1)S(1)} %get-tuple-element.327, bf16[2,3072,128]{1,2,0:T(8,128)(2,1)S(1)} %get-tuple-element.329, s32[]{:T(128)S(6)} %copy.133, bf16[2,512,128]{1,2,0:T(8,128)(2,1)} %get-tuple-element.328), kind=kOutput, calls=%fused_computation.7.clone.1 | convolution fusion | flops 407371264 | bytes 7215104 | tf_op jit(solution)/shard_map/while/body/eval_jaxpr/dot_general | solution.py:19
  122.5 1.8 fusion.82
  133.8 3.5 %fusion.85 = f32[2,3072,128]{1,2,0:T(8,128)S(1)} fusion(f32[2,3072,128]{1,2,0:T(8,128)S(1)} %copy-done.8, s32[]{:T(128)S(6)} %copy.133, f32[512,3072]{1,0:T(8,128)} %copy-done, bf16[2,512,128]{1,2,0:T(8,128)(2,1)S(1)} %get-tuple-element.331), kind=kOutput, calls=%fused_computation.11.clone.1 | convolution fusion | flops 404226048 | bytes 7996416 | tf_op jit(solution)/shard_map/while/body/eval_jaxpr/dot_general | solution.py:39
  139.0 2.2 %bitcast_convert_fusion = bf16[3072,2,128]{0,2,1:T(8,128)(2,1)S(1)} fusion(f32[2,3072,128]{1,2,0:T(8,128)} %get-tuple-element.112), kind=kLoop, calls=%fused_computation.127 | loop fusion | flops 786432 | bytes 4718592 | tf_op jit(solution)/shard_map/convert.41
  144.6 2.3 %slice.346 = f32[1024,2,128]{0,2,1:T(8,128)} slice(f32[3072,2,128]{0,2,1:T(8,128)} %bitcast.209), slice={[0:1024], [0:2], [0:128]} | slice | bytes 2097152 | tf_op jit(solution)/shard_map/slice | solution.py:125
  146.9 2.7 %reshape.615 = f32[1,4,256,256]{2,1,3,0:T(4,128)} reshape(f32[1024,2,128]{0,2,1:T(8,128)} %slice.346) | data formatting | bytes 2097152 | tf_op jit(solution)/shard_map/stack | solution.py:125
  149.6 2.5 %copy.90 = f32[1,4,256,256]{3,2,1,0:T(8,128)} copy(f32[1,4,256,256]{2,1,3,0:T(4,128)} %reshape.615) | data formatting | bytes 2097152 | tf_op jit(solution)/shard_map/stack | solution.py:125
  153.2 1.8 reshape.614
  163.9 5.3 %collective-permute-start.9 = (bf16[2,512,256]{1,2,0:T(8,128)(2,1)}, bf16[2,512,256]{1,2,0:T(8,128)(2,1)}, u32[]{:S(2)}, u32[]{:S(2)}) collective-permute-start(bf16[2,512,256]{1,2,0:T(8,128)(2,1)} %pad_maximum_fusion.3), channel_id=1, source_target_pairs={{0,2},{2,4},{4,6},{6,8},{8,10},{10,12},{12,14},{1,3},{3,5},{5,7},{... | collective-permute-start | bytes 1572872 | tf_op jit(solution)/shard_map/ppermute | solution.py:15
  170.2 4.5 %collective-permute-start.10 = (bf16[2,256,256]{2,1,0:T(8,128)(2,1)}, bf16[2,256,256]{2,1,0:T(8,128)(2,1)}, u32[]{:S(2)}, u32[]{:S(2)}) collective-permute-start(bf16[2,256,256]{2,1,0:T(8,128)(2,1)} %pad_maximum_fusion.6), channel_id=1, source_target_pairs={{0,4},{2,6},{4,8},{6,10},{8,12},{10,14},{1,5},{3,7},{5,9},{7,11},{... | collective-permute-start | bytes 786440 | tf_op jit(solution)/shard_map/ppermute | solution.py:15
  177.0 5.4 %collective-permute-start.11 = (bf16[2,256,256]{2,1,0:T(8,128)(2,1)}, bf16[2,256,256]{2,1,0:T(8,128)(2,1)S(1)}, u32[]{:S(2)}, u32[]{:S(2)}) collective-permute-start(bf16[2,256,256]{2,1,0:T(8,128)(2,1)} %pad_maximum_fusion.7), channel_id=1, source_target_pairs={{0,8},{2,10},{4,12},{6,14},{1,9},{3,11},{5,13},{7,15},{16,24},{18,... | collective-permute-start | bytes 786440 | tf_op jit(solution)/shard_map/ppermute | solution.py:15
  182.4 2.2 %copy.76 = f32[2,512,256]{2,1,0:T(8,128)} copy(bf16[2,512,256]{1,2,0:T(8,128)(2,1)} %collective-permute-done.6) | data formatting | bytes 1572864 | tf_op jit(solution)/shard_map/reshape | solution.py:134
  190.3 2.2 %copy.82 = f32[2,512,256]{2,1,0:T(8,128)} copy(bf16[2,512,256]{1,2,0:T(8,128)(2,1)} %collective-permute-done.9) | data formatting | bytes 1572864 | tf_op jit(solution)/shard_map/reshape | solution.py:134
  200.2 9.0 %reduce-scatter.2.cloned.1.call-done = f32[2,512,256]{2,1,0:T(8,128)} async-done(((f32[2,1024,256]{2,1,0:T(8,128)}), f32[2,512,256]{2,1,0:T(8,128)}) %reduce-scatter.2.cloned.1.call-update) | async-done | bytes 1048592 | tf_op jit(solution)/shard_map/reduce_scatter | solution.py:137
  (244 shorter events, 93.8 us)
Async XLA Ops:
  7.2 13.8 %copy-start.37 = (s32[4]{0:T(128)S(1)}, s32[4]{0:T(128)}, u32[]{:S(2)}) copy-start(s32[4]{0:T(128)} %constant.192.clone.1) | copy-start | bytes 52
  7.2 7.0 %copy-start.28 = (bf16[512,256]{1,0:T(8,128)(2,1)S(1)}, bf16[512,256]{1,0:T(8,128)(2,1)}, u32[]{:S(2)}) copy-start(bf16[512,256]{1,0:T(8,128)(2,1)} %param.19) | copy-start | bytes 786436
  7.2 12.3 %copy-start.29 = (bf16[512,256]{1,0:T(8,128)(2,1)S(1)}, bf16[512,256]{1,0:T(8,128)(2,1)}, u32[]{:S(2)}) copy-start(bf16[512,256]{1,0:T(8,128)(2,1)} %param.22) | copy-start | bytes 786436
  7.2 15.3 %all-gather.2.cloned.1.call-start = ((), (), s32[]{:S(2)}) async-start(), calls=%async_computation.1 | async-start | bytes 1572864 | tf_op jit(solution)/shard_map/all_gather | solution.py:114
  10.4 198.9 %reduce-scatter.2.cloned.1.call-start = ((), (), s32[]{:S(2)}) async-start(), calls=%async_computation.2 | async-start | bytes 3145728 | tf_op jit(solution)/shard_map/reduce_scatter | solution.py:137
  25.5 57.1 %collective-permute-start = (bf16[2,512,256]{2,1,0:T(8,128)(2,1)}, bf16[2,512,256]{2,1,0:T(8,128)(2,1)}, u32[]{:S(2)}, u32[]{:S(2)}) collective-permute-start(bf16[2,512,256]{2,1,0:T(8,128)(2,1)} %bitcast.19), channel_id=1, source_target_pairs={{0,2},{2,4},{4,6},{6,8},{8,10},{10,12},{12,14},{1,3},{3,5},{5,7},{... | collective-permute-start | bytes 1572872 | tf_op jit(solution)/shard_map/ppermute | solution.py:15
  32.2 12.2 %copy-start.10 = (bf16[2,1024,256]{1,2,0:T(8,128)(2,1)S(1)}, bf16[2,1024,256]{1,2,0:T(8,128)(2,1)}, u32[]{:S(2)}) copy-start(bf16[2,1024,256]{1,2,0:T(8,128)(2,1)} %all-gather.2.cloned.1.call-done) | copy-start | bytes 3145732
  32.2 12.4 %collective-permute-start.1 = (bf16[2,256,256]{2,1,0:T(8,128)(2,1)}, bf16[2,256,256]{2,1,0:T(8,128)(2,1)}, u32[]{:S(2)}, u32[]{:S(2)}) collective-permute-start(bf16[2,256,256]{2,1,0:T(8,128)(2,1)} %get-tuple-element.201), channel_id=1, source_target_pairs={{0,4},{2,6},{4,8},{6,10},{8,12},{10,14},{1,5},{3,7},{5,9},{7,11},{... | collective-permute-start | bytes 786440 | tf_op jit(solution)/shard_map/ppermute | solution.py:15
  35.7 11.7 %collective-permute-start.2 = (bf16[2,256,256]{2,1,0:T(8,128)(2,1)}, bf16[2,256,256]{2,1,0:T(8,128)(2,1)}, u32[]{:S(2)}, u32[]{:S(2)}) collective-permute-start(bf16[2,256,256]{2,1,0:T(8,128)(2,1)} %get-tuple-element.200), channel_id=1, source_target_pairs={{0,8},{2,10},{4,12},{6,14},{1,9},{3,11},{5,13},{7,15},{16,24},{18,... | collective-permute-start | bytes 786440 | tf_op jit(solution)/shard_map/ppermute | solution.py:15
  41.8 44.5 %collective-permute-start.3 = (bf16[2,512,256]{2,1,0:T(8,128)(2,1)}, bf16[2,512,256]{2,1,0:T(8,128)(2,1)}, u32[]{:S(2)}, u32[]{:S(2)}) collective-permute-start(bf16[2,512,256]{2,1,0:T(8,128)(2,1)} %bitcast.33), channel_id=1, source_target_pairs={{2,0},{4,2},{6,4},{8,6},{10,8},{12,10},{14,12},{3,1},{5,3},{7,5},{... | collective-permute-start | bytes 1572872 | tf_op jit(solution)/shard_map/ppermute | solution.py:15
  43.1 19.4 %collective-permute-start.4 = (bf16[2,256,256]{2,1,0:T(8,128)(2,1)}, bf16[2,256,256]{2,1,0:T(8,128)(2,1)S(1)}, u32[]{:S(2)}, u32[]{:S(2)}) collective-permute-start(bf16[2,256,256]{2,1,0:T(8,128)(2,1)} %get-tuple-element.199), channel_id=1, source_target_pairs={{4,0},{6,2},{8,4},{10,6},{12,8},{14,10},{5,1},{7,3},{9,5},{11,7},{... | collective-permute-start | bytes 786440 | tf_op jit(solution)/shard_map/ppermute | solution.py:15
  44.6 28.1 %collective-permute-start.5 = (bf16[2,256,256]{2,1,0:T(8,128)(2,1)}, bf16[2,256,256]{2,1,0:T(8,128)(2,1)}, u32[]{:S(2)}, u32[]{:S(2)}) collective-permute-start(bf16[2,256,256]{2,1,0:T(8,128)(2,1)} %get-tuple-element.198), channel_id=1, source_target_pairs={{8,0},{10,2},{12,4},{14,6},{9,1},{11,3},{13,5},{15,7},{24,16},{26,... | collective-permute-start | bytes 786440 | tf_op jit(solution)/shard_map/ppermute | solution.py:15
  98.8 8.0 %copy-start.1 = (bf16[2,3072,128]{1,2,0:T(8,128)(2,1)}, bf16[2,3072,128]{1,2,0:T(8,128)(2,1)S(1)}, u32[]{:S(2)}) copy-start(bf16[2,3072,128]{1,2,0:T(8,128)(2,1)S(1)} %get-tuple-element.330) | copy-start | bytes 4718596 | tf_op jit(solution)/shard_map/while
  98.8 9.2 %copy-start.4 = (bf16[2,3072,128]{1,2,0:T(8,128)(2,1)}, bf16[2,3072,128]{1,2,0:T(8,128)(2,1)S(1)}, u32[]{:S(2)}) copy-start(bf16[2,3072,128]{1,2,0:T(8,128)(2,1)S(1)} %get-tuple-element.329) | copy-start | bytes 4718596 | tf_op jit(solution)/shard_map/while
  113.7 5.2 %copy-start.2 = (bf16[2,3072,128]{1,2,0:T(8,128)(2,1)S(1)}, bf16[2,3072,128]{1,2,0:T(8,128)(2,1)}, u32[]{:S(2)}) copy-start(bf16[2,3072,128]{1,2,0:T(8,128)(2,1)} %copy-done.1) | copy-start | bytes 4718596 | tf_op jit(solution)/shard_map/while
  113.7 5.2 %copy-start.5 = (bf16[2,3072,128]{1,2,0:T(8,128)(2,1)S(1)}, bf16[2,3072,128]{1,2,0:T(8,128)(2,1)}, u32[]{:S(2)}) copy-start(bf16[2,3072,128]{1,2,0:T(8,128)(2,1)} %copy-done.4) | copy-start | bytes 4718596 | tf_op jit(solution)/shard_map/while
  118.9 8.0 %copy-start.1 = (bf16[2,3072,128]{1,2,0:T(8,128)(2,1)}, bf16[2,3072,128]{1,2,0:T(8,128)(2,1)S(1)}, u32[]{:S(2)}) copy-start(bf16[2,3072,128]{1,2,0:T(8,128)(2,1)S(1)} %get-tuple-element.330) | copy-start | bytes 4718596 | tf_op jit(solution)/shard_map/while
  118.9 9.1 %copy-start.4 = (bf16[2,3072,128]{1,2,0:T(8,128)(2,1)}, bf16[2,3072,128]{1,2,0:T(8,128)(2,1)S(1)}, u32[]{:S(2)}) copy-start(bf16[2,3072,128]{1,2,0:T(8,128)(2,1)S(1)} %get-tuple-element.329) | copy-start | bytes 4718596 | tf_op jit(solution)/shard_map/while
  133.8 5.2 %copy-start.5 = (bf16[2,3072,128]{1,2,0:T(8,128)(2,1)S(1)}, bf16[2,3072,128]{1,2,0:T(8,128)(2,1)}, u32[]{:S(2)}) copy-start(bf16[2,3072,128]{1,2,0:T(8,128)(2,1)} %copy-done.4) | copy-start | bytes 4718596 | tf_op jit(solution)/shard_map/while
  154.9 5.8 %copy-start.24 = (bf16[256,2,128]{0,2,1:T(8,128)(2,1)S(1)}, bf16[256,2,128]{0,2,1:T(8,128)(2,1)}, u32[]{:S(2)}) copy-start(bf16[256,2,128]{0,2,1:T(8,128)(2,1)} %get-tuple-element.190) | copy-start | bytes 393220
  155.0 5.9 %copy-start.25 = (bf16[256,2,128]{0,2,1:T(8,128)(2,1)S(1)}, bf16[256,2,128]{0,2,1:T(8,128)(2,1)}, u32[]{:S(2)}) copy-start(bf16[256,2,128]{0,2,1:T(8,128)(2,1)} %get-tuple-element.186) | copy-start | bytes 393220
  156.3 6.7 %copy-start.14 = (bf16[512,2,128]{0,2,1:T(8,128)(2,1)S(1)}, bf16[512,2,128]{0,2,1:T(8,128)(2,1)}, u32[]{:S(2)}) copy-start(bf16[512,2,128]{0,2,1:T(8,128)(2,1)} %get-tuple-element.192) | copy-start | bytes 786436
  156.3 12.9 %copy-start.22 = (bf16[256,2,128]{0,2,1:T(8,128)(2,1)S(1)}, bf16[256,2,128]{0,2,1:T(8,128)(2,1)}, u32[]{:S(2)}) copy-start(bf16[256,2,128]{0,2,1:T(8,128)(2,1)} %get-tuple-element.189) | copy-start | bytes 393220
  156.3 13.0 %copy-start.23 = (bf16[256,2,128]{0,2,1:T(8,128)(2,1)S(1)}, bf16[256,2,128]{0,2,1:T(8,128)(2,1)}, u32[]{:S(2)}) copy-start(bf16[256,2,128]{0,2,1:T(8,128)(2,1)} %get-tuple-element.185) | copy-start | bytes 393220
  157.2 19.8 %collective-permute-start.6 = (bf16[2,512,256]{1,2,0:T(8,128)(2,1)}, bf16[2,512,256]{1,2,0:T(8,128)(2,1)}, u32[]{:S(2)}, u32[]{:S(2)}) collective-permute-start(bf16[2,512,256]{1,2,0:T(8,128)(2,1)} %pad_maximum_fusion.2), channel_id=1, source_target_pairs={{2,0},{4,2},{6,4},{8,6},{10,8},{12,10},{14,12},{3,1},{5,3},{7,5},{... | collective-permute-start | bytes 1572872 | tf_op jit(solution)/shard_map/ppermute | solution.py:15
  158.6 16.1 %copy-start.21 = (bf16[256,2,128]{0,2,1:T(8,128)(2,1)S(1)}, bf16[256,2,128]{0,2,1:T(8,128)(2,1)}, u32[]{:S(2)}) copy-start(bf16[256,2,128]{0,2,1:T(8,128)(2,1)} %get-tuple-element.184) | copy-start | bytes 393220
  158.7 16.1 %copy-start.11 = (f32[1,4,256,256]{3,2,1,0:T(8,128)S(1)}, f32[1,4,256,256]{3,2,1,0:T(8,128)}, u32[]{:S(2)}) copy-start(f32[1,4,256,256]{3,2,1,0:T(8,128)} %copy.90) | copy-start | bytes 3145732
  159.5 27.5 %collective-permute-start.7 = (bf16[2,256,256]{2,1,0:T(8,128)(2,1)}, bf16[2,256,256]{2,1,0:T(8,128)(2,1)}, u32[]{:S(2)}, u32[]{:S(2)}) collective-permute-start(bf16[2,256,256]{2,1,0:T(8,128)(2,1)} %pad_maximum_fusion.4), channel_id=1, source_target_pairs={{4,0},{6,2},{8,4},{10,6},{12,8},{14,10},{5,1},{7,3},{9,5},{11,7},{... | collective-permute-start | bytes 786440 | tf_op jit(solution)/shard_map/ppermute | solution.py:15
  161.7 26.9 %collective-permute-start.8 = (bf16[2,256,256]{2,1,0:T(8,128)(2,1)}, bf16[2,256,256]{2,1,0:T(8,128)(2,1)}, u32[]{:S(2)}, u32[]{:S(2)}) collective-permute-start(bf16[2,256,256]{2,1,0:T(8,128)(2,1)} %pad_maximum_fusion.5), channel_id=1, source_target_pairs={{8,0},{10,2},{12,4},{14,6},{9,1},{11,3},{13,5},{15,7},{24,16},{26,... | collective-permute-start | bytes 786440 | tf_op jit(solution)/shard_map/ppermute | solution.py:15
  163.9 26.4 %collective-permute-start.9 = (bf16[2,512,256]{1,2,0:T(8,128)(2,1)}, bf16[2,512,256]{1,2,0:T(8,128)(2,1)}, u32[]{:S(2)}, u32[]{:S(2)}) collective-permute-start(bf16[2,512,256]{1,2,0:T(8,128)(2,1)} %pad_maximum_fusion.3), channel_id=1, source_target_pairs={{0,2},{2,4},{4,6},{6,8},{8,10},{10,12},{12,14},{1,3},{3,5},{5,7},{... | collective-permute-start | bytes 1572872 | tf_op jit(solution)/shard_map/ppermute | solution.py:15
  170.2 24.7 %collective-permute-start.10 = (bf16[2,256,256]{2,1,0:T(8,128)(2,1)}, bf16[2,256,256]{2,1,0:T(8,128)(2,1)}, u32[]{:S(2)}, u32[]{:S(2)}) collective-permute-start(bf16[2,256,256]{2,1,0:T(8,128)(2,1)} %pad_maximum_fusion.6), channel_id=1, source_target_pairs={{0,4},{2,6},{4,8},{6,10},{8,12},{10,14},{1,5},{3,7},{5,9},{7,11},{... | collective-permute-start | bytes 786440 | tf_op jit(solution)/shard_map/ppermute | solution.py:15
  177.0 19.5 %collective-permute-start.11 = (bf16[2,256,256]{2,1,0:T(8,128)(2,1)}, bf16[2,256,256]{2,1,0:T(8,128)(2,1)S(1)}, u32[]{:S(2)}, u32[]{:S(2)}) collective-permute-start(bf16[2,256,256]{2,1,0:T(8,128)(2,1)} %pad_maximum_fusion.7), channel_id=1, source_target_pairs={{0,8},{2,10},{4,12},{6,14},{1,9},{3,11},{5,13},{7,15},{16,24},{18,... | collective-permute-start | bytes 786440 | tf_op jit(solution)/shard_map/ppermute | solution.py:15
  (32 other events, 90.5 us)
Sparse Core Ops, SparseCore 0:
  10.5 11.7 all-gather.1
  198.8 10.4 reduce-scatter.1
where the time goes:
time: 220 us; the launch traced here: 218 us
  local copies, waits for them, and re-layouts  85 us (39%)
  starting transfers between devices  36.7 us (17%)
  waiting for transfers between devices  28.5 us (13%)
  other arithmetic  27.8 us (13%)
  matrix products  19.9 us (9%)
  between operations  19.7 us (9%)
    ppermute x12, starting transfers between devices, passed_along(): lax.ppermute(value, axis, [(source, source + steps) for source in range(i...  36.7 us
    slice x12, local copies, waits for them, and re-layouts, per_device(): arrived[1]  19.6 us
    ppermute x12, waiting for transfers between devices, passed_along(): lax.ppermute(value, axis, [(source, source + steps) for source in range(i...  19.4 us
    while x48, local copies, waits for them, and re-layouts  9.96 us
    unnamed x74, local copies, waits for them, and re-layouts  9.84 us
    reduce_scatter x1, waiting for transfers between devices, per_device(): lax.psum_scatter(accum.reshape(2, frame_tok, width), 'space', scatter_dim...  9.02 us
    slice x6, local copies, waits for them, and re-layouts, per_device(): arrived[0]  8.65 us
    another operation x4, local copies, waits for them, and re-layouts, per_device(): jnp.stack([grad_k[:frame_tok], grad_v[:frame_tok]])  8.31 us
  transfers between devices with their start and end apart: 14, of which 3 were waited for; matrix products, arithmetic and copies ran while one was open for 24% of the time, Pallas kernels for 0%

commit v1 on v0

v1 whole, which is shorter than its diff:
```python
import functools
import math

import jax
import jax.numpy as jnp
from jax import lax
from jax.experimental import pallas as pl
from jax.experimental.pallas import tpu as pltpu
from jax.sharding import PartitionSpec as P

DH = 128
HEADS = 2
F32 = jnp.float32
BF16 = jnp.bfloat16
VMEM = pl.BlockSpec(memory_space=pltpu.VMEM)
SMEM = pl.BlockSpec(memory_space=pltpu.SMEM)
NEG = -1e30


def dot_nn(a, b):
    return lax.dot_general(a, b, (((1,), (0,)), ((), ())), preferred_element_type=F32)


def dot_nt(a, b):
    return lax.dot_general(a, b, (((1,), (1,)), ((), ())), preferred_element_type=F32)


def dot_tn(a, b):
    return lax.dot_general(a, b, (((0,), (0,)), ((), ())), preferred_element_type=F32)


def partner_pairs(count, distance, second):
    pairs = []
    for frame in range(count):
        up = ((frame // distance) % 2 == 0) != second
        target = frame + distance if up else frame - distance
        pairs.append((frame, target if 0 <= target < count else frame))
    return pairs


def exchanges(count):
    levels = count.bit_length() - 1
    found = []
    for level in range(levels):
        for second in (False, True):
            pairs = partner_pairs(count, 1 << level, second)
            if all(source == target for source, target in pairs):
                continue
            found.append((level, second, 2 if level == 0 else 1, pairs))
    return found


def exchange_partner(tm_index, count, level, second):
    odd = lax.rem(lax.shift_right_logical(tm_index, level), 2)
    goes_up = odd == (1 if second else 0)
    partner = jnp.where(goes_up, tm_index + (1 << level), tm_index - (1 << level))
    exists = jnp.logical_and(partner >= 0, partner < count)
    return partner, goes_up, exists


def slot_of(goes_up, level, k, levels):
    return jnp.where(goes_up, levels + 1, 0) + (0 if level == 0 else level + 1) + k


def wanted_blocks(lists_ref, tm_index, space_index, count, n_space, level, second, k):
    levels = count.bit_length() - 1
    partner, goes_up, exists = exchange_partner(tm_index, count, level, second)
    row = jnp.where(exists, partner, tm_index) * n_space + space_index
    slot = slot_of(jnp.logical_not(goes_up), level, k, levels)
    entry = lists_ref[row, slot]
    return jnp.clip(entry - tm_index * 4, 0, 3), exists


def select_kernel(plan, count, n_space, block, lists, k_own, v_own, k_oth, v_oth, *outs):
    tm_index = lax.axis_index("tm")
    space_index = lax.axis_index("space")
    width = k_own.shape[1]
    per_half = k_own.shape[0] // block
    for (level, second, blocks, _), out in zip(plan, outs):
        for k in range(blocks):
            b, _ = wanted_blocks(lists, tm_index, space_index, count, n_space, level, second, k)
            half = b // per_half
            row = pl.multiple_of((b - half * per_half) * block, block)
            rows = pl.ds(k * block, block)

            @pl.when(half == space_index)
            def _():
                out[rows, :width] = k_own[pl.ds(row, block), :]
                out[rows, width:] = v_own[pl.ds(row, block), :]

            @pl.when(half != space_index)
            def _():
                out[rows, :width] = k_oth[pl.ds(row, block), :]
                out[rows, width:] = v_oth[pl.ds(row, block), :]


def attend_kernel(plan, count, n_space, block, *refs):
    n_far = len(plan)
    lists, q_ref, g_ref, k_own, v_own, k_oth, v_oth = refs[:7]
    far = refs[7 : 7 + n_far]
    o_ref, dq_ref, near_own, near_oth = refs[7 + n_far : 11 + n_far]
    far_out = refs[11 + n_far : 11 + 2 * n_far]
    s_ref, e_ref = refs[11 + 2 * n_far :]
    tm_index = lax.axis_index("tm")
    width = q_ref.shape[1]
    scale = 1.0 / math.sqrt(DH)
    log2e = scale * math.log2(math.e)
    half = k_own.shape[0]

    pieces = []
    for k_ref, v_ref, out in ((k_own, v_own, near_own), (k_oth, v_oth, near_oth)):
        for r in range(0, half, block):
            pieces.append((k_ref, 0, v_ref, 0, r, out, None))
    for (level, second, blocks, _), ref, out in zip(plan, far, far_out):
        _, _, exists = exchange_partner(tm_index, count, level, second)
        for k in range(blocks):
            pieces.append((ref, 0, ref, width, k * block, out, exists))

    for h in range(HEADS):
        cols = slice(h * DH, (h + 1) * DH)
        q = q_ref[:, cols]
        g = g_ref[:, cols]
        top = None
        for j, (k_ref, k_at, _, _, r, _, exists) in enumerate(pieces):
            s = dot_nt(q, k_ref[r : r + block, k_at + h * DH : k_at + (h + 1) * DH])
            if exists is not None:
                s = jnp.where(exists, s, NEG)
            s_ref[j] = s
            for c in range(0, block, DH):
                part = s[:, c : c + DH]
                top = part if top is None else jnp.maximum(top, part)
        peak = jnp.max(top, axis=1, keepdims=True)
        total = None
        acc = None
        for j, (_, _, v_ref, v_at, r, _, _) in enumerate(pieces):
            e = jnp.exp2((s_ref[j] - peak) * log2e)
            for c in range(0, block, DH):
                part = e[:, c : c + DH]
                total = part if total is None else total + part
            eb = e.astype(BF16)
            e_ref[j] = eb
            out = dot_nn(eb, v_ref[r : r + block, v_at + h * DH : v_at + (h + 1) * DH])
            acc = out if acc is None else acc + out
        inv = 1.0 / jnp.sum(total, axis=1, keepdims=True)
        o = (acc * inv).astype(BF16)
        o_ref[:, cols] = o
        gs = (g.astype(F32) * inv).astype(BF16)
        row_dot = jnp.sum(gs.astype(F32) * o.astype(F32), axis=1, keepdims=True)
        dq = None
        for j, (k_ref, k_at, v_ref, v_at, r, out, _) in enumerate(pieces):
            k_blk = k_ref[r : r + block, k_at + h * DH : k_at + (h + 1) * DH]
            v_blk = v_ref[r : r + block, v_at + h * DH : v_at + (h + 1) * DH]
            gp = dot_nt(gs, v_blk)
            eb = e_ref[j]
            ds = (eb.astype(F32) * (gp - row_dot)).astype(BF16)
            part = dot_nn(ds, k_blk)
            dq = part if dq is None else dq + part
            dk = dot_tn(ds, q) * scale
            dv = dot_tn(eb, gs)
            out[r : r + block, h * DH : (h + 1) * DH] = dk.astype(out.dtype)
            out[r : r + block, width + h * DH : width + (h + 1) * DH] = dv.astype(out.dtype)
        dq_ref[:, cols] = (dq * scale).astype(BF16)


def gather_kernel(plan, count, n_space, block, *refs):
    n_far = len(plan)
    lists, near_own, near_oth = refs[:3]
    back = refs[3 : 3 + n_far]
    keep, send = refs[3 + n_far : 5 + n_far]
    acc = refs[5 + n_far]
    tm_index = lax.axis_index("tm")
    space_index = lax.axis_index("space")
    half = near_own.shape[0]
    per_half = half // block
    own_at = pl.multiple_of(space_index * half, half)
    oth_at = pl.multiple_of((1 - space_index) * half, half)
    acc[pl.ds(own_at, half), :] = near_own[...]
    acc[pl.ds(oth_at, half), :] = near_oth[...]
    for (level, second, blocks, _), ref in zip(plan, back):
        for k in range(blocks):
            b, exists = wanted_blocks(lists, tm_index, space_index, count, n_space, level, second, k)
            rows = pl.ds(pl.multiple_of(b * block, block), block)

            @pl.when(exists)
            def _():
                acc[rows, :] += ref[k * block : (k + 1) * block, :].astype(F32)

    keep[...] = acc[pl.ds(own_at, half), :]
    send[...] = acc[pl.ds(oth_at, half), :].astype(BF16)


def finish_kernel(keep, came, dk_ref, dv_ref):
    width = dk_ref.shape[1]
    total = keep[...] + came[...].astype(F32)
    dk_ref[...] = total[:, :width].astype(BF16)
    dv_ref[...] = total[:, width:].astype(BF16)


def call(kernel, ins, out_shape, scratch=(), flops=0, traffic=4 << 20):
    return pl.pallas_call(
        kernel,
        out_shape=out_shape,
        in_specs=ins,
        out_specs=tuple(VMEM for _ in out_shape),
        scratch_shapes=list(scratch),
        compiler_params=pltpu.CompilerParams(vmem_limit_bytes=48 << 20),
        cost_estimate=pl.CostEstimate(flops=flops, bytes_accessed=traffic, transcendentals=0),
    )


def per_device(queries, key_rows, value_rows, out_grad, block_lists):
    s_dev, width = queries.shape
    n_space = lax.axis_size("space")
    count = lax.axis_size("tm")
    block = s_dev * n_space // 4
    plan = exchanges(count)
    n_far = len(plan)
    sds = jax.ShapeDtypeStruct
    common = (plan, count, n_space, block)

    def across(value):
        return lax.ppermute(value, "space", [(0, 1), (1, 0)])

    k_oth = across(key_rows)
    v_oth = across(value_rows)
    sends = call(
        functools.partial(select_kernel, *common),
        [SMEM] + [VMEM] * 4,
        [sds((p[2] * block, 2 * width), BF16) for p in plan],
    )(block_lists, key_rows, value_rows, k_oth, v_oth)
    far = [lax.ppermute(value, "tm", p[3]) for value, p in zip(sends, plan)]
    n_pieces = 2 * s_dev // block + sum(p[2] for p in plan)
    results = call(
        functools.partial(attend_kernel, *common),
        [SMEM] + [VMEM] * (6 + n_far),
        [sds((s_dev, width), BF16)] * 2
        + [sds((s_dev, 2 * width), F32)] * 2
        + [sds((p[2] * block, 2 * width), BF16) for p in plan],
        scratch=[
            pltpu.VMEM((n_pieces, s_dev, block), F32),
            pltpu.VMEM((n_pieces, s_dev, block), BF16),
        ],
        flops=12 * s_dev * n_pieces * block * width,
        traffic=12 << 20,
    )(block_lists, queries, out_grad, key_rows, value_rows, k_oth, v_oth, *far)
    attn_out, grad_q, near_own, near_oth = results[:4]
    back = [lax.ppermute(value, "tm", p[3]) for value, p in zip(results[4:], plan)]
    keep, send = call(
        functools.partial(gather_kernel, *common),
        [SMEM] + [VMEM] * (2 + n_far),
        [sds((s_dev, 2 * width), F32), sds((s_dev, 2 * width), BF16)],
        scratch=[pltpu.VMEM((2 * s_dev, 2 * width), F32)],
    )(block_lists, near_own, near_oth, *back)
    grad_k, grad_v = call(
        finish_kernel, [VMEM] * 2, [sds((s_dev, width), BF16)] * 2
    )(keep, across(send))
    return attn_out, grad_q, grad_k, grad_v


def solution(mesh):
    rows = P(("groups", "tm", "space"), None)
    return jax.shard_map(
        per_device,
        mesh=mesh,
        in_specs=(rows, rows, rows, rows, P("groups", None)),
        out_specs=(rows, rows, rows, rows),
        check_vma=False,
    )
```

time: 220 us -> 97.3 us (0.44)
  local copies, waits for them, and re-layouts: 85 us -> 5.11 us
  other arithmetic: 27.8 us -> 0 us
  waiting for transfers between devices: 28.5 us -> 50.5 us
  matrix products: 19.9 us -> 0 us
  Pallas kernels: 0 us -> 19.6 us
  between operations: 19.7 us -> 0.71 us
  starting transfers between devices: 36.7 us -> 21 us
    slice x30 -> x0, local copies, waits for them, and re-layouts: 37.4 us -> none  [the longest x12 19.6 us: per_device(): arrived[1]]
    ppermute x12 -> x13, waiting for transfers between devices: 19.4 us -> 50.5 us  [the longest x5 24.9 us: per_device(): far = [lax.ppermute(value, 'tm', p[3]) for value, p in zip(sends, plan)]]
    dot_general x12 -> x0, matrix products: 19.9 us -> none  [the longest x2 7.02 us: backward_head(): grad_v = jnp.dot(attn_bf.T, grad_h, preferred_element_type=jnp.float32)]
    pallas_call x0 -> x4, Pallas kernels: none -> 19.6 us  [the longest x1 16.5 us: per_device(): call(functools.partial(attend_kernel, *common), [SMEM] + [VMEM] * (6 + n_...]
    ppermute x12 -> x13, starting transfers between devices: 36.7 us -> 21 us  [the longest x5 11.4 us: per_device(): far = [lax.ppermute(value, 'tm', p[3]) for value, p in zip(sends, plan)]]
    another operation x17 -> x0, other arithmetic: 12 us -> none
    while x48 -> x0, local copies, waits for them, and re-layouts: 9.96 us -> none
    another operation x12 -> x0, local copies, waits for them, and re-layouts: 9.1 us -> none  [the longest x4 8.31 us: per_device(): jnp.stack([grad_k[:frame_tok], grad_v[:frame_tok]])]
  transfers between devices with their start and end apart: 14 -> 13, of which waited for: 3 -> 7; matrix products, arithmetic and copies ran while one was open for 24% -> 1% of each run, Pallas kernels for 0% -> 0%
where the time goes in v1:
time: 97.3 us; the launch traced here: 96.9 us
  waiting for transfers between devices  50.5 us (52%)
  starting transfers between devices  21 us (22%)
  Pallas kernels  19.6 us (20%)
  local copies, waits for them, and re-layouts  5.11 us (5%)
    ppermute x5, waiting for transfers between devices, per_device(): far = [lax.ppermute(value, 'tm', p[3]) for value, p in zip(sends, plan)]  24.9 us
    ppermute x5, waiting for transfers between devices, per_device(): lax.ppermute(value, 'tm', p[3])  22.8 us
    pallas_call x1, Pallas kernels, per_device(): call(functools.partial(attend_kernel, *common), [SMEM] + [VMEM] * (6 + n_...  16.5 us
    ppermute x5, starting transfers between devices, per_device(): far = [lax.ppermute(value, 'tm', p[3]) for value, p in zip(sends, plan)]  11.4 us
    ppermute x5, starting transfers between devices, per_device(): lax.ppermute(value, 'tm', p[3])  8.9 us
    unnamed x13, local copies, waits for them, and re-layouts  5.11 us
    ppermute x3, waiting for transfers between devices, across(): return lax.ppermute(value, 'space', [(0, 1), (1, 0)])  2.81 us
  transfers between devices with their start and end apart: 13, of which 7 were waited for; matrix products, arithmetic and copies ran while one was open for 1% of the time, Pallas kernels for 0%

profile of v1, /device:TPU:0, one launch (start us, length us, event | category | flops | bytes accessed | tf_op | source)
XLA Modules:
  0.0 96.9 jit_solution(320563214414978543)
XLA Ops:
  0.6 0.5 collective-permute-start
  1.1 0.1 collective-permute-start.1
  1.2 0.8 copy.10.lists.refs_0_
  2.0 0.5 collective-permute-done.k_oth.refs_5_
  2.5 0.4 collective-permute-done.1.v_oth.refs_6_
  2.9 0.9 copy-done.2
  3.8 0.9 copy-done.3
  4.8 1.0 shard_map.84
  5.8 3.0 %collective-permute-start.2 = (bf16[512,512]{1,0:T(8,128)(2,1)S(1)}, bf16[512,512]{1,0:T(8,128)(2,1)S(1)}, u32[]{:S(2)}, u32[]{:S(2)}) collective-permute-start(bf16[512,512]{1,0:T(8,128)(2,1)S(1)} %get-tuple-element.22), channel_id=1, source_target_pairs={{0,2},{2,0},{4,6},{6,4},{8,10},{10,8},{12,14},{14,12},{1,3},{3,1},... | collective-permute-start | bytes 1572872 | tf_op jit(solution)/shard_map/ppermute | solution.py:231
  8.7 0.7 collective-permute-start.3
  9.4 2.9 %collective-permute-start.4 = (bf16[256,512]{1,0:T(8,128)(2,1)S(1)}, bf16[256,512]{1,0:T(8,128)(2,1)S(1)}, u32[]{:S(2)}, u32[]{:S(2)}) collective-permute-start(bf16[256,512]{1,0:T(8,128)(2,1)S(1)} %get-tuple-element.24), channel_id=1, source_target_pairs={{0,4},{2,6},{4,0},{6,2},{8,12},{10,14},{12,8},{14,10},{1,5},{3,7},... | collective-permute-start | bytes 786440 | tf_op jit(solution)/shard_map/ppermute | solution.py:231
  12.3 0.7 collective-permute-start.5
  13.0 4.3 %collective-permute-start.6 = (bf16[256,512]{1,0:T(8,128)(2,1)S(1)}, bf16[256,512]{1,0:T(8,128)(2,1)S(1)}, u32[]{:S(2)}, u32[]{:S(2)}) collective-permute-start(bf16[256,512]{1,0:T(8,128)(2,1)S(1)} %get-tuple-element.26), channel_id=1, source_target_pairs={{0,8},{2,10},{4,12},{6,14},{8,0},{10,2},{12,4},{14,6},{1,9},{3,11}... | collective-permute-start | bytes 786440 | tf_op jit(solution)/shard_map/ppermute | solution.py:231
  17.2 12.6 %collective-permute-done.4.refs_9_ = bf16[256,512]{1,0:T(8,128)(2,1)S(1)} collective-permute-done((bf16[256,512]{1,0:T(8,128)(2,1)S(1)}, bf16[256,512]{1,0:T(8,128)(2,1)S(1)}, u32[]{:S(2)}, u32[]{:S(2)}) %collective-permute-start.4) | collective-permute-done | bytes 262176 | tf_op jit(solution)/shard_map/ppermute | solution.py:231
  29.8 0.0 collective-permute-done.5.refs_10_
  29.8 12.3 %collective-permute-done.6.refs_11_ = bf16[256,512]{1,0:T(8,128)(2,1)S(1)} collective-permute-done((bf16[256,512]{1,0:T(8,128)(2,1)S(1)}, bf16[256,512]{1,0:T(8,128)(2,1)S(1)}, u32[]{:S(2)}, u32[]{:S(2)}) %collective-permute-start.6) | collective-permute-done | bytes 262176 | tf_op jit(solution)/shard_map/ppermute | solution.py:231
  42.1 0.0 collective-permute-done.2.refs_7_
  42.1 0.0 collective-permute-done.3.refs_8_
  42.2 16.5 %shard_map.85 = (bf16[512,256]{1,0:T(8,128)(2,1)}, bf16[512,256]{1,0:T(8,128)(2,1)}, f32[512,512]{1,0:T(8,128)}, f32[512,512]{1,0:T(8,128)}, bf16[512,512]{1,0:T...) custom-call(s32[16,8]{1,0:T(8,128)S(1)} %copy.10.lists.refs_0_, ...), custom_call_target="tpu_custom_call" | custom-call | flops 4429185024 | bytes 12582912 | tf_op jit(solution)/shard_map/pallas_call | solution.py:233
  58.7 0.7 collective-permute-start.8
  59.4 4.8 %collective-permute-start.9 = (bf16[256,512]{1,0:T(8,128)(2,1)S(1)}, bf16[256,512]{1,0:T(8,128)(2,1)S(1)}, u32[]{:S(2)}, u32[]{:S(2)}) collective-permute-start(bf16[256,512]{1,0:T(8,128)(2,1)S(1)} %get-tuple-element.33), channel_id=1, source_target_pairs={{0,4},{2,6},{4,0},{6,2},{8,12},{10,14},{12,8},{14,10},{1,5},{3,7},... | collective-permute-start | bytes 786440 | tf_op jit(solution)/shard_map/ppermute | solution.py:247
  64.1 0.7 collective-permute-start.10
  64.8 2.8 %collective-permute-start.11 = (bf16[256,512]{1,0:T(8,128)(2,1)S(1)}, bf16[256,512]{1,0:T(8,128)(2,1)S(1)}, u32[]{:S(2)}, u32[]{:S(2)}) collective-permute-start(bf16[256,512]{1,0:T(8,128)(2,1)S(1)} %get-tuple-element.35), channel_id=1, source_target_pairs={{0,8},{2,10},{4,12},{6,14},{8,0},{10,2},{12,4},{14,6},{1,9},{3,11}... | collective-permute-start | bytes 786440 | tf_op jit(solution)/shard_map/ppermute | solution.py:247
  67.6 14.3 %collective-permute-done.9.refs_5_ = bf16[256,512]{1,0:T(8,128)(2,1)S(1)} collective-permute-done((bf16[256,512]{1,0:T(8,128)(2,1)S(1)}, bf16[256,512]{1,0:T(8,128)(2,1)S(1)}, u32[]{:S(2)}, u32[]{:S(2)}) %collective-permute-start.9) | collective-permute-done | bytes 262176 | tf_op jit(solution)/shard_map/ppermute | solution.py:247
  81.9 0.0 collective-permute-done.10.refs_6_
  81.9 8.5 %collective-permute-done.11.refs_7_ = bf16[256,512]{1,0:T(8,128)(2,1)S(1)} collective-permute-done((bf16[256,512]{1,0:T(8,128)(2,1)S(1)}, bf16[256,512]{1,0:T(8,128)(2,1)S(1)}, u32[]{:S(2)}, u32[]{:S(2)}) %collective-permute-start.11) | collective-permute-done | bytes 262176 | tf_op jit(solution)/shard_map/ppermute | solution.py:247
  90.4 1.2 %copy-done = f32[512,512]{1,0:T(8,128)S(1)} copy-done((f32[512,512]{1,0:T(8,128)S(1)}, f32[512,512]{1,0:T(8,128)}, u32[]{:S(2)}) %copy-start) | copy-done | bytes 1048600
  91.6 1.2 %copy-done.1 = f32[512,512]{1,0:T(8,128)S(1)} copy-done((f32[512,512]{1,0:T(8,128)S(1)}, f32[512,512]{1,0:T(8,128)}, u32[]{:S(2)}) %copy-start.1) | copy-done | bytes 1048600
  92.8 1.2 %shard_map.86 = (f32[512,512]{1,0:T(8,128)S(1)}, bf16[512,512]{1,0:T(8,128)(2,1)S(1)}) custom-call(s32[16,8]{1,0:T(8,128)S(1)} %copy.10.lists.refs_0_, f32[512,512]{1,0:T(8,128)S(1)} %copy-done, f32[512,512]{1,0:T(8,128)S(1)} %copy-done.1, bf16[512,512]{1,0:T(8,128)(2,1)S(1)} %collective-permute-done.7.refs_3_, ...), custom_call_target="tpu_custom_call" | custom-call | bytes 4194304 | tf_op jit(solution)/shard_map/pallas_call | solution.py:248
  94.1 0.1 collective-permute-start.12
  94.1 1.9 %collective-permute-done.12.came = bf16[512,512]{1,0:T(8,128)(2,1)S(1)} collective-permute-done((bf16[512,512]{1,0:T(8,128)(2,1)S(1)}, bf16[512,512]{1,0:T(8,128)(2,1)S(1)}, u32[]{:S(2)}, u32[]{:S(2)}) %collective-permute-start.12) | collective-permute-done | bytes 524320 | tf_op jit(solution)/shard_map/ppermute | solution.py:222
  96.0 0.9 shard_map.87
  (11 shorter events, 0.0 us)
Async XLA Ops:
  0.6 1.9 %collective-permute-start = (bf16[512,256]{1,0:T(8,128)(2,1)}, bf16[512,256]{1,0:T(8,128)(2,1)S(1)}, u32[]{:S(2)}, u32[]{:S(2)}) collective-permute-start(bf16[512,256]{1,0:T(8,128)(2,1)} %refs_3_.1), channel_id=1, source_target_pairs={{0,1},{1,0},{2,3},{3,2},{4,5},{5,4},{6,7},{7,6},{8,9},{9,8},{10,11... | collective-permute-start | bytes 786440 | tf_op jit(solution)/shard_map/ppermute | solution.py:222
  1.1 1.7 %collective-permute-start.1 = (bf16[512,256]{1,0:T(8,128)(2,1)}, bf16[512,256]{1,0:T(8,128)(2,1)S(1)}, u32[]{:S(2)}, u32[]{:S(2)}) collective-permute-start(bf16[512,256]{1,0:T(8,128)(2,1)} %refs_4_.1), channel_id=1, source_target_pairs={{0,1},{1,0},{2,3},{3,2},{4,5},{5,4},{6,7},{7,6},{8,9},{9,8},{10,11... | collective-permute-start | bytes 786440 | tf_op jit(solution)/shard_map/ppermute | solution.py:222
  2.9 0.9 copy-start.2
  3.8 0.9 copy-start.3
  4.8 37.4 %copy-start.4 = (bf16[512,256]{1,0:T(8,128)(2,1)S(1)}, bf16[512,256]{1,0:T(8,128)(2,1)}, u32[]{:S(2)}) copy-start(bf16[512,256]{1,0:T(8,128)(2,1)} %refs_1_.1) | copy-start | bytes 786436
  4.8 37.4 %copy-start.5 = (bf16[512,256]{1,0:T(8,128)(2,1)S(1)}, bf16[512,256]{1,0:T(8,128)(2,1)}, u32[]{:S(2)}) copy-start(bf16[512,256]{1,0:T(8,128)(2,1)} %refs_2_.1) | copy-start | bytes 786436
  5.8 36.4 %collective-permute-start.2 = (bf16[512,512]{1,0:T(8,128)(2,1)S(1)}, bf16[512,512]{1,0:T(8,128)(2,1)S(1)}, u32[]{:S(2)}, u32[]{:S(2)}) collective-permute-start(bf16[512,512]{1,0:T(8,128)(2,1)S(1)} %get-tuple-element.22), channel_id=1, source_target_pairs={{0,2},{2,0},{4,6},{6,4},{8,10},{10,8},{12,14},{14,12},{1,3},{3,1},... | collective-permute-start | bytes 1572872 | tf_op jit(solution)/shard_map/ppermute | solution.py:231
  8.7 33.4 %collective-permute-start.3 = (bf16[512,512]{1,0:T(8,128)(2,1)S(1)}, bf16[512,512]{1,0:T(8,128)(2,1)S(1)}, u32[]{:S(2)}, u32[]{:S(2)}) collective-permute-start(bf16[512,512]{1,0:T(8,128)(2,1)S(1)} %get-tuple-element.23), channel_id=1, source_target_pairs={{0,0},{2,4},{4,2},{6,8},{8,6},{10,12},{12,10},{14,14},{1,1},{3,5},... | collective-permute-start | bytes 1572872 | tf_op jit(solution)/shard_map/ppermute | solution.py:231
  9.4 20.4 %collective-permute-start.4 = (bf16[256,512]{1,0:T(8,128)(2,1)S(1)}, bf16[256,512]{1,0:T(8,128)(2,1)S(1)}, u32[]{:S(2)}, u32[]{:S(2)}) collective-permute-start(bf16[256,512]{1,0:T(8,128)(2,1)S(1)} %get-tuple-element.24), channel_id=1, source_target_pairs={{0,4},{2,6},{4,0},{6,2},{8,12},{10,14},{12,8},{14,10},{1,5},{3,7},... | collective-permute-start | bytes 786440 | tf_op jit(solution)/shard_map/ppermute | solution.py:231
  12.3 17.5 %collective-permute-start.5 = (bf16[256,512]{1,0:T(8,128)(2,1)S(1)}, bf16[256,512]{1,0:T(8,128)(2,1)S(1)}, u32[]{:S(2)}, u32[]{:S(2)}) collective-permute-start(bf16[256,512]{1,0:T(8,128)(2,1)S(1)} %get-tuple-element.25), channel_id=1, source_target_pairs={{0,0},{2,2},{4,8},{6,10},{8,4},{10,6},{12,12},{14,14},{1,1},{3,3},... | collective-permute-start | bytes 786440 | tf_op jit(solution)/shard_map/ppermute | solution.py:231
  13.0 29.2 %collective-permute-start.6 = (bf16[256,512]{1,0:T(8,128)(2,1)S(1)}, bf16[256,512]{1,0:T(8,128)(2,1)S(1)}, u32[]{:S(2)}, u32[]{:S(2)}) collective-permute-start(bf16[256,512]{1,0:T(8,128)(2,1)S(1)} %get-tuple-element.26), channel_id=1, source_target_pairs={{0,8},{2,10},{4,12},{6,14},{8,0},{10,2},{12,4},{14,6},{1,9},{3,11}... | collective-permute-start | bytes 786440 | tf_op jit(solution)/shard_map/ppermute | solution.py:231
  58.7 31.7 %collective-permute-start.7 = (bf16[512,512]{1,0:T(8,128)(2,1)S(1)}, bf16[512,512]{1,0:T(8,128)(2,1)S(1)}, u32[]{:S(2)}, u32[]{:S(2)}) collective-permute-start(bf16[512,512]{1,0:T(8,128)(2,1)S(1)} %get-tuple-element.31), channel_id=1, source_target_pairs={{0,2},{2,0},{4,6},{6,4},{8,10},{10,8},{12,14},{14,12},{1,3},{3,1},... | collective-permute-start | bytes 1572872 | tf_op jit(solution)/shard_map/ppermute | solution.py:247
  58.7 31.7 %collective-permute-start.8 = (bf16[512,512]{1,0:T(8,128)(2,1)S(1)}, bf16[512,512]{1,0:T(8,128)(2,1)S(1)}, u32[]{:S(2)}, u32[]{:S(2)}) collective-permute-start(bf16[512,512]{1,0:T(8,128)(2,1)S(1)} %get-tuple-element.32), channel_id=1, source_target_pairs={{0,0},{2,4},{4,2},{6,8},{8,6},{10,12},{12,10},{14,14},{1,1},{3,5},... | collective-permute-start | bytes 1572872 | tf_op jit(solution)/shard_map/ppermute | solution.py:247
  59.4 22.6 %collective-permute-start.9 = (bf16[256,512]{1,0:T(8,128)(2,1)S(1)}, bf16[256,512]{1,0:T(8,128)(2,1)S(1)}, u32[]{:S(2)}, u32[]{:S(2)}) collective-permute-start(bf16[256,512]{1,0:T(8,128)(2,1)S(1)} %get-tuple-element.33), channel_id=1, source_target_pairs={{0,4},{2,6},{4,0},{6,2},{8,12},{10,14},{12,8},{14,10},{1,5},{3,7},... | collective-permute-start | bytes 786440 | tf_op jit(solution)/shard_map/ppermute | solution.py:247
  64.1 17.8 %collective-permute-start.10 = (bf16[256,512]{1,0:T(8,128)(2,1)S(1)}, bf16[256,512]{1,0:T(8,128)(2,1)S(1)}, u32[]{:S(2)}, u32[]{:S(2)}) collective-permute-start(bf16[256,512]{1,0:T(8,128)(2,1)S(1)} %get-tuple-element.34), channel_id=1, source_target_pairs={{0,0},{2,2},{4,8},{6,10},{8,4},{10,6},{12,12},{14,14},{1,1},{3,3},... | collective-permute-start | bytes 786440 | tf_op jit(solution)/shard_map/ppermute | solution.py:247
  64.8 25.6 %collective-permute-start.11 = (bf16[256,512]{1,0:T(8,128)(2,1)S(1)}, bf16[256,512]{1,0:T(8,128)(2,1)S(1)}, u32[]{:S(2)}, u32[]{:S(2)}) collective-permute-start(bf16[256,512]{1,0:T(8,128)(2,1)S(1)} %get-tuple-element.35), channel_id=1, source_target_pairs={{0,8},{2,10},{4,12},{6,14},{8,0},{10,2},{12,4},{14,6},{1,9},{3,11}... | collective-permute-start | bytes 786440 | tf_op jit(solution)/shard_map/ppermute | solution.py:247
  90.4 1.2 %copy-start = (f32[512,512]{1,0:T(8,128)S(1)}, f32[512,512]{1,0:T(8,128)}, u32[]{:S(2)}) copy-start(f32[512,512]{1,0:T(8,128)} %get-tuple-element.29.refs_1_) | copy-start | bytes 3145732
  91.6 1.2 %copy-start.1 = (f32[512,512]{1,0:T(8,128)S(1)}, f32[512,512]{1,0:T(8,128)}, u32[]{:S(2)}) copy-start(f32[512,512]{1,0:T(8,128)} %get-tuple-element.30.refs_2_) | copy-start | bytes 3145732
  94.1 2.0 %collective-permute-start.12 = (bf16[512,512]{1,0:T(8,128)(2,1)S(1)}, bf16[512,512]{1,0:T(8,128)(2,1)S(1)}, u32[]{:S(2)}, u32[]{:S(2)}) collective-permute-start(bf16[512,512]{1,0:T(8,128)(2,1)S(1)} %get-tuple-element.37), channel_id=1, source_target_pairs={{0,1},{1,0},{2,3},{3,2},{4,5},{5,4},{6,7},{7,6},{8,9},{9,8},{10,11... | collective-permute-start | bytes 1572872 | tf_op jit(solution)/shard_map/ppermute | solution.py:222

commit v2 on v0

v2 whole, which is shorter than its diff:
```python
import functools
import math

import jax
import jax.numpy as jnp
from jax import lax
from jax.experimental import pallas as pl
from jax.experimental.pallas import tpu as pltpu
from jax.sharding import PartitionSpec as P

DH = 128
F32 = jnp.float32
BF16 = jnp.bfloat16
VMEM = pl.BlockSpec(memory_space=pltpu.VMEM)
SMEM = pl.BlockSpec(memory_space=pltpu.SMEM)
NEG = -1e30
SCALE = 1.0 / math.sqrt(DH)
EXP_SCALE = SCALE * math.log2(math.e)
KEY = slice(0, DH)
VALUE = slice(DH, 2 * DH)
sds = jax.ShapeDtypeStruct


def dot_nn(a, b):
    return lax.dot_general(a, b, (((1,), (0,)), ((), ())), preferred_element_type=F32)


def dot_nt(a, b):
    return lax.dot_general(a, b, (((1,), (1,)), ((), ())), preferred_element_type=F32)


def dot_tn(a, b):
    return lax.dot_general(a, b, (((0,), (0,)), ((), ())), preferred_element_type=F32)


def call(kernel, args, out_shape, scratch=(), flops=0):
    traffic = sum(a.size * a.dtype.itemsize for a in (*args, *out_shape))
    return pl.pallas_call(
        kernel,
        out_shape=out_shape,
        in_specs=[SMEM if a.dtype == jnp.int32 else VMEM for a in args],
        out_specs=tuple(VMEM for _ in out_shape),
        scratch_shapes=list(scratch),
        compiler_params=pltpu.CompilerParams(vmem_limit_bytes=40 << 20),
        cost_estimate=pl.CostEstimate(flops=flops, bytes_accessed=traffic, transcendentals=0),
    )(*args)


def swap_pairs(count, distance, second):
    pairs = []
    for frame in range(count):
        up = ((frame // distance) % 2 == 0) != second
        target = frame + distance if up else frame - distance
        pairs.append((frame, target if 0 <= target < count else frame))
    return pairs


class Swap:
    def __init__(self, count, level, second):
        self.count, self.level, self.second = count, level, second
        self.levels = count.bit_length() - 1
        self.pairs = swap_pairs(count, 1 << level, second)
        self.moves = any(source != target for source, target in self.pairs)

    def partner(self, frame):
        odd = lax.rem(lax.shift_right_logical(frame, self.level), 2)
        later = odd == (1 if self.second else 0)
        other = jnp.where(later, frame + (1 << self.level), frame - (1 << self.level))
        return other, later, jnp.logical_and(other >= 0, other < self.count)

    def slot(self, later, k):
        base = 0 if self.level == 0 else self.level + 1
        return jnp.where(later, self.levels + 1, 0) + base + k

    def block_of_mine(self, lists, frame, slab, k):
        other, later, exists = self.partner(frame)
        entry = lists[frame * 2 + slab, self.slot(later, k)]
        return jnp.clip(entry - other * 4, 0, 3), exists

    def block_of_theirs(self, lists, frame, slab, k):
        other, later, exists = self.partner(frame)
        row = jnp.where(exists, other, frame) * 2 + slab
        entry = lists[row, self.slot(jnp.logical_not(later), k)]
        return jnp.clip(entry - frame * 4, 0, 3), exists


def head_cols(head):
    return slice(head * DH, (head + 1) * DH)


def each_core(body):
    core = lax.axis_index("space")
    for mine in range(2):
        pl.when(core == mine)(functools.partial(body, mine))


def pack_kernel(k, v, q, g, kv_out, qg_out):
    def body(mine):
        cols = head_cols(1 - mine)
        kv_out[:, KEY] = k[:, cols]
        kv_out[:, VALUE] = v[:, cols]
        qg_out[:, KEY] = q[:, cols]
        qg_out[:, VALUE] = g[:, cols]

    each_core(body)


def join(mine, a, b, came, out):
    half = a.shape[0]
    cols = head_cols(mine)
    own = slice(mine * half, (mine + 1) * half)
    other = slice((1 - mine) * half, (2 - mine) * half)
    out[own, KEY] = a[:, cols]
    out[own, VALUE] = b[:, cols]
    out[other, :] = came[...]


def frame_kernel(far, block, lists, k, v, came, kv_out, *sends):
    each_core(lambda mine: join(mine, k, v, came, kv_out))
    frame = lax.axis_index("tm")
    for swap, send in zip(far, sends):
        for slab in range(2):
            b, _ = swap.block_of_theirs(lists, frame, slab, 0)
            row = pl.multiple_of(b * block, block)
            send[slab * block : (slab + 1) * block, :] = kv_out[pl.ds(row, block), :]


def join_kernel(q, g, came, out):
    each_core(lambda mine: join(mine, q, g, came, out))


class Piece:
    def __init__(self, kv, row, exists=None, grad=None, grad_row=None, add=False):
        self.kv, self.row, self.exists = kv, row, exists
        self.grad, self.grad_row, self.add = grad, row if grad_row is None else grad_row, add


def forward_slab(q, pieces, block, s_ref, old):
    top = None
    for j, piece in enumerate(pieces):
        s = dot_nt(q, piece.kv[pl.ds(piece.row, block), KEY])
        if piece.exists is not None:
            s = jnp.where(piece.exists, s, NEG)
        s_ref[j] = s
        for c in range(0, block, DH):
            part = s[:, c : c + DH]
            top = part if top is None else jnp.maximum(top, part)
    peak = jnp.max(top, axis=1, keepdims=True)
    if old is not None:
        peak = jnp.maximum(peak, old[0])
    total = None
    acc = None
    for j, piece in enumerate(pieces):
        e = jnp.exp2((s_ref[j] - peak) * EXP_SCALE)
        for c in range(0, block, DH):
            part = e[:, c : c + DH]
            total = part if total is None else total + part
        out = dot_nn(e.astype(BF16), piece.kv[pl.ds(piece.row, block), VALUE])
        acc = out if acc is None else acc + out
    total = jnp.sum(total, axis=1, keepdims=True)
    if old is not None:
        shrink = jnp.exp2((old[0] - peak) * EXP_SCALE)
        total = total + old[1] * shrink
        acc = acc + old[2] * shrink
    return peak, total, acc


def backward_slab(q, g, lse, row_dot, pieces, block):
    dq = None
    for piece in pieces:
        k = piece.kv[pl.ds(piece.row, block), KEY]
        v = piece.kv[pl.ds(piece.row, block), VALUE]
        s = dot_nt(k, q)
        if piece.exists is not None:
            s = jnp.where(piece.exists, s, NEG)
        p = jnp.exp2(s * EXP_SCALE - lse)
        ds = (p * (dot_nt(v, g) - row_dot)).astype(BF16)
        dk = dot_nn(ds, q) * SCALE
        dv = dot_nn(p.astype(BF16), g)
        rows = pl.ds(piece.grad_row, block)
        if piece.add:
            piece.grad[rows, KEY] += dk
            piece.grad[rows, VALUE] += dv
        else:
            piece.grad[rows, KEY] = dk.astype(piece.grad.dtype)
            piece.grad[rows, VALUE] = dv.astype(piece.grad.dtype)
        part = dot_tn(ds, k)
        dq = part if dq is None else dq + part
    return dq


def listed(swap, kv, lists, frame, slab, block, grad=None, count=1):
    pieces = []
    for k in range(count):
        b, exists = swap.block_of_mine(lists, frame, slab, k)
        row = pl.multiple_of(b * block, block)
        pieces.append(Piece(kv, row, exists, grad, add=True))
    return pieces


def arrived(swap, kv, frame, slab, block, grad=None):
    _, _, exists = swap.partner(frame)
    return Piece(kv, slab * block, exists, grad)


def rows_of(slab, half):
    return slice(slab * half, (slab + 1) * half)


def store_state(refs, rows, peak, total, acc):
    stat, acc_ref = refs
    lane = lax.broadcasted_iota(jnp.int32, acc.shape, 1)
    stat[rows, :] = jnp.where(lane == 0, peak, total)
    acc_ref[rows, :] = acc


def load_state(refs, rows):
    stat, acc_ref = refs
    return stat[rows, 0:1], stat[rows, 1:2], acc_ref[rows, :]


def near_kernel(block, qg, kv, stat, acc, s_ref):
    half = qg.shape[0] // 2
    for slab in range(2):
        rows = rows_of(slab, half)
        pieces = [Piece(kv, r) for r in range(0, 2 * half, block)]
        store_state((stat, acc), rows, *forward_slab(qg[rows, KEY], pieces, block, s_ref, None))


def middle_kernel(block, swaps, lists, qg, stat, acc, a_kv, z_kv, y_kv, stat2, acc2, s_ref):
    half = qg.shape[0] // 2
    frame = lax.axis_index("tm")
    a, z, y = swaps
    for slab in range(2):
        rows = rows_of(slab, half)
        pieces = listed(a, a_kv, lists, frame, slab, block, count=2)
        pieces += listed(z, z_kv, lists, frame, slab, block)
        pieces += listed(y, y_kv, lists, frame, slab, block)
        old = load_state((stat, acc), rows)
        new = forward_slab(qg[rows, KEY], pieces, block, s_ref, old)
        store_state((stat2, acc2), rows, *new)


def last_kernel(block, relayed, far, *refs):
    n = len(far)
    lists, qg, stat, acc, c_kv = refs[:5]
    far_kv = refs[5 : 5 + n]
    o_ref, row_ref, dc_ref, dq_ref = refs[5 + n : 9 + n]
    s_ref, grad = refs[9 + n :]
    half = qg.shape[0] // 2
    frame = lax.axis_index("tm")
    grad[...] = jnp.zeros_like(grad)
    for slab in range(2):
        rows = rows_of(slab, half)
        q, g = qg[rows, KEY], qg[rows, VALUE]
        pieces = listed(relayed, c_kv, lists, frame, slab, block, grad, count=2)
        more = [arrived(swap, kv, frame, slab, block) for swap, kv in zip(far, far_kv)]
        old = load_state((stat, acc), rows)
        peak, total, out = forward_slab(q, pieces + more, block, s_ref, old)
        o = (out / total).astype(BF16)
        o_ref[rows, :] = o
        row_dot = jnp.sum(g.astype(F32) * o.astype(F32), axis=1, keepdims=True)
        lse = peak * EXP_SCALE + jnp.log2(total)
        lane = lax.broadcasted_iota(jnp.int32, out.shape, 1)
        turned = jnp.where(lane == 0, lse, row_dot).T[:8, :]
        row_ref[:, rows] = turned
        dq_ref[rows, :] = backward_slab(q, g, turned[0:1, :], turned[1:2, :], pieces, block)
    dc_ref[...] = grad[...].astype(BF16)


def far_kernel(block, far, *refs):
    n = len(far)
    qg, row_ref, dq_old = refs[:3]
    far_kv = refs[3 : 3 + n]
    grads = refs[3 + n : 3 + 2 * n]
    dq_ref = refs[3 + 2 * n]
    half = qg.shape[0] // 2
    frame = lax.axis_index("tm")
    for slab in range(2):
        rows = rows_of(slab, half)
        q, g = qg[rows, KEY], qg[rows, VALUE]
        pieces = [
            arrived(swap, kv, frame, slab, block, out)
            for swap, kv, out in zip(far, far_kv, grads)
        ]
        lse, row_dot = row_ref[0:1, rows], row_ref[1:2, rows]
        dq_ref[rows, :] = dq_old[rows, :] + backward_slab(q, g, lse, row_dot, pieces, block)


def rest_kernel(block, swaps, lists, o, qg, row_ref, dq_old, kv, a_kv, z_kv, y_kv, *refs):
    near, da, dz, dy, keep, send, grad_a = refs
    half = qg.shape[0] // 2
    frame = lax.axis_index("tm")
    a, z, y = swaps
    near[...] = jnp.zeros_like(near)
    grad_a[...] = jnp.zeros_like(grad_a)
    dz[...] = jnp.zeros_like(dz)
    dy[...] = jnp.zeros_like(dy)
    whole = []
    for slab in range(2):
        rows = rows_of(slab, half)
        q, g = qg[rows, KEY], qg[rows, VALUE]
        pieces = listed(z, z_kv, lists, frame, slab, block, dz)
        pieces += listed(y, y_kv, lists, frame, slab, block, dy)
        pieces += listed(a, a_kv, lists, frame, slab, block, grad_a, count=2)
        pieces += [Piece(kv, r, grad=near, add=True) for r in range(0, 2 * half, block)]
        lse, row_dot = row_ref[0:1, rows], row_ref[1:2, rows]
        dq = dq_old[rows, :] + backward_slab(q, g, lse, row_dot, pieces, block)
        whole.append((dq * SCALE).astype(BF16))
    da[...] = grad_a[...].astype(BF16)

    def body(mine):
        for slab in range(2):
            out = keep if slab == mine else send
            out[:, KEY] = o[rows_of(slab, half), :]
            out[:, VALUE] = whole[slab]

    each_core(body)


def forwards_first(frame):
    return lax.rem(frame, 2) == lax.rem(lax.shift_right_logical(frame, 1), 2)


def relay_kernel(z_kv, y_kv, out):
    first = forwards_first(lax.axis_index("tm"))

    @pl.when(first)
    def _():
        out[...] = z_kv[...]

    @pl.when(jnp.logical_not(first))
    def _():
        out[...] = y_kv[...]


def merge_kernel(dz, dy, came, z_out, y_out):
    first = forwards_first(lax.axis_index("tm"))
    more = came[...].astype(F32)
    z_out[...] = (dz[...] + jnp.where(first, more, 0.0)).astype(BF16)
    y_out[...] = (dy[...] + jnp.where(first, 0.0, more)).astype(BF16)


def gather_kernel(block, swaps, far, *refs):
    n = len(far)
    lists, near, da, dz, dy = refs[:5]
    far_back = refs[5 : 5 + n]
    keep, send, total = refs[5 + n :]
    frame = lax.axis_index("tm")
    half = near.shape[0] // 2
    sums = near[...]
    for swap, came in zip(swaps, (da, dz, dy)):
        _, _, exists = swap.partner(frame)
        sums = sums + jnp.where(exists, came[...].astype(F32), 0.0)
    total[...] = sums
    for swap, came in zip(far, far_back):
        for slab in range(2):
            b, exists = swap.block_of_theirs(lists, frame, slab, 0)
            rows = pl.ds(pl.multiple_of(b * block, block), block)
            part = came[slab * block : (slab + 1) * block, :].astype(F32)
            total[rows, :] += jnp.where(exists, part, 0.0)

    def body(mine):
        keep[...] = total[rows_of(mine, half), :].astype(BF16)
        send[...] = total[rows_of(1 - mine, half), :].astype(BF16)

    each_core(body)


def split_kernel(keep, came, first, second):
    def body(mine):
        for head, source in ((mine, keep), (1 - mine, came)):
            first[:, head_cols(head)] = source[:, KEY]
            second[:, head_cols(head)] = source[:, VALUE]

    each_core(body)


def per_device(queries, key_rows, value_rows, out_grad, block_lists):
    s_dev, width = queries.shape
    count = lax.axis_size("tm")
    block = s_dev // 2
    pair = sds((s_dev, 2 * DH), BF16)
    frame_bf = sds((2 * s_dev, 2 * DH), BF16)
    frame_f32 = sds((2 * s_dev, 2 * DH), F32)
    row_f32 = sds((2 * s_dev, DH), F32)
    levels = count.bit_length() - 1
    near_swap, relayed = Swap(count, 0, False), Swap(count, 0, True)
    z_swap, y_swap = Swap(count, 1, False), Swap(count, 1, True)
    swaps = (near_swap, z_swap, y_swap)
    far = [Swap(count, level, second) for level in range(2, levels) for second in (False, True)]
    far = [swap for swap in far if swap.moves]
    product = 2 * 2 * s_dev * block * DH

    def across(value):
        return lax.ppermute(value, "space", [(0, 1), (1, 0)])

    def swapped(value, swap):
        return lax.ppermute(value, "tm", swap.pairs)

    def scores(n):
        return pltpu.VMEM((n, s_dev, block), F32)

    kv_send, qg_send = call(pack_kernel, (key_rows, value_rows, queries, out_grad), [pair, pair])
    kv_came = across(kv_send)
    kv, *far_send = call(
        functools.partial(frame_kernel, far, block),
        (block_lists, key_rows, value_rows, kv_came),
        [frame_bf] + [pair] * len(far),
    )
    a_kv = swapped(kv, near_swap)
    z_kv = swapped(kv, z_swap)
    y_kv = swapped(kv, y_swap)
    (qg,) = call(join_kernel, (queries, out_grad, across(qg_send)), [frame_bf])
    stat, acc = call(
        functools.partial(near_kernel, block),
        (qg, kv),
        [row_f32, row_f32],
        scratch=[scores(4)],
        flops=2 * 4 * 2 * product,
    )
    z_kv, y_kv, stat = lax.optimization_barrier((z_kv, y_kv, stat))
    (relay,) = call(relay_kernel, (z_kv, y_kv), [frame_bf])
    relay, far_send = lax.optimization_barrier((relay, far_send))
    c_kv = swapped(relay, near_swap)
    far_kv = [swapped(value, swap) for value, swap in zip(far_send, far)]
    stat, acc = call(
        functools.partial(middle_kernel, block, swaps),
        (block_lists, qg, stat, acc, a_kv, z_kv, y_kv),
        [row_f32, row_f32],
        scratch=[scores(4)],
        flops=2 * 4 * 2 * product,
    )
    o, row_stat, dc, dq = call(
        functools.partial(last_kernel, block, relayed, far),
        (block_lists, qg, stat, acc, c_kv, *far_kv),
        [sds((2 * s_dev, DH), BF16), sds((8, 2 * s_dev), F32), frame_bf, row_f32],
        scratch=[scores(2 + len(far)), pltpu.VMEM((2 * s_dev, 2 * DH), F32)],
        flops=2 * ((2 + len(far)) * 2 + 10) * product,
    )
    dc_came = swapped(dc, near_swap)
    *far_grad, dq = call(
        functools.partial(far_kernel, block, far),
        (qg, row_stat, dq, *far_kv),
        [pair] * len(far) + [row_f32],
        flops=2 * 5 * len(far) * product,
    )
    far_back = [swapped(value, swap) for value, swap in zip(far_grad, far)]
    near, da, dz, dy, keep, send = call(
        functools.partial(rest_kernel, block, swaps),
        (block_lists, o, qg, row_stat, dq, kv, a_kv, z_kv, y_kv),
        [frame_f32, frame_bf, frame_f32, frame_f32, pair, pair],
        scratch=[pltpu.VMEM((2 * s_dev, 2 * DH), F32)],
        flops=2 * 8 * 5 * product,
    )
    dc_came, far_back = lax.optimization_barrier((dc_came, far_back))
    dz, dy = call(merge_kernel, (dz, dy, dc_came), [frame_bf, frame_bf])
    dz, dy, da = lax.optimization_barrier((dz, dy, da))
    dz_came = swapped(dz, z_swap)
    dy_came = swapped(dy, y_swap)
    da_came = swapped(da, near_swap)
    half_rows = sds((s_dev, width), BF16)
    attn_out, grad_q = call(split_kernel, (keep, across(send)), [half_rows, half_rows])
    keep, send = call(
        functools.partial(gather_kernel, block, swaps, far),
        (block_lists, near, da_came, dz_came, dy_came, *far_back),
        [pair, pair],
        scratch=[pltpu.VMEM((2 * s_dev, 2 * DH), F32)],
    )
    grad_k, grad_v = call(split_kernel, (keep, across(send)), [half_rows, half_rows])
    return attn_out, grad_q, grad_k, grad_v


def solution(mesh):
    rows = P(("groups", "tm", "space"), None)
    return jax.shard_map(
        per_device,
        mesh=mesh,
        in_specs=(rows, rows, rows, rows, P("groups", None)),
        out_specs=(rows, rows, rows, rows),
        check_vma=False,
    )
```

time: 220 us -> 82.3 us (0.37)
  local copies, waits for them, and re-layouts: 85 us -> 3.95 us
  other arithmetic: 27.8 us -> 0 us
  Pallas kernels: 0 us -> 26.8 us
  starting transfers between devices: 36.7 us -> 15 us
  matrix products: 19.9 us -> 0 us
  between operations: 19.7 us -> 0.78 us
  waiting for transfers between devices: 28.5 us -> 34.6 us
    slice x30 -> x0, local copies, waits for them, and re-layouts: 37.4 us -> none  [the longest x12 19.6 us: per_device(): arrived[1]]
    pallas_call x0 -> x13, Pallas kernels: none -> 26.8 us  [call(): pl.pallas_call(kernel, out_shape=out_shape, in_specs=[SMEM if a.dtype ==...]
    ppermute x12 -> x14, starting transfers between devices: 36.7 us -> 15 us  [the longest x10 14.3 us: swapped(): return lax.ppermute(value, 'tm', swap.pairs)]
    dot_general x12 -> x0, matrix products: 19.9 us -> none  [the longest x2 7.02 us: backward_head(): grad_v = jnp.dot(attn_bf.T, grad_h, preferred_element_type=jnp.float32)]
    ppermute x12 -> x14, waiting for transfers between devices: 19.4 us -> 34.6 us  [the longest x10 32.9 us: swapped(): return lax.ppermute(value, 'tm', swap.pairs)]
    another operation x17 -> x0, other arithmetic: 12 us -> none
    while x48 -> x0, local copies, waits for them, and re-layouts: 9.96 us -> none
    another operation x12 -> x0, local copies, waits for them, and re-layouts: 9.1 us -> none  [the longest x4 8.31 us: per_device(): jnp.stack([grad_k[:frame_tok], grad_v[:frame_tok]])]
  transfers between devices with their start and end apart: 14 -> 14, of which waited for: 3 -> 7; matrix products, arithmetic and copies ran while one was open for 24% -> 0% of each run, Pallas kernels for 0% -> 22%
where the time goes in v2:
time: 82.3 us; the launch traced here: 81 us
  waiting for transfers between devices  34.6 us (42%)
  Pallas kernels  26.8 us (33%)
  starting transfers between devices  15 us (18%)
  local copies, waits for them, and re-layouts  3.95 us (5%)
    ppermute x10, waiting for transfers between devices, swapped(): return lax.ppermute(value, 'tm', swap.pairs)  32.9 us
    pallas_call x13, Pallas kernels, call(): pl.pallas_call(kernel, out_shape=out_shape, in_specs=[SMEM if a.dtype ==...  26.8 us
    ppermute x10, starting transfers between devices, swapped(): return lax.ppermute(value, 'tm', swap.pairs)  14.3 us
    unnamed x19, local copies, waits for them, and re-layouts  3.95 us
    ppermute x4, waiting for transfers between devices, across(): return lax.ppermute(value, 'space', [(0, 1), (1, 0)])  1.65 us
  transfers between devices with their start and end apart: 14, of which 7 were waited for; matrix products, arithmetic and copies ran while one was open for 0% of the time, Pallas kernels for 22%

profile of v2, /device:TPU:0, one launch (start us, length us, event | category | flops | bytes accessed | tf_op | source)
XLA Modules:
  0.0 81.0 jit_solution(3345804477102263655)
XLA Ops:
  0.6 0.9 %copy-done = bf16[512,256]{1,0:T(8,128)(2,1)S(1)} copy-done((bf16[512,256]{1,0:T(8,128)(2,1)S(1)}, bf16[512,256]{1,0:T(8,128)(2,1)}, u32[]{:S(2)}) %copy-start) | copy-done | bytes 262168
  1.6 0.9 %copy-done.2 = bf16[512,256]{1,0:T(8,128)(2,1)S(1)} copy-done((bf16[512,256]{1,0:T(8,128)(2,1)S(1)}, bf16[512,256]{1,0:T(8,128)(2,1)}, u32[]{:S(2)}) %copy-start.2) | copy-done | bytes 262168
  2.5 0.9 %copy-done.4 = bf16[512,256]{1,0:T(8,128)(2,1)S(1)} copy-done((bf16[512,256]{1,0:T(8,128)(2,1)S(1)}, bf16[512,256]{1,0:T(8,128)(2,1)}, u32[]{:S(2)}) %copy-start.4) | copy-done | bytes 262168
  3.5 0.9 %copy-done.6 = bf16[512,256]{1,0:T(8,128)(2,1)S(1)} copy-done((bf16[512,256]{1,0:T(8,128)(2,1)S(1)}, bf16[512,256]{1,0:T(8,128)(2,1)}, u32[]{:S(2)}) %copy-start.6) | copy-done | bytes 262168
  4.5 0.5 collective-permute-start.1
  5.2 1.0 %collective-permute-done.1.came = bf16[512,256]{1,0:T(8,128)(2,1)S(1)} collective-permute-done((bf16[512,256]{1,0:T(8,128)(2,1)S(1)}, bf16[512,256]{1,0:T(8,128)(2,1)S(1)}, u32[]{:S(2)}, u32[]{:S(2)}) %collective-permute-start.1) | collective-permute-done | bytes 262176 | tf_op jit(solution)/shard_map/ppermute | solution.py:396
  6.2 0.8 shard_map.86
  7.0 0.7 collective-permute-start.3
  7.7 5.8 %collective-permute-start.2 = (bf16[1024,256]{1,0:T(8,128)(2,1)S(1)}, bf16[1024,256]{1,0:T(8,128)(2,1)S(1)}, u32[]{:S(2)}, u32[]{:S(2)}) collective-permute-start(bf16[1024,256]{1,0:T(8,128)(2,1)S(1)} %get-tuple-element.44.kv), channel_id=1, source_target_pairs={{0,4},{2,6},{4,0},{6,2},{8,12},{10,14},{12,8},{14,10},{1,5},{3,7},... | collective-permute-start | bytes 1572872 | tf_op jit(solution)/shard_map/ppermute | solution.py:399
  13.5 1.5 %collective-permute-start.4 = (bf16[1024,256]{1,0:T(8,128)(2,1)S(1)}, bf16[1024,256]{1,0:T(8,128)(2,1)S(1)}, u32[]{:S(2)}, u32[]{:S(2)}) collective-permute-start(bf16[1024,256]{1,0:T(8,128)(2,1)S(1)} %get-tuple-element.44.kv), channel_id=1, source_target_pairs={{0,2},{2,0},{4,6},{6,4},{8,10},{10,8},{12,14},{14,12},{1,3},{3,1},... | collective-permute-start | bytes 1572872 | tf_op jit(solution)/shard_map/ppermute | solution.py:399
  15.1 2.1 %shard_map.87 = (f32[1024,128]{1,0:T(8,128)S(1)}, f32[1024,128]{1,0:T(8,128)S(1)}) custom-call(bf16[1024,256]{1,0:T(8,128)(2,1)S(1)} %shard_map.85.qg.refs_1_.refs_0_, bf16[1024,256]{1,0:T(8,128)(2,1)S(1)} %get-tuple-element.44.kv), custom_call_target="tpu_custom_call" | custom-call | flops 1073741824 | bytes 2097152 | tf_op jit(solution)/shard_map/pallas_call | solution.py:38
  17.2 8.2 %collective-permute-done.2.z_kv = bf16[1024,256]{1,0:T(8,128)(2,1)S(1)} collective-permute-done((bf16[1024,256]{1,0:T(8,128)(2,1)S(1)}, bf16[1024,256]{1,0:T(8,128)(2,1)S(1)}, u32[]{:S(2)}, u32[]{:S(2)}) %collective-permute-start.2) | collective-permute-done | bytes 524320 | tf_op jit(solution)/shard_map/ppermute | solution.py:399
  25.5 0.2 shard_map.89
  25.7 1.6 %collective-permute-start.5 = (bf16[1024,256]{1,0:T(8,128)(2,1)S(1)}, bf16[1024,256]{1,0:T(8,128)(2,1)S(1)}, u32[]{:S(2)}, u32[]{:S(2)}) collective-permute-start(bf16[1024,256]{1,0:T(8,128)(2,1)S(1)} %shard_map.89), channel_id=1, source_target_pairs={{0,2},{2,0},{4,6},{6,4},{8,10},{10,8},{12,14},{14,12},{1,3},{3,1},... | collective-permute-start | bytes 1572872 | tf_op jit(solution)/shard_map/ppermute | solution.py:399
  27.3 1.6 %collective-permute-start.6 = (bf16[512,256]{1,0:T(8,128)(2,1)S(1)}, bf16[512,256]{1,0:T(8,128)(2,1)S(1)}, u32[]{:S(2)}, u32[]{:S(2)}) collective-permute-start(bf16[512,256]{1,0:T(8,128)(2,1)S(1)} %get-tuple-element.54), channel_id=1, source_target_pairs={{0,8},{2,10},{4,12},{6,14},{8,0},{10,2},{12,4},{14,6},{1,9},{3,11}... | collective-permute-start | bytes 786440 | tf_op jit(solution)/shard_map/ppermute | solution.py:399
  28.9 4.2 %shard_map.88 = (f32[1024,128]{1,0:T(8,128)S(1)}, f32[1024,128]{1,0:T(8,128)S(1)}) custom-call(s32[16,8]{1,0:T(8,128)S(1)} %copy.12.lists.refs_0_, bf16[1024,256]{1,0:T(8,128)(2,1)S(1)} %shard_map.85.qg.refs_1_.refs_0_, f32[1024,128]{1,0:T(8,128)S(1)} %get-tuple-element.46.stat, f32[1024,128]{1,0:T(8,128)S(1)} %get-tuple-element.47.acc, ...), custom_call_target="tpu_custom_call" | custom-call | flops 1073741824 | bytes 4194816 | tf_op jit(solution)/shard_map/pallas_call | solution.py:38
  33.1 7.9 %collective-permute-done.6.refs_5_.refs_3_ = bf16[512,256]{1,0:T(8,128)(2,1)S(1)} collective-permute-done((bf16[512,256]{1,0:T(8,128)(2,1)S(1)}, bf16[512,256]{1,0:T(8,128)(2,1)S(1)}, u32[]{:S(2)}, u32[]{:S(2)}) %collective-permute-start.6) | collective-permute-done | bytes 262176 | tf_op jit(solution)/shard_map/ppermute | solution.py:399
  41.0 6.8 %shard_map.90 = (bf16[1024,128]{1,0:T(8,128)(2,1)S(1)}, f32[8,1024]{1,0:T(8,128)S(1)}, bf16[1024,256]{1,0:T(8,128)(2,1)S(1)}, f32[1024,128]{1,0:T(8,128)S(1)}) custom-call(s32[16,8]{1,0:T(8,128)S(1)} %copy.12.lists.refs_0_, bf16[1024,256]{1,0:T(8,128)(2,1)S(1)} %shard_map.85.qg.refs_1_.refs_0_, f32[1024,128]{1,0:T(8,128)S(1)} %get-tuple-element.50.refs_2_, ...), custom_call_target="tpu_custom_call" | custom-call | flops 2147483648 | bytes 3703296 | tf_op jit(solution)/shard_map/pallas_call | solution.py:38
  47.8 0.6 collective-permute-start.8
  48.4 1.0 %shard_map.91 = (bf16[512,256]{1,0:T(8,128)(2,1)S(1)}, f32[1024,128]{1,0:T(8,128)S(1)}) custom-call(bf16[1024,256]{1,0:T(8,128)(2,1)S(1)} %shard_map.85.qg.refs_1_.refs_0_, f32[8,1024]{1,0:T(8,128)S(1)} %get-tuple-element.56.refs_1_.row_ref, f32[1024,128]{1,0:T(8,128)S(1)} %get-tuple-element.57.refs_2_, ...), custom_call_target="tpu_custom_call" | custom-call | flops 671088640 | bytes 2129920 | tf_op jit(solution)/shard_map/pallas_call | solution.py:38
  49.4 0.3 collective-permute-start.9
  49.7 8.0 %shard_map.92 = (f32[1024,256]{1,0:T(8,128)S(1)}, bf16[1024,256]{1,0:T(8,128)(2,1)S(1)}, f32[1024,256]{1,0:T(8,128)S(1)}, f32[1024,256]{1,0:T(8,128)S(1)}, bf16[...) custom-call(s32[16,8]{1,0:T(8,128)S(1)} %copy.12.lists.refs_0_, bf16[1024,128]{1,0:T(8,128)(2,1)S(1)} %get-tuple-element.55.o, ...), custom_call_target="tpu_custom_call" | custom-call | flops 5368709120 | bytes 7635456 | tf_op jit(solution)/shard_map/pallas_call | solution.py:38
  57.7 4.0 %collective-permute-done.9.refs_5_ = bf16[512,256]{1,0:T(8,128)(2,1)S(1)} collective-permute-done((bf16[512,256]{1,0:T(8,128)(2,1)S(1)}, bf16[512,256]{1,0:T(8,128)(2,1)S(1)}, u32[]{:S(2)}, u32[]{:S(2)}) %collective-permute-start.9) | collective-permute-done | bytes 262176 | tf_op jit(solution)/shard_map/ppermute | solution.py:399
  61.7 0.3 shard_map.94
  62.0 1.5 %collective-permute-start.10 = (bf16[1024,256]{1,0:T(8,128)(2,1)S(1)}, bf16[1024,256]{1,0:T(8,128)(2,1)S(1)}, u32[]{:S(2)}, u32[]{:S(2)}) collective-permute-start(bf16[1024,256]{1,0:T(8,128)(2,1)S(1)} %get-tuple-element.72), channel_id=1, source_target_pairs={{0,2},{2,0},{4,6},{6,4},{8,10},{10,8},{12,14},{14,12},{1,3},{3,1},... | collective-permute-start | bytes 1572872 | tf_op jit(solution)/shard_map/ppermute | solution.py:399
  63.5 0.7 collective-permute-start.12
  64.3 11.3 %collective-permute-done.10.refs_2_ = bf16[1024,256]{1,0:T(8,128)(2,1)S(1)} collective-permute-done((bf16[1024,256]{1,0:T(8,128)(2,1)S(1)}, bf16[1024,256]{1,0:T(8,128)(2,1)S(1)}, u32[]{:S(2)}, u32[]{:S(2)}) %collective-permute-start.10) | collective-permute-done | bytes 524320 | tf_op jit(solution)/shard_map/ppermute | solution.py:399
  75.6 1.5 %collective-permute-done.11.refs_3_ = bf16[1024,256]{1,0:T(8,128)(2,1)S(1)} collective-permute-done((bf16[1024,256]{1,0:T(8,128)(2,1)S(1)}, bf16[1024,256]{1,0:T(8,128)(2,1)S(1)}, u32[]{:S(2)}, u32[]{:S(2)}) %collective-permute-start.11) | collective-permute-done | bytes 524320 | tf_op jit(solution)/shard_map/ppermute | solution.py:399
  77.1 1.5 %shard_map.95 = (bf16[512,256]{1,0:T(8,128)(2,1)S(1)}, bf16[512,256]{1,0:T(8,128)(2,1)S(1)}) custom-call(s32[16,8]{1,0:T(8,128)S(1)} %copy.12.lists.refs_0_, f32[1024,256]{1,0:T(8,128)S(1)} %get-tuple-element.63.refs_1_, bf16[1024,256]{1,0:T(8,128)(2,1)S(1)} %collective-permute-done.10.refs_2_, bf16[1024,256]{1,0:T(8,128)(2,1)S(1)} %collective-permute-done.11.refs_3_, ...), custom_call_target="tpu_custom_call" | custom-call | bytes 3408384 | tf_op jit(solution)/shard_map/pallas_call | solution.py:38
  78.7 0.9 %shard_map.93 = (bf16[512,256]{1,0:T(8,128)(2,1)}, bf16[512,256]{1,0:T(8,128)(2,1)}) custom-call(bf16[512,256]{1,0:T(8,128)(2,1)S(1)} %get-tuple-element.59.keep, bf16[512,256]{1,0:T(8,128)(2,1)S(1)} %collective-permute-done.7.came), custom_call_target="tpu_custom_call" | custom-call | bytes 1048576 | tf_op jit(solution)/shard_map/pallas_call | solution.py:38
  79.5 0.6 collective-permute-done.13.came
  80.2 0.9 %shard_map.96 = (bf16[512,256]{1,0:T(8,128)(2,1)}, bf16[512,256]{1,0:T(8,128)(2,1)}) custom-call(bf16[512,256]{1,0:T(8,128)(2,1)S(1)} %get-tuple-element.76.keep, bf16[512,256]{1,0:T(8,128)(2,1)S(1)} %collective-permute-done.13.came), custom_call_target="tpu_custom_call" | custom-call | bytes 1048576 | tf_op jit(solution)/shard_map/pallas_call | solution.py:38
  (28 shorter events, 0.5 us)
Async XLA Ops:
  0.6 1.0 %copy-start = (bf16[512,256]{1,0:T(8,128)(2,1)S(1)}, bf16[512,256]{1,0:T(8,128)(2,1)}, u32[]{:S(2)}) copy-start(bf16[512,256]{1,0:T(8,128)(2,1)} %k.3) | copy-start | bytes 786436
  1.6 0.9 %copy-start.2 = (bf16[512,256]{1,0:T(8,128)(2,1)S(1)}, bf16[512,256]{1,0:T(8,128)(2,1)}, u32[]{:S(2)}) copy-start(bf16[512,256]{1,0:T(8,128)(2,1)} %v.3) | copy-start | bytes 786436
  2.5 0.9 %copy-start.4 = (bf16[512,256]{1,0:T(8,128)(2,1)S(1)}, bf16[512,256]{1,0:T(8,128)(2,1)}, u32[]{:S(2)}) copy-start(bf16[512,256]{1,0:T(8,128)(2,1)} %q.3) | copy-start | bytes 786436
  3.5 0.9 %copy-start.6 = (bf16[512,256]{1,0:T(8,128)(2,1)S(1)}, bf16[512,256]{1,0:T(8,128)(2,1)}, u32[]{:S(2)}) copy-start(bf16[512,256]{1,0:T(8,128)(2,1)} %g.3) | copy-start | bytes 786436
  4.4 0.7 copy-start.8
  4.4 1.8 %copy-start.1 = (bf16[512,256]{1,0:T(8,128)(2,1)S(1)}, bf16[512,256]{1,0:T(8,128)(2,1)}, u32[]{:S(2)}) copy-start(bf16[512,256]{1,0:T(8,128)(2,1)} %k.3) | copy-start | bytes 786436
  4.4 1.8 %copy-start.3 = (bf16[512,256]{1,0:T(8,128)(2,1)S(1)}, bf16[512,256]{1,0:T(8,128)(2,1)}, u32[]{:S(2)}) copy-start(bf16[512,256]{1,0:T(8,128)(2,1)} %v.3) | copy-start | bytes 786436
  4.5 1.7 %collective-permute-start.1 = (bf16[512,256]{1,0:T(8,128)(2,1)S(1)}, bf16[512,256]{1,0:T(8,128)(2,1)S(1)}, u32[]{:S(2)}, u32[]{:S(2)}) collective-permute-start(bf16[512,256]{1,0:T(8,128)(2,1)S(1)} %get-tuple-element.43), channel_id=1, source_target_pairs={{0,1},{1,0},{2,3},{3,2},{4,5},{5,4},{6,7},{7,6},{8,9},{9,8},{10,11... | collective-permute-start | bytes 786440 | tf_op jit(solution)/shard_map/ppermute | solution.py:396
  5.2 9.9 %copy-start.5 = (bf16[512,256]{1,0:T(8,128)(2,1)S(1)}, bf16[512,256]{1,0:T(8,128)(2,1)}, u32[]{:S(2)}) copy-start(bf16[512,256]{1,0:T(8,128)(2,1)} %q.3) | copy-start | bytes 786436
  5.2 9.9 %copy-start.7 = (bf16[512,256]{1,0:T(8,128)(2,1)S(1)}, bf16[512,256]{1,0:T(8,128)(2,1)}, u32[]{:S(2)}) copy-start(bf16[512,256]{1,0:T(8,128)(2,1)} %g.3) | copy-start | bytes 786436
  7.0 10.2 %collective-permute-start.3 = (bf16[1024,256]{1,0:T(8,128)(2,1)S(1)}, bf16[1024,256]{1,0:T(8,128)(2,1)S(1)}, u32[]{:S(2)}, u32[]{:S(2)}) collective-permute-start(bf16[1024,256]{1,0:T(8,128)(2,1)S(1)} %get-tuple-element.44.kv), channel_id=1, source_target_pairs={{0,0},{2,2},{4,8},{6,10},{8,4},{10,6},{12,12},{14,14},{1,1},{3,3},... | collective-permute-start | bytes 1572872 | tf_op jit(solution)/shard_map/ppermute | solution.py:399
  7.7 17.8 %collective-permute-start.2 = (bf16[1024,256]{1,0:T(8,128)(2,1)S(1)}, bf16[1024,256]{1,0:T(8,128)(2,1)S(1)}, u32[]{:S(2)}, u32[]{:S(2)}) collective-permute-start(bf16[1024,256]{1,0:T(8,128)(2,1)S(1)} %get-tuple-element.44.kv), channel_id=1, source_target_pairs={{0,4},{2,6},{4,0},{6,2},{8,12},{10,14},{12,8},{14,10},{1,5},{3,7},... | collective-permute-start | bytes 1572872 | tf_op jit(solution)/shard_map/ppermute | solution.py:399
  13.5 1.5 %collective-permute-start = (bf16[512,256]{1,0:T(8,128)(2,1)S(1)}, bf16[512,256]{1,0:T(8,128)(2,1)S(1)}, u32[]{:S(2)}, u32[]{:S(2)}) collective-permute-start(bf16[512,256]{1,0:T(8,128)(2,1)S(1)} %get-tuple-element.42), channel_id=1, source_target_pairs={{0,1},{1,0},{2,3},{3,2},{4,5},{5,4},{6,7},{7,6},{8,9},{9,8},{10,11... | collective-permute-start | bytes 786440 | tf_op jit(solution)/shard_map/ppermute | solution.py:396
  13.5 15.4 %collective-permute-start.4 = (bf16[1024,256]{1,0:T(8,128)(2,1)S(1)}, bf16[1024,256]{1,0:T(8,128)(2,1)S(1)}, u32[]{:S(2)}, u32[]{:S(2)}) collective-permute-start(bf16[1024,256]{1,0:T(8,128)(2,1)S(1)} %get-tuple-element.44.kv), channel_id=1, source_target_pairs={{0,2},{2,0},{4,6},{6,4},{8,10},{10,8},{12,14},{14,12},{1,3},{3,1},... | collective-permute-start | bytes 1572872 | tf_op jit(solution)/shard_map/ppermute | solution.py:399
  25.7 15.3 %collective-permute-start.5 = (bf16[1024,256]{1,0:T(8,128)(2,1)S(1)}, bf16[1024,256]{1,0:T(8,128)(2,1)S(1)}, u32[]{:S(2)}, u32[]{:S(2)}) collective-permute-start(bf16[1024,256]{1,0:T(8,128)(2,1)S(1)} %shard_map.89), channel_id=1, source_target_pairs={{0,2},{2,0},{4,6},{6,4},{8,10},{10,8},{12,14},{14,12},{1,3},{3,1},... | collective-permute-start | bytes 1572872 | tf_op jit(solution)/shard_map/ppermute | solution.py:399
  27.3 13.8 %collective-permute-start.6 = (bf16[512,256]{1,0:T(8,128)(2,1)S(1)}, bf16[512,256]{1,0:T(8,128)(2,1)S(1)}, u32[]{:S(2)}, u32[]{:S(2)}) collective-permute-start(bf16[512,256]{1,0:T(8,128)(2,1)S(1)} %get-tuple-element.54), channel_id=1, source_target_pairs={{0,8},{2,10},{4,12},{6,14},{8,0},{10,2},{12,4},{14,6},{1,9},{3,11}... | collective-permute-start | bytes 786440 | tf_op jit(solution)/shard_map/ppermute | solution.py:399
  47.8 13.9 %collective-permute-start.8 = (bf16[1024,256]{1,0:T(8,128)(2,1)S(1)}, bf16[1024,256]{1,0:T(8,128)(2,1)S(1)}, u32[]{:S(2)}, u32[]{:S(2)}) collective-permute-start(bf16[1024,256]{1,0:T(8,128)(2,1)S(1)} %get-tuple-element.66), channel_id=1, source_target_pairs={{0,2},{2,0},{4,6},{6,4},{8,10},{10,8},{12,14},{14,12},{1,3},{3,1},... | collective-permute-start | bytes 1572872 | tf_op jit(solution)/shard_map/ppermute | solution.py:399
  49.4 12.3 %collective-permute-start.9 = (bf16[512,256]{1,0:T(8,128)(2,1)S(1)}, bf16[512,256]{1,0:T(8,128)(2,1)S(1)}, u32[]{:S(2)}, u32[]{:S(2)}) collective-permute-start(bf16[512,256]{1,0:T(8,128)(2,1)S(1)} %get-tuple-element.67), channel_id=1, source_target_pairs={{0,8},{2,10},{4,12},{6,14},{8,0},{10,2},{12,4},{14,6},{1,9},{3,11}... | collective-permute-start | bytes 786440 | tf_op jit(solution)/shard_map/ppermute | solution.py:399
  62.0 13.6 %collective-permute-start.10 = (bf16[1024,256]{1,0:T(8,128)(2,1)S(1)}, bf16[1024,256]{1,0:T(8,128)(2,1)S(1)}, u32[]{:S(2)}, u32[]{:S(2)}) collective-permute-start(bf16[1024,256]{1,0:T(8,128)(2,1)S(1)} %get-tuple-element.72), channel_id=1, source_target_pairs={{0,2},{2,0},{4,6},{6,4},{8,10},{10,8},{12,14},{14,12},{1,3},{3,1},... | collective-permute-start | bytes 1572872 | tf_op jit(solution)/shard_map/ppermute | solution.py:399
  63.5 13.6 %collective-permute-start.11 = (bf16[1024,256]{1,0:T(8,128)(2,1)S(1)}, bf16[1024,256]{1,0:T(8,128)(2,1)S(1)}, u32[]{:S(2)}, u32[]{:S(2)}) collective-permute-start(bf16[1024,256]{1,0:T(8,128)(2,1)S(1)} %get-tuple-element.73), channel_id=1, source_target_pairs={{0,4},{2,6},{4,0},{6,2},{8,12},{10,14},{12,8},{14,10},{1,5},{3,7},... | collective-permute-start | bytes 1572872 | tf_op jit(solution)/shard_map/ppermute | solution.py:399
  63.5 13.6 %collective-permute-start.12 = (bf16[1024,256]{1,0:T(8,128)(2,1)S(1)}, bf16[1024,256]{1,0:T(8,128)(2,1)S(1)}, u32[]{:S(2)}, u32[]{:S(2)}) collective-permute-start(bf16[1024,256]{1,0:T(8,128)(2,1)S(1)} %get-tuple-element.74), channel_id=1, source_target_pairs={{0,0},{2,2},{4,8},{6,10},{8,4},{10,6},{12,12},{14,14},{1,1},{3,3},... | collective-permute-start | bytes 1572872 | tf_op jit(solution)/shard_map/ppermute | solution.py:399
  64.2 14.4 %collective-permute-start.7 = (bf16[512,256]{1,0:T(8,128)(2,1)S(1)}, bf16[512,256]{1,0:T(8,128)(2,1)S(1)}, u32[]{:S(2)}, u32[]{:S(2)}) collective-permute-start(bf16[512,256]{1,0:T(8,128)(2,1)S(1)} %get-tuple-element.60), channel_id=1, source_target_pairs={{0,1},{1,0},{2,3},{3,2},{4,5},{5,4},{6,7},{7,6},{8,9},{9,8},{10,11... | collective-permute-start | bytes 786440 | tf_op jit(solution)/shard_map/ppermute | solution.py:396
  78.6 1.6 %collective-permute-start.13 = (bf16[512,256]{1,0:T(8,128)(2,1)S(1)}, bf16[512,256]{1,0:T(8,128)(2,1)S(1)}, u32[]{:S(2)}, u32[]{:S(2)}) collective-permute-start(bf16[512,256]{1,0:T(8,128)(2,1)S(1)} %get-tuple-element.77), channel_id=1, source_target_pairs={{0,1},{1,0},{2,3},{3,2},{4,5},{5,4},{6,7},{7,6},{8,9},{9,8},{10,11... | collective-permute-start | bytes 786440 | tf_op jit(solution)/shard_map/ppermute | solution.py:396

commit v3 on v2

v3 whole, which is shorter than its diff:
```python
import functools
import math

import jax
import jax.numpy as jnp
from jax import lax
from jax.experimental import pallas as pl
from jax.experimental.pallas import tpu as pltpu
from jax.sharding import PartitionSpec as P

DH = 128
F32 = jnp.float32
BF16 = jnp.bfloat16
VMEM = pl.BlockSpec(memory_space=pltpu.VMEM)
SMEM = pl.BlockSpec(memory_space=pltpu.SMEM)
HBM = pl.BlockSpec(memory_space=pltpu.HBM)
NEG = -1e30
SCALE = 1.0 / math.sqrt(DH)
EXP_SCALE = SCALE * math.log2(math.e)
KEY = slice(0, DH)
VALUE = slice(DH, 2 * DH)
sds = jax.ShapeDtypeStruct


def dot_nn(a, b):
    return lax.dot_general(a, b, (((1,), (0,)), ((), ())), preferred_element_type=F32)


def dot_nt(a, b):
    return lax.dot_general(a, b, (((1,), (1,)), ((), ())), preferred_element_type=F32)


def dot_tn(a, b):
    return lax.dot_general(a, b, (((0,), (0,)), ((), ())), preferred_element_type=F32)


def call(kernel, args, out_shape, scratch=(), flops=0, source=VMEM):
    return pl.pallas_call(
        kernel,
        out_shape=out_shape,
        in_specs=[SMEM if a.dtype == jnp.int32 else source for a in args],
        out_specs=tuple(VMEM for _ in out_shape),
        scratch_shapes=list(scratch),
        compiler_params=pltpu.CompilerParams(vmem_limit_bytes=40 << 20),
        cost_estimate=pl.CostEstimate(flops=flops // 1000, bytes_accessed=1024, transcendentals=0),
    )(*args)


def swap_pairs(count, distance, second):
    pairs = []
    for frame in range(count):
        up = ((frame // distance) % 2 == 0) != second
        target = frame + distance if up else frame - distance
        pairs.append((frame, target if 0 <= target < count else frame))
    return pairs


class Swap:
    def __init__(self, count, level, second):
        self.count, self.level, self.second = count, level, second
        self.levels = count.bit_length() - 1
        self.pairs = swap_pairs(count, 1 << level, second)
        self.moves = any(source != target for source, target in self.pairs)

    def partner(self, frame):
        odd = lax.rem(lax.shift_right_logical(frame, self.level), 2)
        later = odd == (1 if self.second else 0)
        other = jnp.where(later, frame + (1 << self.level), frame - (1 << self.level))
        return other, later, jnp.logical_and(other >= 0, other < self.count)

    def slot(self, later, k):
        base = 0 if self.level == 0 else self.level + 1
        return jnp.where(later, self.levels + 1, 0) + base + k

    def block_of_mine(self, lists, frame, slab, k):
        other, later, exists = self.partner(frame)
        entry = lists[frame * 2 + slab, self.slot(later, k)]
        return jnp.clip(entry - other * 4, 0, 3), exists

    def block_of_theirs(self, lists, frame, slab, k):
        other, later, exists = self.partner(frame)
        row = jnp.where(exists, other, frame) * 2 + slab
        entry = lists[row, self.slot(jnp.logical_not(later), k)]
        return jnp.clip(entry - frame * 4, 0, 3), exists


def head_cols(head):
    return slice(head * DH, (head + 1) * DH)


def rows_of(slab, half):
    return slice(slab * half, (slab + 1) * half)


def each_core(body):
    core = lax.axis_index("space")
    for mine in range(2):
        pl.when(core == mine)(functools.partial(body, mine))


def pack_kernel(k, v, q, g, kv_send, kv_own, qg_send, qg_own, sems):
    def body(mine):
        copies = []
        for a, b, send, own in ((k, v, kv_send, kv_own), (q, g, qg_send, qg_own)):
            for head, out in ((1 - mine, send), (mine, own)):
                for source, cols in ((a, KEY), (b, VALUE)):
                    sem = sems.at[len(copies)]
                    copies.append(
                        pltpu.make_async_copy(source.at[:, head_cols(head)], out.at[:, cols], sem)
                    )
        for copy in copies:
            copy.start()
        for copy in copies:
            copy.wait()

    each_core(body)


def frame_kernel(own, came, kv, keys, values):
    half = own.shape[0]

    def body(mine):
        for slab, source in ((mine, own), (1 - mine, came)):
            rows = rows_of(slab, half)
            part = source[...]
            kv[rows, :] = part
            keys[rows, :] = part[:, KEY]
            values[rows, :] = part[:, VALUE]

    each_core(body)


def join_kernel(own, came, out):
    half = own.shape[0]

    def body(mine):
        out[rows_of(mine, half), :] = own[...]
        out[rows_of(1 - mine, half), :] = came[...]

    each_core(body)


def select_kernel(far, block, lists, kv, *sends):
    frame = lax.axis_index("tm")
    for swap, send in zip(far, sends):
        for slab in range(2):
            b, _ = swap.block_of_theirs(lists, frame, slab, 0)
            row = pl.multiple_of(b * block, block)
            send[slab * block : (slab + 1) * block, :] = kv[pl.ds(row, block), :]


def forwards_first(frame):
    return lax.rem(frame, 2) == lax.rem(lax.shift_right_logical(frame, 1), 2)


def relay_kernel(z, y, out):
    first = forwards_first(lax.axis_index("tm"))

    @pl.when(first)
    def _():
        out[...] = z[...]

    @pl.when(jnp.logical_not(first))
    def _():
        out[...] = y[...]


class Piece:
    def __init__(self, k, v, row, exists=None, dk=None, dv=None, add=True):
        self.k_at, self.v_at, self.row, self.exists = k, v, row, exists
        self.dk, self.dv, self.add = dk, dv, add

    def load(self, at, block):
        ref, cols = at
        return ref[pl.ds(self.row, block), cols]

    def k(self, block):
        return self.load(self.k_at, block)

    def v(self, block):
        return self.load(self.v_at, block)

    def store(self, at, block, value):
        ref, cols = at
        rows = pl.ds(self.row, block)
        if self.add:
            ref[rows, cols] += value
        else:
            ref[rows, cols] = value.astype(ref.dtype)


def listed(swap, lists, frame, slab, block, k, v, count=1, **grads):
    pieces = []
    for n in range(count):
        b, exists = swap.block_of_mine(lists, frame, slab, n)
        pieces.append(Piece(k, v, pl.multiple_of(b * block, block), exists, **grads))
    return pieces


def arrived(swap, frame, slab, block, kv, **grads):
    _, _, exists = swap.partner(frame)
    return Piece((kv, KEY), (kv, VALUE), slab * block, exists, add=False, **grads)


def score_pieces(q, pieces, block, s_ref, peak):
    top = None
    for j, piece in enumerate(pieces):
        s = dot_nt(q, piece.k(block))
        s_ref[j] = s
        part = s[:, :DH]
        for c in range(DH, block, DH):
            part = jnp.maximum(part, s[:, c : c + DH])
        if piece.exists is not None:
            part = jnp.where(piece.exists, part, NEG)
        top = part if top is None else jnp.maximum(top, part)
    top = jnp.max(top, axis=1, keepdims=True)
    return top if peak is None else jnp.maximum(peak, top)


def raise_pieces(pieces, block, s_ref, peak, with_values):
    total = None
    acc = None
    for j, piece in enumerate(pieces):
        base = peak * EXP_SCALE
        if piece.exists is not None:
            base = jnp.where(piece.exists, base, -NEG)
        e = jnp.exp2(s_ref[j] * EXP_SCALE - base)
        for c in range(0, block, DH):
            part = e[:, c : c + DH]
            total = part if total is None else total + part
        if j < with_values:
            out = dot_nn(e.astype(BF16), piece.v(block))
            acc = out if acc is None else acc + out
    return jnp.sum(total, axis=1, keepdims=True), acc


def merge_state(old, peak, total, acc):
    shrink = jnp.exp2((old[0] - peak) * EXP_SCALE)
    total = total + old[1] * shrink
    return total, old[2] * shrink + acc


def probs(piece, q, lse, block):
    if piece.exists is not None:
        lse = jnp.where(piece.exists, lse, -NEG)
    return jnp.exp2(dot_nt(piece.k(block), q) * EXP_SCALE - lse)


def backward_slab(q, g, lse, row_dot, pieces, block, with_dq=True):
    dq = None
    for piece in pieces:
        p = probs(piece, q, lse, block)
        if piece.dv is not None:
            piece.store(piece.dv, block, dot_nn(p.astype(BF16), g))
        ds = (p * (dot_nt(piece.v(block), g) - row_dot)).astype(BF16)
        if piece.dk is not None:
            piece.store(piece.dk, block, dot_nn(ds, q) * SCALE)
        if with_dq:
            part = dot_tn(ds, piece.k(block))
            dq = part if dq is None else dq + part
    return dq


def store_state(refs, rows, peak, total, acc):
    stat, acc_ref = refs
    lane = lax.broadcasted_iota(jnp.int32, acc.shape, 1)
    stat[rows, :] = jnp.where(lane == 0, peak, total)
    acc_ref[rows, :] = acc


def load_state(refs, rows):
    stat, acc_ref = refs
    return stat[rows, 0:1], stat[rows, 1:2], acc_ref[rows, :]


ALL = slice(None)


def near_kernel(block, qg, kv, stat, acc, s_ref):
    half = qg.shape[0] // 2
    for slab in range(2):
        rows = rows_of(slab, half)
        pieces = [Piece((kv, KEY), (kv, VALUE), r) for r in range(0, 2 * half, block)]
        peak = score_pieces(qg[rows, KEY], pieces, block, s_ref, None)
        total, out = raise_pieces(pieces, block, s_ref, peak, len(pieces))
        store_state((stat, acc), rows, peak, total, out)


def middle_kernel(
    block, swaps, lists, qg, stat, acc, a_kv, z_k, y_k, z_v, y_v, stat2, acc2, s_ref
):
    half = qg.shape[0] // 2
    frame = lax.axis_index("tm")
    a, z, y = swaps
    for slab in range(2):
        rows = rows_of(slab, half)
        pieces = listed(a, lists, frame, slab, block, (a_kv, KEY), (a_kv, VALUE), 2)
        pieces += listed(z, lists, frame, slab, block, (z_k, ALL), (z_v, ALL))
        pieces += listed(y, lists, frame, slab, block, (y_k, ALL), (y_v, ALL))
        old = load_state((stat, acc), rows)
        peak = score_pieces(qg[rows, KEY], pieces, block, s_ref, old[0])
        new = raise_pieces(pieces, block, s_ref, peak, len(pieces))
        store_state((stat2, acc2), rows, peak, *merge_state(old, peak, *new))


def close_kernel(block, relayed, far, *refs):
    n = len(far)
    lists, qg, stat, acc, c_k = refs[:5]
    far_kv = refs[5 : 5 + n]
    lse_ref, part_ref, dc_v = refs[5 + n : 8 + n]
    far_dv = refs[8 + n : 8 + 2 * n]
    s_ref, grad = refs[8 + 2 * n :]
    half = qg.shape[0] // 2
    frame = lax.axis_index("tm")
    grad[...] = jnp.zeros_like(grad)
    for slab in range(2):
        rows = rows_of(slab, half)
        q, g = qg[rows, KEY], qg[rows, VALUE]
        pieces = [
            arrived(swap, frame, slab, block, kv, dv=(out, ALL))
            for swap, kv, out in zip(far, far_kv, far_dv)
        ]
        late = listed(
            relayed, lists, frame, slab, block, (c_k, ALL), None, 2, dv=(grad, ALL)
        )
        old = load_state((stat, acc), rows)
        peak = score_pieces(q, pieces + late, block, s_ref, old[0])
        new = raise_pieces(pieces + late, block, s_ref, peak, n)
        total, out = merge_state(old, peak, *new)
        part_ref[rows, :] = out / total
        lse = jnp.broadcast_to(peak * EXP_SCALE + jnp.log2(total), out.shape).T[:8, :]
        lse_ref[:, rows] = lse
        for piece in late + pieces:
            p = probs(piece, q, lse[0:1, :], block).astype(BF16)
            piece.store(piece.dv, block, dot_nn(p, g))
    dc_v[...] = grad[...].astype(BF16)


def late_kernel(block, relayed, lists, qg, lse_ref, part_ref, c_k, c_v, o_ref, dot_ref, dc_k, grad):
    half = qg.shape[0] // 2
    frame = lax.axis_index("tm")
    grad[...] = jnp.zeros_like(grad)
    for slab in range(2):
        rows = rows_of(slab, half)
        q, g = qg[rows, KEY], qg[rows, VALUE]
        lse = lse_ref[0:1, rows]
        late = listed(
            relayed, lists, frame, slab, block, (c_k, ALL), (c_v, ALL), 2, dk=(grad, ALL)
        )
        out = part_ref[rows, :]
        kept = []
        for piece in late:
            p = probs(piece, q, lse, block)
            kept.append(p)
            out = out + dot_tn(p.astype(BF16), piece.v(block))
        o = out.astype(BF16)
        o_ref[rows, :] = o
        row_dot = jnp.sum(g.astype(F32) * o.astype(F32), axis=1, keepdims=True)
        turned = jnp.broadcast_to(row_dot, out.shape).T[:8, :]
        dot_ref[:, rows] = turned
        for piece, p in zip(late, kept):
            ds = (p * (dot_nt(piece.v(block), g) - turned[0:1, :])).astype(BF16)
            piece.store(piece.dk, block, dot_nn(ds, q) * SCALE)
    dc_k[...] = grad[...].astype(BF16)


def far_kernel(block, far, *refs):
    n = len(far)
    qg, lse_ref, dot_ref = refs[:3]
    far_kv = refs[3 : 3 + n]
    far_dk = refs[3 + n : 3 + 2 * n]
    half = qg.shape[0] // 2
    frame = lax.axis_index("tm")
    for slab in range(2):
        rows = rows_of(slab, half)
        pieces = [
            arrived(swap, frame, slab, block, kv, dk=(out, ALL))
            for swap, kv, out in zip(far, far_kv, far_dk)
        ]
        backward_slab(
            qg[rows, KEY], qg[rows, VALUE], lse_ref[0:1, rows], dot_ref[0:1, rows], pieces, block, False
        )


def second_kernel(
    block, swaps, lists, qg, lse_ref, dot_ref, z_k, y_k, z_v, y_v, dz_k, dy_k, dz_v, dy_v, dq_ref
):
    half = qg.shape[0] // 2
    frame = lax.axis_index("tm")
    _, z, y = swaps
    for ref in (dz_k, dy_k, dz_v, dy_v):
        ref[...] = jnp.zeros_like(ref)
    for slab in range(2):
        rows = rows_of(slab, half)
        pieces = listed(
            z, lists, frame, slab, block, (z_k, ALL), (z_v, ALL), dk=(dz_k, ALL), dv=(dz_v, ALL)
        )
        pieces += listed(
            y, lists, frame, slab, block, (y_k, ALL), (y_v, ALL), dk=(dy_k, ALL), dv=(dy_v, ALL)
        )
        dq_ref[rows, :] = backward_slab(
            qg[rows, KEY], qg[rows, VALUE], lse_ref[0:1, rows], dot_ref[0:1, rows], pieces, block
        )


def first_kernel(block, swaps, lists, qg, lse_ref, dot_ref, dq_old, a_kv, da, dq_ref, grad):
    half = qg.shape[0] // 2
    frame = lax.axis_index("tm")
    grad[...] = jnp.zeros_like(grad)
    for slab in range(2):
        rows = rows_of(slab, half)
        pieces = listed(
            swaps[0], lists, frame, slab, block, (a_kv, KEY), (a_kv, VALUE), 2,
            dk=(grad, KEY), dv=(grad, VALUE),
        )
        dq_ref[rows, :] = dq_old[rows, :] + backward_slab(
            qg[rows, KEY], qg[rows, VALUE], lse_ref[0:1, rows], dot_ref[0:1, rows], pieces, block
        )
    da[...] = grad[...].astype(BF16)


def own_kernel(block, relayed, far, *refs):
    n = len(far)
    lists, qg, lse_ref, dot_ref, dq_old, o, kv, c_k, c_v = refs[:9]
    far_kv = refs[9 : 9 + n]
    near, keep, send = refs[9 + n :]
    half = qg.shape[0] // 2
    frame = lax.axis_index("tm")
    near[...] = jnp.zeros_like(near)
    whole = []
    for slab in range(2):
        rows = rows_of(slab, half)
        pieces = [
            Piece((kv, KEY), (kv, VALUE), r, dk=(near, KEY), dv=(near, VALUE))
            for r in range(0, 2 * half, block)
        ]
        pieces += listed(relayed, lists, frame, slab, block, (c_k, ALL), (c_v, ALL), 2)
        pieces += [arrived(swap, frame, slab, block, ref) for swap, ref in zip(far, far_kv)]
        dq = dq_old[rows, :] + backward_slab(
            qg[rows, KEY], qg[rows, VALUE], lse_ref[0:1, rows], dot_ref[0:1, rows], pieces, block
        )
        whole.append((dq * SCALE).astype(BF16))

    def body(mine):
        for slab in range(2):
            out = keep if slab == mine else send
            out[:, KEY] = o[rows_of(slab, half), :]
            out[:, VALUE] = whole[slab]

    each_core(body)


def merge_kernel(dz, dy, came, z_out, y_out):
    first = forwards_first(lax.axis_index("tm"))
    more = came[...].astype(F32)
    z_out[...] = (dz[...] + jnp.where(first, more, 0.0)).astype(BF16)
    y_out[...] = (dy[...] + jnp.where(first, 0.0, more)).astype(BF16)


def place_kernel(block, far, *refs):
    n = len(far)
    lists, near = refs[:2]
    far_dk, far_dv = refs[2 : 2 + n], refs[2 + n : 2 + 2 * n]
    sum_k, sum_v = refs[2 + 2 * n :]
    frame = lax.axis_index("tm")
    sum_k[...] = near[:, KEY]
    sum_v[...] = near[:, VALUE]
    for j, swap in enumerate(far):
        for slab in range(2):
            b, exists = swap.block_of_theirs(lists, frame, slab, 0)
            rows = pl.ds(pl.multiple_of(b * block, block), block)
            for came, out in ((far_dk[j], sum_k), (far_dv[j], sum_v)):
                part = came[slab * block : (slab + 1) * block, :].astype(F32)
                out[rows, :] += jnp.where(exists, part, 0.0)


def gather_kernel(swaps, cols, near, da, dz, dy, keep, send):
    frame = lax.axis_index("tm")
    half = near.shape[0] // 2
    there = [swap.partner(frame)[2] for swap in swaps]

    def body(mine):
        for slab, out in ((mine, keep), (1 - mine, send)):
            rows = rows_of(slab, half)
            total = near[rows, :]
            for exists, part in zip(there, (da[rows, cols], dz[rows, :], dy[rows, :])):
                total = total + jnp.where(exists, part.astype(F32), 0.0)
            out[...] = total.astype(BF16)

    each_core(body)


def heads_kernel(keep, came, out):
    def body(mine):
        out[:, head_cols(mine)] = keep[...]
        out[:, head_cols(1 - mine)] = came[...]

    each_core(body)


def split_kernel(keep, came, first, second):
    def body(mine):
        for head, source in ((mine, keep), (1 - mine, came)):
            first[:, head_cols(head)] = source[:, KEY]
            second[:, head_cols(head)] = source[:, VALUE]

    each_core(body)


def per_device(queries, key_rows, value_rows, out_grad, block_lists):
    s_dev, width = queries.shape
    count = lax.axis_size("tm")
    block = s_dev // 2
    pair = sds((s_dev, 2 * DH), BF16)
    single = sds((s_dev, DH), BF16)
    frame_two = sds((2 * s_dev, 2 * DH), BF16)
    frame_one = sds((2 * s_dev, DH), BF16)
    frame_sum = sds((2 * s_dev, DH), F32)
    stat_row = sds((8, 2 * s_dev), F32)
    levels = count.bit_length() - 1
    near_swap, relayed = Swap(count, 0, False), Swap(count, 0, True)
    z_swap, y_swap = Swap(count, 1, False), Swap(count, 1, True)
    swaps = (near_swap, z_swap, y_swap)
    far = [Swap(count, level, second) for level in range(2, levels) for second in (False, True)]
    far = [swap for swap in far if swap.moves]
    n = len(far)
    product = 2 * 2 * s_dev * block * DH
    grad_one = pltpu.VMEM((2 * s_dev, DH), F32)

    def across(value):
        return lax.ppermute(value, "space", [(0, 1), (1, 0)])

    def swapped(value, swap):
        return lax.ppermute(value, "tm", swap.pairs)

    def scores(pieces):
        return pltpu.VMEM((pieces, s_dev, block), F32)

    kv_send, kv_own, qg_send, qg_own = call(
        pack_kernel,
        (key_rows, value_rows, queries, out_grad),
        [pair] * 4,
        scratch=[pltpu.SemaphoreType.DMA((8,))],
        source=HBM,
    )
    kv, keys, values = call(
        frame_kernel, (kv_own, across(kv_send)), [frame_two, frame_one, frame_one]
    )
    z_k = swapped(keys, z_swap)
    y_k = swapped(keys, y_swap)
    a_kv = swapped(kv, near_swap)
    z_v = swapped(values, z_swap)
    y_v = swapped(values, y_swap)
    far_send = call(functools.partial(select_kernel, far, block), (block_lists, kv), [pair] * n)
    (qg,) = call(join_kernel, (qg_own, across(qg_send)), [frame_two])
    stat, acc = call(
        functools.partial(near_kernel, block),
        (qg, kv),
        [frame_sum, frame_sum],
        scratch=[scores(4)],
        flops=2 * 4 * 2 * product,
    )
    z_k, y_k, stat = lax.optimization_barrier((z_k, y_k, stat))
    (relay_k,) = call(relay_kernel, (z_k, y_k), [frame_one])
    relay_k, far_send = lax.optimization_barrier((relay_k, far_send))
    c_k = swapped(relay_k, near_swap)
    far_kv = [swapped(value, swap) for value, swap in zip(far_send, far)]
    (relay_v,) = call(relay_kernel, (z_v, y_v), [frame_one])
    c_v = swapped(relay_v, near_swap)
    relay_v, stat = lax.optimization_barrier((relay_v, stat))
    stat, acc = call(
        functools.partial(middle_kernel, block, swaps),
        (block_lists, qg, stat, acc, a_kv, z_k, y_k, z_v, y_v),
        [frame_sum, frame_sum],
        scratch=[scores(4)],
        flops=2 * 4 * 2 * product,
    )
    lse, part, dc_v, *far_dv = call(
        functools.partial(close_kernel, block, relayed, far),
        (block_lists, qg, stat, acc, c_k, *far_kv),
        [stat_row, frame_sum, frame_one] + [single] * n,
        scratch=[scores(2 + n), grad_one],
        flops=2 * (2 + n) * 4 * product,
    )
    dc_v_came = swapped(dc_v, near_swap)
    far_dv_came = [swapped(value, swap) for value, swap in zip(far_dv, far)]
    o, row_dot, dc_k = call(
        functools.partial(late_kernel, block, relayed),
        (block_lists, qg, lse, part, c_k, c_v),
        [frame_one, stat_row, frame_one],
        scratch=[grad_one],
        flops=2 * 2 * 4 * product,
    )
    dc_k_came = swapped(dc_k, near_swap)
    far_dk = call(
        functools.partial(far_kernel, block, far),
        (qg, lse, row_dot, *far_kv),
        [single] * n,
        flops=2 * n * 3 * product,
    )
    far_dk_came = [swapped(value, swap) for value, swap in zip(far_dk, far)]
    far_dk, row_dot = lax.optimization_barrier((far_dk, row_dot))
    dz_k, dy_k, dz_v, dy_v, dq = call(
        functools.partial(second_kernel, block, swaps),
        (block_lists, qg, lse, row_dot, z_k, y_k, z_v, y_v),
        [frame_sum] * 5,
        flops=2 * 2 * 5 * product,
    )
    dc_v_came, far_dv_came = lax.optimization_barrier((dc_v_came, far_dv_came))
    dz_v, dy_v = call(merge_kernel, (dz_v, dy_v, dc_v_came), [frame_one, frame_one])
    dz_v_came = swapped(dz_v, z_swap)
    dy_v_came = swapped(dy_v, y_swap)
    dq, dz_v, dy_v = lax.optimization_barrier((dq, dz_v, dy_v))
    da, dq = call(
        functools.partial(first_kernel, block, swaps),
        (block_lists, qg, lse, row_dot, dq, a_kv),
        [frame_two, frame_sum],
        scratch=[pltpu.VMEM((2 * s_dev, 2 * DH), F32)],
        flops=2 * 2 * 5 * product,
    )
    da_came = swapped(da, near_swap)
    dc_k_came, far_dk_came = lax.optimization_barrier((dc_k_came, far_dk_came))
    dz_k, dy_k = call(merge_kernel, (dz_k, dy_k, dc_k_came), [frame_one, frame_one])
    dz_k_came = swapped(dz_k, z_swap)
    dy_k_came = swapped(dy_k, y_swap)
    dq, dz_k, dy_k = lax.optimization_barrier((dq, dz_k, dy_k))
    near, keep, send = call(
        functools.partial(own_kernel, block, relayed, far),
        (block_lists, qg, lse, row_dot, dq, o, kv, c_k, c_v, *far_kv),
        [frame_two_sum(s_dev), pair, pair],
        flops=2 * (4 * 5 + (2 + n) * 3) * product,
    )
    half_rows = sds((s_dev, width), BF16)
    attn_out, grad_q = call(split_kernel, (keep, across(send)), [half_rows, half_rows])
    sum_k, sum_v = call(
        functools.partial(place_kernel, block, far),
        (block_lists, near, *far_dk_came, *far_dv_came),
        [frame_sum, frame_sum],
    )
    outs = []
    for total, cols, dz, dy in (
        (sum_v, VALUE, dz_v_came, dy_v_came),
        (sum_k, KEY, dz_k_came, dy_k_came),
    ):
        keep, send = call(
            functools.partial(gather_kernel, swaps, cols),
            (total, da_came, dz, dy),
            [single, single],
        )
        outs += call(heads_kernel, (keep, across(send)), [half_rows])
    grad_v, grad_k = outs
    return attn_out, grad_q, grad_k, grad_v


def frame_two_sum(s_dev):
    return sds((2 * s_dev, 2 * DH), F32)


def solution(mesh):
    rows = P(("groups", "tm", "space"), None)
    return jax.shard_map(
        per_device,
        mesh=mesh,
        in_specs=(rows, rows, rows, rows, P("groups", None)),
        out_specs=(rows, rows, rows, rows),
        check_vma=False,
    )
```

time: 82.3 us -> 80.7 us (0.981); the launches traced: 81 us -> 80.4 us
  waiting for transfers between devices: 34.6 us -> 11.6 us
  starting transfers between devices: 15 us -> 27.3 us
  Pallas kernels: 26.8 us -> 36.8 us
    ppermute x10 -> x17, waiting for transfers between devices: 32.9 us -> 10.5 us  [swapped(): return lax.ppermute(value, 'tm', swap.pairs)]
    ppermute x10 -> x17, starting transfers between devices: 14.3 us -> 26 us  [swapped(): return lax.ppermute(value, 'tm', swap.pairs)]
    pallas_call x13 -> x22, Pallas kernels: 26.8 us -> 36.8 us  [call(): pl.pallas_call(kernel, out_shape=out_shape, in_specs=[SMEM if a.dtype ==...]
    ppermute x4 -> x5, waiting for transfers between devices: 1.65 us -> 1.09 us  [across(): return lax.ppermute(value, 'space', [(0, 1), (1, 0)])]
    unnamed x19 -> x11, local copies, waits for them, and re-layouts: 3.95 us -> 3.87 us
  transfers between devices with their start and end apart: 14 -> 22, of which waited for: 7 -> 8; matrix products, arithmetic and copies ran while one was open for 0% -> 0% of each run, Pallas kernels for 22% -> 44%
where the time goes in v3:
time: 80.7 us; the launch traced here: 80.4 us
  Pallas kernels  36.8 us (46%)
  starting transfers between devices  27.3 us (34%)
  waiting for transfers between devices  11.6 us (14%)
  local copies, waits for them, and re-layouts  3.87 us (5%)
  between operations  0.87 us (1%)
    pallas_call x22, Pallas kernels, call(): pl.pallas_call(kernel, out_shape=out_shape, in_specs=[SMEM if a.dtype ==...  36.8 us
    ppermute x17, starting transfers between devices, swapped(): return lax.ppermute(value, 'tm', swap.pairs)  26 us
    ppermute x17, waiting for transfers between devices, swapped(): return lax.ppermute(value, 'tm', swap.pairs)  10.5 us
    unnamed x11, local copies, waits for them, and re-layouts  3.87 us
  transfers between devices with their start and end apart: 22, of which 8 were waited for; matrix products, arithmetic and copies ran while one was open for 0% of the time, Pallas kernels for 44%

profile of v3, /device:TPU:0, one launch (start us, length us, event | category | flops | bytes accessed | tf_op | source)
XLA Modules:
  0.0 80.4 jit_solution(8201263304442723040)
XLA Ops:
  0.6 0.9 %copy-done = bf16[512,256]{1,0:T(8,128)(2,1)S(1)} copy-done((bf16[512,256]{1,0:T(8,128)(2,1)S(1)}, bf16[512,256]{1,0:T(8,128)(2,1)}, u32[]{:S(2)}) %copy-start) | copy-done | bytes 262168
  1.6 0.9 %copy-done.1 = bf16[512,256]{1,0:T(8,128)(2,1)S(1)} copy-done((bf16[512,256]{1,0:T(8,128)(2,1)S(1)}, bf16[512,256]{1,0:T(8,128)(2,1)}, u32[]{:S(2)}) %copy-start.1) | copy-done | bytes 262168
  2.5 0.9 %copy-done.2 = bf16[512,256]{1,0:T(8,128)(2,1)S(1)} copy-done((bf16[512,256]{1,0:T(8,128)(2,1)S(1)}, bf16[512,256]{1,0:T(8,128)(2,1)}, u32[]{:S(2)}) %copy-start.2) | copy-done | bytes 262168
  3.5 0.9 %copy-done.3 = bf16[512,256]{1,0:T(8,128)(2,1)S(1)} copy-done((bf16[512,256]{1,0:T(8,128)(2,1)S(1)}, bf16[512,256]{1,0:T(8,128)(2,1)}, u32[]{:S(2)}) %copy-start.3) | copy-done | bytes 262168
  5.3 1.1 %collective-permute-done.1.came = bf16[512,256]{1,0:T(8,128)(2,1)S(1)} collective-permute-done((bf16[512,256]{1,0:T(8,128)(2,1)S(1)}, bf16[512,256]{1,0:T(8,128)(2,1)S(1)}, u32[]{:S(2)}, u32[]{:S(2)}) %collective-permute-start.1) | collective-permute-done | bytes 262176 | tf_op jit(solution)/shard_map/ppermute | solution.py:531
  7.2 5.8 %collective-permute-start.4 = (bf16[1024,128]{1,0:T(8,128)(2,1)S(1)}, bf16[1024,128]{1,0:T(8,128)(2,1)S(1)}, u32[]{:S(2)}, u32[]{:S(2)}) collective-permute-start(bf16[1024,128]{1,0:T(8,128)(2,1)S(1)} %get-tuple-element.62), channel_id=1, source_target_pairs={{0,4},{2,6},{4,0},{6,2},{8,12},{10,14},{12,8},{14,10},{1,5},{3,7},... | collective-permute-start | bytes 786440 | tf_op jit(solution)/shard_map/ppermute | solution.py:534
  13.0 1.5 %collective-permute-start.6 = (bf16[1024,256]{1,0:T(8,128)(2,1)S(1)}, bf16[1024,256]{1,0:T(8,128)(2,1)S(1)}, u32[]{:S(2)}, u32[]{:S(2)}) collective-permute-start(bf16[1024,256]{1,0:T(8,128)(2,1)S(1)} %get-tuple-element.63.kv.refs_6_), channel_id=1, source_target_pairs={{0,2},{2,0},{4,6},{6,4},{8,10},{10,8},{12,14},{14,12},{1,3},{3,1},... | collective-permute-start | bytes 1572872 | tf_op jit(solution)/shard_map/ppermute | solution.py:534
  14.6 0.7 shard_map.91
  16.0 1.8 %collective-permute-start.2 = (bf16[1024,128]{1,0:T(8,128)(2,1)S(1)}, bf16[1024,128]{1,0:T(8,128)(2,1)S(1)}, u32[]{:S(2)}, u32[]{:S(2)}) collective-permute-start(bf16[1024,128]{1,0:T(8,128)(2,1)S(1)} %get-tuple-element.61), channel_id=1, source_target_pairs={{0,4},{2,6},{4,0},{6,2},{8,12},{10,14},{12,8},{14,10},{1,5},{3,7},... | collective-permute-start | bytes 786440 | tf_op jit(solution)/shard_map/ppermute | solution.py:534
  17.9 2.1 %shard_map.88 = (f32[1024,128]{1,0:T(8,128)S(1)}, f32[1024,128]{1,0:T(8,128)S(1)}) custom-call(bf16[1024,256]{1,0:T(8,128)(2,1)S(1)} %shard_map.85.qg.refs_1_.refs_0_, bf16[1024,256]{1,0:T(8,128)(2,1)S(1)} %get-tuple-element.63.kv.refs_6_), custom_call_target="tpu_custom_call" | custom-call | flops 1073741 | bytes 1024 | tf_op jit(solution)/shard_map/pallas_call | solution.py:38
  20.2 1.6 %collective-permute-start.7 = (bf16[1024,128]{1,0:T(8,128)(2,1)S(1)}, bf16[1024,128]{1,0:T(8,128)(2,1)S(1)}, u32[]{:S(2)}, u32[]{:S(2)}) collective-permute-start(bf16[1024,128]{1,0:T(8,128)(2,1)S(1)} %shard_map.90), channel_id=1, source_target_pairs={{0,2},{2,0},{4,6},{6,4},{8,10},{10,8},{12,14},{14,12},{1,3},{3,1},... | collective-permute-start | bytes 786440 | tf_op jit(solution)/shard_map/ppermute | solution.py:534
  21.7 1.9 %collective-permute-start.8 = (bf16[512,256]{1,0:T(8,128)(2,1)S(1)}, bf16[512,256]{1,0:T(8,128)(2,1)S(1)}, u32[]{:S(2)}, u32[]{:S(2)}) collective-permute-start(bf16[512,256]{1,0:T(8,128)(2,1)S(1)} %shard_map.91), channel_id=1, source_target_pairs={{0,8},{2,10},{4,12},{6,14},{8,0},{10,2},{12,4},{14,6},{1,9},{3,11}... | collective-permute-start | bytes 786440 | tf_op jit(solution)/shard_map/ppermute | solution.py:534
  23.7 2.1 %collective-permute-done.2.z.z_v = bf16[1024,128]{1,0:T(8,128)(2,1)S(1)} collective-permute-done((bf16[1024,128]{1,0:T(8,128)(2,1)S(1)}, bf16[1024,128]{1,0:T(8,128)(2,1)S(1)}, u32[]{:S(2)}, u32[]{:S(2)}) %collective-permute-start.2) | collective-permute-done | bytes 262176 | tf_op jit(solution)/shard_map/ppermute | solution.py:534
  26.0 1.4 %collective-permute-start.9 = (bf16[1024,128]{1,0:T(8,128)(2,1)S(1)}, bf16[1024,128]{1,0:T(8,128)(2,1)S(1)}, u32[]{:S(2)}, u32[]{:S(2)}) collective-permute-start(bf16[1024,128]{1,0:T(8,128)(2,1)S(1)} %shard_map.87), channel_id=1, source_target_pairs={{0,2},{2,0},{4,6},{6,4},{8,10},{10,8},{12,14},{14,12},{1,3},{3,1},... | collective-permute-start | bytes 786440 | tf_op jit(solution)/shard_map/ppermute | solution.py:534
  27.9 4.6 %shard_map.89 = (f32[1024,128]{1,0:T(8,128)S(1)}, f32[1024,128]{1,0:T(8,128)S(1)}) custom-call(s32[16,8]{1,0:T(8,128)S(1)} %copy.15.lists.refs_0_, bf16[1024,256]{1,0:T(8,128)(2,1)S(1)} %shard_map.85.qg.refs_1_.refs_0_, f32[1024,128]{1,0:T(8,128)S(1)} %get-tuple-element.66.stat, f32[1024,128]{1,0:T(8,128)S(1)} %get-tuple-element.67.acc, ...), custom_call_target="tpu_custom_call" | custom-call | flops 1073741 | bytes 1024 | tf_op jit(solution)/shard_map/pallas_call | solution.py:38
  32.5 1.0 %collective-permute-done.7.refs_4_.c_k.refs_7_ = bf16[1024,128]{1,0:T(8,128)(2,1)S(1)} collective-permute-done((bf16[1024,128]{1,0:T(8,128)(2,1)S(1)}, bf16[1024,128]{1,0:T(8,128)(2,1)S(1)}, u32[]{:S(2)}, u32[]{:S(2)}) %collective-permute-start.7) | collective-permute-done | bytes 262176 | tf_op jit(solution)/shard_map/ppermute | solution.py:534
  33.5 2.5 %collective-permute-done.8.refs_5_.refs_3_.refs_9_ = bf16[512,256]{1,0:T(8,128)(2,1)S(1)} collective-permute-done((bf16[512,256]{1,0:T(8,128)(2,1)S(1)}, bf16[512,256]{1,0:T(8,128)(2,1)S(1)}, u32[]{:S(2)}, u32[]{:S(2)}) %collective-permute-start.8) | collective-permute-done | bytes 262176 | tf_op jit(solution)/shard_map/ppermute | solution.py:534
  36.0 7.8 %shard_map.92 = (f32[8,1024]{1,0:T(8,128)S(1)}, f32[1024,128]{1,0:T(8,128)S(1)}, bf16[1024,128]{1,0:T(8,128)(2,1)S(1)}, bf16[512,128]{1,0:T(8,128)(2,1)S(1)}) custom-call(s32[16,8]{1,0:T(8,128)S(1)} %copy.15.lists.refs_0_, bf16[1024,256]{1,0:T(8,128)(2,1)S(1)} %shard_map.85.qg.refs_1_.refs_0_, f32[1024,128]{1,0:T(8,128)S(1)} %get-tuple-element.70.refs_2_, ...), custom_call_target="tpu_custom_call" | custom-call | flops 1610612 | bytes 1024 | tf_op jit(solution)/shard_map/pallas_call | solution.py:38
  43.8 1.6 %collective-permute-start.10 = (bf16[1024,128]{1,0:T(8,128)(2,1)S(1)}, bf16[1024,128]{1,0:T(8,128)(2,1)S(1)}, u32[]{:S(2)}, u32[]{:S(2)}) collective-permute-start(bf16[1024,128]{1,0:T(8,128)(2,1)S(1)} %get-tuple-element.81), channel_id=1, source_target_pairs={{0,2},{2,0},{4,6},{6,4},{8,10},{10,8},{12,14},{14,12},{1,3},{3,1},... | collective-permute-start | bytes 786440 | tf_op jit(solution)/shard_map/ppermute | solution.py:534
  45.4 2.9 %shard_map.93 = (bf16[1024,128]{1,0:T(8,128)(2,1)S(1)}, f32[8,1024]{1,0:T(8,128)S(1)}, bf16[1024,128]{1,0:T(8,128)(2,1)S(1)}) custom-call(s32[16,8]{1,0:T(8,128)S(1)} %copy.15.lists.refs_0_, bf16[1024,256]{1,0:T(8,128)(2,1)S(1)} %shard_map.85.qg.refs_1_.refs_0_, f32[8,1024]{1,0:T(8,128)S(1)} %get-tuple-element.74.lse_ref.refs_1_.refs_2_, ...), custom_call_target="tpu_custom_call" | custom-call | flops 1073741 | bytes 1024 | tf_op jit(solution)/shard_map/pallas_call | solution.py:38
  48.3 0.7 shard_map.94
  49.6 3.4 %shard_map.95 = (f32[1024,128]{1,0:T(8,128)S(1)}, f32[1024,128]{1,0:T(8,128)S(1)}, f32[1024,128]{1,0:T(8,128)S(1)}, f32[1024,128]{1,0:T(8,128)S(1)}, f32[1024,128]{1,0:T(8,128)S(1)}) custom-call(s32[16,8]{1,0:T(8,128)S(1)} %copy.15.lists.refs_0_, bf16[1024,256]{1,0:T(8,128)(2,1)S(1)} %shard_map.85.qg.refs_1_.refs_0_, ...), custom_call_target="tpu_custom_call" | custom-call | flops 1342177 | bytes 1024 | tf_op jit(solution)/shard_map/pallas_call | solution.py:38
  53.5 3.0 %shard_map.97 = (bf16[1024,256]{1,0:T(8,128)(2,1)S(1)}, f32[1024,128]{1,0:T(8,128)S(1)}) custom-call(s32[16,8]{1,0:T(8,128)S(1)} %copy.15.lists.refs_0_, bf16[1024,256]{1,0:T(8,128)(2,1)S(1)} %shard_map.85.qg.refs_1_.refs_0_, f32[8,1024]{1,0:T(8,128)S(1)} %get-tuple-element.74.lse_ref.refs_1_.refs_2_, ...), custom_call_target="tpu_custom_call" | custom-call | flops 1342177 | bytes 1024 | tf_op jit(solution)/shard_map/pallas_call | solution.py:38
  56.5 1.4 %collective-permute-start.15 = (bf16[1024,256]{1,0:T(8,128)(2,1)S(1)}, bf16[1024,256]{1,0:T(8,128)(2,1)S(1)}, u32[]{:S(2)}, u32[]{:S(2)}) collective-permute-start(bf16[1024,256]{1,0:T(8,128)(2,1)S(1)} %get-tuple-element.104), channel_id=1, source_target_pairs={{0,2},{2,0},{4,6},{6,4},{8,10},{10,8},{12,14},{14,12},{1,3},{3,1},... | collective-permute-start | bytes 1572872 | tf_op jit(solution)/shard_map/ppermute | solution.py:534
  57.8 2.8 %collective-permute-start.13 = (bf16[512,128]{1,0:T(8,128)(2,1)S(1)}, bf16[512,128]{1,0:T(8,128)(2,1)S(1)}, u32[]{:S(2)}, u32[]{:S(2)}) collective-permute-start(bf16[512,128]{1,0:T(8,128)(2,1)S(1)} %shard_map.94), channel_id=1, source_target_pairs={{0,8},{2,10},{4,12},{6,14},{8,0},{10,2},{12,4},{14,6},{1,9},{3,11}... | collective-permute-start | bytes 393224 | tf_op jit(solution)/shard_map/ppermute | solution.py:534
  61.5 4.0 %collective-permute-done.13.refs_2_ = bf16[512,128]{1,0:T(8,128)(2,1)S(1)} collective-permute-done((bf16[512,128]{1,0:T(8,128)(2,1)S(1)}, bf16[512,128]{1,0:T(8,128)(2,1)S(1)}, u32[]{:S(2)}, u32[]{:S(2)}) %collective-permute-start.13) | collective-permute-done | bytes 131104 | tf_op jit(solution)/shard_map/ppermute | solution.py:534
  65.6 2.7 %collective-permute-start.16 = (bf16[1024,128]{1,0:T(8,128)(2,1)S(1)}, bf16[1024,128]{1,0:T(8,128)(2,1)S(1)}, u32[]{:S(2)}, u32[]{:S(2)}) collective-permute-start(bf16[1024,128]{1,0:T(8,128)(2,1)S(1)} %get-tuple-element.92), channel_id=1, source_target_pairs={{0,4},{2,6},{4,0},{6,2},{8,12},{10,14},{12,8},{14,10},{1,5},{3,7},... | collective-permute-start | bytes 786440 | tf_op jit(solution)/shard_map/ppermute | solution.py:534
  69.0 7.0 %shard_map.99 = (f32[1024,256]{1,0:T(8,128)S(1)}, bf16[512,256]{1,0:T(8,128)(2,1)S(1)}, bf16[512,256]{1,0:T(8,128)(2,1)S(1)}) custom-call(s32[16,8]{1,0:T(8,128)S(1)} %copy.15.lists.refs_0_, bf16[1024,256]{1,0:T(8,128)(2,1)S(1)} %shard_map.85.qg.refs_1_.refs_0_, f32[8,1024]{1,0:T(8,128)S(1)} %get-tuple-element.74.lse_ref.refs_1_.refs_2_, ...), custom_call_target="tpu_custom_call" | custom-call | flops 3892314 | bytes 1024 | tf_op jit(solution)/shard_map/pallas_call | solution.py:38
  76.1 0.8 shard_map.101
  78.0 0.9 %shard_map.100 = (bf16[512,256]{1,0:T(8,128)(2,1)}, bf16[512,256]{1,0:T(8,128)(2,1)}) custom-call(bf16[512,256]{1,0:T(8,128)(2,1)S(1)} %get-tuple-element.96.keep, bf16[512,256]{1,0:T(8,128)(2,1)S(1)} %collective-permute-done.14.came), custom_call_target="tpu_custom_call" | custom-call | bytes 1024 | tf_op jit(solution)/shard_map/pallas_call | solution.py:38
  78.9 0.8 shard_map.105
  79.6 0.8 shard_map.103
  (45 shorter events, 7.0 us)
Async XLA Ops:
  0.6 1.0 %copy-start = (bf16[512,256]{1,0:T(8,128)(2,1)S(1)}, bf16[512,256]{1,0:T(8,128)(2,1)}, u32[]{:S(2)}) copy-start(bf16[512,256]{1,0:T(8,128)(2,1)} %k.1) | copy-start | bytes 786436
  1.6 0.9 %copy-start.1 = (bf16[512,256]{1,0:T(8,128)(2,1)S(1)}, bf16[512,256]{1,0:T(8,128)(2,1)}, u32[]{:S(2)}) copy-start(bf16[512,256]{1,0:T(8,128)(2,1)} %v.1) | copy-start | bytes 786436
  2.5 0.9 %copy-start.2 = (bf16[512,256]{1,0:T(8,128)(2,1)S(1)}, bf16[512,256]{1,0:T(8,128)(2,1)}, u32[]{:S(2)}) copy-start(bf16[512,256]{1,0:T(8,128)(2,1)} %q.1) | copy-start | bytes 786436
  3.5 0.9 %copy-start.3 = (bf16[512,256]{1,0:T(8,128)(2,1)S(1)}, bf16[512,256]{1,0:T(8,128)(2,1)}, u32[]{:S(2)}) copy-start(bf16[512,256]{1,0:T(8,128)(2,1)} %g.1) | copy-start | bytes 786436
  4.7 1.7 %collective-permute-start.1 = (bf16[512,256]{1,0:T(8,128)(2,1)S(1)}, bf16[512,256]{1,0:T(8,128)(2,1)S(1)}, u32[]{:S(2)}, u32[]{:S(2)}) collective-permute-start(bf16[512,256]{1,0:T(8,128)(2,1)S(1)} %get-tuple-element.60), channel_id=1, source_target_pairs={{0,1},{1,0},{2,3},{3,2},{4,5},{5,4},{6,7},{7,6},{8,9},{9,8},{10,11... | collective-permute-start | bytes 786440 | tf_op jit(solution)/shard_map/ppermute | solution.py:531
  5.2 10.8 %collective-permute-start = (bf16[512,256]{1,0:T(8,128)(2,1)S(1)}, bf16[512,256]{1,0:T(8,128)(2,1)S(1)}, u32[]{:S(2)}, u32[]{:S(2)}) collective-permute-start(bf16[512,256]{1,0:T(8,128)(2,1)S(1)} %get-tuple-element.58), channel_id=1, source_target_pairs={{0,1},{1,0},{2,3},{3,2},{4,5},{5,4},{6,7},{7,6},{8,9},{9,8},{10,11... | collective-permute-start | bytes 786440 | tf_op jit(solution)/shard_map/ppermute | solution.py:531
  6.4 8.1 %copy-start.4 = (s32[16,8]{0,1:T(8,128)S(1)}, s32[16,8]{0,1:T(8,128)}, u32[]{:S(2)}) copy-start(s32[16,8]{0,1:T(8,128)} %param.9) | copy-start | bytes 1540
  6.5 13.5 %collective-permute-start.5 = (bf16[1024,128]{1,0:T(8,128)(2,1)S(1)}, bf16[1024,128]{1,0:T(8,128)(2,1)S(1)}, u32[]{:S(2)}, u32[]{:S(2)}) collective-permute-start(bf16[1024,128]{1,0:T(8,128)(2,1)S(1)} %get-tuple-element.62), channel_id=1, source_target_pairs={{0,0},{2,2},{4,8},{6,10},{8,4},{10,6},{12,12},{14,14},{1,1},{3,3},... | collective-permute-start | bytes 786440 | tf_op jit(solution)/shard_map/ppermute | solution.py:534
  7.2 12.9 %collective-permute-start.4 = (bf16[1024,128]{1,0:T(8,128)(2,1)S(1)}, bf16[1024,128]{1,0:T(8,128)(2,1)S(1)}, u32[]{:S(2)}, u32[]{:S(2)}) collective-permute-start(bf16[1024,128]{1,0:T(8,128)(2,1)S(1)} %get-tuple-element.62), channel_id=1, source_target_pairs={{0,4},{2,6},{4,0},{6,2},{8,12},{10,14},{12,8},{14,10},{1,5},{3,7},... | collective-permute-start | bytes 786440 | tf_op jit(solution)/shard_map/ppermute | solution.py:534
  13.0 14.8 %collective-permute-start.6 = (bf16[1024,256]{1,0:T(8,128)(2,1)S(1)}, bf16[1024,256]{1,0:T(8,128)(2,1)S(1)}, u32[]{:S(2)}, u32[]{:S(2)}) collective-permute-start(bf16[1024,256]{1,0:T(8,128)(2,1)S(1)} %get-tuple-element.63.kv.refs_6_), channel_id=1, source_target_pairs={{0,2},{2,0},{4,6},{6,4},{8,10},{10,8},{12,14},{14,12},{1,3},{3,1},... | collective-permute-start | bytes 1572872 | tf_op jit(solution)/shard_map/ppermute | solution.py:534
  15.3 8.4 %collective-permute-start.3 = (bf16[1024,128]{1,0:T(8,128)(2,1)S(1)}, bf16[1024,128]{1,0:T(8,128)(2,1)S(1)}, u32[]{:S(2)}, u32[]{:S(2)}) collective-permute-start(bf16[1024,128]{1,0:T(8,128)(2,1)S(1)} %get-tuple-element.61), channel_id=1, source_target_pairs={{0,0},{2,2},{4,8},{6,10},{8,4},{10,6},{12,12},{14,14},{1,1},{3,3},... | collective-permute-start | bytes 786440 | tf_op jit(solution)/shard_map/ppermute | solution.py:534
  16.0 9.7 %collective-permute-start.2 = (bf16[1024,128]{1,0:T(8,128)(2,1)S(1)}, bf16[1024,128]{1,0:T(8,128)(2,1)S(1)}, u32[]{:S(2)}, u32[]{:S(2)}) collective-permute-start(bf16[1024,128]{1,0:T(8,128)(2,1)S(1)} %get-tuple-element.61), channel_id=1, source_target_pairs={{0,4},{2,6},{4,0},{6,2},{8,12},{10,14},{12,8},{14,10},{1,5},{3,7},... | collective-permute-start | bytes 786440 | tf_op jit(solution)/shard_map/ppermute | solution.py:534
  20.2 13.3 %collective-permute-start.7 = (bf16[1024,128]{1,0:T(8,128)(2,1)S(1)}, bf16[1024,128]{1,0:T(8,128)(2,1)S(1)}, u32[]{:S(2)}, u32[]{:S(2)}) collective-permute-start(bf16[1024,128]{1,0:T(8,128)(2,1)S(1)} %shard_map.90), channel_id=1, source_target_pairs={{0,2},{2,0},{4,6},{6,4},{8,10},{10,8},{12,14},{14,12},{1,3},{3,1},... | collective-permute-start | bytes 786440 | tf_op jit(solution)/shard_map/ppermute | solution.py:534
  21.7 14.2 %collective-permute-start.8 = (bf16[512,256]{1,0:T(8,128)(2,1)S(1)}, bf16[512,256]{1,0:T(8,128)(2,1)S(1)}, u32[]{:S(2)}, u32[]{:S(2)}) collective-permute-start(bf16[512,256]{1,0:T(8,128)(2,1)S(1)} %shard_map.91), channel_id=1, source_target_pairs={{0,8},{2,10},{4,12},{6,14},{8,0},{10,2},{12,4},{14,6},{1,9},{3,11}... | collective-permute-start | bytes 786440 | tf_op jit(solution)/shard_map/ppermute | solution.py:534
  26.0 19.4 %collective-permute-start.9 = (bf16[1024,128]{1,0:T(8,128)(2,1)S(1)}, bf16[1024,128]{1,0:T(8,128)(2,1)S(1)}, u32[]{:S(2)}, u32[]{:S(2)}) collective-permute-start(bf16[1024,128]{1,0:T(8,128)(2,1)S(1)} %shard_map.87), channel_id=1, source_target_pairs={{0,2},{2,0},{4,6},{6,4},{8,10},{10,8},{12,14},{14,12},{1,3},{3,1},... | collective-permute-start | bytes 786440 | tf_op jit(solution)/shard_map/ppermute | solution.py:534
  43.8 9.6 %collective-permute-start.10 = (bf16[1024,128]{1,0:T(8,128)(2,1)S(1)}, bf16[1024,128]{1,0:T(8,128)(2,1)S(1)}, u32[]{:S(2)}, u32[]{:S(2)}) collective-permute-start(bf16[1024,128]{1,0:T(8,128)(2,1)S(1)} %get-tuple-element.81), channel_id=1, source_target_pairs={{0,2},{2,0},{4,6},{6,4},{8,10},{10,8},{12,14},{14,12},{1,3},{3,1},... | collective-permute-start | bytes 786440 | tf_op jit(solution)/shard_map/ppermute | solution.py:534
  45.4 8.0 %collective-permute-start.11 = (bf16[512,128]{1,0:T(8,128)(2,1)S(1)}, bf16[512,128]{1,0:T(8,128)(2,1)S(1)}, u32[]{:S(2)}, u32[]{:S(2)}) collective-permute-start(bf16[512,128]{1,0:T(8,128)(2,1)S(1)} %get-tuple-element.82), channel_id=1, source_target_pairs={{0,8},{2,10},{4,12},{6,14},{8,0},{10,2},{12,4},{14,6},{1,9},{3,11}... | collective-permute-start | bytes 393224 | tf_op jit(solution)/shard_map/ppermute | solution.py:534
  49.1 16.4 %collective-permute-start.12 = (bf16[1024,128]{1,0:T(8,128)(2,1)S(1)}, bf16[1024,128]{1,0:T(8,128)(2,1)S(1)}, u32[]{:S(2)}, u32[]{:S(2)}) collective-permute-start(bf16[1024,128]{1,0:T(8,128)(2,1)S(1)} %get-tuple-element.90), channel_id=1, source_target_pairs={{0,2},{2,0},{4,6},{6,4},{8,10},{10,8},{12,14},{14,12},{1,3},{3,1},... | collective-permute-start | bytes 786440 | tf_op jit(solution)/shard_map/ppermute | solution.py:534
  56.5 20.5 %collective-permute-start.15 = (bf16[1024,256]{1,0:T(8,128)(2,1)S(1)}, bf16[1024,256]{1,0:T(8,128)(2,1)S(1)}, u32[]{:S(2)}, u32[]{:S(2)}) collective-permute-start(bf16[1024,256]{1,0:T(8,128)(2,1)S(1)} %get-tuple-element.104), channel_id=1, source_target_pairs={{0,2},{2,0},{4,6},{6,4},{8,10},{10,8},{12,14},{14,12},{1,3},{3,1},... | collective-permute-start | bytes 1572872 | tf_op jit(solution)/shard_map/ppermute | solution.py:534
  57.8 7.6 %collective-permute-start.13 = (bf16[512,128]{1,0:T(8,128)(2,1)S(1)}, bf16[512,128]{1,0:T(8,128)(2,1)S(1)}, u32[]{:S(2)}, u32[]{:S(2)}) collective-permute-start(bf16[512,128]{1,0:T(8,128)(2,1)S(1)} %shard_map.94), channel_id=1, source_target_pairs={{0,8},{2,10},{4,12},{6,14},{8,0},{10,2},{12,4},{14,6},{1,9},{3,11}... | collective-permute-start | bytes 393224 | tf_op jit(solution)/shard_map/ppermute | solution.py:534
  60.7 15.4 %collective-permute-start.19 = (bf16[1024,128]{1,0:T(8,128)(2,1)S(1)}, bf16[1024,128]{1,0:T(8,128)(2,1)S(1)}, u32[]{:S(2)}, u32[]{:S(2)}) collective-permute-start(bf16[1024,128]{1,0:T(8,128)(2,1)S(1)} %get-tuple-element.84), channel_id=1, source_target_pairs={{0,4},{2,6},{4,0},{6,2},{8,12},{10,14},{12,8},{14,10},{1,5},{3,7},... | collective-permute-start | bytes 786440 | tf_op jit(solution)/shard_map/ppermute | solution.py:534
  60.8 16.1 %collective-permute-start.20 = (bf16[1024,128]{1,0:T(8,128)(2,1)S(1)}, bf16[1024,128]{1,0:T(8,128)(2,1)S(1)}, u32[]{:S(2)}, u32[]{:S(2)}) collective-permute-start(bf16[1024,128]{1,0:T(8,128)(2,1)S(1)} %get-tuple-element.85), channel_id=1, source_target_pairs={{0,0},{2,2},{4,8},{6,10},{8,4},{10,6},{12,12},{14,14},{1,1},{3,3},... | collective-permute-start | bytes 786440 | tf_op jit(solution)/shard_map/ppermute | solution.py:534
  65.6 12.1 %collective-permute-start.16 = (bf16[1024,128]{1,0:T(8,128)(2,1)S(1)}, bf16[1024,128]{1,0:T(8,128)(2,1)S(1)}, u32[]{:S(2)}, u32[]{:S(2)}) collective-permute-start(bf16[1024,128]{1,0:T(8,128)(2,1)S(1)} %get-tuple-element.92), channel_id=1, source_target_pairs={{0,4},{2,6},{4,0},{6,2},{8,12},{10,14},{12,8},{14,10},{1,5},{3,7},... | collective-permute-start | bytes 786440 | tf_op jit(solution)/shard_map/ppermute | solution.py:534
  68.3 9.4 %collective-permute-start.17 = (bf16[1024,128]{1,0:T(8,128)(2,1)S(1)}, bf16[1024,128]{1,0:T(8,128)(2,1)S(1)}, u32[]{:S(2)}, u32[]{:S(2)}) collective-permute-start(bf16[1024,128]{1,0:T(8,128)(2,1)S(1)} %get-tuple-element.93), channel_id=1, source_target_pairs={{0,0},{2,2},{4,8},{6,10},{8,4},{10,6},{12,12},{14,14},{1,1},{3,3},... | collective-permute-start | bytes 786440 | tf_op jit(solution)/shard_map/ppermute | solution.py:534
  76.0 2.0 %collective-permute-start.14 = (bf16[512,256]{1,0:T(8,128)(2,1)S(1)}, bf16[512,256]{1,0:T(8,128)(2,1)S(1)}, u32[]{:S(2)}, u32[]{:S(2)}) collective-permute-start(bf16[512,256]{1,0:T(8,128)(2,1)S(1)} %get-tuple-element.97), channel_id=1, source_target_pairs={{0,1},{1,0},{2,3},{3,2},{4,5},{5,4},{6,7},{7,6},{8,9},{9,8},{10,11... | collective-permute-start | bytes 786440 | tf_op jit(solution)/shard_map/ppermute | solution.py:531
  77.1 1.7 %collective-permute-start.21 = (bf16[512,128]{1,0:T(8,128)(2,1)S(1)}, bf16[512,128]{1,0:T(8,128)(2,1)S(1)}, u32[]{:S(2)}, u32[]{:S(2)}) collective-permute-start(bf16[512,128]{1,0:T(8,128)(2,1)S(1)} %get-tuple-element.109), channel_id=1, source_target_pairs={{0,1},{1,0},{2,3},{3,2},{4,5},{5,4},{6,7},{7,6},{8,9},{9,8},{10,11... | collective-permute-start | bytes 393224 | tf_op jit(solution)/shard_map/ppermute | solution.py:531
  77.9 1.8 %collective-permute-start.18 = (bf16[512,128]{1,0:T(8,128)(2,1)S(1)}, bf16[512,128]{1,0:T(8,128)(2,1)S(1)}, u32[]{:S(2)}, u32[]{:S(2)}) collective-permute-start(bf16[512,128]{1,0:T(8,128)(2,1)S(1)} %get-tuple-element.106), channel_id=1, source_target_pairs={{0,1},{1,0},{2,3},{3,2},{4,5},{5,4},{6,7},{7,6},{8,9},{9,8},{10,11... | collective-permute-start | bytes 393224 | tf_op jit(solution)/shard_map/ppermute | solution.py:531

commit v4 on v3

v4 whole, which is shorter than its diff:
```python
import functools
import math

import jax
import jax.numpy as jnp
from jax import lax
from jax.experimental import pallas as pl
from jax.experimental.pallas import tpu as pltpu
from jax.sharding import PartitionSpec as P

DH = 128
F32 = jnp.float32
BF16 = jnp.bfloat16
VMEM = pl.BlockSpec(memory_space=pltpu.VMEM)
SMEM = pl.BlockSpec(memory_space=pltpu.SMEM)
HBM = pl.BlockSpec(memory_space=pltpu.HBM)
NEG = -1e30
SCALE = 1.0 / math.sqrt(DH)
EXP_SCALE = SCALE * math.log2(math.e)
KEY = slice(0, DH)
VALUE = slice(DH, 2 * DH)
sds = jax.ShapeDtypeStruct


def dot_nn(a, b):
    return lax.dot_general(a, b, (((1,), (0,)), ((), ())), preferred_element_type=F32)


def dot_nt(a, b):
    return lax.dot_general(a, b, (((1,), (1,)), ((), ())), preferred_element_type=F32)


def dot_tn(a, b):
    return lax.dot_general(a, b, (((0,), (0,)), ((), ())), preferred_element_type=F32)


def call(kernel, args, out_shape, scratch=(), flops=0, source=VMEM):
    return pl.pallas_call(
        kernel,
        out_shape=out_shape,
        in_specs=[SMEM if a.dtype == jnp.int32 else source for a in args],
        out_specs=tuple(VMEM for _ in out_shape),
        scratch_shapes=list(scratch),
        compiler_params=pltpu.CompilerParams(vmem_limit_bytes=40 << 20),
        cost_estimate=pl.CostEstimate(flops=flops // 1000, bytes_accessed=1024, transcendentals=0),
    )(*args)


def swap_pairs(count, distance, second):
    pairs = []
    for frame in range(count):
        up = ((frame // distance) % 2 == 0) != second
        target = frame + distance if up else frame - distance
        pairs.append((frame, target if 0 <= target < count else frame))
    return pairs


class Swap:
    def __init__(self, count, level, second):
        self.count, self.level, self.second = count, level, second
        self.levels = count.bit_length() - 1
        self.pairs = swap_pairs(count, 1 << level, second)
        self.moves = any(source != target for source, target in self.pairs)

    def partner(self, frame):
        odd = lax.rem(lax.shift_right_logical(frame, self.level), 2)
        later = odd == (1 if self.second else 0)
        other = jnp.where(later, frame + (1 << self.level), frame - (1 << self.level))
        return other, later, jnp.logical_and(other >= 0, other < self.count)

    def slot(self, later, k):
        base = 0 if self.level == 0 else self.level + 1
        return jnp.where(later, self.levels + 1, 0) + base + k

    def block_of_mine(self, lists, frame, slab, k):
        other, later, exists = self.partner(frame)
        entry = lists[frame * 2 + slab, self.slot(later, k)]
        return jnp.clip(entry - other * 4, 0, 3), exists

    def block_of_theirs(self, lists, frame, slab, k):
        other, later, exists = self.partner(frame)
        row = jnp.where(exists, other, frame) * 2 + slab
        entry = lists[row, self.slot(jnp.logical_not(later), k)]
        return jnp.clip(entry - frame * 4, 0, 3), exists


def head_cols(head):
    return slice(head * DH, (head + 1) * DH)


def rows_of(slab, half):
    return slice(slab * half, (slab + 1) * half)


def each_core(body):
    core = lax.axis_index("space")
    for mine in range(2):
        pl.when(core == mine)(functools.partial(body, mine))


def pack_kernel(k, v, q, g, kv_send, kv_own, qg_send, qg_own, sems):
    def body(mine):
        copies = []
        for a, b, send, own in ((k, v, kv_send, kv_own), (q, g, qg_send, qg_own)):
            for head, out in ((1 - mine, send), (mine, own)):
                for source, cols in ((a, KEY), (b, VALUE)):
                    sem = sems.at[len(copies)]
                    copies.append(
                        pltpu.make_async_copy(source.at[:, head_cols(head)], out.at[:, cols], sem)
                    )
        for copy in copies:
            copy.start()
        for copy in copies:
            copy.wait()

    each_core(body)


def frame_kernel(own, came, kv, keys, values):
    half = own.shape[0]

    def body(mine):
        for slab, source in ((mine, own), (1 - mine, came)):
            rows = rows_of(slab, half)
            part = source[...]
            kv[rows, :] = part
            keys[rows, :] = part[:, KEY]
            values[rows, :] = part[:, VALUE]

    each_core(body)


def select_kernel(far, block, lists, kv, *sends):
    frame = lax.axis_index("tm")
    for swap, send in zip(far, sends):
        for slab in range(2):
            b, _ = swap.block_of_theirs(lists, frame, slab, 0)
            row = pl.multiple_of(b * block, block)
            send[slab * block : (slab + 1) * block, :] = kv[pl.ds(row, block), :]


def forwards_first(frame):
    return lax.rem(frame, 2) == lax.rem(lax.shift_right_logical(frame, 1), 2)


def relay_kernel(z, y, out):
    first = forwards_first(lax.axis_index("tm"))

    @pl.when(first)
    def _():
        out[...] = z[...]

    @pl.when(jnp.logical_not(first))
    def _():
        out[...] = y[...]


class Piece:
    def __init__(self, k, v, row, size, exists=None, dk=None, dv=None, add=True):
        self.k_at, self.v_at, self.exists = k, v, exists
        self.rows, self.size = pl.ds(row, size), size
        self.dk, self.dv, self.add = dk, dv, add

    def store(self, at, value):
        ref, cols = at
        if self.add:
            ref[self.rows, cols] += value
        else:
            ref[self.rows, cols] = value.astype(ref.dtype)


def stack(parts):
    return parts[0] if len(parts) == 1 else jnp.concatenate(parts, axis=0)


def keys_of(group):
    return stack([p.k_at[0][p.rows, p.k_at[1]] for p in group])


def values_of(group):
    return stack([p.v_at[0][p.rows, p.v_at[1]] for p in group])


def by_piece(group, value):
    at = 0
    for piece in group:
        yield piece, value[at : at + piece.size, :]
        at += piece.size


def store_grads(group, value, name):
    for piece, part in by_piece(group, value):
        piece.store(getattr(piece, name), part)


def listed(swap, lists, frame, slab, block, k, v, count=1, **grads):
    pieces = []
    for n in range(count):
        b, exists = swap.block_of_mine(lists, frame, slab, n)
        pieces.append(Piece(k, v, pl.multiple_of(b * block, block), block, exists, **grads))
    return pieces


def arrived(swap, frame, slab, block, kv, **grads):
    _, _, exists = swap.partner(frame)
    return Piece((kv, KEY), (kv, VALUE), slab * block, block, exists, add=False, **grads)


def raised(group, s, base):
    parts = []
    for piece, part in by_piece(group, s):
        low = base if piece.exists is None else jnp.where(piece.exists, base, -NEG)
        parts.append(jnp.exp2(part * EXP_SCALE - low))
    return stack(parts)


def score_groups(q, groups, s_ref, peak):
    at = 0
    for group in groups:
        s = dot_nt(keys_of(group), q)
        s_ref[at : at + s.shape[0], :] = s
        at += s.shape[0]
        for piece, part in by_piece(group, s):
            top = jnp.max(part, axis=0, keepdims=True)
            if piece.exists is not None:
                top = jnp.where(piece.exists, top, NEG)
            peak = top if peak is None else jnp.maximum(peak, top)
    return peak


def group_scores(groups, s_ref):
    at = 0
    for group in groups:
        size = sum(piece.size for piece in group)
        yield group, s_ref[at : at + size, :]
        at += size


def forward_slab(q, groups, with_values, s_ref, old):
    peak = score_groups(q, groups, s_ref, None if old is None else old[0])
    total, acc = 0.0, 0.0
    if old is not None:
        shrink = jnp.exp2((old[0] - peak) * EXP_SCALE)
        total, acc = old[1] * shrink, old[2] * shrink
    for j, (group, s) in enumerate(group_scores(groups, s_ref)):
        e = raised(group, s, peak * EXP_SCALE)
        total = total + jnp.sum(e, axis=0, keepdims=True)
        if j < with_values:
            acc = acc + dot_tn(values_of(group), e.astype(BF16))
    return peak, total, acc


def backward_group(q, g, lse, row_dot, group, p=None):
    k = keys_of(group)
    if p is None:
        p = raised(group, dot_nt(k, q), lse)
    if group[0].dv is not None:
        store_grads(group, dot_nn(p.astype(BF16), g), "dv")
    ds = (p * (dot_nt(values_of(group), g) - row_dot)).astype(BF16)
    if group[0].dk is not None:
        store_grads(group, dot_nn(ds, q) * SCALE, "dk")
    return dot_tn(k, ds)


def join_kernel(own, came, out, turned):
    half = own.shape[0]

    def body(mine):
        for slab, source in ((mine, own), (1 - mine, came)):
            rows = rows_of(slab, half)
            out[rows, :] = source[...]
            turned[:, rows] = source[:, VALUE].T

    each_core(body)


ALL = slice(None)


def store_state(refs, rows, peak, total, acc):
    stat, acc_ref = refs
    stat[0:1, rows] = peak
    stat[1:2, rows] = total
    acc_ref[:, rows] = acc


def load_state(refs, rows):
    stat, acc_ref = refs
    return stat[0:1, rows], stat[1:2, rows], acc_ref[:, rows]


def own_groups(kv, half, **grads):
    return [
        [Piece((kv, KEY), (kv, VALUE), r, half, **grads)] for r in range(0, kv.shape[0], half)
    ]


def near_kernel(qg, kv, stat, acc, s_ref):
    half = qg.shape[0] // 2
    for slab in range(2):
        rows = rows_of(slab, half)
        groups = own_groups(kv, half)
        store_state((stat, acc), rows, *forward_slab(qg[rows, KEY], groups, 2, s_ref, None))


def middle_kernel(
    block, swaps, lists, qg, stat, acc, a_kv, z_k, y_k, z_v, y_v, stat2, acc2, s_ref
):
    half = qg.shape[0] // 2
    frame = lax.axis_index("tm")
    a, z, y = swaps
    for slab in range(2):
        rows = rows_of(slab, half)
        at = (lists, frame, slab, block)
        groups = [
            listed(z, *at, (z_k, ALL), (z_v, ALL)) + listed(y, *at, (y_k, ALL), (y_v, ALL)),
            listed(a, *at, (a_kv, KEY), (a_kv, VALUE), 2),
        ]
        old = load_state((stat, acc), rows)
        store_state((stat2, acc2), rows, *forward_slab(qg[rows, KEY], groups, 2, s_ref, old))


def close_kernel(block, relayed, far, *refs):
    n = len(far)
    lists, qg, stat, acc, c_k = refs[:5]
    far_kv = refs[5 : 5 + n]
    lse_ref, part_ref, dc_v, p_ref = refs[5 + n : 9 + n]
    far_dv = refs[9 + n : 9 + 2 * n]
    s_ref, grad = refs[9 + 2 * n :]
    half = qg.shape[0] // 2
    frame = lax.axis_index("tm")
    grad[...] = jnp.zeros_like(grad)
    for slab in range(2):
        rows = rows_of(slab, half)
        q, g = qg[rows, KEY], qg[rows, VALUE]
        groups = [
            [arrived(swap, frame, slab, block, kv, dv=(out, ALL))]
            for swap, kv, out in zip(far, far_kv, far_dv)
        ]
        groups.append(
            listed(relayed, lists, frame, slab, block, (c_k, ALL), None, 2, dv=(grad, ALL))
        )
        old = load_state((stat, acc), rows)
        peak, total, out = forward_slab(q, groups, n, s_ref, old)
        part_ref[:, rows] = out / total
        lse = peak * EXP_SCALE + jnp.log2(total)
        lse_ref[0:1, rows] = lse
        for j, (group, s) in enumerate(group_scores(groups, s_ref)):
            p = raised(group, s, lse)
            store_grads(group, dot_nn(p.astype(BF16), g), "dv")
            if j == n:
                p_ref[slab] = p
    dc_v[...] = grad[...].astype(BF16)


def late_kernel(
    block, relayed, lists, qg, turned, lse_ref, part_ref, p_ref, c_k, c_v,
    o_ref, dot_ref, dc_k, dq_ref, grad,
):
    half = qg.shape[0] // 2
    frame = lax.axis_index("tm")
    grad[...] = jnp.zeros_like(grad)
    for slab in range(2):
        rows = rows_of(slab, half)
        q, g = qg[rows, KEY], qg[rows, VALUE]
        group = listed(
            relayed, lists, frame, slab, block, (c_k, ALL), (c_v, ALL), 2, dk=(grad, ALL)
        )
        p = p_ref[slab]
        o = (part_ref[:, rows] + dot_tn(values_of(group), p.astype(BF16))).astype(BF16)
        o_ref[:, rows] = o
        products = turned[:, rows].astype(F32) * o.astype(F32)
        row_dot = jnp.sum(products, axis=0, keepdims=True)
        dot_ref[0:1, rows] = row_dot
        dq_ref[:, rows] = backward_group(q, g, None, row_dot, group, p)
    dc_k[...] = grad[...].astype(BF16)


def far_kernel(block, far, *refs):
    n = len(far)
    qg, lse_ref, dot_ref, dq_old = refs[:4]
    far_kv = refs[4 : 4 + n]
    far_dk = refs[4 + n : 4 + 2 * n]
    dq_ref = refs[4 + 2 * n]
    half = qg.shape[0] // 2
    frame = lax.axis_index("tm")
    for slab in range(2):
        rows = rows_of(slab, half)
        q, g, lse, row_dot = qg[rows, KEY], qg[rows, VALUE], lse_ref[0:1, rows], dot_ref[0:1, rows]
        dq = dq_old[:, rows]
        for swap, kv, out in zip(far, far_kv, far_dk):
            group = [arrived(swap, frame, slab, block, kv, dk=(out, ALL))]
            dq = dq + backward_group(q, g, lse, row_dot, group)
        dq_ref[:, rows] = dq


def second_kernel(
    block, swaps, lists, qg, lse_ref, dot_ref, dq_old, z_k, y_k, z_v, y_v, dz_k, dy_k, dz_v, dy_v, dq_ref
):
    half = qg.shape[0] // 2
    frame = lax.axis_index("tm")
    _, z, y = swaps
    for ref in (dz_k, dy_k, dz_v, dy_v):
        ref[...] = jnp.zeros_like(ref)
    for slab in range(2):
        rows = rows_of(slab, half)
        q, g, lse, row_dot = qg[rows, KEY], qg[rows, VALUE], lse_ref[0:1, rows], dot_ref[0:1, rows]
        at = (lists, frame, slab, block)
        group = listed(z, *at, (z_k, ALL), (z_v, ALL), dk=(dz_k, ALL), dv=(dz_v, ALL))
        group += listed(y, *at, (y_k, ALL), (y_v, ALL), dk=(dy_k, ALL), dv=(dy_v, ALL))
        dq_ref[:, rows] = dq_old[:, rows] + backward_group(q, g, lse, row_dot, group)


def first_kernel(block, swaps, lists, qg, lse_ref, dot_ref, dq_old, a_kv, da, dq_ref, grad):
    half = qg.shape[0] // 2
    frame = lax.axis_index("tm")
    grad[...] = jnp.zeros_like(grad)
    for slab in range(2):
        rows = rows_of(slab, half)
        q, g, lse, row_dot = qg[rows, KEY], qg[rows, VALUE], lse_ref[0:1, rows], dot_ref[0:1, rows]
        group = listed(
            swaps[0], lists, frame, slab, block, (a_kv, KEY), (a_kv, VALUE), 2,
            dk=(grad, KEY), dv=(grad, VALUE),
        )
        dq_ref[:, rows] = dq_old[:, rows] + backward_group(q, g, lse, row_dot, group)
    da[...] = grad[...].astype(BF16)


def own_kernel(qg, lse_ref, dot_ref, dq_old, o, kv, near, keep, send):
    half = qg.shape[0] // 2
    whole = []
    for slab in range(2):
        rows = rows_of(slab, half)
        q, g, lse, row_dot = qg[rows, KEY], qg[rows, VALUE], lse_ref[0:1, rows], dot_ref[0:1, rows]
        dq = dq_old[:, rows]
        for group in own_groups(kv, half, dk=(near, KEY), dv=(near, VALUE), add=slab > 0):
            dq = dq + backward_group(q, g, lse, row_dot, group)
        whole.append((dq.T * SCALE).astype(BF16))

    def body(mine):
        for slab in range(2):
            out = keep if slab == mine else send
            out[:, KEY] = o[:, rows_of(slab, half)].T
            out[:, VALUE] = whole[slab]

    each_core(body)


def merge_kernel(dz, dy, came, z_out, y_out):
    first = forwards_first(lax.axis_index("tm"))
    more = came[...].astype(F32)
    z_out[...] = (dz[...] + jnp.where(first, more, 0.0)).astype(BF16)
    y_out[...] = (dy[...] + jnp.where(first, 0.0, more)).astype(BF16)


def place_kernel(block, far, *refs):
    n = len(far)
    lists, near = refs[:2]
    far_dk, far_dv = refs[2 : 2 + n], refs[2 + n : 2 + 2 * n]
    sum_k, sum_v = refs[2 + 2 * n :]
    frame = lax.axis_index("tm")
    sum_k[...] = near[:, KEY]
    sum_v[...] = near[:, VALUE]
    for j, swap in enumerate(far):
        for slab in range(2):
            b, exists = swap.block_of_theirs(lists, frame, slab, 0)
            rows = pl.ds(pl.multiple_of(b * block, block), block)
            for came, out in ((far_dk[j], sum_k), (far_dv[j], sum_v)):
                part = came[slab * block : (slab + 1) * block, :].astype(F32)
                out[rows, :] += jnp.where(exists, part, 0.0)


def gather_kernel(swaps, cols, near, da, dz, dy, keep, send):
    frame = lax.axis_index("tm")
    half = near.shape[0] // 2
    there = [swap.partner(frame)[2] for swap in swaps]

    def body(mine):
        for slab, out in ((mine, keep), (1 - mine, send)):
            rows = rows_of(slab, half)
            total = near[rows, :]
            for exists, part in zip(there, (da[rows, cols], dz[rows, :], dy[rows, :])):
                total = total + jnp.where(exists, part.astype(F32), 0.0)
            out[...] = total.astype(BF16)

    each_core(body)


def heads_kernel(keep, came, out):
    def body(mine):
        out[:, head_cols(mine)] = keep[...]
        out[:, head_cols(1 - mine)] = came[...]

    each_core(body)


def split_kernel(keep, came, first, second):
    def body(mine):
        for head, source in ((mine, keep), (1 - mine, came)):
            first[:, head_cols(head)] = source[:, KEY]
            second[:, head_cols(head)] = source[:, VALUE]

    each_core(body)


def per_device(queries, key_rows, value_rows, out_grad, block_lists):
    s_dev, width = queries.shape
    count = lax.axis_size("tm")
    block = s_dev // 2
    pair = sds((s_dev, 2 * DH), BF16)
    single = sds((s_dev, DH), BF16)
    frame_two = sds((2 * s_dev, 2 * DH), BF16)
    frame_one = sds((2 * s_dev, DH), BF16)
    frame_sum = sds((2 * s_dev, DH), F32)
    stat_row = sds((8, 2 * s_dev), F32)
    turned_sum = sds((DH, 2 * s_dev), F32)
    turned_bf = sds((DH, 2 * s_dev), BF16)
    levels = count.bit_length() - 1
    near_swap, relayed = Swap(count, 0, False), Swap(count, 0, True)
    z_swap, y_swap = Swap(count, 1, False), Swap(count, 1, True)
    swaps = (near_swap, z_swap, y_swap)
    far = [Swap(count, level, second) for level in range(2, levels) for second in (False, True)]
    far = [swap for swap in far if swap.moves]
    n = len(far)
    product = 2 * 2 * s_dev * block * DH
    grad_one = pltpu.VMEM((2 * s_dev, DH), F32)

    def across(value):
        return lax.ppermute(value, "space", [(0, 1), (1, 0)])

    def swapped(value, swap):
        return lax.ppermute(value, "tm", swap.pairs)

    def scores(pieces):
        return pltpu.VMEM((pieces * block, s_dev), F32)

    kv_send, kv_own, qg_send, qg_own = call(
        pack_kernel,
        tuple(pltpu.with_memory_space_constraint(a, pltpu.HBM) for a in (key_rows, value_rows, queries, out_grad)),
        [pair] * 4,
        scratch=[pltpu.SemaphoreType.DMA((8,))],
        source=HBM,
    )
    kv, keys, values = call(
        frame_kernel, (kv_own, across(kv_send)), [frame_two, frame_one, frame_one]
    )
    z_k = swapped(keys, z_swap)
    y_k = swapped(keys, y_swap)
    a_kv = swapped(kv, near_swap)
    z_v = swapped(values, z_swap)
    y_v = swapped(values, y_swap)
    far_send = call(functools.partial(select_kernel, far, block), (block_lists, kv), [pair] * n)
    qg, turned = call(join_kernel, (qg_own, across(qg_send)), [frame_two, turned_bf])
    stat, acc = call(
        near_kernel,
        (qg, kv),
        [stat_row, turned_sum],
        scratch=[scores(4)],
        flops=2 * 4 * 2 * product,
    )
    z_k, y_k, stat = lax.optimization_barrier((z_k, y_k, stat))
    (relay_k,) = call(relay_kernel, (z_k, y_k), [frame_one])
    relay_k, far_send = lax.optimization_barrier((relay_k, far_send))
    c_k = swapped(relay_k, near_swap)
    far_kv = [swapped(value, swap) for value, swap in zip(far_send, far)]
    (relay_v,) = call(relay_kernel, (z_v, y_v), [frame_one])
    c_v = swapped(relay_v, near_swap)
    relay_v, stat = lax.optimization_barrier((relay_v, stat))
    stat, acc = call(
        functools.partial(middle_kernel, block, swaps),
        (block_lists, qg, stat, acc, a_kv, z_k, y_k, z_v, y_v),
        [stat_row, turned_sum],
        scratch=[scores(4)],
        flops=2 * 4 * 2 * product,
    )
    lse, part, dc_v, probs, *far_dv = call(
        functools.partial(close_kernel, block, relayed, far),
        (block_lists, qg, stat, acc, c_k, *far_kv),
        [stat_row, turned_sum, frame_one, sds((2, s_dev, s_dev), F32)] + [single] * n,
        scratch=[scores(2 + n), grad_one],
        flops=2 * (2 + n) * 4 * product,
    )
    dc_v_came = swapped(dc_v, near_swap)
    far_dv_came = [swapped(value, swap) for value, swap in zip(far_dv, far)]
    o, row_dot, dc_k, dq = call(
        functools.partial(late_kernel, block, relayed),
        (block_lists, qg, turned, lse, part, probs, c_k, c_v),
        [turned_bf, stat_row, frame_one, turned_sum],
        scratch=[grad_one],
        flops=2 * 2 * 4 * product,
    )
    dc_k_came = swapped(dc_k, near_swap)
    *far_dk, dq = call(
        functools.partial(far_kernel, block, far),
        (qg, lse, row_dot, dq, *far_kv),
        [single] * n + [turned_sum],
        flops=2 * n * 3 * product,
    )
    far_dk_came = [swapped(value, swap) for value, swap in zip(far_dk, far)]
    dz_k, dy_k, dz_v, dy_v, dq = call(
        functools.partial(second_kernel, block, swaps),
        (block_lists, qg, lse, row_dot, dq, z_k, y_k, z_v, y_v),
        [frame_sum] * 4 + [turned_sum],
        flops=2 * 2 * 5 * product,
    )
    dc_v_came, far_dv_came = lax.optimization_barrier((dc_v_came, far_dv_came))
    dz_v, dy_v = call(merge_kernel, (dz_v, dy_v, dc_v_came), [frame_one, frame_one])
    dz_v_came = swapped(dz_v, z_swap)
    dy_v_came = swapped(dy_v, y_swap)
    dq, dz_v, dy_v = lax.optimization_barrier((dq, dz_v, dy_v))
    da, dq = call(
        functools.partial(first_kernel, block, swaps),
        (block_lists, qg, lse, row_dot, dq, a_kv),
        [frame_two, turned_sum],
        scratch=[pltpu.VMEM((2 * s_dev, 2 * DH), F32)],
        flops=2 * 2 * 5 * product,
    )
    da_came = swapped(da, near_swap)
    dc_k_came, far_dk_came = lax.optimization_barrier((dc_k_came, far_dk_came))
    dz_k, dy_k = call(merge_kernel, (dz_k, dy_k, dc_k_came), [frame_one, frame_one])
    dz_k_came = swapped(dz_k, z_swap)
    dy_k_came = swapped(dy_k, y_swap)
    dq, dz_k, dy_k = lax.optimization_barrier((dq, dz_k, dy_k))
    near, keep, send = call(
        own_kernel,
        (qg, lse, row_dot, dq, o, kv),
        [sds((2 * s_dev, 2 * DH), F32), pair, pair],
        flops=2 * 4 * 5 * product,
    )
    half_rows = sds((s_dev, width), BF16)
    attn_out, grad_q = call(split_kernel, (keep, across(send)), [half_rows, half_rows])
    sum_k, sum_v = call(
        functools.partial(place_kernel, block, far),
        (block_lists, near, *far_dk_came, *far_dv_came),
        [frame_sum, frame_sum],
    )
    outs = []
    for total, cols, dz, dy in (
        (sum_v, VALUE, dz_v_came, dy_v_came),
        (sum_k, KEY, dz_k_came, dy_k_came),
    ):
        keep, send = call(
            functools.partial(gather_kernel, swaps, cols),
            (total, da_came, dz, dy),
            [single, single],
        )
        outs += call(heads_kernel, (keep, across(send)), [half_rows])
    grad_v, grad_k = outs
    return attn_out, grad_q, grad_k, grad_v


def solution(mesh):
    rows = P(("groups", "tm", "space"), None)
    return jax.shard_map(
        per_device,
        mesh=mesh,
        in_specs=(rows, rows, rows, rows, P("groups", None)),
        out_specs=(rows, rows, rows, rows),
        check_vma=False,
    )
```

time: 80.7 us -> 69.7 us (0.86)
  the two profiles are of different devices: /device:TPU:0 before, /device:TPU:11 now
where the time goes in v4:
time: 69.7 us; the launch traced here: 69.5 us
  starting transfers between devices  33.9 us (49%)
  Pallas kernels  24.6 us (35%)
  waiting for transfers between devices  9.43 us (14%)
  between operations  0.89 us (1%)
  local copies, waits for them, and re-layouts  0.76 us (1%)
    ppermute x17, starting transfers between devices, swapped(): return lax.ppermute(value, 'tm', swap.pairs)  27 us
    pallas_call x22, Pallas kernels, call(): pl.pallas_call(kernel, out_shape=out_shape, in_specs=[SMEM if a.dtype ==...  24.6 us
    ppermute x17, waiting for transfers between devices, swapped(): return lax.ppermute(value, 'tm', swap.pairs)  8.34 us
    ppermute x5, starting transfers between devices, across(): return lax.ppermute(value, 'space', [(0, 1), (1, 0)])  6.86 us
  transfers between devices with their start and end apart: 22, of which 6 were waited for; matrix products, arithmetic and copies ran while one was open for 1% of the time, Pallas kernels for 32%

profile of v4, /device:TPU:11, one launch (start us, length us, event | category | flops | bytes accessed | tf_op | source)
XLA Modules:
  0.0 69.5 jit_solution(10038469749075780749)
XLA Ops:
  0.6 1.4 %shard_map.84 = (bf16[512,256]{1,0:T(8,128)(2,1)S(1)}, bf16[512,256]{1,0:T(8,128)(2,1)S(1)}, bf16[512,256]{1,0:T(8,128)(2,1)S(1)}, bf16[512,256]{1,0:T(8,128)(2,1)S(1)}) custom-call(bf16[512,256]{1,0:T(8,128)(2,1)} %k.1, bf16[512,256]{1,0:T(8,128)(2,1)} %v.1, bf16[512,256]{1,0:T(8,128)(2,1)} %q.1, bf16[512,256]{1,0:T(8,128)(2,1)} %g.1), custom_call_target="tpu_custom_call" | custom-call | bytes 1024 | tf_op jit(solution)/shard_map/pallas_call | solution.py:38
  2.8 1.1 %collective-permute-done.1.came = bf16[512,256]{1,0:T(8,128)(2,1)S(1)} collective-permute-done((bf16[512,256]{1,0:T(8,128)(2,1)S(1)}, bf16[512,256]{1,0:T(8,128)(2,1)S(1)}, u32[]{:S(2)}, u32[]{:S(2)}) %collective-permute-start.1) | collective-permute-done | bytes 262176 | tf_op jit(solution)/shard_map/ppermute | solution.py:529
  4.0 3.2 %collective-permute-start.5 = (bf16[1024,128]{1,0:T(8,128)(2,1)S(1)}, bf16[1024,128]{1,0:T(8,128)(2,1)S(1)}, u32[]{:S(2)}, u32[]{:S(2)}) collective-permute-start(bf16[1024,128]{1,0:T(8,128)(2,1)S(1)} %get-tuple-element.68), channel_id=1, source_target_pairs={{0,0},{2,2},{4,8},{6,10},{8,4},{10,6},{12,12},{14,14},{1,1},{3,3},... | collective-permute-start | bytes 786440 | tf_op jit(solution)/shard_map/ppermute | solution.py:532
  7.3 1.3 %collective-permute-start.6 = (bf16[1024,256]{1,0:T(8,128)(2,1)S(1)}, bf16[1024,256]{1,0:T(8,128)(2,1)S(1)}, u32[]{:S(2)}, u32[]{:S(2)}) collective-permute-start(bf16[1024,256]{1,0:T(8,128)(2,1)S(1)} %get-tuple-element.69.kv), channel_id=1, source_target_pairs={{0,2},{2,0},{4,6},{6,4},{8,10},{10,8},{12,14},{14,12},{1,3},{3,1},... | collective-permute-start | bytes 1572872 | tf_op jit(solution)/shard_map/ppermute | solution.py:532
  8.6 0.8 %copy.11.lists.refs_0_ = s32[16,8]{1,0:T(8,128)S(1)} copy(s32[16,8]{0,1:T(8,128)} %param.9) | data formatting | bytes 1024 | tf_op args[4]
  10.1 2.1 %collective-permute-start.3 = (bf16[1024,128]{1,0:T(8,128)(2,1)S(1)}, bf16[1024,128]{1,0:T(8,128)(2,1)S(1)}, u32[]{:S(2)}, u32[]{:S(2)}) collective-permute-start(bf16[1024,128]{1,0:T(8,128)(2,1)S(1)} %get-tuple-element.67), channel_id=1, source_target_pairs={{0,0},{2,2},{4,8},{6,10},{8,4},{10,6},{12,12},{14,14},{1,1},{3,3},... | collective-permute-start | bytes 786440 | tf_op jit(solution)/shard_map/ppermute | solution.py:532
  12.4 2.0 %shard_map.88 = (f32[8,1024]{1,0:T(8,128)S(1)}, f32[128,1024]{1,0:T(8,128)S(1)}) custom-call(bf16[1024,256]{1,0:T(8,128)(2,1)S(1)} %get-tuple-element.64.qg.refs_1_.refs_0_, bf16[1024,256]{1,0:T(8,128)(2,1)S(1)} %get-tuple-element.69.kv), custom_call_target="tpu_custom_call" | custom-call | flops 1073741 | bytes 1024 | tf_op jit(solution)/shard_map/pallas_call | solution.py:38
  14.5 1.3 %collective-permute-start.7 = (bf16[1024,128]{1,0:T(8,128)(2,1)S(1)}, bf16[1024,128]{1,0:T(8,128)(2,1)S(1)}, u32[]{:S(2)}, u32[]{:S(2)}) collective-permute-start(bf16[1024,128]{1,0:T(8,128)(2,1)S(1)} %shard_map.90), channel_id=1, source_target_pairs={{0,2},{2,0},{4,6},{6,4},{8,10},{10,8},{12,14},{14,12},{1,3},{3,1},... | collective-permute-start | bytes 786440 | tf_op jit(solution)/shard_map/ppermute | solution.py:532
  15.8 1.4 %collective-permute-start.8 = (bf16[512,256]{1,0:T(8,128)(2,1)S(1)}, bf16[512,256]{1,0:T(8,128)(2,1)S(1)}, u32[]{:S(2)}, u32[]{:S(2)}) collective-permute-start(bf16[512,256]{1,0:T(8,128)(2,1)S(1)} %shard_map.91), channel_id=1, source_target_pairs={{0,8},{2,10},{4,12},{6,14},{8,0},{10,2},{12,4},{14,6},{1,9},{3,11}... | collective-permute-start | bytes 786440 | tf_op jit(solution)/shard_map/ppermute | solution.py:532
  17.3 1.6 %collective-permute-done.3.y.y_v = bf16[1024,128]{1,0:T(8,128)(2,1)S(1)} collective-permute-done((bf16[1024,128]{1,0:T(8,128)(2,1)S(1)}, bf16[1024,128]{1,0:T(8,128)(2,1)S(1)}, u32[]{:S(2)}, u32[]{:S(2)}) %collective-permute-start.3) | collective-permute-done | bytes 262176 | tf_op jit(solution)/shard_map/ppermute | solution.py:532
  18.8 1.3 %collective-permute-done.2.z.z_v = bf16[1024,128]{1,0:T(8,128)(2,1)S(1)} collective-permute-done((bf16[1024,128]{1,0:T(8,128)(2,1)S(1)}, bf16[1024,128]{1,0:T(8,128)(2,1)S(1)}, u32[]{:S(2)}, u32[]{:S(2)}) %collective-permute-start.2) | collective-permute-done | bytes 262176 | tf_op jit(solution)/shard_map/ppermute | solution.py:532
  20.3 1.3 %collective-permute-start.9 = (bf16[1024,128]{1,0:T(8,128)(2,1)S(1)}, bf16[1024,128]{1,0:T(8,128)(2,1)S(1)}, u32[]{:S(2)}, u32[]{:S(2)}) collective-permute-start(bf16[1024,128]{1,0:T(8,128)(2,1)S(1)} %shard_map.87), channel_id=1, source_target_pairs={{0,2},{2,0},{4,6},{6,4},{8,10},{10,8},{12,14},{14,12},{1,3},{3,1},... | collective-permute-start | bytes 786440 | tf_op jit(solution)/shard_map/ppermute | solution.py:532
  21.6 2.6 %shard_map.89 = (f32[8,1024]{1,0:T(8,128)S(1)}, f32[128,1024]{1,0:T(8,128)S(1)}) custom-call(s32[16,8]{1,0:T(8,128)S(1)} %copy.11.lists.refs_0_, bf16[1024,256]{1,0:T(8,128)(2,1)S(1)} %get-tuple-element.64.qg.refs_1_.refs_0_, f32[8,1024]{1,0:T(8,128)S(1)} %get-tuple-element.72.stat, f32[128,1024]{1,0:T(8,128)S(1)} %get-tuple-element.73.acc, ...), custom_call_target="tpu_custom_call" | custom-call | flops 1073741 | bytes 1024 | tf_op jit(solution)/shard_map/pallas_call | solution.py:38
  24.3 1.5 %collective-permute-done.7.refs_4_.c_k = bf16[1024,128]{1,0:T(8,128)(2,1)S(1)} collective-permute-done((bf16[1024,128]{1,0:T(8,128)(2,1)S(1)}, bf16[1024,128]{1,0:T(8,128)(2,1)S(1)}, u32[]{:S(2)}, u32[]{:S(2)}) %collective-permute-start.7) | collective-permute-done | bytes 262176 | tf_op jit(solution)/shard_map/ppermute | solution.py:532
  25.8 3.6 %collective-permute-done.8.refs_5_.refs_4_ = bf16[512,256]{1,0:T(8,128)(2,1)S(1)} collective-permute-done((bf16[512,256]{1,0:T(8,128)(2,1)S(1)}, bf16[512,256]{1,0:T(8,128)(2,1)S(1)}, u32[]{:S(2)}, u32[]{:S(2)}) %collective-permute-start.8) | collective-permute-done | bytes 262176 | tf_op jit(solution)/shard_map/ppermute | solution.py:532
  29.4 3.0 %shard_map.92 = (f32[8,1024]{1,0:T(8,128)S(1)}, f32[128,1024]{1,0:T(8,128)S(1)}, bf16[1024,128]{1,0:T(8,128)(2,1)S(1)}, f32[2,512,512]{2,1,0:T(8,128)S(1)}, bf16[512,128]{1,0:T(8,128)(2,1)S(1)}) custom-call(s32[16,8]{1,0:T(8,128)S(1)} %copy.11.lists.refs_0_, bf16[1024,256]{1,0:T(8,128)(2,1)S(1)} %get-tuple-element.64.qg.refs_1_.refs_0_, ...), custom_call_target="tpu_custom_call" | custom-call | flops 1610612 | bytes 1024 | tf_op jit(solution)/shard_map/pallas_call | solution.py:38
  32.4 1.3 %collective-permute-start.10 = (bf16[1024,128]{1,0:T(8,128)(2,1)S(1)}, bf16[1024,128]{1,0:T(8,128)(2,1)S(1)}, u32[]{:S(2)}, u32[]{:S(2)}) collective-permute-start(bf16[1024,128]{1,0:T(8,128)(2,1)S(1)} %get-tuple-element.90), channel_id=1, source_target_pairs={{0,2},{2,0},{4,6},{6,4},{8,10},{10,8},{12,14},{14,12},{1,3},{3,1},... | collective-permute-start | bytes 786440 | tf_op jit(solution)/shard_map/ppermute | solution.py:532
  33.7 3.1 %collective-permute-start.11 = (bf16[512,128]{1,0:T(8,128)(2,1)S(1)}, bf16[512,128]{1,0:T(8,128)(2,1)S(1)}, u32[]{:S(2)}, u32[]{:S(2)}) collective-permute-start(bf16[512,128]{1,0:T(8,128)(2,1)S(1)} %get-tuple-element.91), channel_id=1, source_target_pairs={{0,8},{2,10},{4,12},{6,14},{8,0},{10,2},{12,4},{14,6},{1,9},{3,11}... | collective-permute-start | bytes 393224 | tf_op jit(solution)/shard_map/ppermute | solution.py:532
  36.8 1.9 %shard_map.93 = (bf16[128,1024]{1,0:T(8,128)(2,1)S(1)}, f32[8,1024]{1,0:T(8,128)S(1)}, bf16[1024,128]{1,0:T(8,128)(2,1)S(1)}, f32[128,1024]{1,0:T(8,128)S(1)}) custom-call(s32[16,8]{1,0:T(8,128)S(1)} %copy.11.lists.refs_0_, bf16[1024,256]{1,0:T(8,128)(2,1)S(1)} %get-tuple-element.64.qg.refs_1_.refs_0_, bf16[128,1024]{1,0:T(8,128)(2,1)S(1)} %get-tuple-element.81.turned, ...), custom_call_target="tpu_custom_call" | custom-call | flops 1073741 | bytes 1024 | tf_op jit(solution)/shard_map/pallas_call | solution.py:38
  39.0 0.8 %shard_map.94 = (bf16[512,128]{1,0:T(8,128)(2,1)S(1)}, f32[128,1024]{1,0:T(8,128)S(1)}) custom-call(bf16[1024,256]{1,0:T(8,128)(2,1)S(1)} %get-tuple-element.64.qg.refs_1_.refs_0_, f32[8,1024]{1,0:T(8,128)S(1)} %get-tuple-element.80.lse_ref.refs_1_, f32[8,1024]{1,0:T(8,128)S(1)} %get-tuple-element.84.refs_2_.dot_ref, ...), custom_call_target="tpu_custom_call" | custom-call | flops 402653 | bytes 1024 | tf_op jit(solution)/shard_map/pallas_call | solution.py:38
  39.8 2.3 %shard_map.95 = (f32[1024,128]{1,0:T(8,128)S(1)}, f32[1024,128]{1,0:T(8,128)S(1)}, f32[1024,128]{1,0:T(8,128)S(1)}, f32[1024,128]{1,0:T(8,128)S(1)}, f32[128,1024]{1,0:T(8,128)S(1)}) custom-call(s32[16,8]{1,0:T(8,128)S(1)} %copy.11.lists.refs_0_, bf16[1024,256]{1,0:T(8,128)(2,1)S(1)} %get-tuple-element.64.qg.refs_1_.refs_0_, ...), custom_call_target="tpu_custom_call" | custom-call | flops 1342177 | bytes 1024 | tf_op jit(solution)/shard_map/pallas_call | solution.py:38
  42.3 2.3 %shard_map.97 = (bf16[1024,256]{1,0:T(8,128)(2,1)S(1)}, f32[128,1024]{1,0:T(8,128)S(1)}) custom-call(s32[16,8]{1,0:T(8,128)S(1)} %copy.11.lists.refs_0_, bf16[1024,256]{1,0:T(8,128)(2,1)S(1)} %get-tuple-element.64.qg.refs_1_.refs_0_, f32[8,1024]{1,0:T(8,128)S(1)} %get-tuple-element.80.lse_ref.refs_1_, f32[8,1024]{1,0:T(8,128)S(1)} %get-tuple-element.84.refs_2_.dot_ref, ...), custom_call_target="tpu_custom_call" | custom-call | flops 1342177 | bytes 1024 | tf_op jit(solution)/shard_map/pallas_call | solution.py:38
  44.7 1.3 %collective-permute-start.15 = (bf16[1024,256]{1,0:T(8,128)(2,1)S(1)}, bf16[1024,256]{1,0:T(8,128)(2,1)S(1)}, u32[]{:S(2)}, u32[]{:S(2)}) collective-permute-start(bf16[1024,256]{1,0:T(8,128)(2,1)S(1)} %get-tuple-element.114), channel_id=1, source_target_pairs={{0,2},{2,0},{4,6},{6,4},{8,10},{10,8},{12,14},{14,12},{1,3},{3,1},... | collective-permute-start | bytes 1572872 | tf_op jit(solution)/shard_map/ppermute | solution.py:532
  47.3 3.2 %collective-permute-start.20 = (bf16[1024,128]{1,0:T(8,128)(2,1)S(1)}, bf16[1024,128]{1,0:T(8,128)(2,1)S(1)}, u32[]{:S(2)}, u32[]{:S(2)}) collective-permute-start(bf16[1024,128]{1,0:T(8,128)(2,1)S(1)} %get-tuple-element.94), channel_id=1, source_target_pairs={{0,0},{2,2},{4,8},{6,10},{8,4},{10,6},{12,12},{14,14},{1,1},{3,3},... | collective-permute-start | bytes 786440 | tf_op jit(solution)/shard_map/ppermute | solution.py:532
  50.9 3.6 %collective-permute-start.16 = (bf16[1024,128]{1,0:T(8,128)(2,1)S(1)}, bf16[1024,128]{1,0:T(8,128)(2,1)S(1)}, u32[]{:S(2)}, u32[]{:S(2)}) collective-permute-start(bf16[1024,128]{1,0:T(8,128)(2,1)S(1)} %get-tuple-element.102), channel_id=1, source_target_pairs={{0,4},{2,6},{4,0},{6,2},{8,12},{10,14},{12,8},{14,10},{1,5},{3,7},... | collective-permute-start | bytes 786440 | tf_op jit(solution)/shard_map/ppermute | solution.py:532
  54.5 2.1 %collective-permute-start.17 = (bf16[1024,128]{1,0:T(8,128)(2,1)S(1)}, bf16[1024,128]{1,0:T(8,128)(2,1)S(1)}, u32[]{:S(2)}, u32[]{:S(2)}) collective-permute-start(bf16[1024,128]{1,0:T(8,128)(2,1)S(1)} %get-tuple-element.103), channel_id=1, source_target_pairs={{0,0},{2,2},{4,8},{6,10},{8,4},{10,6},{12,12},{14,14},{1,1},{3,3},... | collective-permute-start | bytes 786440 | tf_op jit(solution)/shard_map/ppermute | solution.py:532
  56.6 3.2 %shard_map.99 = (f32[1024,256]{1,0:T(8,128)S(1)}, bf16[512,256]{1,0:T(8,128)(2,1)S(1)}, bf16[512,256]{1,0:T(8,128)(2,1)S(1)}) custom-call(bf16[1024,256]{1,0:T(8,128)(2,1)S(1)} %get-tuple-element.64.qg.refs_1_.refs_0_, f32[8,1024]{1,0:T(8,128)S(1)} %get-tuple-element.80.lse_ref.refs_1_, f32[8,1024]{1,0:T(8,128)S(1)} %get-tuple-element.84.refs_2_.dot_ref, ...), custom_call_target="tpu_custom_call" | custom-call | flops 2684354 | bytes 1024 | tf_op jit(solution)/shard_map/pallas_call | solution.py:38
  59.8 5.0 %collective-permute-start.14 = (bf16[512,256]{1,0:T(8,128)(2,1)S(1)}, bf16[512,256]{1,0:T(8,128)(2,1)S(1)}, u32[]{:S(2)}, u32[]{:S(2)}) collective-permute-start(bf16[512,256]{1,0:T(8,128)(2,1)S(1)} %get-tuple-element.107), channel_id=1, source_target_pairs={{0,1},{1,0},{2,3},{3,2},{4,5},{5,4},{6,7},{7,6},{8,9},{9,8},{10,11... | collective-permute-start | bytes 786440 | tf_op jit(solution)/shard_map/ppermute | solution.py:529
  64.8 0.8 %shard_map.101 = (f32[1024,128]{1,0:T(8,128)S(1)}, f32[1024,128]{1,0:T(8,128)S(1)}) custom-call(s32[16,8]{1,0:T(8,128)S(1)} %copy.11.lists.refs_0_, f32[1024,256]{1,0:T(8,128)S(1)} %get-tuple-element.110.refs_1_, bf16[512,128]{1,0:T(8,128)(2,1)S(1)} %collective-permute-done.13.refs_2_, bf16[512,128]{1,0:T(8,128)(2,1)S(1)} %collective-permute-done.11.refs_3_), custom_call_target="tpu_custom_call" | custom-call | bytes 1024 | tf_op jit(solution)/shard_map/pallas_call | solution.py:38
  66.2 0.9 %collective-permute-start.18 = (bf16[512,128]{1,0:T(8,128)(2,1)S(1)}, bf16[512,128]{1,0:T(8,128)(2,1)S(1)}, u32[]{:S(2)}, u32[]{:S(2)}) collective-permute-start(bf16[512,128]{1,0:T(8,128)(2,1)S(1)} %get-tuple-element.116), channel_id=1, source_target_pairs={{0,1},{1,0},{2,3},{3,2},{4,5},{5,4},{6,7},{7,6},{8,9},{9,8},{10,11... | collective-permute-start | bytes 393224 | tf_op jit(solution)/shard_map/ppermute | solution.py:529
  67.1 0.9 %shard_map.100 = (bf16[512,256]{1,0:T(8,128)(2,1)}, bf16[512,256]{1,0:T(8,128)(2,1)}) custom-call(bf16[512,256]{1,0:T(8,128)(2,1)S(1)} %get-tuple-element.106.keep, bf16[512,256]{1,0:T(8,128)(2,1)S(1)} %collective-permute-done.14.came), custom_call_target="tpu_custom_call" | custom-call | bytes 1024 | tf_op jit(solution)/shard_map/pallas_call | solution.py:38
  68.0 0.7 %shard_map.105 = bf16[512,256]{1,0:T(8,128)(2,1)} custom-call(bf16[512,128]{1,0:T(8,128)(2,1)S(1)} %get-tuple-element.118.keep, bf16[512,128]{1,0:T(8,128)(2,1)S(1)} %collective-permute-done.21.came), custom_call_target="tpu_custom_call" | custom-call | bytes 1024 | tf_op jit(solution)/shard_map/pallas_call | solution.py:38
  (35 shorter events, 5.6 us)
Async XLA Ops:
  2.0 1.9 %collective-permute-start.1 = (bf16[512,256]{1,0:T(8,128)(2,1)S(1)}, bf16[512,256]{1,0:T(8,128)(2,1)S(1)}, u32[]{:S(2)}, u32[]{:S(2)}) collective-permute-start(bf16[512,256]{1,0:T(8,128)(2,1)S(1)} %get-tuple-element.66), channel_id=1, source_target_pairs={{0,1},{1,0},{2,3},{3,2},{4,5},{5,4},{6,7},{7,6},{8,9},{9,8},{10,11... | collective-permute-start | bytes 786440 | tf_op jit(solution)/shard_map/ppermute | solution.py:529
  2.7 9.4 %collective-permute-start = (bf16[512,256]{1,0:T(8,128)(2,1)S(1)}, bf16[512,256]{1,0:T(8,128)(2,1)S(1)}, u32[]{:S(2)}, u32[]{:S(2)}) collective-permute-start(bf16[512,256]{1,0:T(8,128)(2,1)S(1)} %get-tuple-element.63), channel_id=1, source_target_pairs={{0,1},{1,0},{2,3},{3,2},{4,5},{5,4},{6,7},{7,6},{8,9},{9,8},{10,11... | collective-permute-start | bytes 786440 | tf_op jit(solution)/shard_map/ppermute | solution.py:529
  4.0 10.4 %collective-permute-start.5 = (bf16[1024,128]{1,0:T(8,128)(2,1)S(1)}, bf16[1024,128]{1,0:T(8,128)(2,1)S(1)}, u32[]{:S(2)}, u32[]{:S(2)}) collective-permute-start(bf16[1024,128]{1,0:T(8,128)(2,1)S(1)} %get-tuple-element.68), channel_id=1, source_target_pairs={{0,0},{2,2},{4,8},{6,10},{8,4},{10,6},{12,12},{14,14},{1,1},{3,3},... | collective-permute-start | bytes 786440 | tf_op jit(solution)/shard_map/ppermute | solution.py:532
  7.2 7.3 %collective-permute-start.4 = (bf16[1024,128]{1,0:T(8,128)(2,1)S(1)}, bf16[1024,128]{1,0:T(8,128)(2,1)S(1)}, u32[]{:S(2)}, u32[]{:S(2)}) collective-permute-start(bf16[1024,128]{1,0:T(8,128)(2,1)S(1)} %get-tuple-element.68), channel_id=1, source_target_pairs={{0,4},{2,6},{4,0},{6,2},{8,12},{10,14},{12,8},{14,10},{1,5},{3,7},... | collective-permute-start | bytes 786440 | tf_op jit(solution)/shard_map/ppermute | solution.py:532
  7.3 14.3 %collective-permute-start.6 = (bf16[1024,256]{1,0:T(8,128)(2,1)S(1)}, bf16[1024,256]{1,0:T(8,128)(2,1)S(1)}, u32[]{:S(2)}, u32[]{:S(2)}) collective-permute-start(bf16[1024,256]{1,0:T(8,128)(2,1)S(1)} %get-tuple-element.69.kv), channel_id=1, source_target_pairs={{0,2},{2,0},{4,6},{6,4},{8,10},{10,8},{12,14},{14,12},{1,3},{3,1},... | collective-permute-start | bytes 1572872 | tf_op jit(solution)/shard_map/ppermute | solution.py:532
  10.1 8.8 %collective-permute-start.3 = (bf16[1024,128]{1,0:T(8,128)(2,1)S(1)}, bf16[1024,128]{1,0:T(8,128)(2,1)S(1)}, u32[]{:S(2)}, u32[]{:S(2)}) collective-permute-start(bf16[1024,128]{1,0:T(8,128)(2,1)S(1)} %get-tuple-element.67), channel_id=1, source_target_pairs={{0,0},{2,2},{4,8},{6,10},{8,4},{10,6},{12,12},{14,14},{1,1},{3,3},... | collective-permute-start | bytes 786440 | tf_op jit(solution)/shard_map/ppermute | solution.py:532
  12.2 8.0 %collective-permute-start.2 = (bf16[1024,128]{1,0:T(8,128)(2,1)S(1)}, bf16[1024,128]{1,0:T(8,128)(2,1)S(1)}, u32[]{:S(2)}, u32[]{:S(2)}) collective-permute-start(bf16[1024,128]{1,0:T(8,128)(2,1)S(1)} %get-tuple-element.67), channel_id=1, source_target_pairs={{0,4},{2,6},{4,0},{6,2},{8,12},{10,14},{12,8},{14,10},{1,5},{3,7},... | collective-permute-start | bytes 786440 | tf_op jit(solution)/shard_map/ppermute | solution.py:532
  14.5 11.3 %collective-permute-start.7 = (bf16[1024,128]{1,0:T(8,128)(2,1)S(1)}, bf16[1024,128]{1,0:T(8,128)(2,1)S(1)}, u32[]{:S(2)}, u32[]{:S(2)}) collective-permute-start(bf16[1024,128]{1,0:T(8,128)(2,1)S(1)} %shard_map.90), channel_id=1, source_target_pairs={{0,2},{2,0},{4,6},{6,4},{8,10},{10,8},{12,14},{14,12},{1,3},{3,1},... | collective-permute-start | bytes 786440 | tf_op jit(solution)/shard_map/ppermute | solution.py:532
  15.8 13.6 %collective-permute-start.8 = (bf16[512,256]{1,0:T(8,128)(2,1)S(1)}, bf16[512,256]{1,0:T(8,128)(2,1)S(1)}, u32[]{:S(2)}, u32[]{:S(2)}) collective-permute-start(bf16[512,256]{1,0:T(8,128)(2,1)S(1)} %shard_map.91), channel_id=1, source_target_pairs={{0,8},{2,10},{4,12},{6,14},{8,0},{10,2},{12,4},{14,6},{1,9},{3,11}... | collective-permute-start | bytes 786440 | tf_op jit(solution)/shard_map/ppermute | solution.py:532
  20.3 16.5 %collective-permute-start.9 = (bf16[1024,128]{1,0:T(8,128)(2,1)S(1)}, bf16[1024,128]{1,0:T(8,128)(2,1)S(1)}, u32[]{:S(2)}, u32[]{:S(2)}) collective-permute-start(bf16[1024,128]{1,0:T(8,128)(2,1)S(1)} %shard_map.87), channel_id=1, source_target_pairs={{0,2},{2,0},{4,6},{6,4},{8,10},{10,8},{12,14},{14,12},{1,3},{3,1},... | collective-permute-start | bytes 786440 | tf_op jit(solution)/shard_map/ppermute | solution.py:532
  32.4 9.8 %collective-permute-start.10 = (bf16[1024,128]{1,0:T(8,128)(2,1)S(1)}, bf16[1024,128]{1,0:T(8,128)(2,1)S(1)}, u32[]{:S(2)}, u32[]{:S(2)}) collective-permute-start(bf16[1024,128]{1,0:T(8,128)(2,1)S(1)} %get-tuple-element.90), channel_id=1, source_target_pairs={{0,2},{2,0},{4,6},{6,4},{8,10},{10,8},{12,14},{14,12},{1,3},{3,1},... | collective-permute-start | bytes 786440 | tf_op jit(solution)/shard_map/ppermute | solution.py:532
  33.7 8.5 %collective-permute-start.11 = (bf16[512,128]{1,0:T(8,128)(2,1)S(1)}, bf16[512,128]{1,0:T(8,128)(2,1)S(1)}, u32[]{:S(2)}, u32[]{:S(2)}) collective-permute-start(bf16[512,128]{1,0:T(8,128)(2,1)S(1)} %get-tuple-element.91), channel_id=1, source_target_pairs={{0,8},{2,10},{4,12},{6,14},{8,0},{10,2},{12,4},{14,6},{1,9},{3,11}... | collective-permute-start | bytes 393224 | tf_op jit(solution)/shard_map/ppermute | solution.py:532
  38.7 12.1 %collective-permute-start.12 = (bf16[1024,128]{1,0:T(8,128)(2,1)S(1)}, bf16[1024,128]{1,0:T(8,128)(2,1)S(1)}, u32[]{:S(2)}, u32[]{:S(2)}) collective-permute-start(bf16[1024,128]{1,0:T(8,128)(2,1)S(1)} %get-tuple-element.99), channel_id=1, source_target_pairs={{0,2},{2,0},{4,6},{6,4},{8,10},{10,8},{12,14},{14,12},{1,3},{3,1},... | collective-permute-start | bytes 786440 | tf_op jit(solution)/shard_map/ppermute | solution.py:532
  44.7 21.0 %collective-permute-start.15 = (bf16[1024,256]{1,0:T(8,128)(2,1)S(1)}, bf16[1024,256]{1,0:T(8,128)(2,1)S(1)}, u32[]{:S(2)}, u32[]{:S(2)}) collective-permute-start(bf16[1024,256]{1,0:T(8,128)(2,1)S(1)} %get-tuple-element.114), channel_id=1, source_target_pairs={{0,2},{2,0},{4,6},{6,4},{8,10},{10,8},{12,14},{14,12},{1,3},{3,1},... | collective-permute-start | bytes 1572872 | tf_op jit(solution)/shard_map/ppermute | solution.py:532
  46.0 4.8 %collective-permute-start.13 = (bf16[512,128]{1,0:T(8,128)(2,1)S(1)}, bf16[512,128]{1,0:T(8,128)(2,1)S(1)}, u32[]{:S(2)}, u32[]{:S(2)}) collective-permute-start(bf16[512,128]{1,0:T(8,128)(2,1)S(1)} %get-tuple-element.100), channel_id=1, source_target_pairs={{0,8},{2,10},{4,12},{6,14},{8,0},{10,2},{12,4},{14,6},{1,9},{3,11}... | collective-permute-start | bytes 393224 | tf_op jit(solution)/shard_map/ppermute | solution.py:532
  46.7 13.1 %collective-permute-start.19 = (bf16[1024,128]{1,0:T(8,128)(2,1)S(1)}, bf16[1024,128]{1,0:T(8,128)(2,1)S(1)}, u32[]{:S(2)}, u32[]{:S(2)}) collective-permute-start(bf16[1024,128]{1,0:T(8,128)(2,1)S(1)} %get-tuple-element.93), channel_id=1, source_target_pairs={{0,4},{2,6},{4,0},{6,2},{8,12},{10,14},{12,8},{14,10},{1,5},{3,7},... | collective-permute-start | bytes 786440 | tf_op jit(solution)/shard_map/ppermute | solution.py:532
  47.3 18.3 %collective-permute-start.20 = (bf16[1024,128]{1,0:T(8,128)(2,1)S(1)}, bf16[1024,128]{1,0:T(8,128)(2,1)S(1)}, u32[]{:S(2)}, u32[]{:S(2)}) collective-permute-start(bf16[1024,128]{1,0:T(8,128)(2,1)S(1)} %get-tuple-element.94), channel_id=1, source_target_pairs={{0,0},{2,2},{4,8},{6,10},{8,4},{10,6},{12,12},{14,14},{1,1},{3,3},... | collective-permute-start | bytes 786440 | tf_op jit(solution)/shard_map/ppermute | solution.py:532
  50.9 15.0 %collective-permute-start.16 = (bf16[1024,128]{1,0:T(8,128)(2,1)S(1)}, bf16[1024,128]{1,0:T(8,128)(2,1)S(1)}, u32[]{:S(2)}, u32[]{:S(2)}) collective-permute-start(bf16[1024,128]{1,0:T(8,128)(2,1)S(1)} %get-tuple-element.102), channel_id=1, source_target_pairs={{0,4},{2,6},{4,0},{6,2},{8,12},{10,14},{12,8},{14,10},{1,5},{3,7},... | collective-permute-start | bytes 786440 | tf_op jit(solution)/shard_map/ppermute | solution.py:532
  54.5 11.4 %collective-permute-start.17 = (bf16[1024,128]{1,0:T(8,128)(2,1)S(1)}, bf16[1024,128]{1,0:T(8,128)(2,1)S(1)}, u32[]{:S(2)}, u32[]{:S(2)}) collective-permute-start(bf16[1024,128]{1,0:T(8,128)(2,1)S(1)} %get-tuple-element.103), channel_id=1, source_target_pairs={{0,0},{2,2},{4,8},{6,10},{8,4},{10,6},{12,12},{14,14},{1,1},{3,3},... | collective-permute-start | bytes 786440 | tf_op jit(solution)/shard_map/ppermute | solution.py:532
  59.8 7.3 %collective-permute-start.14 = (bf16[512,256]{1,0:T(8,128)(2,1)S(1)}, bf16[512,256]{1,0:T(8,128)(2,1)S(1)}, u32[]{:S(2)}, u32[]{:S(2)}) collective-permute-start(bf16[512,256]{1,0:T(8,128)(2,1)S(1)} %get-tuple-element.107), channel_id=1, source_target_pairs={{0,1},{1,0},{2,3},{3,2},{4,5},{5,4},{6,7},{7,6},{8,9},{9,8},{10,11... | collective-permute-start | bytes 786440 | tf_op jit(solution)/shard_map/ppermute | solution.py:529
  65.9 2.1 %collective-permute-start.21 = (bf16[512,128]{1,0:T(8,128)(2,1)S(1)}, bf16[512,128]{1,0:T(8,128)(2,1)S(1)}, u32[]{:S(2)}, u32[]{:S(2)}) collective-permute-start(bf16[512,128]{1,0:T(8,128)(2,1)S(1)} %get-tuple-element.119), channel_id=1, source_target_pairs={{0,1},{1,0},{2,3},{3,2},{4,5},{5,4},{6,7},{7,6},{8,9},{9,8},{10,11... | collective-permute-start | bytes 393224 | tf_op jit(solution)/shard_map/ppermute | solution.py:529
  66.2 2.6 %collective-permute-start.18 = (bf16[512,128]{1,0:T(8,128)(2,1)S(1)}, bf16[512,128]{1,0:T(8,128)(2,1)S(1)}, u32[]{:S(2)}, u32[]{:S(2)}) collective-permute-start(bf16[512,128]{1,0:T(8,128)(2,1)S(1)} %get-tuple-element.116), channel_id=1, source_target_pairs={{0,1},{1,0},{2,3},{3,2},{4,5},{5,4},{6,7},{7,6},{8,9},{9,8},{10,11... | collective-permute-start | bytes 393224 | tf_op jit(solution)/shard_map/ppermute | solution.py:529

commit v5 on v4

v5 whole, which is shorter than its diff:
```python
import functools
import math

import jax
import jax.numpy as jnp
from jax import lax
from jax.experimental import pallas as pl
from jax.experimental.pallas import tpu as pltpu
from jax.sharding import PartitionSpec as P

DH = 128
F32 = jnp.float32
BF16 = jnp.bfloat16
VMEM = pl.BlockSpec(memory_space=pltpu.VMEM)
SMEM = pl.BlockSpec(memory_space=pltpu.SMEM)
HBM = pl.BlockSpec(memory_space=pltpu.HBM)
NEG = -1e30
SCALE = 1.0 / math.sqrt(DH)
EXP_SCALE = SCALE * math.log2(math.e)
KEY = slice(0, DH)
VALUE = slice(DH, 2 * DH)
sds = jax.ShapeDtypeStruct


def dot_nn(a, b):
    return lax.dot_general(a, b, (((1,), (0,)), ((), ())), preferred_element_type=F32)


def dot_nt(a, b):
    return lax.dot_general(a, b, (((1,), (1,)), ((), ())), preferred_element_type=F32)


def dot_tn(a, b):
    return lax.dot_general(a, b, (((0,), (0,)), ((), ())), preferred_element_type=F32)


def call(kernel, args, out_shape, scratch=(), source=VMEM, flops=1024):
    return pl.pallas_call(
        kernel,
        out_shape=out_shape,
        in_specs=[SMEM if a.dtype == jnp.int32 else source for a in args],
        out_specs=tuple(VMEM for _ in out_shape),
        scratch_shapes=list(scratch),
        compiler_params=pltpu.CompilerParams(vmem_limit_bytes=40 << 20),
        cost_estimate=pl.CostEstimate(flops=flops, bytes_accessed=1024, transcendentals=0),
    )(*args)


def swap_pairs(count, distance, second):
    pairs = []
    for frame in range(count):
        up = ((frame // distance) % 2 == 0) != second
        target = frame + distance if up else frame - distance
        pairs.append((frame, target if 0 <= target < count else frame))
    return pairs


class Swap:
    def __init__(self, count, level, second):
        self.count, self.level, self.second = count, level, second
        self.levels = count.bit_length() - 1
        self.pairs = swap_pairs(count, 1 << level, second)
        self.moves = any(source != target for source, target in self.pairs)

    def partner(self, frame):
        odd = lax.rem(lax.shift_right_logical(frame, self.level), 2)
        later = odd == (1 if self.second else 0)
        other = jnp.where(later, frame + (1 << self.level), frame - (1 << self.level))
        return other, later, jnp.logical_and(other >= 0, other < self.count)

    def slot(self, later, k):
        base = 0 if self.level == 0 else self.level + 1
        return jnp.where(later, self.levels + 1, 0) + base + k

    def block_of_mine(self, lists, frame, slab, k):
        other, later, exists = self.partner(frame)
        entry = lists[self.slot(later, k), frame * 2 + slab]
        return jnp.clip(entry - other * 4, 0, 3), exists

    def block_of_theirs(self, lists, frame, slab, k):
        other, later, exists = self.partner(frame)
        row = jnp.where(exists, other, frame) * 2 + slab
        entry = lists[self.slot(jnp.logical_not(later), k), row]
        return jnp.clip(entry - frame * 4, 0, 3), exists


def head_cols(head):
    return slice(head * DH, (head + 1) * DH)


def rows_of(slab, half):
    return slice(slab * half, (slab + 1) * half)


def each_core(body):
    core = lax.axis_index("space")
    for mine in range(2):
        pl.when(core == mine)(functools.partial(body, mine))


def pack_kernel(a, b, send, own, sems):
    def body(mine):
        copies = []
        for head, out in ((1 - mine, send), (mine, own)):
            for source, cols in ((a, KEY), (b, VALUE)):
                sem = sems.at[len(copies)]
                copies.append(
                    pltpu.make_async_copy(source.at[:, head_cols(head)], out.at[:, cols], sem)
                )
        for copy in copies:
            copy.start()
        for copy in copies:
            copy.wait()

    each_core(body)


def frame_kernel(own, came, kv, keys, values):
    half = own.shape[0]

    def body(mine):
        for slab, source in ((mine, own), (1 - mine, came)):
            rows = rows_of(slab, half)
            part = source[...]
            kv[rows, :] = part
            keys[rows, :] = part[:, KEY]
            values[rows, :] = part[:, VALUE]

    each_core(body)


def select_kernel(far, block, lists, kv, *sends):
    frame = lax.axis_index("tm")
    for swap, send in zip(far, sends):
        for slab in range(2):
            b, _ = swap.block_of_theirs(lists, frame, slab, 0)
            row = pl.multiple_of(b * block, block)
            send[slab * block : (slab + 1) * block, :] = kv[pl.ds(row, block), :]


def forwards_first(frame):
    return lax.rem(frame, 2) == lax.rem(lax.shift_right_logical(frame, 1), 2)


def relay_kernel(y, z, out):
    first = forwards_first(lax.axis_index("tm"))

    @pl.when(first)
    def _():
        out[...] = z[...]

    @pl.when(jnp.logical_not(first))
    def _():
        out[...] = y[...]


class Piece:
    def __init__(self, k, v, row, size, exists=None, dk=None, dv=None, add=True):
        self.k_at, self.v_at, self.exists = k, v, exists
        self.rows, self.size = pl.ds(row, size), size
        self.dk, self.dv, self.add = dk, dv, add

    def store(self, at, value):
        ref, cols = at
        if self.add:
            ref[self.rows, cols] += value
        else:
            ref[self.rows, cols] = value.astype(ref.dtype)


def stack(parts):
    return parts[0] if len(parts) == 1 else jnp.concatenate(parts, axis=0)


def keys_of(group):
    return stack([p.k_at[0][p.rows, p.k_at[1]] for p in group])


def values_of(group):
    return stack([p.v_at[0][p.rows, p.v_at[1]] for p in group])


def by_piece(group, value):
    at = 0
    for piece in group:
        yield piece, value[at : at + piece.size, :]
        at += piece.size


def store_grads(group, value, name):
    for piece, part in by_piece(group, value):
        piece.store(getattr(piece, name), part)


def listed(swap, lists, frame, slab, block, k, v, count=1, **grads):
    pieces = []
    for n in range(count):
        b, exists = swap.block_of_mine(lists, frame, slab, n)
        pieces.append(Piece(k, v, pl.multiple_of(b * block, block), block, exists, **grads))
    return pieces


def arrived(swap, frame, slab, block, kv, **grads):
    _, _, exists = swap.partner(frame)
    return Piece((kv, KEY), (kv, VALUE), slab * block, block, exists, add=False, **grads)


def raised(group, s, base):
    parts = []
    for piece, part in by_piece(group, s):
        low = base if piece.exists is None else jnp.where(piece.exists, base, -NEG)
        parts.append(jnp.exp2(part * EXP_SCALE - low))
    return stack(parts)


def score_groups(q, groups, s_ref, peak):
    at = 0
    for group in groups:
        s = dot_nt(keys_of(group), q)
        s_ref[at : at + s.shape[0], :] = s
        at += s.shape[0]
        for piece, part in by_piece(group, s):
            top = jnp.max(part, axis=0, keepdims=True)
            if piece.exists is not None:
                top = jnp.where(piece.exists, top, NEG)
            peak = top if peak is None else jnp.maximum(peak, top)
    return peak


def group_scores(groups, s_ref):
    at = 0
    for group in groups:
        size = sum(piece.size for piece in group)
        yield group, s_ref[at : at + size, :]
        at += size


def forward_slab(q, groups, with_values, s_ref, old):
    peak = score_groups(q, groups, s_ref, None if old is None else old[0])
    total, acc = 0.0, 0.0
    if old is not None:
        shrink = jnp.exp2((old[0] - peak) * EXP_SCALE)
        total, acc = old[1] * shrink, old[2] * shrink
    for j, (group, s) in enumerate(group_scores(groups, s_ref)):
        e = raised(group, s, peak * EXP_SCALE)
        total = total + jnp.sum(e, axis=0, keepdims=True)
        if j < with_values:
            acc = acc + dot_tn(values_of(group), e.astype(BF16))
    return peak, total, acc


def backward_group(q, g, lse, row_dot, group, p=None):
    k = keys_of(group)
    if p is None:
        p = raised(group, dot_nt(k, q), lse)
    if group[0].dv is not None:
        store_grads(group, dot_nn(p.astype(BF16), g), "dv")
    ds = (p * (dot_nt(values_of(group), g) - row_dot)).astype(BF16)
    if group[0].dk is not None:
        store_grads(group, dot_nn(ds, q) * SCALE, "dk")
    return dot_tn(k, ds)


def join_kernel(own, came, out, turned):
    half = own.shape[0]

    def body(mine):
        for slab, source in ((mine, own), (1 - mine, came)):
            rows = rows_of(slab, half)
            out[rows, :] = source[...]
            turned[:, rows] = source[:, VALUE].T

    each_core(body)


ALL = slice(None)


def store_state(refs, rows, peak, total, acc):
    stat, acc_ref = refs
    stat[0:1, rows] = peak
    stat[1:2, rows] = total
    acc_ref[:, rows] = acc


def load_state(refs, rows):
    stat, acc_ref = refs
    return stat[0:1, rows], stat[1:2, rows], acc_ref[:, rows]


def own_groups(kv, half, **grads):
    return [
        [Piece((kv, KEY), (kv, VALUE), r, half, **grads)] for r in range(0, kv.shape[0], half)
    ]


def near_kernel(block, swap, lists, qg, kv, a_kv, stat, acc, s_ref):
    half = qg.shape[0] // 2
    frame = lax.axis_index("tm")
    for slab in range(2):
        rows = rows_of(slab, half)
        groups = own_groups(kv, half)
        groups.append(
            listed(swap, lists, frame, slab, block, (a_kv, KEY), (a_kv, VALUE), 2)
        )
        store_state((stat, acc), rows, *forward_slab(qg[rows, KEY], groups, 3, s_ref, None))


def middle_kernel(block, swaps, lists, qg, stat, acc, y_k, z_k, y_v, z_v, stat2, acc2, s_ref):
    half = qg.shape[0] // 2
    frame = lax.axis_index("tm")
    z, y = swaps
    for slab in range(2):
        rows = rows_of(slab, half)
        at = (lists, frame, slab, block)
        group = listed(z, *at, (z_k, ALL), (z_v, ALL)) + listed(y, *at, (y_k, ALL), (y_v, ALL))
        old = load_state((stat, acc), rows)
        store_state((stat2, acc2), rows, *forward_slab(qg[rows, KEY], [group], 1, s_ref, old))


def close_kernel(block, relayed, far, *refs):
    n = len(far)
    lists, qg, stat, acc, c_k = refs[:5]
    far_kv = refs[5 : 5 + n]
    lse_ref, part_ref, dc_v, p_ref, s_ref, grad = refs[5 + n :]
    half = qg.shape[0] // 2
    frame = lax.axis_index("tm")
    grad[...] = jnp.zeros_like(grad)
    for slab in range(2):
        rows = rows_of(slab, half)
        q, g = qg[rows, KEY], qg[rows, VALUE]
        groups = [[arrived(swap, frame, slab, block, kv)] for swap, kv in zip(far, far_kv)]
        groups.append(
            listed(relayed, lists, frame, slab, block, (c_k, ALL), None, 2, dv=(grad, ALL))
        )
        old = load_state((stat, acc), rows)
        peak, total, out = forward_slab(q, groups, n, s_ref, old)
        part_ref[:, rows] = out / total
        lse = peak * EXP_SCALE + jnp.log2(total)
        lse_ref[0:1, rows] = lse
        late, s = list(group_scores(groups, s_ref))[-1]
        p = raised(late, s, lse)
        p_ref[slab] = p
        store_grads(late, dot_nn(p.astype(BF16), g), "dv")
    dc_v[...] = grad[...].astype(BF16)


def late_kernel(block, relayed, far, *refs):
    n = len(far)
    lists, qg, turned, lse_ref, part_ref, p_ref, c_k, c_v = refs[:8]
    far_kv = refs[8 : 8 + n]
    o_ref, dot_ref, dc_k, dq_ref = refs[8 + n : 12 + n]
    far_grad = refs[12 + n : 12 + 2 * n]
    grad = refs[12 + 2 * n]
    half = qg.shape[0] // 2
    frame = lax.axis_index("tm")
    grad[...] = jnp.zeros_like(grad)
    for slab in range(2):
        rows = rows_of(slab, half)
        q, g, lse = qg[rows, KEY], qg[rows, VALUE], lse_ref[0:1, rows]
        group = listed(
            relayed, lists, frame, slab, block, (c_k, ALL), (c_v, ALL), 2, dk=(grad, ALL)
        )
        p = p_ref[slab]
        o = (part_ref[:, rows] + dot_tn(values_of(group), p.astype(BF16))).astype(BF16)
        o_ref[:, rows] = o
        products = turned[:, rows].astype(F32) * o.astype(F32)
        row_dot = jnp.sum(products, axis=0, keepdims=True)
        dot_ref[0:1, rows] = row_dot
        dq = backward_group(q, g, lse, row_dot, group, p)
        for swap, kv, out in zip(far, far_kv, far_grad):
            group = [arrived(swap, frame, slab, block, kv, dk=(out, KEY), dv=(out, VALUE))]
            dq = dq + backward_group(q, g, lse, row_dot, group)
        dq_ref[:, rows] = dq
    dc_k[...] = grad[...].astype(BF16)


def first_kernel(block, swap, lists, qg, lse_ref, dot_ref, dq_old, a_kv, da, dq_ref, grad):
    half = qg.shape[0] // 2
    frame = lax.axis_index("tm")
    grad[...] = jnp.zeros_like(grad)
    for slab in range(2):
        rows = rows_of(slab, half)
        q, g, lse, row_dot = qg[rows, KEY], qg[rows, VALUE], lse_ref[0:1, rows], dot_ref[0:1, rows]
        group = listed(
            swap, lists, frame, slab, block, (a_kv, KEY), (a_kv, VALUE), 2,
            dk=(grad, KEY), dv=(grad, VALUE),
        )
        dq_ref[:, rows] = dq_old[:, rows] + backward_group(q, g, lse, row_dot, group)
    da[...] = grad[...].astype(BF16)


def second_kernel(
    block, swaps, lists, qg, lse_ref, dot_ref, dq_old, came, y_k, z_k, y_v, z_v, dz, dy, dq_ref
):
    half = qg.shape[0] // 2
    frame = lax.axis_index("tm")
    z, y = swaps
    relays = forwards_first(frame)
    more = came[...].astype(F32)
    for ref, takes in ((dz, relays), (dy, jnp.logical_not(relays))):
        ref[:, KEY] = jnp.zeros_like(more)
        ref[:, VALUE] = jnp.where(takes, more, 0.0)
    for slab in range(2):
        rows = rows_of(slab, half)
        q, g, lse, row_dot = qg[rows, KEY], qg[rows, VALUE], lse_ref[0:1, rows], dot_ref[0:1, rows]
        at = (lists, frame, slab, block)
        group = listed(z, *at, (z_k, ALL), (z_v, ALL), dk=(dz, KEY), dv=(dz, VALUE))
        group += listed(y, *at, (y_k, ALL), (y_v, ALL), dk=(dy, KEY), dv=(dy, VALUE))
        dq_ref[:, rows] = dq_old[:, rows] + backward_group(q, g, lse, row_dot, group)


def own_kernel(qg, lse_ref, dot_ref, dq_old, o, kv, placed, near, keep, send):
    half = qg.shape[0] // 2
    near[...] = placed[...]
    whole = []
    for slab in range(2):
        rows = rows_of(slab, half)
        q, g, lse, row_dot = qg[rows, KEY], qg[rows, VALUE], lse_ref[0:1, rows], dot_ref[0:1, rows]
        dq = dq_old[:, rows]
        for group in own_groups(kv, half, dk=(near, KEY), dv=(near, VALUE)):
            dq = dq + backward_group(q, g, lse, row_dot, group)
        whole.append((dq.T * SCALE).astype(BF16))

    def body(mine):
        for slab in range(2):
            out = keep if slab == mine else send
            out[:, KEY] = o[:, rows_of(slab, half)].T
            out[:, VALUE] = whole[slab]

    each_core(body)


def merge_kernel(dz, dy, came, z_out, y_out):
    first = forwards_first(lax.axis_index("tm"))
    more = came[...].astype(F32)
    z_out[:, KEY] = (dz[:, KEY] + jnp.where(first, more, 0.0)).astype(BF16)
    y_out[:, KEY] = (dy[:, KEY] + jnp.where(first, 0.0, more)).astype(BF16)
    z_out[:, VALUE] = dz[:, VALUE].astype(BF16)
    y_out[:, VALUE] = dy[:, VALUE].astype(BF16)


def place_kernel(block, far, *refs):
    lists, total = refs[0], refs[-1]
    frame = lax.axis_index("tm")
    total[...] = jnp.zeros_like(total)
    for swap, came in zip(far, refs[1:-1]):
        for slab in range(2):
            b, exists = swap.block_of_theirs(lists, frame, slab, 0)
            rows = pl.ds(pl.multiple_of(b * block, block), block)
            part = came[slab * block : (slab + 1) * block, :].astype(F32)
            total[rows, :] += jnp.where(exists, part, 0.0)


def gather_kernel(swaps, near, da, dz, dy, keep, send):
    frame = lax.axis_index("tm")
    half = near.shape[0] // 2
    there = [swap.partner(frame)[2] for swap in swaps]

    def body(mine):
        for slab, out in ((1 - mine, send), (mine, keep)):
            rows = rows_of(slab, half)
            total = near[rows, :]
            for exists, part in zip(there, (da, dz, dy)):
                total = total + jnp.where(exists, part[rows, :].astype(F32), 0.0)
            out[...] = total.astype(BF16)

    each_core(body)


def finish_kernel(q_keep, q_came, k_keep, k_came, *outs):
    def body(mine):
        for head, sources in ((mine, (q_keep, k_keep)), (1 - mine, (q_came, k_came))):
            for source, first, second in zip(sources, outs[::2], outs[1::2]):
                first[:, head_cols(head)] = source[:, KEY]
                second[:, head_cols(head)] = source[:, VALUE]

    each_core(body)


def per_device(queries, key_rows, value_rows, out_grad, block_lists):
    s_dev, width = queries.shape
    count = lax.axis_size("tm")
    block = s_dev // 2
    pair = sds((s_dev, 2 * DH), BF16)
    frame_two = sds((2 * s_dev, 2 * DH), BF16)
    frame_one = sds((2 * s_dev, DH), BF16)
    frame_sum = sds((2 * s_dev, 2 * DH), F32)
    stat_row = sds((8, 2 * s_dev), F32)
    turned_sum = sds((DH, 2 * s_dev), F32)
    turned_bf = sds((DH, 2 * s_dev), BF16)
    levels = count.bit_length() - 1
    near_swap, relayed = Swap(count, 0, False), Swap(count, 0, True)
    z_swap, y_swap = Swap(count, 1, False), Swap(count, 1, True)
    swaps = (near_swap, z_swap, y_swap)
    far = [Swap(count, level, second) for level in range(2, levels) for second in (False, True)]
    far = [swap for swap in far if swap.moves]
    n = len(far)
    grad_one = pltpu.VMEM((2 * s_dev, DH), F32)

    def across(value):
        return lax.ppermute(value, "space", [(0, 1), (1, 0)])

    def swapped(value, swap):
        return lax.ppermute(value, "tm", swap.pairs)

    def scores(pieces):
        return pltpu.VMEM((pieces * block, s_dev), F32)

    lists = block_lists.T

    def packed(*pair_in):
        return call(
            pack_kernel,
            tuple(pltpu.with_memory_space_constraint(a, pltpu.HBM) for a in pair_in),
            [pair] * 2,
            scratch=[pltpu.SemaphoreType.DMA((4,))],
            source=HBM,
        )

    kv_send, kv_own = packed(key_rows, value_rows)
    kv_came = across(kv_send)
    qg_send, qg_own = packed(queries, out_grad)
    kv_came, qg_own = lax.optimization_barrier((kv_came, qg_own))
    kv, keys, values = call(
        frame_kernel, (kv_own, kv_came), [frame_two, frame_one, frame_one]
    )
    y_k = swapped(keys, y_swap)
    z_k = swapped(keys, z_swap)
    a_kv = swapped(kv, near_swap)
    y_v = swapped(values, y_swap)
    z_v = swapped(values, z_swap)
    far_send = call(functools.partial(select_kernel, far, block), (lists, kv), [pair] * n)
    qg_came, y_k = lax.optimization_barrier((across(qg_send), y_k))
    work = 4 * s_dev * s_dev * DH
    qg, turned = call(join_kernel, (qg_own, qg_came), [frame_two, turned_bf], flops=20 * work)
    y_k, z_k, turned = lax.optimization_barrier((y_k, z_k, turned))
    (relay_k,) = call(relay_kernel, (y_k, z_k), [frame_one])
    relay_k, far_send = lax.optimization_barrier((relay_k, far_send))
    a_kv, _ = lax.optimization_barrier((a_kv, relay_k))
    c_k = swapped(relay_k, near_swap)
    far_kv = [swapped(value, swap) for value, swap in zip(far_send, far)]
    stat, acc = call(
        functools.partial(near_kernel, block, near_swap),
        (lists, qg, kv, a_kv),
        [stat_row, turned_sum],
        scratch=[scores(6)],
    )
    y_v, z_v, stat = lax.optimization_barrier((y_v, z_v, stat))
    (relay_v,) = call(relay_kernel, (y_v, z_v), [frame_one])
    relay_v, stat = lax.optimization_barrier((relay_v, stat))
    c_v = swapped(relay_v, near_swap)
    stat, acc = call(
        functools.partial(middle_kernel, block, (z_swap, y_swap)),
        (lists, qg, stat, acc, y_k, z_k, y_v, z_v),
        [stat_row, turned_sum],
        scratch=[scores(2)],
    )
    lse, part, dc_v, probs = call(
        functools.partial(close_kernel, block, relayed, far),
        (lists, qg, stat, acc, c_k, *far_kv),
        [stat_row, turned_sum, frame_one, sds((2, s_dev, s_dev), F32)],
        scratch=[scores(2 + n), grad_one],
    )
    dc_v_came = swapped(dc_v, near_swap)
    o, row_dot, dc_k, dq, *far_grad = call(
        functools.partial(late_kernel, block, relayed, far),
        (lists, qg, turned, lse, part, probs, c_k, c_v, *far_kv),
        [turned_bf, stat_row, frame_one, turned_sum] + [pair] * n,
        scratch=[grad_one],
    )
    far_came = [swapped(value, swap) for value, swap in zip(far_grad, far)]
    dc_k_came = swapped(dc_k, near_swap)
    da, dq = call(
        functools.partial(first_kernel, block, near_swap),
        (lists, qg, lse, row_dot, dq, a_kv),
        [frame_two, turned_sum],
        scratch=[pltpu.VMEM((2 * s_dev, 2 * DH), F32)],
    )
    da_came = swapped(da, near_swap)
    dz, dy, dq = call(
        functools.partial(second_kernel, block, (z_swap, y_swap)),
        (lists, qg, lse, row_dot, dq, dc_v_came, y_k, z_k, y_v, z_v),
        [frame_sum, frame_sum, turned_sum],
    )
    dz, dy = call(merge_kernel, (dz, dy, dc_k_came), [frame_two, frame_two])
    dy_came = swapped(dy, y_swap)
    dz_came = swapped(dz, z_swap)
    dq, dz, dy = lax.optimization_barrier((dq, dz, dy))
    (placed,) = call(functools.partial(place_kernel, block, far), (lists, *far_came), [frame_sum])
    near, q_keep, q_send = call(
        own_kernel,
        (qg, lse, row_dot, dq, o, kv, placed),
        [frame_sum, pair, pair],
        flops=40 * work,
    )
    k_keep, k_send = call(
        functools.partial(gather_kernel, swaps),
        (near, da_came, dz_came, dy_came),
        [pair, pair],
    )
    return call(
        finish_kernel,
        (q_keep, across(q_send), k_keep, across(k_send)),
        [sds((s_dev, width), BF16)] * 4,
    )


def solution(mesh):
    rows = P(("groups", "tm", "space"), None)
    return jax.shard_map(
        per_device,
        mesh=mesh,
        in_specs=(rows, rows, rows, rows, P("groups", None)),
        out_specs=(rows, rows, rows, rows),
        check_vma=False,
    )
```

time: 69.7 us -> 70.6 us (1.013)
  the two profiles are of different devices: /device:TPU:11 before, /device:TPU:0 now
where the time goes in v5:
time: 70.6 us; the launch traced here: 70.4 us
  waiting for transfers between devices  27.8 us (39%)
  Pallas kernels  23.9 us (34%)
  starting transfers between devices  17.1 us (24%)
  between operations  0.86 us (1%)
    ppermute x14, waiting for transfers between devices, swapped(): return lax.ppermute(value, 'tm', swap.pairs)  26.3 us
    pallas_call x18, Pallas kernels, call(): pl.pallas_call(kernel, out_shape=out_shape, in_specs=[SMEM if a.dtype ==...  23.9 us
    ppermute x14, starting transfers between devices, swapped(): return lax.ppermute(value, 'tm', swap.pairs)  16.4 us
    ppermute x4, waiting for transfers between devices, across(): return lax.ppermute(value, 'space', [(0, 1), (1, 0)])  1.54 us
  transfers between devices with their start and end apart: 18, of which 8 were waited for; matrix products, arithmetic and copies ran while one was open for 0% of the time, Pallas kernels for 31%

profile of v5, /device:TPU:0, one launch (start us, length us, event | category | flops | bytes accessed | tf_op | source)
XLA Modules:
  0.0 70.4 jit_solution(14486506641082380904)
XLA Ops:
  0.6 1.1 %shard_map.84 = (bf16[512,256]{1,0:T(8,128)(2,1)S(1)}, bf16[512,256]{1,0:T(8,128)(2,1)S(1)}) custom-call(bf16[512,256]{1,0:T(8,128)(2,1)} %a.2, bf16[512,256]{1,0:T(8,128)(2,1)} %b.2), custom_call_target="tpu_custom_call" | custom-call | flops 1024 | bytes 1024 | tf_op jit(solution)/shard_map/pallas_call | solution.py:38
  1.8 0.5 collective-permute-start
  2.3 1.1 %shard_map.85 = (bf16[512,256]{1,0:T(8,128)(2,1)S(1)}, bf16[512,256]{1,0:T(8,128)(2,1)S(1)}) custom-call(bf16[512,256]{1,0:T(8,128)(2,1)} %a.3, bf16[512,256]{1,0:T(8,128)(2,1)} %b.3), custom_call_target="tpu_custom_call" | custom-call | flops 1024 | bytes 1024 | tf_op jit(solution)/shard_map/pallas_call | solution.py:38
  3.6 2.9 %collective-permute-start.5 = (bf16[1024,256]{1,0:T(8,128)(2,1)S(1)}, bf16[1024,256]{1,0:T(8,128)(2,1)S(1)}, u32[]{:S(2)}, u32[]{:S(2)}) collective-permute-start(bf16[1024,256]{1,0:T(8,128)(2,1)S(1)} %get-tuple-element.64.kv), channel_id=1, source_target_pairs={{0,2},{2,0},{4,6},{6,4},{8,10},{10,8},{12,14},{14,12},{1,3},{3,1},... | collective-permute-start | bytes 1572872 | tf_op jit(solution)/shard_map/ppermute | solution.py:505
  6.5 0.7 collective-permute-start.2
  7.2 4.4 %collective-permute-start.6 = (bf16[1024,128]{1,0:T(8,128)(2,1)S(1)}, bf16[1024,128]{1,0:T(8,128)(2,1)S(1)}, u32[]{:S(2)}, u32[]{:S(2)}) collective-permute-start(bf16[1024,128]{1,0:T(8,128)(2,1)S(1)} %get-tuple-element.60), channel_id=1, source_target_pairs={{0,4},{2,6},{4,0},{6,2},{8,12},{10,14},{12,8},{14,10},{1,5},{3,7},... | collective-permute-start | bytes 786440 | tf_op jit(solution)/shard_map/ppermute | solution.py:505
  11.7 0.7 collective-permute-start.3
  12.4 0.7 copy-done
  13.1 0.6 shard_map.89
  13.9 4.8 %collective-permute-done.6.z.z_k = bf16[1024,128]{1,0:T(8,128)(2,1)S(1)} collective-permute-done((bf16[1024,128]{1,0:T(8,128)(2,1)S(1)}, bf16[1024,128]{1,0:T(8,128)(2,1)S(1)}, u32[]{:S(2)}, u32[]{:S(2)}) %collective-permute-start.6) | collective-permute-done | bytes 262176 | tf_op jit(solution)/shard_map/ppermute | solution.py:505
  18.8 2.0 %collective-permute-start.8 = (bf16[512,256]{1,0:T(8,128)(2,1)S(1)}, bf16[512,256]{1,0:T(8,128)(2,1)S(1)}, u32[]{:S(2)}, u32[]{:S(2)}) collective-permute-start(bf16[512,256]{1,0:T(8,128)(2,1)S(1)} %shard_map.89), channel_id=1, source_target_pairs={{0,8},{2,10},{4,12},{6,14},{8,0},{10,2},{12,4},{14,6},{1,9},{3,11}... | collective-permute-start | bytes 786440 | tf_op jit(solution)/shard_map/ppermute | solution.py:505
  21.3 3.5 %shard_map.90 = (f32[8,1024]{1,0:T(8,128)S(1)}, f32[128,1024]{1,0:T(8,128)S(1)}) custom-call(s32[8,16]{1,0:T(8,128)S(1)} %bitcast.2, bf16[1024,256]{1,0:T(8,128)(2,1)S(1)} %get-tuple-element.62.qg.refs_1_, bf16[1024,256]{1,0:T(8,128)(2,1)S(1)} %get-tuple-element.64.kv, bf16[1024,256]{1,0:T(8,128)(2,1)S(1)} %collective-permute-done.5.a_kv), custom_call_target="tpu_custom_call" | custom-call | flops 1024 | bytes 1024 | tf_op jit(solution)/shard_map/pallas_call | solution.py:38
  25.0 1.6 %collective-permute-start.9 = (bf16[1024,128]{1,0:T(8,128)(2,1)S(1)}, bf16[1024,128]{1,0:T(8,128)(2,1)S(1)}, u32[]{:S(2)}, u32[]{:S(2)}) collective-permute-start(bf16[1024,128]{1,0:T(8,128)(2,1)S(1)} %shard_map.91), channel_id=1, source_target_pairs={{0,2},{2,0},{4,6},{6,4},{8,10},{10,8},{12,14},{14,12},{1,3},{3,1},... | collective-permute-start | bytes 786440 | tf_op jit(solution)/shard_map/ppermute | solution.py:505
  26.6 1.8 %shard_map.92 = (f32[8,1024]{1,0:T(8,128)S(1)}, f32[128,1024]{1,0:T(8,128)S(1)}) custom-call(s32[8,16]{1,0:T(8,128)S(1)} %bitcast.3, bf16[1024,256]{1,0:T(8,128)(2,1)S(1)} %get-tuple-element.62.qg.refs_1_, f32[8,1024]{1,0:T(8,128)S(1)} %get-tuple-element.75.stat, f32[128,1024]{1,0:T(8,128)S(1)} %get-tuple-element.76.acc, ...), custom_call_target="tpu_custom_call" | custom-call | flops 1024 | bytes 1024 | tf_op jit(solution)/shard_map/pallas_call | solution.py:38
  28.4 6.5 %collective-permute-done.8.refs_5_.refs_8_ = bf16[512,256]{1,0:T(8,128)(2,1)S(1)} collective-permute-done((bf16[512,256]{1,0:T(8,128)(2,1)S(1)}, bf16[512,256]{1,0:T(8,128)(2,1)S(1)}, u32[]{:S(2)}, u32[]{:S(2)}) %collective-permute-start.8) | collective-permute-done | bytes 262176 | tf_op jit(solution)/shard_map/ppermute | solution.py:505
  35.0 2.6 %shard_map.93 = (f32[8,1024]{1,0:T(8,128)S(1)}, f32[128,1024]{1,0:T(8,128)S(1)}, bf16[1024,128]{1,0:T(8,128)(2,1)S(1)}, f32[2,512,512]{2,1,0:T(8,128)S(1)}) custom-call(s32[8,16]{1,0:T(8,128)S(1)} %bitcast.4, bf16[1024,256]{1,0:T(8,128)(2,1)S(1)} %get-tuple-element.62.qg.refs_1_, f32[8,1024]{1,0:T(8,128)S(1)} %get-tuple-element.77.refs_2_, ...), custom_call_target="tpu_custom_call" | custom-call | flops 1024 | bytes 1024 | tf_op jit(solution)/shard_map/pallas_call | solution.py:38
  37.6 0.6 collective-permute-start.10
  38.2 2.5 %shard_map.94 = (bf16[128,1024]{1,0:T(8,128)(2,1)S(1)}, f32[8,1024]{1,0:T(8,128)S(1)}, bf16[1024,128]{1,0:T(8,128)(2,1)S(1)}, f32[128,1024]{1,0:T(8,128)S(1)}, bf16[512,256]{1,0:T(8,128)(2,1)S(1)}) custom-call(s32[8,16]{1,0:T(8,128)S(1)} %bitcast.5, bf16[1024,256]{1,0:T(8,128)(2,1)S(1)} %get-tuple-element.62.qg.refs_1_, ...), custom_call_target="tpu_custom_call" | custom-call | flops 1024 | bytes 1024 | tf_op jit(solution)/shard_map/pallas_call | solution.py:38
  40.7 1.6 %collective-permute-start.11 = (bf16[1024,128]{1,0:T(8,128)(2,1)S(1)}, bf16[1024,128]{1,0:T(8,128)(2,1)S(1)}, u32[]{:S(2)}, u32[]{:S(2)}) collective-permute-start(bf16[1024,128]{1,0:T(8,128)(2,1)S(1)} %get-tuple-element.92), channel_id=1, source_target_pairs={{0,2},{2,0},{4,6},{6,4},{8,10},{10,8},{12,14},{14,12},{1,3},{3,1},... | collective-permute-start | bytes 786440 | tf_op jit(solution)/shard_map/ppermute | solution.py:505
  42.3 2.2 %shard_map.95 = (bf16[1024,256]{1,0:T(8,128)(2,1)S(1)}, f32[128,1024]{1,0:T(8,128)S(1)}) custom-call(s32[8,16]{1,0:T(8,128)S(1)} %bitcast.6, bf16[1024,256]{1,0:T(8,128)(2,1)S(1)} %get-tuple-element.62.qg.refs_1_, f32[8,1024]{1,0:T(8,128)S(1)} %get-tuple-element.80.refs_3_.lse_ref, f32[8,1024]{1,0:T(8,128)S(1)} %get-tuple-element.85.dot_ref, ...), custom_call_target="tpu_custom_call" | custom-call | flops 1024 | bytes 1024 | tf_op jit(solution)/shard_map/pallas_call | solution.py:38
  44.6 0.6 collective-permute-start.14
  45.2 1.8 %collective-permute-done.10.came = bf16[1024,128]{1,0:T(8,128)(2,1)S(1)} collective-permute-done((bf16[1024,128]{1,0:T(8,128)(2,1)S(1)}, bf16[1024,128]{1,0:T(8,128)(2,1)S(1)}, u32[]{:S(2)}, u32[]{:S(2)}) %collective-permute-start.10) | collective-permute-done | bytes 262176 | tf_op jit(solution)/shard_map/ppermute | solution.py:505
  46.9 2.2 %shard_map.96 = (f32[1024,256]{1,0:T(8,128)S(1)}, f32[1024,256]{1,0:T(8,128)S(1)}, f32[128,1024]{1,0:T(8,128)S(1)}) custom-call(s32[8,16]{1,0:T(8,128)S(1)} %bitcast.7, bf16[1024,256]{1,0:T(8,128)(2,1)S(1)} %get-tuple-element.62.qg.refs_1_, f32[8,1024]{1,0:T(8,128)S(1)} %get-tuple-element.80.refs_3_.lse_ref, f32[8,1024]{1,0:T(8,128)S(1)} %get-tuple-element.85.dot_ref, ...), custom_call_target="tpu_custom_call" | custom-call | flops 1024 | bytes 1024 | tf_op jit(solution)/shard_map/pallas_call | solution.py:38
  49.2 3.4 %collective-permute-done.11.came = bf16[1024,128]{1,0:T(8,128)(2,1)S(1)} collective-permute-done((bf16[1024,128]{1,0:T(8,128)(2,1)S(1)}, bf16[1024,128]{1,0:T(8,128)(2,1)S(1)}, u32[]{:S(2)}, u32[]{:S(2)}) %collective-permute-start.11) | collective-permute-done | bytes 262176 | tf_op jit(solution)/shard_map/ppermute | solution.py:505
  52.9 0.7 collective-permute-start.16
  53.6 2.6 %collective-permute-done.12.refs_1_ = bf16[512,256]{1,0:T(8,128)(2,1)S(1)} collective-permute-done((bf16[512,256]{1,0:T(8,128)(2,1)S(1)}, bf16[512,256]{1,0:T(8,128)(2,1)S(1)}, u32[]{:S(2)}, u32[]{:S(2)}) %collective-permute-start.12) | collective-permute-done | bytes 262176 | tf_op jit(solution)/shard_map/ppermute | solution.py:505
  56.2 0.7 %shard_map.98.placed = f32[1024,256]{1,0:T(8,128)S(1)} custom-call(s32[8,16]{1,0:T(8,128)S(1)} %bitcast.8, bf16[512,256]{1,0:T(8,128)(2,1)S(1)} %collective-permute-done.12.refs_1_), custom_call_target="tpu_custom_call" | custom-call | flops 1024 | bytes 1024 | tf_op jit(solution)/shard_map/pallas_call | solution.py:38
  56.9 3.2 %shard_map.99 = (f32[1024,256]{1,0:T(8,128)S(1)}, bf16[512,256]{1,0:T(8,128)(2,1)S(1)}, bf16[512,256]{1,0:T(8,128)(2,1)S(1)}) custom-call(bf16[1024,256]{1,0:T(8,128)(2,1)S(1)} %get-tuple-element.62.qg.refs_1_, f32[8,1024]{1,0:T(8,128)S(1)} %get-tuple-element.80.refs_3_.lse_ref, f32[8,1024]{1,0:T(8,128)S(1)} %get-tuple-element.85.dot_ref, ...), custom_call_target="tpu_custom_call" | custom-call | flops 5368709120 | bytes 1024 | tf_op jit(solution)/shard_map/pallas_call | solution.py:38
  60.2 2.2 %collective-permute-done.14.da = bf16[1024,256]{1,0:T(8,128)(2,1)S(1)} collective-permute-done((bf16[1024,256]{1,0:T(8,128)(2,1)S(1)}, bf16[1024,256]{1,0:T(8,128)(2,1)S(1)}, u32[]{:S(2)}, u32[]{:S(2)}) %collective-permute-start.14) | collective-permute-done | bytes 524320 | tf_op jit(solution)/shard_map/ppermute | solution.py:505
  62.4 4.9 %collective-permute-done.15.dz = bf16[1024,256]{1,0:T(8,128)(2,1)S(1)} collective-permute-done((bf16[1024,256]{1,0:T(8,128)(2,1)S(1)}, bf16[1024,256]{1,0:T(8,128)(2,1)S(1)}, u32[]{:S(2)}, u32[]{:S(2)}) %collective-permute-start.15) | collective-permute-done | bytes 524320 | tf_op jit(solution)/shard_map/ppermute | solution.py:505
  67.7 1.5 %collective-permute-done.17.k_came = bf16[512,256]{1,0:T(8,128)(2,1)S(1)} collective-permute-done((bf16[512,256]{1,0:T(8,128)(2,1)S(1)}, bf16[512,256]{1,0:T(8,128)(2,1)S(1)}, u32[]{:S(2)}, u32[]{:S(2)}) %collective-permute-start.17) | collective-permute-done | bytes 262176 | tf_op jit(solution)/shard_map/ppermute | solution.py:502
  69.2 1.1 %shard_map.101 = (bf16[512,256]{1,0:T(8,128)(2,1)}, bf16[512,256]{1,0:T(8,128)(2,1)}, bf16[512,256]{1,0:T(8,128)(2,1)}, bf16[512,256]{1,0:T(8,128)(2,1)}) custom-call(bf16[512,256]{1,0:T(8,128)(2,1)S(1)} %get-tuple-element.98.q_keep, bf16[512,256]{1,0:T(8,128)(2,1)S(1)} %collective-permute-done.13.q_came, bf16[512,256]{1,0:T(8,128)(2,1)S(1)} %get-tuple-element.102.k_keep, ...), custom_call_target="tpu_custom_call" | custom-call | flops 1024 | bytes 1024 | tf_op jit(solution)/shard_map/pallas_call | solution.py:38
  (26 shorter events, 1.9 us)
Async XLA Ops:
  1.8 1.7 %collective-permute-start = (bf16[512,256]{1,0:T(8,128)(2,1)S(1)}, bf16[512,256]{1,0:T(8,128)(2,1)S(1)}, u32[]{:S(2)}, u32[]{:S(2)}) collective-permute-start(bf16[512,256]{1,0:T(8,128)(2,1)S(1)} %get-tuple-element.54), channel_id=1, source_target_pairs={{0,1},{1,0},{2,3},{3,2},{4,5},{5,4},{6,7},{7,6},{8,9},{9,8},{10,11... | collective-permute-start | bytes 786440 | tf_op jit(solution)/shard_map/ppermute | solution.py:502
  3.6 17.7 %collective-permute-start.5 = (bf16[1024,256]{1,0:T(8,128)(2,1)S(1)}, bf16[1024,256]{1,0:T(8,128)(2,1)S(1)}, u32[]{:S(2)}, u32[]{:S(2)}) collective-permute-start(bf16[1024,256]{1,0:T(8,128)(2,1)S(1)} %get-tuple-element.64.kv), channel_id=1, source_target_pairs={{0,2},{2,0},{4,6},{6,4},{8,10},{10,8},{12,14},{14,12},{1,3},{3,1},... | collective-permute-start | bytes 1572872 | tf_op jit(solution)/shard_map/ppermute | solution.py:505
  6.5 5.2 %collective-permute-start.1 = (bf16[512,256]{1,0:T(8,128)(2,1)S(1)}, bf16[512,256]{1,0:T(8,128)(2,1)S(1)}, u32[]{:S(2)}, u32[]{:S(2)}) collective-permute-start(bf16[512,256]{1,0:T(8,128)(2,1)S(1)} %get-tuple-element.57), channel_id=1, source_target_pairs={{0,1},{1,0},{2,3},{3,2},{4,5},{5,4},{6,7},{7,6},{8,9},{9,8},{10,11... | collective-permute-start | bytes 786440 | tf_op jit(solution)/shard_map/ppermute | solution.py:502
  6.5 7.2 %collective-permute-start.2 = (bf16[1024,128]{1,0:T(8,128)(2,1)S(1)}, bf16[1024,128]{1,0:T(8,128)(2,1)S(1)}, u32[]{:S(2)}, u32[]{:S(2)}) collective-permute-start(bf16[1024,128]{1,0:T(8,128)(2,1)S(1)} %get-tuple-element.60), channel_id=1, source_target_pairs={{0,0},{2,2},{4,8},{6,10},{8,4},{10,6},{12,12},{14,14},{1,1},{3,3},... | collective-permute-start | bytes 786440 | tf_op jit(solution)/shard_map/ppermute | solution.py:505
  7.2 11.5 %collective-permute-start.6 = (bf16[1024,128]{1,0:T(8,128)(2,1)S(1)}, bf16[1024,128]{1,0:T(8,128)(2,1)S(1)}, u32[]{:S(2)}, u32[]{:S(2)}) collective-permute-start(bf16[1024,128]{1,0:T(8,128)(2,1)S(1)} %get-tuple-element.60), channel_id=1, source_target_pairs={{0,4},{2,6},{4,0},{6,2},{8,12},{10,14},{12,8},{14,10},{1,5},{3,7},... | collective-permute-start | bytes 786440 | tf_op jit(solution)/shard_map/ppermute | solution.py:505
  11.6 13.1 %collective-permute-start.4 = (bf16[1024,128]{1,0:T(8,128)(2,1)S(1)}, bf16[1024,128]{1,0:T(8,128)(2,1)S(1)}, u32[]{:S(2)}, u32[]{:S(2)}) collective-permute-start(bf16[1024,128]{1,0:T(8,128)(2,1)S(1)} %get-tuple-element.63), channel_id=1, source_target_pairs={{0,4},{2,6},{4,0},{6,2},{8,12},{10,14},{12,8},{14,10},{1,5},{3,7},... | collective-permute-start | bytes 786440 | tf_op jit(solution)/shard_map/ppermute | solution.py:505
  11.7 13.0 %collective-permute-start.3 = (bf16[1024,128]{1,0:T(8,128)(2,1)S(1)}, bf16[1024,128]{1,0:T(8,128)(2,1)S(1)}, u32[]{:S(2)}, u32[]{:S(2)}) collective-permute-start(bf16[1024,128]{1,0:T(8,128)(2,1)S(1)} %get-tuple-element.63), channel_id=1, source_target_pairs={{0,0},{2,2},{4,8},{6,10},{8,4},{10,6},{12,12},{14,14},{1,1},{3,3},... | collective-permute-start | bytes 786440 | tf_op jit(solution)/shard_map/ppermute | solution.py:505
  12.4 0.7 copy-start
  13.7 7.5 %copy-start.1 = (s32[16,8]{0,1:T(8,128)S(1)}, s32[16,8]{0,1:T(8,128)}, u32[]{:S(2)}) copy-start(s32[16,8]{0,1:T(8,128)} %param.9) | copy-start | bytes 1540
  18.8 16.2 %collective-permute-start.8 = (bf16[512,256]{1,0:T(8,128)(2,1)S(1)}, bf16[512,256]{1,0:T(8,128)(2,1)S(1)}, u32[]{:S(2)}, u32[]{:S(2)}) collective-permute-start(bf16[512,256]{1,0:T(8,128)(2,1)S(1)} %shard_map.89), channel_id=1, source_target_pairs={{0,8},{2,10},{4,12},{6,14},{8,0},{10,2},{12,4},{14,6},{1,9},{3,11}... | collective-permute-start | bytes 786440 | tf_op jit(solution)/shard_map/ppermute | solution.py:505
  20.8 14.2 %collective-permute-start.7 = (bf16[1024,128]{1,0:T(8,128)(2,1)S(1)}, bf16[1024,128]{1,0:T(8,128)(2,1)S(1)}, u32[]{:S(2)}, u32[]{:S(2)}) collective-permute-start(bf16[1024,128]{1,0:T(8,128)(2,1)S(1)} %shard_map.88), channel_id=1, source_target_pairs={{0,2},{2,0},{4,6},{6,4},{8,10},{10,8},{12,14},{14,12},{1,3},{3,1},... | collective-permute-start | bytes 786440 | tf_op jit(solution)/shard_map/ppermute | solution.py:505
  25.0 13.2 %collective-permute-start.9 = (bf16[1024,128]{1,0:T(8,128)(2,1)S(1)}, bf16[1024,128]{1,0:T(8,128)(2,1)S(1)}, u32[]{:S(2)}, u32[]{:S(2)}) collective-permute-start(bf16[1024,128]{1,0:T(8,128)(2,1)S(1)} %shard_map.91), channel_id=1, source_target_pairs={{0,2},{2,0},{4,6},{6,4},{8,10},{10,8},{12,14},{14,12},{1,3},{3,1},... | collective-permute-start | bytes 786440 | tf_op jit(solution)/shard_map/ppermute | solution.py:505
  37.6 9.3 %collective-permute-start.10 = (bf16[1024,128]{1,0:T(8,128)(2,1)S(1)}, bf16[1024,128]{1,0:T(8,128)(2,1)S(1)}, u32[]{:S(2)}, u32[]{:S(2)}) collective-permute-start(bf16[1024,128]{1,0:T(8,128)(2,1)S(1)} %get-tuple-element.88), channel_id=1, source_target_pairs={{0,2},{2,0},{4,6},{6,4},{8,10},{10,8},{12,14},{14,12},{1,3},{3,1},... | collective-permute-start | bytes 786440 | tf_op jit(solution)/shard_map/ppermute | solution.py:505
  40.7 11.8 %collective-permute-start.11 = (bf16[1024,128]{1,0:T(8,128)(2,1)S(1)}, bf16[1024,128]{1,0:T(8,128)(2,1)S(1)}, u32[]{:S(2)}, u32[]{:S(2)}) collective-permute-start(bf16[1024,128]{1,0:T(8,128)(2,1)S(1)} %get-tuple-element.92), channel_id=1, source_target_pairs={{0,2},{2,0},{4,6},{6,4},{8,10},{10,8},{12,14},{14,12},{1,3},{3,1},... | collective-permute-start | bytes 786440 | tf_op jit(solution)/shard_map/ppermute | solution.py:505
  42.3 13.9 %collective-permute-start.12 = (bf16[512,256]{1,0:T(8,128)(2,1)S(1)}, bf16[512,256]{1,0:T(8,128)(2,1)S(1)}, u32[]{:S(2)}, u32[]{:S(2)}) collective-permute-start(bf16[512,256]{1,0:T(8,128)(2,1)S(1)} %get-tuple-element.97), channel_id=1, source_target_pairs={{0,8},{2,10},{4,12},{6,14},{8,0},{10,2},{12,4},{14,6},{1,9},{3,11}... | collective-permute-start | bytes 786440 | tf_op jit(solution)/shard_map/ppermute | solution.py:505
  44.6 17.8 %collective-permute-start.14 = (bf16[1024,256]{1,0:T(8,128)(2,1)S(1)}, bf16[1024,256]{1,0:T(8,128)(2,1)S(1)}, u32[]{:S(2)}, u32[]{:S(2)}) collective-permute-start(bf16[1024,256]{1,0:T(8,128)(2,1)S(1)} %get-tuple-element.101), channel_id=1, source_target_pairs={{0,2},{2,0},{4,6},{6,4},{8,10},{10,8},{12,14},{14,12},{1,3},{3,1},... | collective-permute-start | bytes 1572872 | tf_op jit(solution)/shard_map/ppermute | solution.py:505
  52.8 14.5 %collective-permute-start.15 = (bf16[1024,256]{1,0:T(8,128)(2,1)S(1)}, bf16[1024,256]{1,0:T(8,128)(2,1)S(1)}, u32[]{:S(2)}, u32[]{:S(2)}) collective-permute-start(bf16[1024,256]{1,0:T(8,128)(2,1)S(1)} %get-tuple-element.93), channel_id=1, source_target_pairs={{0,4},{2,6},{4,0},{6,2},{8,12},{10,14},{12,8},{14,10},{1,5},{3,7},... | collective-permute-start | bytes 1572872 | tf_op jit(solution)/shard_map/ppermute | solution.py:505
  52.9 14.4 %collective-permute-start.16 = (bf16[1024,256]{1,0:T(8,128)(2,1)S(1)}, bf16[1024,256]{1,0:T(8,128)(2,1)S(1)}, u32[]{:S(2)}, u32[]{:S(2)}) collective-permute-start(bf16[1024,256]{1,0:T(8,128)(2,1)S(1)} %get-tuple-element.94), channel_id=1, source_target_pairs={{0,0},{2,2},{4,8},{6,10},{8,4},{10,6},{12,12},{14,14},{1,1},{3,3},... | collective-permute-start | bytes 1572872 | tf_op jit(solution)/shard_map/ppermute | solution.py:505
  60.1 7.6 %collective-permute-start.13 = (bf16[512,256]{1,0:T(8,128)(2,1)S(1)}, bf16[512,256]{1,0:T(8,128)(2,1)S(1)}, u32[]{:S(2)}, u32[]{:S(2)}) collective-permute-start(bf16[512,256]{1,0:T(8,128)(2,1)S(1)} %get-tuple-element.99), channel_id=1, source_target_pairs={{0,1},{1,0},{2,3},{3,2},{4,5},{5,4},{6,7},{7,6},{8,9},{9,8},{10,11... | collective-permute-start | bytes 786440 | tf_op jit(solution)/shard_map/ppermute | solution.py:502
  67.6 1.6 %collective-permute-start.17 = (bf16[512,256]{1,0:T(8,128)(2,1)S(1)}, bf16[512,256]{1,0:T(8,128)(2,1)S(1)}, u32[]{:S(2)}, u32[]{:S(2)}) collective-permute-start(bf16[512,256]{1,0:T(8,128)(2,1)S(1)} %get-tuple-element.103), channel_id=1, source_target_pairs={{0,1},{1,0},{2,3},{3,2},{4,5},{5,4},{6,7},{7,6},{8,9},{9,8},{10,11... | collective-permute-start | bytes 786440 | tf_op jit(solution)/shard_map/ppermute | solution.py:502

commit v6 on v5

--- a/solution.py
+++ b/solution.py
@@ -318,30 +318,52 @@
         store_state((stat2, acc2), rows, *forward_slab(qg[rows, KEY], [group], 1, s_ref, old))
 
 
-def close_kernel(block, relayed, far, *refs):
+def relayed_kernel(block, relayed, lists, qg, stat, acc, c_k, stat2, acc2, s_ref):
+    half = qg.shape[0] // 2
+    frame = lax.axis_index("tm")
+    for slab in range(2):
+        rows = rows_of(slab, half)
+        group = listed(relayed, lists, frame, slab, block, (c_k, ALL), None, 2)
+        old = load_state((stat, acc), rows)
+        new = forward_slab(qg[rows, KEY], [group], 0, s_ref.at[slab], old)
+        store_state((stat2, acc2), rows, *new)
+
+
+def close_kernel(block, far, qg, stat, acc, *refs):
     n = len(far)
-    lists, qg, stat, acc, c_k = refs[:5]
-    far_kv = refs[5 : 5 + n]
-    lse_ref, part_ref, dc_v, p_ref, s_ref, grad = refs[5 + n :]
-    half = qg.shape[0] // 2
-    frame = lax.axis_index("tm")
-    grad[...] = jnp.zeros_like(grad)
+    far_kv = refs[:n]
+    lse_ref, part_ref = refs[n : n + 2]
+    far_dv = refs[n + 2 : 2 * n + 2]
+    s_ref = refs[2 * n + 2]
+    half = qg.shape[0] // 2
+    frame = lax.axis_index("tm")
     for slab in range(2):
         rows = rows_of(slab, half)
         q, g = qg[rows, KEY], qg[rows, VALUE]
-        groups = [[arrived(swap, frame, slab, block, kv)] for swap, kv in zip(far, far_kv)]
-        groups.append(
-            listed(relayed, lists, frame, slab, block, (c_k, ALL), None, 2, dv=(grad, ALL))
-        )
+        groups = [
+            [arrived(swap, frame, slab, block, kv, dv=(out, ALL))]
+            for swap, kv, out in zip(far, far_kv, far_dv)
+        ]
         old = load_state((stat, acc), rows)
         peak, total, out = forward_slab(q, groups, n, s_ref, old)
         part_ref[:, rows] = out / total
         lse = peak * EXP_SCALE + jnp.log2(total)
         lse_ref[0:1, rows] = lse
-        late, s = list(group_scores(groups, s_ref))[-1]
-        p = raised(late, s, lse)
+        for group, s in group_scores(groups, s_ref):
+            p = raised(group, s, lse)
+            store_grads(group, dot_nn(p.astype(BF16), g), "dv")
+
+
+def values_kernel(block, relayed, lists, qg, lse_ref, s_ref, dc_v, p_ref, grad):
+    half = qg.shape[0] // 2
+    frame = lax.axis_index("tm")
+    grad[...] = jnp.zeros_like(grad)
+    for slab in range(2):
+        rows = rows_of(slab, half)
+        group = listed(relayed, lists, frame, slab, block, None, None, 2, dv=(grad, ALL))
+        p = raised(group, s_ref[slab], lse_ref[0:1, rows])
         p_ref[slab] = p
-        store_grads(late, dot_nn(p.astype(BF16), g), "dv")
+        store_grads(group, dot_nn(p.astype(BF16), qg[rows, VALUE]), "dv")
     dc_v[...] = grad[...].astype(BF16)
 
 
@@ -369,7 +391,7 @@
         dot_ref[0:1, rows] = row_dot
         dq = backward_group(q, g, lse, row_dot, group, p)
         for swap, kv, out in zip(far, far_kv, far_grad):
-            group = [arrived(swap, frame, slab, block, kv, dk=(out, KEY), dv=(out, VALUE))]
+            group = [arrived(swap, frame, slab, block, kv, dk=(out, ALL))]
             dq = dq + backward_group(q, g, lse, row_dot, group)
         dq_ref[:, rows] = dq
     dc_k[...] = grad[...].astype(BF16)
@@ -441,15 +463,17 @@
 
 
 def place_kernel(block, far, *refs):
+    n = len(far)
     lists, total = refs[0], refs[-1]
     frame = lax.axis_index("tm")
     total[...] = jnp.zeros_like(total)
-    for swap, came in zip(far, refs[1:-1]):
+    for swap, came_k, came_v in zip(far, refs[1 : 1 + n], refs[1 + n : -1]):
         for slab in range(2):
             b, exists = swap.block_of_theirs(lists, frame, slab, 0)
             rows = pl.ds(pl.multiple_of(b * block, block), block)
-            part = came[slab * block : (slab + 1) * block, :].astype(F32)
-            total[rows, :] += jnp.where(exists, part, 0.0)
+            for came, cols in ((came_k, KEY), (came_v, VALUE)):
+                part = came[rows_of(slab, block), :].astype(F32)
+                total[rows, cols] += jnp.where(exists, part, 0.0)
 
 
 def gather_kernel(swaps, near, da, dz, dy, keep, send):
@@ -483,6 +507,7 @@
     count = lax.axis_size("tm")
     block = s_dev // 2
     pair = sds((s_dev, 2 * DH), BF16)
+    single = sds((s_dev, DH), BF16)
     frame_two = sds((2 * s_dev, 2 * DH), BF16)
     frame_one = sds((2 * s_dev, DH), BF16)
     frame_sum = sds((2 * s_dev, 2 * DH), F32)
@@ -533,7 +558,7 @@
     far_send = call(functools.partial(select_kernel, far, block), (lists, kv), [pair] * n)
     qg_came, y_k = lax.optimization_barrier((across(qg_send), y_k))
     work = 4 * s_dev * s_dev * DH
-    qg, turned = call(join_kernel, (qg_own, qg_came), [frame_two, turned_bf], flops=20 * work)
+    qg, turned = call(join_kernel, (qg_own, qg_came), [frame_two, turned_bf], flops=15 * work)
     y_k, z_k, turned = lax.optimization_barrier((y_k, z_k, turned))
     (relay_k,) = call(relay_kernel, (y_k, z_k), [frame_one])
     relay_k, far_send = lax.optimization_barrier((relay_k, far_send))
@@ -556,20 +581,34 @@
         [stat_row, turned_sum],
         scratch=[scores(2)],
     )
-    lse, part, dc_v, probs = call(
-        functools.partial(close_kernel, block, relayed, far),
-        (lists, qg, stat, acc, c_k, *far_kv),
-        [stat_row, turned_sum, frame_one, sds((2, s_dev, s_dev), F32)],
-        scratch=[scores(2 + n), grad_one],
+    score_two = sds((2, s_dev, s_dev), F32)
+    stat, acc, late_scores = call(
+        functools.partial(relayed_kernel, block, relayed),
+        (lists, qg, stat, acc, c_k),
+        [stat_row, turned_sum, score_two],
+    )
+    acc, far_kv = lax.optimization_barrier((acc, far_kv))
+    lse, part, *far_dv = call(
+        functools.partial(close_kernel, block, far),
+        (qg, stat, acc, *far_kv),
+        [stat_row, turned_sum] + [single] * n,
+        scratch=[scores(n)],
+    )
+    dc_v, probs = call(
+        functools.partial(values_kernel, block, relayed),
+        (lists, qg, lse, late_scores),
+        [frame_one, score_two],
+        scratch=[grad_one],
     )
     dc_v_came = swapped(dc_v, near_swap)
+    far_dv_came = [swapped(value, swap) for value, swap in zip(far_dv, far)]
     o, row_dot, dc_k, dq, *far_grad = call(
         functools.partial(late_kernel, block, relayed, far),
         (lists, qg, turned, lse, part, probs, c_k, c_v, *far_kv),
-        [turned_bf, stat_row, frame_one, turned_sum] + [pair] * n,
+        [turned_bf, stat_row, frame_one, turned_sum] + [single] * n,
         scratch=[grad_one],
     )
-    far_came = [swapped(value, swap) for value, swap in zip(far_grad, far)]
+    far_dk_came = [swapped(value, swap) for value, swap in zip(far_grad, far)]
     dc_k_came = swapped(dc_k, near_swap)
     da, dq = call(
         functools.partial(first_kernel, block, near_swap),
@@ -578,16 +617,18 @@
         scratch=[pltpu.VMEM((2 * s_dev, 2 * DH), F32)],
     )
     da_came = swapped(da, near_swap)
+    dc_v_came, far_dv_came = lax.optimization_barrier((dc_v_came, far_dv_came))
     dz, dy, dq = call(
         functools.partial(second_kernel, block, (z_swap, y_swap)),
         (lists, qg, lse, row_dot, dq, dc_v_came, y_k, z_k, y_v, z_v),
         [frame_sum, frame_sum, turned_sum],
+        flops=20 * work,
     )
     dz, dy = call(merge_kernel, (dz, dy, dc_k_came), [frame_two, frame_two])
     dy_came = swapped(dy, y_swap)
     dz_came = swapped(dz, z_swap)
     dq, dz, dy = lax.optimization_barrier((dq, dz, dy))
-    (placed,) = call(functools.partial(place_kernel, block, far), (lists, *far_came), [frame_sum])
+    (placed,) = call(functools.partial(place_kernel, block, far), (lists, *far_dk_came, *far_dv_came), [frame_sum])
     near, q_keep, q_send = call(
         own_kernel,
         (qg, lse, row_dot, dq, o, kv, placed),

time: 70.6 us -> 65.7 us (0.931)
  waiting for transfers between devices: 27.8 us -> 16.9 us
  starting transfers between devices: 17.1 us -> 21.8 us
    ppermute x14 -> x15, waiting for transfers between devices: 26.3 us -> 15.3 us  [swapped(): return lax.ppermute(value, 'tm', swap.pairs)]
    ppermute x14 -> x15, starting transfers between devices: 16.4 us -> 21 us  [swapped(): return lax.ppermute(value, 'tm', swap.pairs)]
    pallas_call x18 -> x20, Pallas kernels: 23.9 us -> 24.6 us  [call(): pl.pallas_call(kernel, out_shape=out_shape, in_specs=[SMEM if a.dtype ==...]
  transfers between devices with their start and end apart: 18 -> 19, of which waited for: 8 -> 7; matrix products, arithmetic and copies ran while one was open for 0% -> 0% of each run, Pallas kernels for 31% -> 34%
where the time goes in v6:
time: 65.7 us; the launch traced here: 64.8 us
  Pallas kernels  24.6 us (37%)
  starting transfers between devices  21.8 us (33%)
  waiting for transfers between devices  16.9 us (26%)
  between operations  0.89 us (1%)
  local copies, waits for them, and re-layouts  0.69 us (1%)
    pallas_call x20, Pallas kernels, call(): pl.pallas_call(kernel, out_shape=out_shape, in_specs=[SMEM if a.dtype ==...  24.6 us
    ppermute x15, starting transfers between devices, swapped(): return lax.ppermute(value, 'tm', swap.pairs)  21 us
    ppermute x15, waiting for transfers between devices, swapped(): return lax.ppermute(value, 'tm', swap.pairs)  15.3 us
    ppermute x4, waiting for transfers between devices, across(): return lax.ppermute(value, 'space', [(0, 1), (1, 0)])  1.52 us
  transfers between devices with their start and end apart: 19, of which 7 were waited for; matrix products, arithmetic and copies ran while one was open for 0% of the time, Pallas kernels for 34%

profile of v6, /device:TPU:0, one launch (start us, length us, event | category | flops | bytes accessed | tf_op | source)
XLA Modules:
  0.0 64.8 jit_solution(12433394885122561305)
XLA Ops:
  0.6 1.1 %shard_map.84 = (bf16[512,256]{1,0:T(8,128)(2,1)S(1)}, bf16[512,256]{1,0:T(8,128)(2,1)S(1)}) custom-call(bf16[512,256]{1,0:T(8,128)(2,1)} %a.2, bf16[512,256]{1,0:T(8,128)(2,1)} %b.2), custom_call_target="tpu_custom_call" | custom-call | flops 1024 | bytes 1024 | tf_op jit(solution)/shard_map/pallas_call | solution.py:38
  2.3 1.1 %shard_map.85 = (bf16[512,256]{1,0:T(8,128)(2,1)S(1)}, bf16[512,256]{1,0:T(8,128)(2,1)S(1)}) custom-call(bf16[512,256]{1,0:T(8,128)(2,1)} %a.3, bf16[512,256]{1,0:T(8,128)(2,1)} %b.3), custom_call_target="tpu_custom_call" | custom-call | flops 1024 | bytes 1024 | tf_op jit(solution)/shard_map/pallas_call | solution.py:38
  3.7 0.7 %collective-permute-start.2 = (bf16[1024,128]{1,0:T(8,128)(2,1)S(1)}, bf16[1024,128]{1,0:T(8,128)(2,1)S(1)}, u32[]{:S(2)}, u32[]{:S(2)}) collective-permute-start(bf16[1024,128]{1,0:T(8,128)(2,1)S(1)} %get-tuple-element.68), channel_id=1, source_target_pairs={{0,0},{2,2},{4,8},{6,10},{8,4},{10,6},{12,12},{14,14},{1,1},{3,3},... | collective-permute-start | bytes 786440 | tf_op jit(solution)/shard_map/ppermute | solution.py:530
  4.3 3.0 %collective-permute-start.5 = (bf16[1024,256]{1,0:T(8,128)(2,1)S(1)}, bf16[1024,256]{1,0:T(8,128)(2,1)S(1)}, u32[]{:S(2)}, u32[]{:S(2)}) collective-permute-start(bf16[1024,256]{1,0:T(8,128)(2,1)S(1)} %get-tuple-element.72.kv), channel_id=1, source_target_pairs={{0,2},{2,0},{4,6},{6,4},{8,10},{10,8},{12,14},{14,12},{1,3},{3,1},... | collective-permute-start | bytes 1572872 | tf_op jit(solution)/shard_map/ppermute | solution.py:530
  7.4 4.4 %collective-permute-start.6 = (bf16[1024,128]{1,0:T(8,128)(2,1)S(1)}, bf16[1024,128]{1,0:T(8,128)(2,1)S(1)}, u32[]{:S(2)}, u32[]{:S(2)}) collective-permute-start(bf16[1024,128]{1,0:T(8,128)(2,1)S(1)} %get-tuple-element.68), channel_id=1, source_target_pairs={{0,4},{2,6},{4,0},{6,2},{8,12},{10,14},{12,8},{14,10},{1,5},{3,7},... | collective-permute-start | bytes 786440 | tf_op jit(solution)/shard_map/ppermute | solution.py:530
  11.8 0.7 %copy-done = s32[16,8]{0,1:T(8,128)S(1)} copy-done((s32[16,8]{0,1:T(8,128)S(1)}, s32[16,8]{0,1:T(8,128)}, u32[]{:S(2)}) %copy-start) | copy-done | bytes 536
  13.2 0.7 %collective-permute-start.3 = (bf16[1024,128]{1,0:T(8,128)(2,1)S(1)}, bf16[1024,128]{1,0:T(8,128)(2,1)S(1)}, u32[]{:S(2)}, u32[]{:S(2)}) collective-permute-start(bf16[1024,128]{1,0:T(8,128)(2,1)S(1)} %get-tuple-element.71), channel_id=1, source_target_pairs={{0,0},{2,2},{4,8},{6,10},{8,4},{10,6},{12,12},{14,14},{1,1},{3,3},... | collective-permute-start | bytes 786440 | tf_op jit(solution)/shard_map/ppermute | solution.py:530
  14.0 4.9 %collective-permute-done.6.z.z_k = bf16[1024,128]{1,0:T(8,128)(2,1)S(1)} collective-permute-done((bf16[1024,128]{1,0:T(8,128)(2,1)S(1)}, bf16[1024,128]{1,0:T(8,128)(2,1)S(1)}, u32[]{:S(2)}, u32[]{:S(2)}) %collective-permute-start.6) | collective-permute-done | bytes 262176 | tf_op jit(solution)/shard_map/ppermute | solution.py:530
  19.5 1.9 %collective-permute-start.8 = (bf16[512,256]{1,0:T(8,128)(2,1)S(1)}, bf16[512,256]{1,0:T(8,128)(2,1)S(1)}, u32[]{:S(2)}, u32[]{:S(2)}) collective-permute-start(bf16[512,256]{1,0:T(8,128)(2,1)S(1)} %shard_map.89), channel_id=1, source_target_pairs={{0,8},{2,10},{4,12},{6,14},{8,0},{10,2},{12,4},{14,6},{1,9},{3,11}... | collective-permute-start | bytes 786440 | tf_op jit(solution)/shard_map/ppermute | solution.py:530
  21.5 3.5 %shard_map.90 = (f32[8,1024]{1,0:T(8,128)S(1)}, f32[128,1024]{1,0:T(8,128)S(1)}) custom-call(s32[8,16]{1,0:T(8,128)S(1)} %bitcast.2, bf16[1024,256]{1,0:T(8,128)(2,1)S(1)} %get-tuple-element.70.qg.refs_1_, bf16[1024,256]{1,0:T(8,128)(2,1)S(1)} %get-tuple-element.72.kv, bf16[1024,256]{1,0:T(8,128)(2,1)S(1)} %collective-permute-done.5.a_kv), custom_call_target="tpu_custom_call" | custom-call | flops 1024 | bytes 1024 | tf_op jit(solution)/shard_map/pallas_call | solution.py:38
  25.2 1.6 %collective-permute-start.9 = (bf16[1024,128]{1,0:T(8,128)(2,1)S(1)}, bf16[1024,128]{1,0:T(8,128)(2,1)S(1)}, u32[]{:S(2)}, u32[]{:S(2)}) collective-permute-start(bf16[1024,128]{1,0:T(8,128)(2,1)S(1)} %shard_map.91), channel_id=1, source_target_pairs={{0,2},{2,0},{4,6},{6,4},{8,10},{10,8},{12,14},{14,12},{1,3},{3,1},... | collective-permute-start | bytes 786440 | tf_op jit(solution)/shard_map/ppermute | solution.py:530
  26.8 1.9 %shard_map.92 = (f32[8,1024]{1,0:T(8,128)S(1)}, f32[128,1024]{1,0:T(8,128)S(1)}) custom-call(s32[8,16]{1,0:T(8,128)S(1)} %bitcast.3, bf16[1024,256]{1,0:T(8,128)(2,1)S(1)} %get-tuple-element.70.qg.refs_1_, f32[8,1024]{1,0:T(8,128)S(1)} %get-tuple-element.83.stat, f32[128,1024]{1,0:T(8,128)S(1)} %get-tuple-element.84.acc, ...), custom_call_target="tpu_custom_call" | custom-call | flops 1024 | bytes 1024 | tf_op jit(solution)/shard_map/pallas_call | solution.py:38
  28.7 1.4 %shard_map.93 = (f32[8,1024]{1,0:T(8,128)S(1)}, f32[128,1024]{1,0:T(8,128)S(1)}, f32[2,512,512]{2,1,0:T(8,128)S(1)}) custom-call(s32[8,16]{1,0:T(8,128)S(1)} %bitcast.4, bf16[1024,256]{1,0:T(8,128)(2,1)S(1)} %get-tuple-element.70.qg.refs_1_, f32[8,1024]{1,0:T(8,128)S(1)} %get-tuple-element.85.stat, f32[128,1024]{1,0:T(8,128)S(1)} %get-tuple-element.86.acc, ...), custom_call_target="tpu_custom_call" | custom-call | flops 1024 | bytes 1024 | tf_op jit(solution)/shard_map/pallas_call | solution.py:38
  30.1 4.8 %collective-permute-done.8.refs_0_.refs_8_ = bf16[512,256]{1,0:T(8,128)(2,1)S(1)} collective-permute-done((bf16[512,256]{1,0:T(8,128)(2,1)S(1)}, bf16[512,256]{1,0:T(8,128)(2,1)S(1)}, u32[]{:S(2)}, u32[]{:S(2)}) %collective-permute-start.8) | collective-permute-done | bytes 262176 | tf_op jit(solution)/shard_map/ppermute | solution.py:530
  34.9 1.0 %shard_map.94 = (f32[8,1024]{1,0:T(8,128)S(1)}, f32[128,1024]{1,0:T(8,128)S(1)}, bf16[512,128]{1,0:T(8,128)(2,1)S(1)}) custom-call(bf16[1024,256]{1,0:T(8,128)(2,1)S(1)} %get-tuple-element.70.qg.refs_1_, f32[8,1024]{1,0:T(8,128)S(1)} %get-tuple-element.87.stat, f32[128,1024]{1,0:T(8,128)S(1)} %get-tuple-element.90.acc, ...), custom_call_target="tpu_custom_call" | custom-call | flops 1024 | bytes 1024 | tf_op jit(solution)/shard_map/pallas_call | solution.py:38
  35.9 1.1 %shard_map.95 = (bf16[1024,128]{1,0:T(8,128)(2,1)S(1)}, f32[2,512,512]{2,1,0:T(8,128)S(1)}) custom-call(s32[8,16]{1,0:T(8,128)S(1)} %bitcast.5, bf16[1024,256]{1,0:T(8,128)(2,1)S(1)} %get-tuple-element.70.qg.refs_1_, f32[8,1024]{1,0:T(8,128)S(1)} %get-tuple-element.92.lse_ref.refs_3_, f32[2,512,512]{2,1,0:T(8,128)S(1)} %get-tuple-element.95.s_ref), custom_call_target="tpu_custom_call" | custom-call | flops 1024 | bytes 1024 | tf_op jit(solution)/shard_map/pallas_call | solution.py:38
  37.6 2.0 %collective-permute-start.11 = (bf16[512,128]{1,0:T(8,128)(2,1)S(1)}, bf16[512,128]{1,0:T(8,128)(2,1)S(1)}, u32[]{:S(2)}, u32[]{:S(2)}) collective-permute-start(bf16[512,128]{1,0:T(8,128)(2,1)S(1)} %get-tuple-element.102), channel_id=1, source_target_pairs={{0,8},{2,10},{4,12},{6,14},{8,0},{10,2},{12,4},{14,6},{1,9},{3,11}... | collective-permute-start | bytes 393224 | tf_op jit(solution)/shard_map/ppermute | solution.py:530
  39.7 2.3 %shard_map.96 = (bf16[128,1024]{1,0:T(8,128)(2,1)S(1)}, f32[8,1024]{1,0:T(8,128)S(1)}, bf16[1024,128]{1,0:T(8,128)(2,1)S(1)}, f32[128,1024]{1,0:T(8,128)S(1)}, bf16[512,128]{1,0:T(8,128)(2,1)S(1)}) custom-call(s32[8,16]{1,0:T(8,128)S(1)} %bitcast.6, bf16[1024,256]{1,0:T(8,128)(2,1)S(1)} %get-tuple-element.70.qg.refs_1_, ...), custom_call_target="tpu_custom_call" | custom-call | flops 1024 | bytes 1024 | tf_op jit(solution)/shard_map/pallas_call | solution.py:38
  42.5 1.9 %collective-permute-start.13 = (bf16[512,128]{1,0:T(8,128)(2,1)S(1)}, bf16[512,128]{1,0:T(8,128)(2,1)S(1)}, u32[]{:S(2)}, u32[]{:S(2)}) collective-permute-start(bf16[512,128]{1,0:T(8,128)(2,1)S(1)} %get-tuple-element.112), channel_id=1, source_target_pairs={{0,8},{2,10},{4,12},{6,14},{8,0},{10,2},{12,4},{14,6},{1,9},{3,11}... | collective-permute-start | bytes 393224 | tf_op jit(solution)/shard_map/ppermute | solution.py:530
  44.4 2.2 %shard_map.97 = (bf16[1024,256]{1,0:T(8,128)(2,1)S(1)}, f32[128,1024]{1,0:T(8,128)S(1)}) custom-call(s32[8,16]{1,0:T(8,128)S(1)} %bitcast.7, bf16[1024,256]{1,0:T(8,128)(2,1)S(1)} %get-tuple-element.70.qg.refs_1_, f32[8,1024]{1,0:T(8,128)S(1)} %get-tuple-element.92.lse_ref.refs_3_, f32[8,1024]{1,0:T(8,128)S(1)} %get-tuple-element.98.dot_ref, ...), custom_call_target="tpu_custom_call" | custom-call | flops 1024 | bytes 1024 | tf_op jit(solution)/shard_map/pallas_call | solution.py:38
  46.7 0.8 %collective-permute-done.11.refs_2_ = bf16[512,128]{1,0:T(8,128)(2,1)S(1)} collective-permute-done((bf16[512,128]{1,0:T(8,128)(2,1)S(1)}, bf16[512,128]{1,0:T(8,128)(2,1)S(1)}, u32[]{:S(2)}, u32[]{:S(2)}) %collective-permute-start.11) | collective-permute-done | bytes 131104 | tf_op jit(solution)/shard_map/ppermute | solution.py:530
  47.4 1.1 %collective-permute-start.15 = (bf16[1024,256]{1,0:T(8,128)(2,1)S(1)}, bf16[1024,256]{1,0:T(8,128)(2,1)S(1)}, u32[]{:S(2)}, u32[]{:S(2)}) collective-permute-start(bf16[1024,256]{1,0:T(8,128)(2,1)S(1)} %get-tuple-element.117), channel_id=1, source_target_pairs={{0,2},{2,0},{4,6},{6,4},{8,10},{10,8},{12,14},{14,12},{1,3},{3,1},... | collective-permute-start | bytes 1572872 | tf_op jit(solution)/shard_map/ppermute | solution.py:530
  48.6 2.2 %shard_map.98 = (f32[1024,256]{1,0:T(8,128)S(1)}, f32[1024,256]{1,0:T(8,128)S(1)}, f32[128,1024]{1,0:T(8,128)S(1)}) custom-call(s32[8,16]{1,0:T(8,128)S(1)} %bitcast.8, bf16[1024,256]{1,0:T(8,128)(2,1)S(1)} %get-tuple-element.70.qg.refs_1_, f32[8,1024]{1,0:T(8,128)S(1)} %get-tuple-element.92.lse_ref.refs_3_, f32[8,1024]{1,0:T(8,128)S(1)} %get-tuple-element.98.dot_ref, ...), custom_call_target="tpu_custom_call" | custom-call | flops 2684354560 | bytes 1024 | tf_op jit(solution)/shard_map/pallas_call | solution.py:38
  50.8 0.7 %collective-permute-done.12.came = bf16[1024,128]{1,0:T(8,128)(2,1)S(1)} collective-permute-done((bf16[1024,128]{1,0:T(8,128)(2,1)S(1)}, bf16[1024,128]{1,0:T(8,128)(2,1)S(1)}, u32[]{:S(2)}, u32[]{:S(2)}) %collective-permute-start.12) | collective-permute-done | bytes 262176 | tf_op jit(solution)/shard_map/ppermute | solution.py:530
  51.8 1.2 %collective-permute-start.16 = (bf16[1024,256]{1,0:T(8,128)(2,1)S(1)}, bf16[1024,256]{1,0:T(8,128)(2,1)S(1)}, u32[]{:S(2)}, u32[]{:S(2)}) collective-permute-start(bf16[1024,256]{1,0:T(8,128)(2,1)S(1)} %get-tuple-element.108), channel_id=1, source_target_pairs={{0,4},{2,6},{4,0},{6,2},{8,12},{10,14},{12,8},{14,10},{1,5},{3,7},... | collective-permute-start | bytes 1572872 | tf_op jit(solution)/shard_map/ppermute | solution.py:530
  52.9 0.7 %collective-permute-start.17 = (bf16[1024,256]{1,0:T(8,128)(2,1)S(1)}, bf16[1024,256]{1,0:T(8,128)(2,1)S(1)}, u32[]{:S(2)}, u32[]{:S(2)}) collective-permute-start(bf16[1024,256]{1,0:T(8,128)(2,1)S(1)} %get-tuple-element.109), channel_id=1, source_target_pairs={{0,0},{2,2},{4,8},{6,10},{8,4},{10,6},{12,12},{14,14},{1,1},{3,3},... | collective-permute-start | bytes 1572872 | tf_op jit(solution)/shard_map/ppermute | solution.py:530
  53.6 0.7 %shard_map.100.placed = f32[1024,256]{1,0:T(8,128)S(1)} custom-call(s32[8,16]{1,0:T(8,128)S(1)} %bitcast.9, bf16[512,128]{1,0:T(8,128)(2,1)S(1)} %collective-permute-done.13.refs_1_, bf16[512,128]{1,0:T(8,128)(2,1)S(1)} %collective-permute-done.11.refs_2_), custom_call_target="tpu_custom_call" | custom-call | flops 1024 | bytes 1024 | tf_op jit(solution)/shard_map/pallas_call | solution.py:38
  54.4 3.2 %shard_map.101 = (f32[1024,256]{1,0:T(8,128)S(1)}, bf16[512,256]{1,0:T(8,128)(2,1)S(1)}, bf16[512,256]{1,0:T(8,128)(2,1)S(1)}) custom-call(bf16[1024,256]{1,0:T(8,128)(2,1)S(1)} %get-tuple-element.70.qg.refs_1_, f32[8,1024]{1,0:T(8,128)S(1)} %get-tuple-element.92.lse_ref.refs_3_, f32[8,1024]{1,0:T(8,128)S(1)} %get-tuple-element.98.dot_ref, ...), custom_call_target="tpu_custom_call" | custom-call | flops 5368709120 | bytes 1024 | tf_op jit(solution)/shard_map/pallas_call | solution.py:38
  57.6 2.5 %collective-permute-done.15.da = bf16[1024,256]{1,0:T(8,128)(2,1)S(1)} collective-permute-done((bf16[1024,256]{1,0:T(8,128)(2,1)S(1)}, bf16[1024,256]{1,0:T(8,128)(2,1)S(1)}, u32[]{:S(2)}, u32[]{:S(2)}) %collective-permute-start.15) | collective-permute-done | bytes 524320 | tf_op jit(solution)/shard_map/ppermute | solution.py:530
  60.2 1.6 %collective-permute-done.16.dz = bf16[1024,256]{1,0:T(8,128)(2,1)S(1)} collective-permute-done((bf16[1024,256]{1,0:T(8,128)(2,1)S(1)}, bf16[1024,256]{1,0:T(8,128)(2,1)S(1)}, u32[]{:S(2)}, u32[]{:S(2)}) %collective-permute-start.16) | collective-permute-done | bytes 524320 | tf_op jit(solution)/shard_map/ppermute | solution.py:530
  62.2 1.5 %collective-permute-done.18.k_came = bf16[512,256]{1,0:T(8,128)(2,1)S(1)} collective-permute-done((bf16[512,256]{1,0:T(8,128)(2,1)S(1)}, bf16[512,256]{1,0:T(8,128)(2,1)S(1)}, u32[]{:S(2)}, u32[]{:S(2)}) %collective-permute-start.18) | collective-permute-done | bytes 262176 | tf_op jit(solution)/shard_map/ppermute | solution.py:527
  63.7 1.1 %shard_map.103 = (bf16[512,256]{1,0:T(8,128)(2,1)}, bf16[512,256]{1,0:T(8,128)(2,1)}, bf16[512,256]{1,0:T(8,128)(2,1)}, bf16[512,256]{1,0:T(8,128)(2,1)}) custom-call(bf16[512,256]{1,0:T(8,128)(2,1)S(1)} %get-tuple-element.114.q_keep, bf16[512,256]{1,0:T(8,128)(2,1)S(1)} %collective-permute-done.14.q_came, bf16[512,256]{1,0:T(8,128)(2,1)S(1)} %get-tuple-element.118.k_keep, ...), custom_call_target="tpu_custom_call" | custom-call | flops 1024 | bytes 1024 | tf_op jit(solution)/shard_map/pallas_call | solution.py:38
  (30 shorter events, 4.3 us)
Async XLA Ops:
  1.8 1.8 %collective-permute-start = (bf16[512,256]{1,0:T(8,128)(2,1)S(1)}, bf16[512,256]{1,0:T(8,128)(2,1)S(1)}, u32[]{:S(2)}, u32[]{:S(2)}) collective-permute-start(bf16[512,256]{1,0:T(8,128)(2,1)S(1)} %get-tuple-element.62), channel_id=1, source_target_pairs={{0,1},{1,0},{2,3},{3,2},{4,5},{5,4},{6,7},{7,6},{8,9},{9,8},{10,11... | collective-permute-start | bytes 786440 | tf_op jit(solution)/shard_map/ppermute | solution.py:527
  3.4 9.8 %collective-permute-start.1 = (bf16[512,256]{1,0:T(8,128)(2,1)S(1)}, bf16[512,256]{1,0:T(8,128)(2,1)S(1)}, u32[]{:S(2)}, u32[]{:S(2)}) collective-permute-start(bf16[512,256]{1,0:T(8,128)(2,1)S(1)} %get-tuple-element.65), channel_id=1, source_target_pairs={{0,1},{1,0},{2,3},{3,2},{4,5},{5,4},{6,7},{7,6},{8,9},{9,8},{10,11... | collective-permute-start | bytes 786440 | tf_op jit(solution)/shard_map/ppermute | solution.py:527
  3.7 10.2 %collective-permute-start.2 = (bf16[1024,128]{1,0:T(8,128)(2,1)S(1)}, bf16[1024,128]{1,0:T(8,128)(2,1)S(1)}, u32[]{:S(2)}, u32[]{:S(2)}) collective-permute-start(bf16[1024,128]{1,0:T(8,128)(2,1)S(1)} %get-tuple-element.68), channel_id=1, source_target_pairs={{0,0},{2,2},{4,8},{6,10},{8,4},{10,6},{12,12},{14,14},{1,1},{3,3},... | collective-permute-start | bytes 786440 | tf_op jit(solution)/shard_map/ppermute | solution.py:530
  4.3 17.1 %collective-permute-start.5 = (bf16[1024,256]{1,0:T(8,128)(2,1)S(1)}, bf16[1024,256]{1,0:T(8,128)(2,1)S(1)}, u32[]{:S(2)}, u32[]{:S(2)}) collective-permute-start(bf16[1024,256]{1,0:T(8,128)(2,1)S(1)} %get-tuple-element.72.kv), channel_id=1, source_target_pairs={{0,2},{2,0},{4,6},{6,4},{8,10},{10,8},{12,14},{14,12},{1,3},{3,1},... | collective-permute-start | bytes 1572872 | tf_op jit(solution)/shard_map/ppermute | solution.py:530
  7.4 11.6 %collective-permute-start.6 = (bf16[1024,128]{1,0:T(8,128)(2,1)S(1)}, bf16[1024,128]{1,0:T(8,128)(2,1)S(1)}, u32[]{:S(2)}, u32[]{:S(2)}) collective-permute-start(bf16[1024,128]{1,0:T(8,128)(2,1)S(1)} %get-tuple-element.68), channel_id=1, source_target_pairs={{0,4},{2,6},{4,0},{6,2},{8,12},{10,14},{12,8},{14,10},{1,5},{3,7},... | collective-permute-start | bytes 786440 | tf_op jit(solution)/shard_map/ppermute | solution.py:530
  11.8 0.7 %copy-start = (s32[16,8]{0,1:T(8,128)S(1)}, s32[16,8]{0,1:T(8,128)}, u32[]{:S(2)}) copy-start(s32[16,8]{0,1:T(8,128)} %param.9) | copy-start | bytes 1540
  13.1 8.4 %copy-start.1 = (s32[16,8]{0,1:T(8,128)S(1)}, s32[16,8]{0,1:T(8,128)}, u32[]{:S(2)}) copy-start(s32[16,8]{0,1:T(8,128)} %param.9) | copy-start | bytes 1540
  13.1 11.9 %collective-permute-start.4 = (bf16[1024,128]{1,0:T(8,128)(2,1)S(1)}, bf16[1024,128]{1,0:T(8,128)(2,1)S(1)}, u32[]{:S(2)}, u32[]{:S(2)}) collective-permute-start(bf16[1024,128]{1,0:T(8,128)(2,1)S(1)} %get-tuple-element.71), channel_id=1, source_target_pairs={{0,4},{2,6},{4,0},{6,2},{8,12},{10,14},{12,8},{14,10},{1,5},{3,7},... | collective-permute-start | bytes 786440 | tf_op jit(solution)/shard_map/ppermute | solution.py:530
  13.2 11.8 %collective-permute-start.3 = (bf16[1024,128]{1,0:T(8,128)(2,1)S(1)}, bf16[1024,128]{1,0:T(8,128)(2,1)S(1)}, u32[]{:S(2)}, u32[]{:S(2)}) collective-permute-start(bf16[1024,128]{1,0:T(8,128)(2,1)S(1)} %get-tuple-element.71), channel_id=1, source_target_pairs={{0,0},{2,2},{4,8},{6,10},{8,4},{10,6},{12,12},{14,14},{1,1},{3,3},... | collective-permute-start | bytes 786440 | tf_op jit(solution)/shard_map/ppermute | solution.py:530
  19.0 9.7 %collective-permute-start.7 = (bf16[1024,128]{1,0:T(8,128)(2,1)S(1)}, bf16[1024,128]{1,0:T(8,128)(2,1)S(1)}, u32[]{:S(2)}, u32[]{:S(2)}) collective-permute-start(bf16[1024,128]{1,0:T(8,128)(2,1)S(1)} %shard_map.88), channel_id=1, source_target_pairs={{0,2},{2,0},{4,6},{6,4},{8,10},{10,8},{12,14},{14,12},{1,3},{3,1},... | collective-permute-start | bytes 786440 | tf_op jit(solution)/shard_map/ppermute | solution.py:530
  19.5 15.3 %collective-permute-start.8 = (bf16[512,256]{1,0:T(8,128)(2,1)S(1)}, bf16[512,256]{1,0:T(8,128)(2,1)S(1)}, u32[]{:S(2)}, u32[]{:S(2)}) collective-permute-start(bf16[512,256]{1,0:T(8,128)(2,1)S(1)} %shard_map.89), channel_id=1, source_target_pairs={{0,8},{2,10},{4,12},{6,14},{8,0},{10,2},{12,4},{14,6},{1,9},{3,11}... | collective-permute-start | bytes 786440 | tf_op jit(solution)/shard_map/ppermute | solution.py:530
  25.2 14.4 %collective-permute-start.9 = (bf16[1024,128]{1,0:T(8,128)(2,1)S(1)}, bf16[1024,128]{1,0:T(8,128)(2,1)S(1)}, u32[]{:S(2)}, u32[]{:S(2)}) collective-permute-start(bf16[1024,128]{1,0:T(8,128)(2,1)S(1)} %shard_map.91), channel_id=1, source_target_pairs={{0,2},{2,0},{4,6},{6,4},{8,10},{10,8},{12,14},{14,12},{1,3},{3,1},... | collective-permute-start | bytes 786440 | tf_op jit(solution)/shard_map/ppermute | solution.py:530
  37.0 10.4 %collective-permute-start.10 = (bf16[1024,128]{1,0:T(8,128)(2,1)S(1)}, bf16[1024,128]{1,0:T(8,128)(2,1)S(1)}, u32[]{:S(2)}, u32[]{:S(2)}) collective-permute-start(bf16[1024,128]{1,0:T(8,128)(2,1)S(1)} %get-tuple-element.101), channel_id=1, source_target_pairs={{0,2},{2,0},{4,6},{6,4},{8,10},{10,8},{12,14},{14,12},{1,3},{3,1},... | collective-permute-start | bytes 786440 | tf_op jit(solution)/shard_map/ppermute | solution.py:530
  37.6 9.8 %collective-permute-start.11 = (bf16[512,128]{1,0:T(8,128)(2,1)S(1)}, bf16[512,128]{1,0:T(8,128)(2,1)S(1)}, u32[]{:S(2)}, u32[]{:S(2)}) collective-permute-start(bf16[512,128]{1,0:T(8,128)(2,1)S(1)} %get-tuple-element.102), channel_id=1, source_target_pairs={{0,8},{2,10},{4,12},{6,14},{8,0},{10,2},{12,4},{14,6},{1,9},{3,11}... | collective-permute-start | bytes 393224 | tf_op jit(solution)/shard_map/ppermute | solution.py:530
  41.9 9.6 %collective-permute-start.12 = (bf16[1024,128]{1,0:T(8,128)(2,1)S(1)}, bf16[1024,128]{1,0:T(8,128)(2,1)S(1)}, u32[]{:S(2)}, u32[]{:S(2)}) collective-permute-start(bf16[1024,128]{1,0:T(8,128)(2,1)S(1)} %get-tuple-element.107), channel_id=1, source_target_pairs={{0,2},{2,0},{4,6},{6,4},{8,10},{10,8},{12,14},{14,12},{1,3},{3,1},... | collective-permute-start | bytes 786440 | tf_op jit(solution)/shard_map/ppermute | solution.py:530
  42.5 11.1 %collective-permute-start.13 = (bf16[512,128]{1,0:T(8,128)(2,1)S(1)}, bf16[512,128]{1,0:T(8,128)(2,1)S(1)}, u32[]{:S(2)}, u32[]{:S(2)}) collective-permute-start(bf16[512,128]{1,0:T(8,128)(2,1)S(1)} %get-tuple-element.112), channel_id=1, source_target_pairs={{0,8},{2,10},{4,12},{6,14},{8,0},{10,2},{12,4},{14,6},{1,9},{3,11}... | collective-permute-start | bytes 393224 | tf_op jit(solution)/shard_map/ppermute | solution.py:530
  47.4 12.7 %collective-permute-start.15 = (bf16[1024,256]{1,0:T(8,128)(2,1)S(1)}, bf16[1024,256]{1,0:T(8,128)(2,1)S(1)}, u32[]{:S(2)}, u32[]{:S(2)}) collective-permute-start(bf16[1024,256]{1,0:T(8,128)(2,1)S(1)} %get-tuple-element.117), channel_id=1, source_target_pairs={{0,2},{2,0},{4,6},{6,4},{8,10},{10,8},{12,14},{14,12},{1,3},{3,1},... | collective-permute-start | bytes 1572872 | tf_op jit(solution)/shard_map/ppermute | solution.py:530
  51.8 10.0 %collective-permute-start.16 = (bf16[1024,256]{1,0:T(8,128)(2,1)S(1)}, bf16[1024,256]{1,0:T(8,128)(2,1)S(1)}, u32[]{:S(2)}, u32[]{:S(2)}) collective-permute-start(bf16[1024,256]{1,0:T(8,128)(2,1)S(1)} %get-tuple-element.108), channel_id=1, source_target_pairs={{0,4},{2,6},{4,0},{6,2},{8,12},{10,14},{12,8},{14,10},{1,5},{3,7},... | collective-permute-start | bytes 1572872 | tf_op jit(solution)/shard_map/ppermute | solution.py:530
  52.9 8.8 %collective-permute-start.17 = (bf16[1024,256]{1,0:T(8,128)(2,1)S(1)}, bf16[1024,256]{1,0:T(8,128)(2,1)S(1)}, u32[]{:S(2)}, u32[]{:S(2)}) collective-permute-start(bf16[1024,256]{1,0:T(8,128)(2,1)S(1)} %get-tuple-element.109), channel_id=1, source_target_pairs={{0,0},{2,2},{4,8},{6,10},{8,4},{10,6},{12,12},{14,14},{1,1},{3,3},... | collective-permute-start | bytes 1572872 | tf_op jit(solution)/shard_map/ppermute | solution.py:530
  57.5 4.6 %collective-permute-start.14 = (bf16[512,256]{1,0:T(8,128)(2,1)S(1)}, bf16[512,256]{1,0:T(8,128)(2,1)S(1)}, u32[]{:S(2)}, u32[]{:S(2)}) collective-permute-start(bf16[512,256]{1,0:T(8,128)(2,1)S(1)} %get-tuple-element.115), channel_id=1, source_target_pairs={{0,1},{1,0},{2,3},{3,2},{4,5},{5,4},{6,7},{7,6},{8,9},{9,8},{10,11... | collective-permute-start | bytes 786440 | tf_op jit(solution)/shard_map/ppermute | solution.py:527
  62.1 1.6 %collective-permute-start.18 = (bf16[512,256]{1,0:T(8,128)(2,1)S(1)}, bf16[512,256]{1,0:T(8,128)(2,1)S(1)}, u32[]{:S(2)}, u32[]{:S(2)}) collective-permute-start(bf16[512,256]{1,0:T(8,128)(2,1)S(1)} %get-tuple-element.119), channel_id=1, source_target_pairs={{0,1},{1,0},{2,3},{3,2},{4,5},{5,4},{6,7},{7,6},{8,9},{9,8},{10,11... | collective-permute-start | bytes 786440 | tf_op jit(solution)/shard_map/ppermute | solution.py:527

commit v7 on v6

--- a/solution.py
+++ b/solution.py
@@ -34,11 +34,11 @@
     return lax.dot_general(a, b, (((0,), (0,)), ((), ())), preferred_element_type=F32)
 
 
-def call(kernel, args, out_shape, scratch=(), source=VMEM, flops=1024):
+def call(kernel, args, out_shape, scratch=(), source=VMEM, scalars=SMEM, flops=1024):
     return pl.pallas_call(
         kernel,
         out_shape=out_shape,
-        in_specs=[SMEM if a.dtype == jnp.int32 else source for a in args],
+        in_specs=[scalars if a.dtype == jnp.int32 else source for a in args],
         out_specs=tuple(VMEM for _ in out_shape),
         scratch_shapes=list(scratch),
         compiler_params=pltpu.CompilerParams(vmem_limit_bytes=40 << 20),
@@ -98,9 +98,15 @@
         pl.when(core == mine)(functools.partial(body, mine))
 
 
-def pack_kernel(a, b, send, own, sems):
+def pack_kernel(a, b, *refs):
+    *extra, sems = refs
+    n = (len(extra) - 2) // 2
+    send, own = extra[n : n + 2]
+
     def body(mine):
         copies = []
+        for source, out in zip(extra[:n], extra[n + 2 :]):
+            copies.append(pltpu.make_async_copy(source, out, sems.at[len(copies)]))
         for head, out in ((1 - mine, send), (mine, own)):
             for source, cols in ((a, KEY), (b, VALUE)):
                 sem = sems.at[len(copies)]
@@ -306,27 +312,21 @@
         store_state((stat, acc), rows, *forward_slab(qg[rows, KEY], groups, 3, s_ref, None))
 
 
-def middle_kernel(block, swaps, lists, qg, stat, acc, y_k, z_k, y_v, z_v, stat2, acc2, s_ref):
-    half = qg.shape[0] // 2
-    frame = lax.axis_index("tm")
-    z, y = swaps
+def middle_kernel(
+    block, swaps, lists, qg, stat, acc, y_k, z_k, y_v, z_v, c_k, stat2, acc2, late, s_ref
+):
+    half = qg.shape[0] // 2
+    frame = lax.axis_index("tm")
+    z, y, relayed = swaps
     for slab in range(2):
         rows = rows_of(slab, half)
         at = (lists, frame, slab, block)
         group = listed(z, *at, (z_k, ALL), (z_v, ALL)) + listed(y, *at, (y_k, ALL), (y_v, ALL))
+        more = listed(relayed, *at, (c_k, ALL), None, 2)
         old = load_state((stat, acc), rows)
-        store_state((stat2, acc2), rows, *forward_slab(qg[rows, KEY], [group], 1, s_ref, old))
-
-
-def relayed_kernel(block, relayed, lists, qg, stat, acc, c_k, stat2, acc2, s_ref):
-    half = qg.shape[0] // 2
-    frame = lax.axis_index("tm")
-    for slab in range(2):
-        rows = rows_of(slab, half)
-        group = listed(relayed, lists, frame, slab, block, (c_k, ALL), None, 2)
-        old = load_state((stat, acc), rows)
-        new = forward_slab(qg[rows, KEY], [group], 0, s_ref.at[slab], old)
+        new = forward_slab(qg[rows, KEY], [group, more], 1, s_ref, old)
         store_state((stat2, acc2), rows, *new)
+        late[slab] = s_ref[2 * block :, :]
 
 
 def close_kernel(block, far, qg, stat, acc, *refs):
@@ -476,28 +476,33 @@
                 total[rows, cols] += jnp.where(exists, part, 0.0)
 
 
-def gather_kernel(swaps, near, da, dz, dy, keep, send):
-    frame = lax.axis_index("tm")
+def add_kernel(swaps, near, *refs):
+    frame = lax.axis_index("tm")
+    total = near[...]
+    for swap, came in zip(swaps, refs[:-1]):
+        _, _, exists = swap.partner(frame)
+        total = total + jnp.where(exists, came[...].astype(F32), 0.0)
+    refs[-1][...] = total
+
+
+def gather_kernel(swap, near, came, keep, send):
+    _, _, exists = swap.partner(lax.axis_index("tm"))
     half = near.shape[0] // 2
-    there = [swap.partner(frame)[2] for swap in swaps]
 
     def body(mine):
         for slab, out in ((1 - mine, send), (mine, keep)):
             rows = rows_of(slab, half)
-            total = near[rows, :]
-            for exists, part in zip(there, (da, dz, dy)):
-                total = total + jnp.where(exists, part[rows, :].astype(F32), 0.0)
-            out[...] = total.astype(BF16)
+            part = jnp.where(exists, came[rows, :].astype(F32), 0.0)
+            out[...] = (near[rows, :] + part).astype(BF16)
 
     each_core(body)
 
 
-def finish_kernel(q_keep, q_came, k_keep, k_came, *outs):
+def finish_kernel(keep, came, first, second):
     def body(mine):
-        for head, sources in ((mine, (q_keep, k_keep)), (1 - mine, (q_came, k_came))):
-            for source, first, second in zip(sources, outs[::2], outs[1::2]):
-                first[:, head_cols(head)] = source[:, KEY]
-                second[:, head_cols(head)] = source[:, VALUE]
+        for head, source in ((mine, keep), (1 - mine, came)):
+            first[:, head_cols(head)] = source[:, KEY]
+            second[:, head_cols(head)] = source[:, VALUE]
 
     each_core(body)
 
@@ -517,7 +522,6 @@
     levels = count.bit_length() - 1
     near_swap, relayed = Swap(count, 0, False), Swap(count, 0, True)
     z_swap, y_swap = Swap(count, 1, False), Swap(count, 1, True)
-    swaps = (near_swap, z_swap, y_swap)
     far = [Swap(count, level, second) for level in range(2, levels) for second in (False, True)]
     far = [swap for swap in far if swap.moves]
     n = len(far)
@@ -532,34 +536,36 @@
     def scores(pieces):
         return pltpu.VMEM((pieces * block, s_dev), F32)
 
-    lists = block_lists.T
-
-    def packed(*pair_in):
+
+    def packed(*arrays):
         return call(
             pack_kernel,
-            tuple(pltpu.with_memory_space_constraint(a, pltpu.HBM) for a in pair_in),
-            [pair] * 2,
-            scratch=[pltpu.SemaphoreType.DMA((4,))],
+            tuple(pltpu.with_memory_space_constraint(a, pltpu.HBM) for a in arrays),
+            [pair] * 2 + [sds(a.shape, a.dtype) for a in arrays[2:]],
+            scratch=[pltpu.SemaphoreType.DMA((2 + len(arrays),))],
             source=HBM,
+            scalars=HBM,
         )
 
     kv_send, kv_own = packed(key_rows, value_rows)
     kv_came = across(kv_send)
-    qg_send, qg_own = packed(queries, out_grad)
+    qg_send, qg_own, lists = packed(queries, out_grad, block_lists.T)
     kv_came, qg_own = lax.optimization_barrier((kv_came, qg_own))
     kv, keys, values = call(
         frame_kernel, (kv_own, kv_came), [frame_two, frame_one, frame_one]
     )
+    qg_send, keys = lax.optimization_barrier((qg_send, keys))
     y_k = swapped(keys, y_swap)
     z_k = swapped(keys, z_swap)
     a_kv = swapped(kv, near_swap)
     y_v = swapped(values, y_swap)
     z_v = swapped(values, z_swap)
-    far_send = call(functools.partial(select_kernel, far, block), (lists, kv), [pair] * n)
-    qg_came, y_k = lax.optimization_barrier((across(qg_send), y_k))
+    y_k, qg_came = lax.optimization_barrier((y_k, across(qg_send)))
     work = 4 * s_dev * s_dev * DH
     qg, turned = call(join_kernel, (qg_own, qg_came), [frame_two, turned_bf], flops=15 * work)
     y_k, z_k, turned = lax.optimization_barrier((y_k, z_k, turned))
+    kv, _ = lax.optimization_barrier((kv, turned))
+    far_send = call(functools.partial(select_kernel, far, block), (lists, kv), [pair] * n)
     (relay_k,) = call(relay_kernel, (y_k, z_k), [frame_one])
     relay_k, far_send = lax.optimization_barrier((relay_k, far_send))
     a_kv, _ = lax.optimization_barrier((a_kv, relay_k))
@@ -571,21 +577,16 @@
         [stat_row, turned_sum],
         scratch=[scores(6)],
     )
+    score_two = sds((2, s_dev, s_dev), F32)
     y_v, z_v, stat = lax.optimization_barrier((y_v, z_v, stat))
     (relay_v,) = call(relay_kernel, (y_v, z_v), [frame_one])
     relay_v, stat = lax.optimization_barrier((relay_v, stat))
     c_v = swapped(relay_v, near_swap)
-    stat, acc = call(
-        functools.partial(middle_kernel, block, (z_swap, y_swap)),
-        (lists, qg, stat, acc, y_k, z_k, y_v, z_v),
-        [stat_row, turned_sum],
-        scratch=[scores(2)],
-    )
-    score_two = sds((2, s_dev, s_dev), F32)
     stat, acc, late_scores = call(
-        functools.partial(relayed_kernel, block, relayed),
-        (lists, qg, stat, acc, c_k),
+        functools.partial(middle_kernel, block, (z_swap, y_swap, relayed)),
+        (lists, qg, stat, acc, y_k, z_k, y_v, z_v, c_k),
         [stat_row, turned_sum, score_two],
+        scratch=[scores(4)],
     )
     acc, far_kv = lax.optimization_barrier((acc, far_kv))
     lse, part, *far_dv = call(
@@ -628,23 +629,28 @@
     dy_came = swapped(dy, y_swap)
     dz_came = swapped(dz, z_swap)
     dq, dz, dy = lax.optimization_barrier((dq, dz, dy))
+    far_dk_came, dq = lax.optimization_barrier((far_dk_came, dq))
     (placed,) = call(functools.partial(place_kernel, block, far), (lists, *far_dk_came, *far_dv_came), [frame_sum])
     near, q_keep, q_send = call(
         own_kernel,
         (qg, lse, row_dot, dq, o, kv, placed),
         [frame_sum, pair, pair],
-        flops=40 * work,
+        flops=20 * work,
+    )
+    outputs = [sds((s_dev, width), BF16)] * 2
+    attn_out, grad_q = call(finish_kernel, (q_keep, across(q_send)), outputs)
+    near, attn_out, grad_q = lax.optimization_barrier((near, attn_out, grad_q))
+    (near,) = call(
+        functools.partial(add_kernel, (near_swap, y_swap)),
+        (near, da_came, dy_came),
+        [frame_sum],
+        flops=20 * work,
     )
     k_keep, k_send = call(
-        functools.partial(gather_kernel, swaps),
-        (near, da_came, dz_came, dy_came),
-        [pair, pair],
-    )
-    return call(
-        finish_kernel,
-        (q_keep, across(q_send), k_keep, across(k_send)),
-        [sds((s_dev, width), BF16)] * 4,
-    )
+        functools.partial(gather_kernel, z_swap), (near, dz_came), [pair, pair]
+    )
+    grad_k, grad_v = call(finish_kernel, (k_keep, across(k_send)), outputs)
+    return attn_out, grad_q, grad_k, grad_v
 
 
 def solution(mesh):

time: 65.7 us -> 64.5 us (0.982); the launches traced: 64.8 us -> 64.3 us
  starting transfers between devices: 21.8 us -> 22.7 us
  waiting for transfers between devices: 16.9 us -> 16.2 us
  local copies, waits for them, and re-layouts: 0.69 us -> 0 us
    ppermute x15, waiting for transfers between devices: 15.3 us -> 13.1 us  [swapped(): return lax.ppermute(value, 'tm', swap.pairs)]
    ppermute x4, waiting for transfers between devices: 1.52 us -> 3.05 us  [across(): return lax.ppermute(value, 'space', [(0, 1), (1, 0)])]
    unnamed x4 -> x0, local copies, waits for them, and re-layouts: 0.69 us -> none
    pallas_call x20 -> x21, Pallas kernels: 24.6 us -> 24.7 us  [call(): pl.pallas_call(kernel, out_shape=out_shape, in_specs=[scalars if a.dtype...]
  transfers between devices with their start and end apart: 19 -> 19, of which waited for: 7 -> 8; matrix products, arithmetic and copies ran while one was open for 0% -> 0% of each run, Pallas kernels for 34% -> 35%
where the time goes in v7:
time: 64.5 us; the launch traced here: 64.3 us
  Pallas kernels  24.7 us (38%)
  starting transfers between devices  22.7 us (35%)
  waiting for transfers between devices  16.2 us (25%)
  between operations  0.84 us (1%)
    pallas_call x21, Pallas kernels, call(): pl.pallas_call(kernel, out_shape=out_shape, in_specs=[scalars if a.dtype...  24.7 us
    ppermute x15, starting transfers between devices, swapped(): return lax.ppermute(value, 'tm', swap.pairs)  21.6 us
    ppermute x15, waiting for transfers between devices, swapped(): return lax.ppermute(value, 'tm', swap.pairs)  13.1 us
    ppermute x4, waiting for transfers between devices, across(): return lax.ppermute(value, 'space', [(0, 1), (1, 0)])  3.05 us
  transfers between devices with their start and end apart: 19, of which 8 were waited for; matrix products, arithmetic and copies ran while one was open for 0% of the time, Pallas kernels for 35%

profile of v7, /device:TPU:0, one launch (start us, length us, event | category | flops | bytes accessed | tf_op | source)
XLA Modules:
  0.0 64.3 jit_solution(633228343390149968)
XLA Ops:
  0.6 1.1 %shard_map.84 = (bf16[512,256]{1,0:T(8,128)(2,1)S(1)}, bf16[512,256]{1,0:T(8,128)(2,1)S(1)}) custom-call(bf16[512,256]{1,0:T(8,128)(2,1)} %a.2, bf16[512,256]{1,0:T(8,128)(2,1)} %b.2), custom_call_target="tpu_custom_call" | custom-call | flops 1024 | bytes 1024 | tf_op jit(solution)/shard_map/pallas_call | solution.py:38
  2.3 1.2 %shard_map.85 = (bf16[512,256]{1,0:T(8,128)(2,1)S(1)}, bf16[512,256]{1,0:T(8,128)(2,1)S(1)}, s32[8,16]{1,0:T(8,128)S(1)}) custom-call(bf16[512,256]{1,0:T(8,128)(2,1)} %a.3, bf16[512,256]{1,0:T(8,128)(2,1)} %b.3, s32[8,16]{1,0:T(8,128)} %bitcast.1), custom_call_target="tpu_custom_call" | custom-call | flops 1024 | bytes 1024 | tf_op jit(solution)/shard_map/pallas_call | solution.py:38
  4.0 0.7 %collective-permute-start.1 = (bf16[1024,128]{1,0:T(8,128)(2,1)S(1)}, bf16[1024,128]{1,0:T(8,128)(2,1)S(1)}, u32[]{:S(2)}, u32[]{:S(2)}) collective-permute-start(bf16[1024,128]{1,0:T(8,128)(2,1)S(1)} %get-tuple-element.80), channel_id=1, source_target_pairs={{0,0},{2,2},{4,8},{6,10},{8,4},{10,6},{12,12},{14,14},{1,1},{3,3},... | collective-permute-start | bytes 786440 | tf_op jit(solution)/shard_map/ppermute | solution.py:534
  4.7 2.7 %collective-permute-start.6 = (bf16[1024,256]{1,0:T(8,128)(2,1)S(1)}, bf16[1024,256]{1,0:T(8,128)(2,1)S(1)}, u32[]{:S(2)}, u32[]{:S(2)}) collective-permute-start(bf16[1024,256]{1,0:T(8,128)(2,1)S(1)} %get-tuple-element.90.kv), channel_id=1, source_target_pairs={{0,2},{2,0},{4,6},{6,4},{8,10},{10,8},{12,14},{14,12},{1,3},{3,1},... | collective-permute-start | bytes 1572872 | tf_op jit(solution)/shard_map/ppermute | solution.py:534
  7.4 4.4 %collective-permute-start.5 = (bf16[1024,128]{1,0:T(8,128)(2,1)S(1)}, bf16[1024,128]{1,0:T(8,128)(2,1)S(1)}, u32[]{:S(2)}, u32[]{:S(2)}) collective-permute-start(bf16[1024,128]{1,0:T(8,128)(2,1)S(1)} %get-tuple-element.80), channel_id=1, source_target_pairs={{0,4},{2,6},{4,0},{6,2},{8,12},{10,14},{12,8},{14,10},{1,5},{3,7},... | collective-permute-start | bytes 786440 | tf_op jit(solution)/shard_map/ppermute | solution.py:534
  11.8 0.7 %collective-permute-start.3 = (bf16[1024,128]{1,0:T(8,128)(2,1)S(1)}, bf16[1024,128]{1,0:T(8,128)(2,1)S(1)}, u32[]{:S(2)}, u32[]{:S(2)}) collective-permute-start(bf16[1024,128]{1,0:T(8,128)(2,1)S(1)} %get-tuple-element.85), channel_id=1, source_target_pairs={{0,0},{2,2},{4,8},{6,10},{8,4},{10,6},{12,12},{14,14},{1,1},{3,3},... | collective-permute-start | bytes 786440 | tf_op jit(solution)/shard_map/ppermute | solution.py:534
  12.7 6.3 %collective-permute-done.5.z.z_k = bf16[1024,128]{1,0:T(8,128)(2,1)S(1)} collective-permute-done((bf16[1024,128]{1,0:T(8,128)(2,1)S(1)}, bf16[1024,128]{1,0:T(8,128)(2,1)S(1)}, u32[]{:S(2)}, u32[]{:S(2)}) %collective-permute-start.5) | collective-permute-done | bytes 262176 | tf_op jit(solution)/shard_map/ppermute | solution.py:534
  18.9 0.6 shard_map.89
  20.2 1.9 %collective-permute-start.8 = (bf16[512,256]{1,0:T(8,128)(2,1)S(1)}, bf16[512,256]{1,0:T(8,128)(2,1)S(1)}, u32[]{:S(2)}, u32[]{:S(2)}) collective-permute-start(bf16[512,256]{1,0:T(8,128)(2,1)S(1)} %shard_map.89), channel_id=1, source_target_pairs={{0,8},{2,10},{4,12},{6,14},{8,0},{10,2},{12,4},{14,6},{1,9},{3,11}... | collective-permute-start | bytes 786440 | tf_op jit(solution)/shard_map/ppermute | solution.py:534
  22.2 3.5 %shard_map.90 = (f32[8,1024]{1,0:T(8,128)S(1)}, f32[128,1024]{1,0:T(8,128)S(1)}) custom-call(s32[8,16]{1,0:T(8,128)S(1)} %get-tuple-element.84.lists.refs_0_, bf16[1024,256]{1,0:T(8,128)(2,1)S(1)} %get-tuple-element.83.qg.refs_1_, bf16[1024,256]{1,0:T(8,128)(2,1)S(1)} %get-tuple-element.90.kv, bf16[1024,256]{1,0:T(8,128)(2,1)S(1)} %collective-permute-done.6.a_kv), custom_call_target="tpu_custom_call" | custom-call | flops 1024 | bytes 1024 | tf_op jit(solution)/shard_map/pallas_call | solution.py:38
  25.9 1.6 %collective-permute-start.9 = (bf16[1024,128]{1,0:T(8,128)(2,1)S(1)}, bf16[1024,128]{1,0:T(8,128)(2,1)S(1)}, u32[]{:S(2)}, u32[]{:S(2)}) collective-permute-start(bf16[1024,128]{1,0:T(8,128)(2,1)S(1)} %shard_map.91), channel_id=1, source_target_pairs={{0,2},{2,0},{4,6},{6,4},{8,10},{10,8},{12,14},{14,12},{1,3},{3,1},... | collective-permute-start | bytes 786440 | tf_op jit(solution)/shard_map/ppermute | solution.py:534
  27.5 2.6 %shard_map.92 = (f32[8,1024]{1,0:T(8,128)S(1)}, f32[128,1024]{1,0:T(8,128)S(1)}, f32[2,512,512]{2,1,0:T(8,128)S(1)}) custom-call(s32[8,16]{1,0:T(8,128)S(1)} %get-tuple-element.84.lists.refs_0_, bf16[1024,256]{1,0:T(8,128)(2,1)S(1)} %get-tuple-element.83.qg.refs_1_, f32[8,1024]{1,0:T(8,128)S(1)} %get-tuple-element.99.stat, ...), custom_call_target="tpu_custom_call" | custom-call | flops 1024 | bytes 1024 | tf_op jit(solution)/shard_map/pallas_call | solution.py:38
  30.1 3.7 %collective-permute-done.8.refs_0_.refs_8_ = bf16[512,256]{1,0:T(8,128)(2,1)S(1)} collective-permute-done((bf16[512,256]{1,0:T(8,128)(2,1)S(1)}, bf16[512,256]{1,0:T(8,128)(2,1)S(1)}, u32[]{:S(2)}, u32[]{:S(2)}) %collective-permute-start.8) | collective-permute-done | bytes 262176 | tf_op jit(solution)/shard_map/ppermute | solution.py:534
  33.8 1.0 %shard_map.93 = (f32[8,1024]{1,0:T(8,128)S(1)}, f32[128,1024]{1,0:T(8,128)S(1)}, bf16[512,128]{1,0:T(8,128)(2,1)S(1)}) custom-call(bf16[1024,256]{1,0:T(8,128)(2,1)S(1)} %get-tuple-element.83.qg.refs_1_, f32[8,1024]{1,0:T(8,128)S(1)} %get-tuple-element.101.stat, f32[128,1024]{1,0:T(8,128)S(1)} %get-tuple-element.104.acc, ...), custom_call_target="tpu_custom_call" | custom-call | flops 1024 | bytes 1024 | tf_op jit(solution)/shard_map/pallas_call | solution.py:38
  34.8 1.1 %shard_map.94 = (bf16[1024,128]{1,0:T(8,128)(2,1)S(1)}, f32[2,512,512]{2,1,0:T(8,128)S(1)}) custom-call(s32[8,16]{1,0:T(8,128)S(1)} %get-tuple-element.84.lists.refs_0_, bf16[1024,256]{1,0:T(8,128)(2,1)S(1)} %get-tuple-element.83.qg.refs_1_, f32[8,1024]{1,0:T(8,128)S(1)} %get-tuple-element.106.lse_ref.refs_3_, f32[2,512,512]{2,1,0:T(8,128)S(1)} %get-tuple-element.108.s_ref), custom_call_target="tpu_custom_call" | custom-call | flops 1024 | bytes 1024 | tf_op jit(solution)/shard_map/pallas_call | solution.py:38
  36.0 1.2 %collective-permute-start.11 = (bf16[1024,128]{1,0:T(8,128)(2,1)S(1)}, bf16[1024,128]{1,0:T(8,128)(2,1)S(1)}, u32[]{:S(2)}, u32[]{:S(2)}) collective-permute-start(bf16[1024,128]{1,0:T(8,128)(2,1)S(1)} %get-tuple-element.115), channel_id=1, source_target_pairs={{0,2},{2,0},{4,6},{6,4},{8,10},{10,8},{12,14},{14,12},{1,3},{3,1},... | collective-permute-start | bytes 786440 | tf_op jit(solution)/shard_map/ppermute | solution.py:534
  37.2 2.3 %shard_map.95 = (bf16[128,1024]{1,0:T(8,128)(2,1)S(1)}, f32[8,1024]{1,0:T(8,128)S(1)}, bf16[1024,128]{1,0:T(8,128)(2,1)S(1)}, f32[128,1024]{1,0:T(8,128)S(1)}, bf16[512,128]{1,0:T(8,128)(2,1)S(1)}) custom-call(s32[8,16]{1,0:T(8,128)S(1)} %get-tuple-element.84.lists.refs_0_, bf16[1024,256]{1,0:T(8,128)(2,1)S(1)} %get-tuple-element.83.qg.refs_1_, ...), custom_call_target="tpu_custom_call" | custom-call | flops 1024 | bytes 1024 | tf_op jit(solution)/shard_map/pallas_call | solution.py:38
  39.5 0.9 %collective-permute-start.13 = (bf16[1024,128]{1,0:T(8,128)(2,1)S(1)}, bf16[1024,128]{1,0:T(8,128)(2,1)S(1)}, u32[]{:S(2)}, u32[]{:S(2)}) collective-permute-start(bf16[1024,128]{1,0:T(8,128)(2,1)S(1)} %get-tuple-element.121), channel_id=1, source_target_pairs={{0,2},{2,0},{4,6},{6,4},{8,10},{10,8},{12,14},{14,12},{1,3},{3,1},... | collective-permute-start | bytes 786440 | tf_op jit(solution)/shard_map/ppermute | solution.py:534
  40.4 2.9 %collective-permute-start.10 = (bf16[512,128]{1,0:T(8,128)(2,1)S(1)}, bf16[512,128]{1,0:T(8,128)(2,1)S(1)}, u32[]{:S(2)}, u32[]{:S(2)}) collective-permute-start(bf16[512,128]{1,0:T(8,128)(2,1)S(1)} %get-tuple-element.112), channel_id=1, source_target_pairs={{0,8},{2,10},{4,12},{6,14},{8,0},{10,2},{12,4},{14,6},{1,9},{3,11}... | collective-permute-start | bytes 393224 | tf_op jit(solution)/shard_map/ppermute | solution.py:534
  43.4 2.2 %shard_map.96 = (bf16[1024,256]{1,0:T(8,128)(2,1)S(1)}, f32[128,1024]{1,0:T(8,128)S(1)}) custom-call(s32[8,16]{1,0:T(8,128)S(1)} %get-tuple-element.84.lists.refs_0_, bf16[1024,256]{1,0:T(8,128)(2,1)S(1)} %get-tuple-element.83.qg.refs_1_, f32[8,1024]{1,0:T(8,128)S(1)} %get-tuple-element.106.lse_ref.refs_3_, f32[8,1024]{1,0:T(8,128)S(1)} %get-tuple-element.111.dot_ref, ...), custom_call_target="tpu_custom_call" | custom-call | flops 1024 | bytes 1024 | tf_op jit(solution)/shard_map/pallas_call | solution.py:38
  45.6 1.3 %collective-permute-done.12.refs_2_ = bf16[512,128]{1,0:T(8,128)(2,1)S(1)} collective-permute-done((bf16[512,128]{1,0:T(8,128)(2,1)S(1)}, bf16[512,128]{1,0:T(8,128)(2,1)S(1)}, u32[]{:S(2)}, u32[]{:S(2)}) %collective-permute-start.12) | collective-permute-done | bytes 131104 | tf_op jit(solution)/shard_map/ppermute | solution.py:534
  46.9 2.2 %shard_map.97 = (f32[1024,256]{1,0:T(8,128)S(1)}, f32[1024,256]{1,0:T(8,128)S(1)}, f32[128,1024]{1,0:T(8,128)S(1)}) custom-call(s32[8,16]{1,0:T(8,128)S(1)} %get-tuple-element.84.lists.refs_0_, bf16[1024,256]{1,0:T(8,128)(2,1)S(1)} %get-tuple-element.83.qg.refs_1_, f32[8,1024]{1,0:T(8,128)S(1)} %get-tuple-element.106.lse_ref.refs_3_, ...), custom_call_target="tpu_custom_call" | custom-call | flops 2684354560 | bytes 1024 | tf_op jit(solution)/shard_map/pallas_call | solution.py:38
  49.1 1.1 %collective-permute-done.13.came = bf16[1024,128]{1,0:T(8,128)(2,1)S(1)} collective-permute-done((bf16[1024,128]{1,0:T(8,128)(2,1)S(1)}, bf16[1024,128]{1,0:T(8,128)(2,1)S(1)}, u32[]{:S(2)}, u32[]{:S(2)}) %collective-permute-start.13) | collective-permute-done | bytes 262176 | tf_op jit(solution)/shard_map/ppermute | solution.py:534
  50.5 0.7 %collective-permute-start.16 = (bf16[1024,256]{1,0:T(8,128)(2,1)S(1)}, bf16[1024,256]{1,0:T(8,128)(2,1)S(1)}, u32[]{:S(2)}, u32[]{:S(2)}) collective-permute-start(bf16[1024,256]{1,0:T(8,128)(2,1)S(1)} %get-tuple-element.123), channel_id=1, source_target_pairs={{0,0},{2,2},{4,8},{6,10},{8,4},{10,6},{12,12},{14,14},{1,1},{3,3},... | collective-permute-start | bytes 1572872 | tf_op jit(solution)/shard_map/ppermute | solution.py:534
  51.2 3.3 %collective-permute-start.17 = (bf16[1024,256]{1,0:T(8,128)(2,1)S(1)}, bf16[1024,256]{1,0:T(8,128)(2,1)S(1)}, u32[]{:S(2)}, u32[]{:S(2)}) collective-permute-start(bf16[1024,256]{1,0:T(8,128)(2,1)S(1)} %get-tuple-element.122), channel_id=1, source_target_pairs={{0,4},{2,6},{4,0},{6,2},{8,12},{10,14},{12,8},{14,10},{1,5},{3,7},... | collective-permute-start | bytes 1572872 | tf_op jit(solution)/shard_map/ppermute | solution.py:534
  54.4 0.7 %shard_map.99.placed = f32[1024,256]{1,0:T(8,128)S(1)} custom-call(s32[8,16]{1,0:T(8,128)S(1)} %get-tuple-element.84.lists.refs_0_, bf16[512,128]{1,0:T(8,128)(2,1)S(1)} %collective-permute-done.10.refs_1_, bf16[512,128]{1,0:T(8,128)(2,1)S(1)} %collective-permute-done.12.refs_2_), custom_call_target="tpu_custom_call" | custom-call | flops 1024 | bytes 1024 | tf_op jit(solution)/shard_map/pallas_call | solution.py:38
  55.2 3.2 %shard_map.100 = (f32[1024,256]{1,0:T(8,128)S(1)}, bf16[512,256]{1,0:T(8,128)(2,1)S(1)}, bf16[512,256]{1,0:T(8,128)(2,1)S(1)}) custom-call(bf16[1024,256]{1,0:T(8,128)(2,1)S(1)} %get-tuple-element.83.qg.refs_1_, f32[8,1024]{1,0:T(8,128)S(1)} %get-tuple-element.106.lse_ref.refs_3_, f32[8,1024]{1,0:T(8,128)S(1)} %get-tuple-element.111.dot_ref, ...), custom_call_target="tpu_custom_call" | custom-call | flops 2684354560 | bytes 1024 | tf_op jit(solution)/shard_map/pallas_call | solution.py:38
  58.4 1.5 %collective-permute-done.14.came = bf16[512,256]{1,0:T(8,128)(2,1)S(1)} collective-permute-done((bf16[512,256]{1,0:T(8,128)(2,1)S(1)}, bf16[512,256]{1,0:T(8,128)(2,1)S(1)}, u32[]{:S(2)}, u32[]{:S(2)}) %collective-permute-start.14) | collective-permute-done | bytes 262176 | tf_op jit(solution)/shard_map/ppermute | solution.py:531
  60.0 0.9 %shard_map.101 = (bf16[512,256]{1,0:T(8,128)(2,1)}, bf16[512,256]{1,0:T(8,128)(2,1)}) custom-call(bf16[512,256]{1,0:T(8,128)(2,1)S(1)} %get-tuple-element.130.keep, bf16[512,256]{1,0:T(8,128)(2,1)S(1)} %collective-permute-done.14.came), custom_call_target="tpu_custom_call" | custom-call | flops 1024 | bytes 1024 | tf_op jit(solution)/shard_map/pallas_call | solution.py:38
  61.1 0.6 %collective-permute-done.17.came = bf16[1024,256]{1,0:T(8,128)(2,1)S(1)} collective-permute-done((bf16[1024,256]{1,0:T(8,128)(2,1)S(1)}, bf16[1024,256]{1,0:T(8,128)(2,1)S(1)}, u32[]{:S(2)}, u32[]{:S(2)}) %collective-permute-start.17) | collective-permute-done | bytes 524320 | tf_op jit(solution)/shard_map/ppermute | solution.py:534
  61.9 1.5 %collective-permute-done.18.came = bf16[512,256]{1,0:T(8,128)(2,1)S(1)} collective-permute-done((bf16[512,256]{1,0:T(8,128)(2,1)S(1)}, bf16[512,256]{1,0:T(8,128)(2,1)S(1)}, u32[]{:S(2)}, u32[]{:S(2)}) %collective-permute-start.18) | collective-permute-done | bytes 262176 | tf_op jit(solution)/shard_map/ppermute | solution.py:531
  63.5 0.9 %shard_map.104 = (bf16[512,256]{1,0:T(8,128)(2,1)}, bf16[512,256]{1,0:T(8,128)(2,1)}) custom-call(bf16[512,256]{1,0:T(8,128)(2,1)S(1)} %get-tuple-element.138.keep, bf16[512,256]{1,0:T(8,128)(2,1)S(1)} %collective-permute-done.18.came), custom_call_target="tpu_custom_call" | custom-call | flops 1024 | bytes 1024 | tf_op jit(solution)/shard_map/pallas_call | solution.py:38
  (27 shorter events, 2.8 us)
Async XLA Ops:
  1.8 1.7 %collective-permute-start = (bf16[512,256]{1,0:T(8,128)(2,1)S(1)}, bf16[512,256]{1,0:T(8,128)(2,1)S(1)}, u32[]{:S(2)}, u32[]{:S(2)}) collective-permute-start(bf16[512,256]{1,0:T(8,128)(2,1)S(1)} %get-tuple-element.73), channel_id=1, source_target_pairs={{0,1},{1,0},{2,3},{3,2},{4,5},{5,4},{6,7},{7,6},{8,9},{9,8},{10,11... | collective-permute-start | bytes 786440 | tf_op jit(solution)/shard_map/ppermute | solution.py:531
  3.6 8.2 %collective-permute-start.2 = (bf16[512,256]{1,0:T(8,128)(2,1)S(1)}, bf16[512,256]{1,0:T(8,128)(2,1)S(1)}, u32[]{:S(2)}, u32[]{:S(2)}) collective-permute-start(bf16[512,256]{1,0:T(8,128)(2,1)S(1)} %get-tuple-element.81), channel_id=1, source_target_pairs={{0,1},{1,0},{2,3},{3,2},{4,5},{5,4},{6,7},{7,6},{8,9},{9,8},{10,11... | collective-permute-start | bytes 786440 | tf_op jit(solution)/shard_map/ppermute | solution.py:531
  4.0 8.5 %collective-permute-start.1 = (bf16[1024,128]{1,0:T(8,128)(2,1)S(1)}, bf16[1024,128]{1,0:T(8,128)(2,1)S(1)}, u32[]{:S(2)}, u32[]{:S(2)}) collective-permute-start(bf16[1024,128]{1,0:T(8,128)(2,1)S(1)} %get-tuple-element.80), channel_id=1, source_target_pairs={{0,0},{2,2},{4,8},{6,10},{8,4},{10,6},{12,12},{14,14},{1,1},{3,3},... | collective-permute-start | bytes 786440 | tf_op jit(solution)/shard_map/ppermute | solution.py:534
  4.7 17.5 %collective-permute-start.6 = (bf16[1024,256]{1,0:T(8,128)(2,1)S(1)}, bf16[1024,256]{1,0:T(8,128)(2,1)S(1)}, u32[]{:S(2)}, u32[]{:S(2)}) collective-permute-start(bf16[1024,256]{1,0:T(8,128)(2,1)S(1)} %get-tuple-element.90.kv), channel_id=1, source_target_pairs={{0,2},{2,0},{4,6},{6,4},{8,10},{10,8},{12,14},{14,12},{1,3},{3,1},... | collective-permute-start | bytes 1572872 | tf_op jit(solution)/shard_map/ppermute | solution.py:534
  7.4 11.5 %collective-permute-start.5 = (bf16[1024,128]{1,0:T(8,128)(2,1)S(1)}, bf16[1024,128]{1,0:T(8,128)(2,1)S(1)}, u32[]{:S(2)}, u32[]{:S(2)}) collective-permute-start(bf16[1024,128]{1,0:T(8,128)(2,1)S(1)} %get-tuple-element.80), channel_id=1, source_target_pairs={{0,4},{2,6},{4,0},{6,2},{8,12},{10,14},{12,8},{14,10},{1,5},{3,7},... | collective-permute-start | bytes 786440 | tf_op jit(solution)/shard_map/ppermute | solution.py:534
  11.8 13.9 %collective-permute-start.4 = (bf16[1024,128]{1,0:T(8,128)(2,1)S(1)}, bf16[1024,128]{1,0:T(8,128)(2,1)S(1)}, u32[]{:S(2)}, u32[]{:S(2)}) collective-permute-start(bf16[1024,128]{1,0:T(8,128)(2,1)S(1)} %get-tuple-element.85), channel_id=1, source_target_pairs={{0,4},{2,6},{4,0},{6,2},{8,12},{10,14},{12,8},{14,10},{1,5},{3,7},... | collective-permute-start | bytes 786440 | tf_op jit(solution)/shard_map/ppermute | solution.py:534
  11.8 13.9 %collective-permute-start.3 = (bf16[1024,128]{1,0:T(8,128)(2,1)S(1)}, bf16[1024,128]{1,0:T(8,128)(2,1)S(1)}, u32[]{:S(2)}, u32[]{:S(2)}) collective-permute-start(bf16[1024,128]{1,0:T(8,128)(2,1)S(1)} %get-tuple-element.85), channel_id=1, source_target_pairs={{0,0},{2,2},{4,8},{6,10},{8,4},{10,6},{12,12},{14,14},{1,1},{3,3},... | collective-permute-start | bytes 786440 | tf_op jit(solution)/shard_map/ppermute | solution.py:534
  19.6 7.8 %collective-permute-start.7 = (bf16[1024,128]{1,0:T(8,128)(2,1)S(1)}, bf16[1024,128]{1,0:T(8,128)(2,1)S(1)}, u32[]{:S(2)}, u32[]{:S(2)}) collective-permute-start(bf16[1024,128]{1,0:T(8,128)(2,1)S(1)} %shard_map.88), channel_id=1, source_target_pairs={{0,2},{2,0},{4,6},{6,4},{8,10},{10,8},{12,14},{14,12},{1,3},{3,1},... | collective-permute-start | bytes 786440 | tf_op jit(solution)/shard_map/ppermute | solution.py:534
  20.2 13.6 %collective-permute-start.8 = (bf16[512,256]{1,0:T(8,128)(2,1)S(1)}, bf16[512,256]{1,0:T(8,128)(2,1)S(1)}, u32[]{:S(2)}, u32[]{:S(2)}) collective-permute-start(bf16[512,256]{1,0:T(8,128)(2,1)S(1)} %shard_map.89), channel_id=1, source_target_pairs={{0,8},{2,10},{4,12},{6,14},{8,0},{10,2},{12,4},{14,6},{1,9},{3,11}... | collective-permute-start | bytes 786440 | tf_op jit(solution)/shard_map/ppermute | solution.py:534
  25.9 11.3 %collective-permute-start.9 = (bf16[1024,128]{1,0:T(8,128)(2,1)S(1)}, bf16[1024,128]{1,0:T(8,128)(2,1)S(1)}, u32[]{:S(2)}, u32[]{:S(2)}) collective-permute-start(bf16[1024,128]{1,0:T(8,128)(2,1)S(1)} %shard_map.91), channel_id=1, source_target_pairs={{0,2},{2,0},{4,6},{6,4},{8,10},{10,8},{12,14},{14,12},{1,3},{3,1},... | collective-permute-start | bytes 786440 | tf_op jit(solution)/shard_map/ppermute | solution.py:534
  36.0 10.9 %collective-permute-start.11 = (bf16[1024,128]{1,0:T(8,128)(2,1)S(1)}, bf16[1024,128]{1,0:T(8,128)(2,1)S(1)}, u32[]{:S(2)}, u32[]{:S(2)}) collective-permute-start(bf16[1024,128]{1,0:T(8,128)(2,1)S(1)} %get-tuple-element.115), channel_id=1, source_target_pairs={{0,2},{2,0},{4,6},{6,4},{8,10},{10,8},{12,14},{14,12},{1,3},{3,1},... | collective-permute-start | bytes 786440 | tf_op jit(solution)/shard_map/ppermute | solution.py:534
  37.2 9.7 %collective-permute-start.12 = (bf16[512,128]{1,0:T(8,128)(2,1)S(1)}, bf16[512,128]{1,0:T(8,128)(2,1)S(1)}, u32[]{:S(2)}, u32[]{:S(2)}) collective-permute-start(bf16[512,128]{1,0:T(8,128)(2,1)S(1)} %get-tuple-element.116), channel_id=1, source_target_pairs={{0,8},{2,10},{4,12},{6,14},{8,0},{10,2},{12,4},{14,6},{1,9},{3,11}... | collective-permute-start | bytes 393224 | tf_op jit(solution)/shard_map/ppermute | solution.py:534
  39.5 10.7 %collective-permute-start.13 = (bf16[1024,128]{1,0:T(8,128)(2,1)S(1)}, bf16[1024,128]{1,0:T(8,128)(2,1)S(1)}, u32[]{:S(2)}, u32[]{:S(2)}) collective-permute-start(bf16[1024,128]{1,0:T(8,128)(2,1)S(1)} %get-tuple-element.121), channel_id=1, source_target_pairs={{0,2},{2,0},{4,6},{6,4},{8,10},{10,8},{12,14},{14,12},{1,3},{3,1},... | collective-permute-start | bytes 786440 | tf_op jit(solution)/shard_map/ppermute | solution.py:534
  40.4 14.0 %collective-permute-start.10 = (bf16[512,128]{1,0:T(8,128)(2,1)S(1)}, bf16[512,128]{1,0:T(8,128)(2,1)S(1)}, u32[]{:S(2)}, u32[]{:S(2)}) collective-permute-start(bf16[512,128]{1,0:T(8,128)(2,1)S(1)} %get-tuple-element.112), channel_id=1, source_target_pairs={{0,8},{2,10},{4,12},{6,14},{8,0},{10,2},{12,4},{14,6},{1,9},{3,11}... | collective-permute-start | bytes 393224 | tf_op jit(solution)/shard_map/ppermute | solution.py:534
  46.9 13.9 %collective-permute-start.15 = (bf16[1024,256]{1,0:T(8,128)(2,1)S(1)}, bf16[1024,256]{1,0:T(8,128)(2,1)S(1)}, u32[]{:S(2)}, u32[]{:S(2)}) collective-permute-start(bf16[1024,256]{1,0:T(8,128)(2,1)S(1)} %get-tuple-element.137), channel_id=1, source_target_pairs={{0,2},{2,0},{4,6},{6,4},{8,10},{10,8},{12,14},{14,12},{1,3},{3,1},... | collective-permute-start | bytes 1572872 | tf_op jit(solution)/shard_map/ppermute | solution.py:534
  50.5 10.4 %collective-permute-start.16 = (bf16[1024,256]{1,0:T(8,128)(2,1)S(1)}, bf16[1024,256]{1,0:T(8,128)(2,1)S(1)}, u32[]{:S(2)}, u32[]{:S(2)}) collective-permute-start(bf16[1024,256]{1,0:T(8,128)(2,1)S(1)} %get-tuple-element.123), channel_id=1, source_target_pairs={{0,0},{2,2},{4,8},{6,10},{8,4},{10,6},{12,12},{14,14},{1,1},{3,3},... | collective-permute-start | bytes 1572872 | tf_op jit(solution)/shard_map/ppermute | solution.py:534
  51.2 10.6 %collective-permute-start.17 = (bf16[1024,256]{1,0:T(8,128)(2,1)S(1)}, bf16[1024,256]{1,0:T(8,128)(2,1)S(1)}, u32[]{:S(2)}, u32[]{:S(2)}) collective-permute-start(bf16[1024,256]{1,0:T(8,128)(2,1)S(1)} %get-tuple-element.122), channel_id=1, source_target_pairs={{0,4},{2,6},{4,0},{6,2},{8,12},{10,14},{12,8},{14,10},{1,5},{3,7},... | collective-permute-start | bytes 1572872 | tf_op jit(solution)/shard_map/ppermute | solution.py:534
  58.4 1.6 %collective-permute-start.14 = (bf16[512,256]{1,0:T(8,128)(2,1)S(1)}, bf16[512,256]{1,0:T(8,128)(2,1)S(1)}, u32[]{:S(2)}, u32[]{:S(2)}) collective-permute-start(bf16[512,256]{1,0:T(8,128)(2,1)S(1)} %get-tuple-element.131), channel_id=1, source_target_pairs={{0,1},{1,0},{2,3},{3,2},{4,5},{5,4},{6,7},{7,6},{8,9},{9,8},{10,11... | collective-permute-start | bytes 786440 | tf_op jit(solution)/shard_map/ppermute | solution.py:531
  61.9 1.6 %collective-permute-start.18 = (bf16[512,256]{1,0:T(8,128)(2,1)S(1)}, bf16[512,256]{1,0:T(8,128)(2,1)S(1)}, u32[]{:S(2)}, u32[]{:S(2)}) collective-permute-start(bf16[512,256]{1,0:T(8,128)(2,1)S(1)} %get-tuple-element.139), channel_id=1, source_target_pairs={{0,1},{1,0},{2,3},{3,2},{4,5},{5,4},{6,7},{7,6},{8,9},{9,8},{10,11... | collective-permute-start | bytes 786440 | tf_op jit(solution)/shard_map/ppermute | solution.py:531

commit v8 on v7

--- a/solution.py
+++ b/solution.py
@@ -98,21 +98,17 @@
         pl.when(core == mine)(functools.partial(body, mine))
 
 
-def pack_kernel(a, b, *refs):
-    *extra, sems = refs
-    n = (len(extra) - 2) // 2
-    send, own = extra[n : n + 2]
-
+def pack_kernel(k, v, q, g, lists, k_own, v_own, qg_own, qg_send, lists_out, sems):
     def body(mine):
-        copies = []
-        for source, out in zip(extra[:n], extra[n + 2 :]):
-            copies.append(pltpu.make_async_copy(source, out, sems.at[len(copies)]))
-        for head, out in ((1 - mine, send), (mine, own)):
-            for source, cols in ((a, KEY), (b, VALUE)):
-                sem = sems.at[len(copies)]
-                copies.append(
-                    pltpu.make_async_copy(source.at[:, head_cols(head)], out.at[:, cols], sem)
-                )
+        moves = [(lists, lists_out)]
+        for source, out in ((k, k_own), (v, v_own)):
+            moves.append((source.at[:, head_cols(mine)], out))
+        for head, out in ((mine, qg_own), (1 - mine, qg_send)):
+            for source, cols in ((q, KEY), (g, VALUE)):
+                moves.append((source.at[:, head_cols(head)], out.at[:, cols]))
+        copies = [
+            pltpu.make_async_copy(source, out, sems.at[n]) for n, (source, out) in enumerate(moves)
+        ]
         for copy in copies:
             copy.start()
         for copy in copies:
@@ -121,16 +117,25 @@
     each_core(body)
 
 
-def frame_kernel(own, came, kv, keys, values):
+def keys_kernel(own, came, keys):
     half = own.shape[0]
 
     def body(mine):
-        for slab, source in ((mine, own), (1 - mine, came)):
+        keys[rows_of(mine, half), :] = own[...]
+        keys[rows_of(1 - mine, half), :] = came[:, head_cols(mine)]
+
+    each_core(body)
+
+
+def values_kernel(keys, own, came, values, kv):
+    half = own.shape[0]
+
+    def body(mine):
+        for slab, part in ((mine, own[...]), (1 - mine, came[:, head_cols(mine)])):
             rows = rows_of(slab, half)
-            part = source[...]
-            kv[rows, :] = part
-            keys[rows, :] = part[:, KEY]
-            values[rows, :] = part[:, VALUE]
+            values[rows, :] = part
+            kv[rows, VALUE] = part
+            kv[rows, KEY] = keys[rows, :]
 
     each_core(body)
 
@@ -354,7 +359,7 @@
             store_grads(group, dot_nn(p.astype(BF16), g), "dv")
 
 
-def values_kernel(block, relayed, lists, qg, lse_ref, s_ref, dc_v, p_ref, grad):
+def shares_kernel(block, relayed, lists, qg, lse_ref, s_ref, dc_v, p_ref, grad):
     half = qg.shape[0] // 2
     frame = lax.axis_index("tm")
     grad[...] = jnp.zeros_like(grad)
@@ -537,24 +542,19 @@
         return pltpu.VMEM((pieces * block, s_dev), F32)
 
 
-    def packed(*arrays):
-        return call(
-            pack_kernel,
-            tuple(pltpu.with_memory_space_constraint(a, pltpu.HBM) for a in arrays),
-            [pair] * 2 + [sds(a.shape, a.dtype) for a in arrays[2:]],
-            scratch=[pltpu.SemaphoreType.DMA((2 + len(arrays),))],
-            source=HBM,
-            scalars=HBM,
-        )
-
-    kv_send, kv_own = packed(key_rows, value_rows)
-    kv_came = across(kv_send)
-    qg_send, qg_own, lists = packed(queries, out_grad, block_lists.T)
-    kv_came, qg_own = lax.optimization_barrier((kv_came, qg_own))
-    kv, keys, values = call(
-        frame_kernel, (kv_own, kv_came), [frame_two, frame_one, frame_one]
-    )
-    qg_send, keys = lax.optimization_barrier((qg_send, keys))
+    k_came, v_came = across(key_rows), across(value_rows)
+    sources = (key_rows, value_rows, queries, out_grad, block_lists.T)
+    k_own, v_own, qg_own, qg_send, lists = call(
+        pack_kernel,
+        tuple(pltpu.with_memory_space_constraint(a, pltpu.HBM) for a in sources),
+        [single, single, pair, pair, sds(sources[4].shape, jnp.int32)],
+        scratch=[pltpu.SemaphoreType.DMA((7,))],
+        source=HBM,
+        scalars=HBM,
+    )
+    (keys,) = call(keys_kernel, (k_own, k_came), [frame_one])
+    values, kv = call(values_kernel, (keys, v_own, v_came), [frame_one, frame_two])
+    qg_send, _ = lax.optimization_barrier((qg_send, kv))
     y_k = swapped(keys, y_swap)
     z_k = swapped(keys, z_swap)
     a_kv = swapped(kv, near_swap)
@@ -596,7 +596,7 @@
         scratch=[scores(n)],
     )
     dc_v, probs = call(
-        functools.partial(values_kernel, block, relayed),
+        functools.partial(shares_kernel, block, relayed),
         (lists, qg, lse, late_scores),
         [frame_one, score_two],
         scratch=[grad_one],
@@ -617,6 +617,7 @@
         [frame_two, turned_sum],
         scratch=[pltpu.VMEM((2 * s_dev, 2 * DH), F32)],
     )
+    da, dc_k_came = lax.optimization_barrier((da, dc_k_came))
     da_came = swapped(da, near_swap)
     dc_v_came, far_dv_came = lax.optimization_barrier((dc_v_came, far_dv_came))
     dz, dy, dq = call(

time: 64.5 us -> 68.1 us (1.056)
  waiting for transfers between devices: 16.2 us -> 20.1 us
  Pallas kernels: 24.7 us -> 23.7 us
    ppermute x15, waiting for transfers between devices: 13.1 us -> 17 us  [swapped(): return lax.ppermute(value, 'tm', swap.pairs)]
    pallas_call x21, Pallas kernels: 24.7 us -> 23.7 us  [call(): pl.pallas_call(kernel, out_shape=out_shape, in_specs=[scalars if a.dtype...]
    ppermute x4 -> x5, waiting for transfers between devices: 3.05 us -> 3.06 us  [across(): return lax.ppermute(value, 'space', [(0, 1), (1, 0)])]
  transfers between devices with their start and end apart: 19 -> 20, of which waited for: 8 -> 6; matrix products, arithmetic and copies ran while one was open for 0% -> 0% of each run, Pallas kernels for 35% -> 34%
where the time goes in v8:
time: 68.1 us; the launch traced here: 67.8 us
  Pallas kernels  23.7 us (35%)
  starting transfers between devices  23.1 us (34%)
  waiting for transfers between devices  20.1 us (30%)
  between operations  0.86 us (1%)
    pallas_call x21, Pallas kernels, call(): pl.pallas_call(kernel, out_shape=out_shape, in_specs=[scalars if a.dtype...  23.7 us
    ppermute x15, starting transfers between devices, swapped(): return lax.ppermute(value, 'tm', swap.pairs)  21.9 us
    ppermute x15, waiting for transfers between devices, swapped(): return lax.ppermute(value, 'tm', swap.pairs)  17 us
    ppermute x5, waiting for transfers between devices, across(): return lax.ppermute(value, 'space', [(0, 1), (1, 0)])  3.06 us
  transfers between devices with their start and end apart: 20, of which 6 were waited for; matrix products, arithmetic and copies ran while one was open for 0% of the time, Pallas kernels for 34%

profile of v8, /device:TPU:0, one launch (start us, length us, event | category | flops | bytes accessed | tf_op | source)
XLA Modules:
  0.0 67.8 jit_solution(12528470903225367419)
XLA Ops:
  1.2 1.3 %shard_map.84 = (bf16[512,128]{1,0:T(8,128)(2,1)S(1)}, bf16[512,128]{1,0:T(8,128)(2,1)S(1)}, bf16[512,256]{1,0:T(8,128)(2,1)S(1)}, bf16[512,256]{1,0:T(8,128)(2,1)S(1)}, s32[8,16]{1,0:T(8,128)S(1)}) custom-call(bf16[512,256]{1,0:T(8,128)(2,1)} %k.1, bf16[512,256]{1,0:T(8,128)(2,1)} %v.1, bf16[512,256]{1,0:T(8,128)(2,1)} %q.1, bf16[512,256]{1,0:T(8,128)(2,1)} %g.1, ...), custom_call_target="tpu_custom_call" | custom-call | flops 1024 | bytes 1024 | tf_op jit(solution)/shard_map/pallas_call | solution.py:38
  2.6 0.7 collective-permute-start.1
  3.9 2.6 %collective-permute-start.7 = (bf16[1024,256]{1,0:T(8,128)(2,1)S(1)}, bf16[1024,256]{1,0:T(8,128)(2,1)S(1)}, u32[]{:S(2)}, u32[]{:S(2)}) collective-permute-start(bf16[1024,256]{1,0:T(8,128)(2,1)S(1)} %get-tuple-element.84.kv), channel_id=1, source_target_pairs={{0,2},{2,0},{4,6},{6,4},{8,10},{10,8},{12,14},{14,12},{1,3},{3,1},... | collective-permute-start | bytes 1572872 | tf_op jit(solution)/shard_map/ppermute | solution.py:539
  6.5 4.4 %collective-permute-start.6 = (bf16[1024,128]{1,0:T(8,128)(2,1)S(1)}, bf16[1024,128]{1,0:T(8,128)(2,1)S(1)}, u32[]{:S(2)}, u32[]{:S(2)}) collective-permute-start(bf16[1024,128]{1,0:T(8,128)(2,1)S(1)} %shard_map.85.keys), channel_id=1, source_target_pairs={{0,4},{2,6},{4,0},{6,2},{8,12},{10,14},{12,8},{14,10},{1,5},{3,7},... | collective-permute-start | bytes 786440 | tf_op jit(solution)/shard_map/ppermute | solution.py:539
  10.9 0.7 collective-permute-start.4
  11.7 6.2 %collective-permute-done.6.z.z_k = bf16[1024,128]{1,0:T(8,128)(2,1)S(1)} collective-permute-done((bf16[1024,128]{1,0:T(8,128)(2,1)S(1)}, bf16[1024,128]{1,0:T(8,128)(2,1)S(1)}, u32[]{:S(2)}, u32[]{:S(2)}) %collective-permute-start.6) | collective-permute-done | bytes 262176 | tf_op jit(solution)/shard_map/ppermute | solution.py:539
  18.0 0.6 shard_map.89
  18.7 0.6 collective-permute-start.8
  19.2 2.3 %collective-permute-start.9 = (bf16[512,256]{1,0:T(8,128)(2,1)S(1)}, bf16[512,256]{1,0:T(8,128)(2,1)S(1)}, u32[]{:S(2)}, u32[]{:S(2)}) collective-permute-start(bf16[512,256]{1,0:T(8,128)(2,1)S(1)} %shard_map.89), channel_id=1, source_target_pairs={{0,8},{2,10},{4,12},{6,14},{8,0},{10,2},{12,4},{14,6},{1,9},{3,11}... | collective-permute-start | bytes 786440 | tf_op jit(solution)/shard_map/ppermute | solution.py:539
  21.6 3.5 %shard_map.90 = (f32[8,1024]{1,0:T(8,128)S(1)}, f32[128,1024]{1,0:T(8,128)S(1)}) custom-call(s32[8,16]{1,0:T(8,128)S(1)} %get-tuple-element.79.lists.refs_0_, bf16[1024,256]{1,0:T(8,128)(2,1)S(1)} %get-tuple-element.78.qg.refs_1_, bf16[1024,256]{1,0:T(8,128)(2,1)S(1)} %get-tuple-element.84.kv, bf16[1024,256]{1,0:T(8,128)(2,1)S(1)} %collective-permute-done.7.a_kv), custom_call_target="tpu_custom_call" | custom-call | flops 1024 | bytes 1024 | tf_op jit(solution)/shard_map/pallas_call | solution.py:38
  25.3 1.2 %collective-permute-start.10 = (bf16[1024,128]{1,0:T(8,128)(2,1)S(1)}, bf16[1024,128]{1,0:T(8,128)(2,1)S(1)}, u32[]{:S(2)}, u32[]{:S(2)}) collective-permute-start(bf16[1024,128]{1,0:T(8,128)(2,1)S(1)} %shard_map.91), channel_id=1, source_target_pairs={{0,2},{2,0},{4,6},{6,4},{8,10},{10,8},{12,14},{14,12},{1,3},{3,1},... | collective-permute-start | bytes 786440 | tf_op jit(solution)/shard_map/ppermute | solution.py:539
  26.5 2.6 %shard_map.92 = (f32[8,1024]{1,0:T(8,128)S(1)}, f32[128,1024]{1,0:T(8,128)S(1)}, f32[2,512,512]{2,1,0:T(8,128)S(1)}) custom-call(s32[8,16]{1,0:T(8,128)S(1)} %get-tuple-element.79.lists.refs_0_, bf16[1024,256]{1,0:T(8,128)(2,1)S(1)} %get-tuple-element.78.qg.refs_1_, f32[8,1024]{1,0:T(8,128)S(1)} %get-tuple-element.93.stat, ...), custom_call_target="tpu_custom_call" | custom-call | flops 1024 | bytes 1024 | tf_op jit(solution)/shard_map/pallas_call | solution.py:38
  29.2 6.6 %collective-permute-done.9.refs_0_.refs_8_ = bf16[512,256]{1,0:T(8,128)(2,1)S(1)} collective-permute-done((bf16[512,256]{1,0:T(8,128)(2,1)S(1)}, bf16[512,256]{1,0:T(8,128)(2,1)S(1)}, u32[]{:S(2)}, u32[]{:S(2)}) %collective-permute-start.9) | collective-permute-done | bytes 262176 | tf_op jit(solution)/shard_map/ppermute | solution.py:539
  35.8 1.0 %shard_map.93 = (f32[8,1024]{1,0:T(8,128)S(1)}, f32[128,1024]{1,0:T(8,128)S(1)}, bf16[512,128]{1,0:T(8,128)(2,1)S(1)}) custom-call(bf16[1024,256]{1,0:T(8,128)(2,1)S(1)} %get-tuple-element.78.qg.refs_1_, f32[8,1024]{1,0:T(8,128)S(1)} %get-tuple-element.95.stat, f32[128,1024]{1,0:T(8,128)S(1)} %get-tuple-element.98.acc, ...), custom_call_target="tpu_custom_call" | custom-call | flops 1024 | bytes 1024 | tf_op jit(solution)/shard_map/pallas_call | solution.py:38
  36.8 1.1 %shard_map.94 = (bf16[1024,128]{1,0:T(8,128)(2,1)S(1)}, f32[2,512,512]{2,1,0:T(8,128)S(1)}) custom-call(s32[8,16]{1,0:T(8,128)S(1)} %get-tuple-element.79.lists.refs_0_, bf16[1024,256]{1,0:T(8,128)(2,1)S(1)} %get-tuple-element.78.qg.refs_1_, f32[8,1024]{1,0:T(8,128)S(1)} %get-tuple-element.100.lse_ref.refs_3_, f32[2,512,512]{2,1,0:T(8,128)S(1)} %get-tuple-element.102.s_ref), custom_call_target="tpu_custom_call" | custom-call | flops 1024 | bytes 1024 | tf_op jit(solution)/shard_map/pallas_call | solution.py:38
  37.9 1.6 %collective-permute-start.12 = (bf16[1024,128]{1,0:T(8,128)(2,1)S(1)}, bf16[1024,128]{1,0:T(8,128)(2,1)S(1)}, u32[]{:S(2)}, u32[]{:S(2)}) collective-permute-start(bf16[1024,128]{1,0:T(8,128)(2,1)S(1)} %get-tuple-element.109), channel_id=1, source_target_pairs={{0,2},{2,0},{4,6},{6,4},{8,10},{10,8},{12,14},{14,12},{1,3},{3,1},... | collective-permute-start | bytes 786440 | tf_op jit(solution)/shard_map/ppermute | solution.py:539
  39.5 1.2 %collective-permute-start.13 = (bf16[512,128]{1,0:T(8,128)(2,1)S(1)}, bf16[512,128]{1,0:T(8,128)(2,1)S(1)}, u32[]{:S(2)}, u32[]{:S(2)}) collective-permute-start(bf16[512,128]{1,0:T(8,128)(2,1)S(1)} %get-tuple-element.110), channel_id=1, source_target_pairs={{0,8},{2,10},{4,12},{6,14},{8,0},{10,2},{12,4},{14,6},{1,9},{3,11}... | collective-permute-start | bytes 393224 | tf_op jit(solution)/shard_map/ppermute | solution.py:539
  40.7 2.3 %shard_map.95 = (bf16[128,1024]{1,0:T(8,128)(2,1)S(1)}, f32[8,1024]{1,0:T(8,128)S(1)}, bf16[1024,128]{1,0:T(8,128)(2,1)S(1)}, f32[128,1024]{1,0:T(8,128)S(1)}, bf16[512,128]{1,0:T(8,128)(2,1)S(1)}) custom-call(s32[8,16]{1,0:T(8,128)S(1)} %get-tuple-element.79.lists.refs_0_, bf16[1024,256]{1,0:T(8,128)(2,1)S(1)} %get-tuple-element.78.qg.refs_1_, ...), custom_call_target="tpu_custom_call" | custom-call | flops 1024 | bytes 1024 | tf_op jit(solution)/shard_map/pallas_call | solution.py:38
  43.0 1.6 %collective-permute-start.14 = (bf16[1024,128]{1,0:T(8,128)(2,1)S(1)}, bf16[1024,128]{1,0:T(8,128)(2,1)S(1)}, u32[]{:S(2)}, u32[]{:S(2)}) collective-permute-start(bf16[1024,128]{1,0:T(8,128)(2,1)S(1)} %get-tuple-element.116), channel_id=1, source_target_pairs={{0,2},{2,0},{4,6},{6,4},{8,10},{10,8},{12,14},{14,12},{1,3},{3,1},... | collective-permute-start | bytes 786440 | tf_op jit(solution)/shard_map/ppermute | solution.py:539
  44.6 1.2 %collective-permute-start.11 = (bf16[512,128]{1,0:T(8,128)(2,1)S(1)}, bf16[512,128]{1,0:T(8,128)(2,1)S(1)}, u32[]{:S(2)}, u32[]{:S(2)}) collective-permute-start(bf16[512,128]{1,0:T(8,128)(2,1)S(1)} %get-tuple-element.106), channel_id=1, source_target_pairs={{0,8},{2,10},{4,12},{6,14},{8,0},{10,2},{12,4},{14,6},{1,9},{3,11}... | collective-permute-start | bytes 393224 | tf_op jit(solution)/shard_map/ppermute | solution.py:539
  45.8 2.2 %shard_map.96 = (bf16[1024,256]{1,0:T(8,128)(2,1)S(1)}, f32[128,1024]{1,0:T(8,128)S(1)}) custom-call(s32[8,16]{1,0:T(8,128)S(1)} %get-tuple-element.79.lists.refs_0_, bf16[1024,256]{1,0:T(8,128)(2,1)S(1)} %get-tuple-element.78.qg.refs_1_, f32[8,1024]{1,0:T(8,128)S(1)} %get-tuple-element.100.lse_ref.refs_3_, f32[8,1024]{1,0:T(8,128)S(1)} %get-tuple-element.105.dot_ref, ...), custom_call_target="tpu_custom_call" | custom-call | flops 1024 | bytes 1024 | tf_op jit(solution)/shard_map/pallas_call | solution.py:38
  48.0 1.3 %collective-permute-done.13.refs_2_ = bf16[512,128]{1,0:T(8,128)(2,1)S(1)} collective-permute-done((bf16[512,128]{1,0:T(8,128)(2,1)S(1)}, bf16[512,128]{1,0:T(8,128)(2,1)S(1)}, u32[]{:S(2)}, u32[]{:S(2)}) %collective-permute-start.13) | collective-permute-done | bytes 131104 | tf_op jit(solution)/shard_map/ppermute | solution.py:539
  49.3 2.2 %shard_map.97 = (f32[1024,256]{1,0:T(8,128)S(1)}, f32[1024,256]{1,0:T(8,128)S(1)}, f32[128,1024]{1,0:T(8,128)S(1)}) custom-call(s32[8,16]{1,0:T(8,128)S(1)} %get-tuple-element.79.lists.refs_0_, bf16[1024,256]{1,0:T(8,128)(2,1)S(1)} %get-tuple-element.78.qg.refs_1_, f32[8,1024]{1,0:T(8,128)S(1)} %get-tuple-element.100.lse_ref.refs_3_, ...), custom_call_target="tpu_custom_call" | custom-call | flops 2684354560 | bytes 1024 | tf_op jit(solution)/shard_map/pallas_call | solution.py:38
  52.0 0.7 %collective-permute-start.17 = (bf16[1024,256]{1,0:T(8,128)(2,1)S(1)}, bf16[1024,256]{1,0:T(8,128)(2,1)S(1)}, u32[]{:S(2)}, u32[]{:S(2)}) collective-permute-start(bf16[1024,256]{1,0:T(8,128)(2,1)S(1)} %get-tuple-element.119), channel_id=1, source_target_pairs={{0,0},{2,2},{4,8},{6,10},{8,4},{10,6},{12,12},{14,14},{1,1},{3,3},... | collective-permute-start | bytes 1572872 | tf_op jit(solution)/shard_map/ppermute | solution.py:539
  52.7 3.0 %collective-permute-start.18 = (bf16[1024,256]{1,0:T(8,128)(2,1)S(1)}, bf16[1024,256]{1,0:T(8,128)(2,1)S(1)}, u32[]{:S(2)}, u32[]{:S(2)}) collective-permute-start(bf16[1024,256]{1,0:T(8,128)(2,1)S(1)} %get-tuple-element.118), channel_id=1, source_target_pairs={{0,4},{2,6},{4,0},{6,2},{8,12},{10,14},{12,8},{14,10},{1,5},{3,7},... | collective-permute-start | bytes 1572872 | tf_op jit(solution)/shard_map/ppermute | solution.py:539
  55.7 0.7 %shard_map.99.placed = f32[1024,256]{1,0:T(8,128)S(1)} custom-call(s32[8,16]{1,0:T(8,128)S(1)} %get-tuple-element.79.lists.refs_0_, bf16[512,128]{1,0:T(8,128)(2,1)S(1)} %collective-permute-done.11.refs_1_, bf16[512,128]{1,0:T(8,128)(2,1)S(1)} %collective-permute-done.13.refs_2_), custom_call_target="tpu_custom_call" | custom-call | flops 1024 | bytes 1024 | tf_op jit(solution)/shard_map/pallas_call | solution.py:38
  56.4 3.2 %shard_map.100 = (f32[1024,256]{1,0:T(8,128)S(1)}, bf16[512,256]{1,0:T(8,128)(2,1)S(1)}, bf16[512,256]{1,0:T(8,128)(2,1)S(1)}) custom-call(bf16[1024,256]{1,0:T(8,128)(2,1)S(1)} %get-tuple-element.78.qg.refs_1_, f32[8,1024]{1,0:T(8,128)S(1)} %get-tuple-element.100.lse_ref.refs_3_, f32[8,1024]{1,0:T(8,128)S(1)} %get-tuple-element.105.dot_ref, ...), custom_call_target="tpu_custom_call" | custom-call | flops 2684354560 | bytes 1024 | tf_op jit(solution)/shard_map/pallas_call | solution.py:38
  59.7 1.5 %collective-permute-done.15.came = bf16[512,256]{1,0:T(8,128)(2,1)S(1)} collective-permute-done((bf16[512,256]{1,0:T(8,128)(2,1)S(1)}, bf16[512,256]{1,0:T(8,128)(2,1)S(1)}, u32[]{:S(2)}, u32[]{:S(2)}) %collective-permute-start.15) | collective-permute-done | bytes 262176 | tf_op jit(solution)/shard_map/ppermute | solution.py:536
  61.2 0.9 %shard_map.101 = (bf16[512,256]{1,0:T(8,128)(2,1)}, bf16[512,256]{1,0:T(8,128)(2,1)}) custom-call(bf16[512,256]{1,0:T(8,128)(2,1)S(1)} %get-tuple-element.126.keep, bf16[512,256]{1,0:T(8,128)(2,1)S(1)} %collective-permute-done.15.came), custom_call_target="tpu_custom_call" | custom-call | flops 1024 | bytes 1024 | tf_op jit(solution)/shard_map/pallas_call | solution.py:38
  62.3 2.9 %collective-permute-done.18.came = bf16[1024,256]{1,0:T(8,128)(2,1)S(1)} collective-permute-done((bf16[1024,256]{1,0:T(8,128)(2,1)S(1)}, bf16[1024,256]{1,0:T(8,128)(2,1)S(1)}, u32[]{:S(2)}, u32[]{:S(2)}) %collective-permute-start.18) | collective-permute-done | bytes 524320 | tf_op jit(solution)/shard_map/ppermute | solution.py:539
  65.4 1.5 %collective-permute-done.19.came = bf16[512,256]{1,0:T(8,128)(2,1)S(1)} collective-permute-done((bf16[512,256]{1,0:T(8,128)(2,1)S(1)}, bf16[512,256]{1,0:T(8,128)(2,1)S(1)}, u32[]{:S(2)}, u32[]{:S(2)}) %collective-permute-start.19) | collective-permute-done | bytes 262176 | tf_op jit(solution)/shard_map/ppermute | solution.py:536
  67.0 0.9 %shard_map.104 = (bf16[512,256]{1,0:T(8,128)(2,1)}, bf16[512,256]{1,0:T(8,128)(2,1)}) custom-call(bf16[512,256]{1,0:T(8,128)(2,1)S(1)} %get-tuple-element.134.keep, bf16[512,256]{1,0:T(8,128)(2,1)S(1)} %collective-permute-done.19.came), custom_call_target="tpu_custom_call" | custom-call | flops 1024 | bytes 1024 | tf_op jit(solution)/shard_map/pallas_call | solution.py:38
  (29 shorter events, 2.7 us)
Async XLA Ops:
  0.6 1.9 %collective-permute-start = (bf16[512,256]{1,0:T(8,128)(2,1)}, bf16[512,256]{1,0:T(8,128)(2,1)S(1)}, u32[]{:S(2)}, u32[]{:S(2)}) collective-permute-start(bf16[512,256]{1,0:T(8,128)(2,1)} %k.1), channel_id=1, source_target_pairs={{0,1},{1,0},{2,3},{3,2},{4,5},{5,4},{6,7},{7,6},{8,9},{9,8},{10,11... | collective-permute-start | bytes 786440 | tf_op jit(solution)/shard_map/ppermute | solution.py:536
  1.2 2.1 %collective-permute-start.2 = (bf16[512,256]{1,0:T(8,128)(2,1)}, bf16[512,256]{1,0:T(8,128)(2,1)S(1)}, u32[]{:S(2)}, u32[]{:S(2)}) collective-permute-start(bf16[512,256]{1,0:T(8,128)(2,1)} %v.1), channel_id=1, source_target_pairs={{0,1},{1,0},{2,3},{3,2},{4,5},{5,4},{6,7},{7,6},{8,9},{9,8},{10,11... | collective-permute-start | bytes 786440 | tf_op jit(solution)/shard_map/ppermute | solution.py:536
  2.6 8.3 %collective-permute-start.1 = (bf16[1024,128]{1,0:T(8,128)(2,1)S(1)}, bf16[1024,128]{1,0:T(8,128)(2,1)S(1)}, u32[]{:S(2)}, u32[]{:S(2)}) collective-permute-start(bf16[1024,128]{1,0:T(8,128)(2,1)S(1)} %shard_map.85.keys), channel_id=1, source_target_pairs={{0,0},{2,2},{4,8},{6,10},{8,4},{10,6},{12,12},{14,14},{1,1},{3,3},... | collective-permute-start | bytes 786440 | tf_op jit(solution)/shard_map/ppermute | solution.py:539
  3.4 8.2 %collective-permute-start.3 = (bf16[512,256]{1,0:T(8,128)(2,1)S(1)}, bf16[512,256]{1,0:T(8,128)(2,1)S(1)}, u32[]{:S(2)}, u32[]{:S(2)}) collective-permute-start(bf16[512,256]{1,0:T(8,128)(2,1)S(1)} %get-tuple-element.76), channel_id=1, source_target_pairs={{0,1},{1,0},{2,3},{3,2},{4,5},{5,4},{6,7},{7,6},{8,9},{9,8},{10,11... | collective-permute-start | bytes 786440 | tf_op jit(solution)/shard_map/ppermute | solution.py:536
  3.9 17.7 %collective-permute-start.7 = (bf16[1024,256]{1,0:T(8,128)(2,1)S(1)}, bf16[1024,256]{1,0:T(8,128)(2,1)S(1)}, u32[]{:S(2)}, u32[]{:S(2)}) collective-permute-start(bf16[1024,256]{1,0:T(8,128)(2,1)S(1)} %get-tuple-element.84.kv), channel_id=1, source_target_pairs={{0,2},{2,0},{4,6},{6,4},{8,10},{10,8},{12,14},{14,12},{1,3},{3,1},... | collective-permute-start | bytes 1572872 | tf_op jit(solution)/shard_map/ppermute | solution.py:539
  6.5 11.5 %collective-permute-start.6 = (bf16[1024,128]{1,0:T(8,128)(2,1)S(1)}, bf16[1024,128]{1,0:T(8,128)(2,1)S(1)}, u32[]{:S(2)}, u32[]{:S(2)}) collective-permute-start(bf16[1024,128]{1,0:T(8,128)(2,1)S(1)} %shard_map.85.keys), channel_id=1, source_target_pairs={{0,4},{2,6},{4,0},{6,2},{8,12},{10,14},{12,8},{14,10},{1,5},{3,7},... | collective-permute-start | bytes 786440 | tf_op jit(solution)/shard_map/ppermute | solution.py:539
  10.9 14.2 %collective-permute-start.5 = (bf16[1024,128]{1,0:T(8,128)(2,1)S(1)}, bf16[1024,128]{1,0:T(8,128)(2,1)S(1)}, u32[]{:S(2)}, u32[]{:S(2)}) collective-permute-start(bf16[1024,128]{1,0:T(8,128)(2,1)S(1)} %get-tuple-element.80), channel_id=1, source_target_pairs={{0,4},{2,6},{4,0},{6,2},{8,12},{10,14},{12,8},{14,10},{1,5},{3,7},... | collective-permute-start | bytes 786440 | tf_op jit(solution)/shard_map/ppermute | solution.py:539
  10.9 14.2 %collective-permute-start.4 = (bf16[1024,128]{1,0:T(8,128)(2,1)S(1)}, bf16[1024,128]{1,0:T(8,128)(2,1)S(1)}, u32[]{:S(2)}, u32[]{:S(2)}) collective-permute-start(bf16[1024,128]{1,0:T(8,128)(2,1)S(1)} %get-tuple-element.80), channel_id=1, source_target_pairs={{0,0},{2,2},{4,8},{6,10},{8,4},{10,6},{12,12},{14,14},{1,1},{3,3},... | collective-permute-start | bytes 786440 | tf_op jit(solution)/shard_map/ppermute | solution.py:539
  18.7 7.9 %collective-permute-start.8 = (bf16[1024,128]{1,0:T(8,128)(2,1)S(1)}, bf16[1024,128]{1,0:T(8,128)(2,1)S(1)}, u32[]{:S(2)}, u32[]{:S(2)}) collective-permute-start(bf16[1024,128]{1,0:T(8,128)(2,1)S(1)} %shard_map.88), channel_id=1, source_target_pairs={{0,2},{2,0},{4,6},{6,4},{8,10},{10,8},{12,14},{14,12},{1,3},{3,1},... | collective-permute-start | bytes 786440 | tf_op jit(solution)/shard_map/ppermute | solution.py:539
  19.2 16.5 %collective-permute-start.9 = (bf16[512,256]{1,0:T(8,128)(2,1)S(1)}, bf16[512,256]{1,0:T(8,128)(2,1)S(1)}, u32[]{:S(2)}, u32[]{:S(2)}) collective-permute-start(bf16[512,256]{1,0:T(8,128)(2,1)S(1)} %shard_map.89), channel_id=1, source_target_pairs={{0,8},{2,10},{4,12},{6,14},{8,0},{10,2},{12,4},{14,6},{1,9},{3,11}... | collective-permute-start | bytes 786440 | tf_op jit(solution)/shard_map/ppermute | solution.py:539
  25.3 15.4 %collective-permute-start.10 = (bf16[1024,128]{1,0:T(8,128)(2,1)S(1)}, bf16[1024,128]{1,0:T(8,128)(2,1)S(1)}, u32[]{:S(2)}, u32[]{:S(2)}) collective-permute-start(bf16[1024,128]{1,0:T(8,128)(2,1)S(1)} %shard_map.91), channel_id=1, source_target_pairs={{0,2},{2,0},{4,6},{6,4},{8,10},{10,8},{12,14},{14,12},{1,3},{3,1},... | collective-permute-start | bytes 786440 | tf_op jit(solution)/shard_map/ppermute | solution.py:539
  37.9 11.4 %collective-permute-start.12 = (bf16[1024,128]{1,0:T(8,128)(2,1)S(1)}, bf16[1024,128]{1,0:T(8,128)(2,1)S(1)}, u32[]{:S(2)}, u32[]{:S(2)}) collective-permute-start(bf16[1024,128]{1,0:T(8,128)(2,1)S(1)} %get-tuple-element.109), channel_id=1, source_target_pairs={{0,2},{2,0},{4,6},{6,4},{8,10},{10,8},{12,14},{14,12},{1,3},{3,1},... | collective-permute-start | bytes 786440 | tf_op jit(solution)/shard_map/ppermute | solution.py:539
  39.5 9.8 %collective-permute-start.13 = (bf16[512,128]{1,0:T(8,128)(2,1)S(1)}, bf16[512,128]{1,0:T(8,128)(2,1)S(1)}, u32[]{:S(2)}, u32[]{:S(2)}) collective-permute-start(bf16[512,128]{1,0:T(8,128)(2,1)S(1)} %get-tuple-element.110), channel_id=1, source_target_pairs={{0,8},{2,10},{4,12},{6,14},{8,0},{10,2},{12,4},{14,6},{1,9},{3,11}... | collective-permute-start | bytes 393224 | tf_op jit(solution)/shard_map/ppermute | solution.py:539
  43.0 8.5 %collective-permute-start.14 = (bf16[1024,128]{1,0:T(8,128)(2,1)S(1)}, bf16[1024,128]{1,0:T(8,128)(2,1)S(1)}, u32[]{:S(2)}, u32[]{:S(2)}) collective-permute-start(bf16[1024,128]{1,0:T(8,128)(2,1)S(1)} %get-tuple-element.116), channel_id=1, source_target_pairs={{0,2},{2,0},{4,6},{6,4},{8,10},{10,8},{12,14},{14,12},{1,3},{3,1},... | collective-permute-start | bytes 786440 | tf_op jit(solution)/shard_map/ppermute | solution.py:539
  44.6 11.1 %collective-permute-start.11 = (bf16[512,128]{1,0:T(8,128)(2,1)S(1)}, bf16[512,128]{1,0:T(8,128)(2,1)S(1)}, u32[]{:S(2)}, u32[]{:S(2)}) collective-permute-start(bf16[512,128]{1,0:T(8,128)(2,1)S(1)} %get-tuple-element.106), channel_id=1, source_target_pairs={{0,8},{2,10},{4,12},{6,14},{8,0},{10,2},{12,4},{14,6},{1,9},{3,11}... | collective-permute-start | bytes 393224 | tf_op jit(solution)/shard_map/ppermute | solution.py:539
  51.5 10.5 %collective-permute-start.16 = (bf16[1024,256]{1,0:T(8,128)(2,1)S(1)}, bf16[1024,256]{1,0:T(8,128)(2,1)S(1)}, u32[]{:S(2)}, u32[]{:S(2)}) collective-permute-start(bf16[1024,256]{1,0:T(8,128)(2,1)S(1)} %get-tuple-element.133), channel_id=1, source_target_pairs={{0,2},{2,0},{4,6},{6,4},{8,10},{10,8},{12,14},{14,12},{1,3},{3,1},... | collective-permute-start | bytes 1572872 | tf_op jit(solution)/shard_map/ppermute | solution.py:539
  52.0 10.1 %collective-permute-start.17 = (bf16[1024,256]{1,0:T(8,128)(2,1)S(1)}, bf16[1024,256]{1,0:T(8,128)(2,1)S(1)}, u32[]{:S(2)}, u32[]{:S(2)}) collective-permute-start(bf16[1024,256]{1,0:T(8,128)(2,1)S(1)} %get-tuple-element.119), channel_id=1, source_target_pairs={{0,0},{2,2},{4,8},{6,10},{8,4},{10,6},{12,12},{14,14},{1,1},{3,3},... | collective-permute-start | bytes 1572872 | tf_op jit(solution)/shard_map/ppermute | solution.py:539
  52.7 12.5 %collective-permute-start.18 = (bf16[1024,256]{1,0:T(8,128)(2,1)S(1)}, bf16[1024,256]{1,0:T(8,128)(2,1)S(1)}, u32[]{:S(2)}, u32[]{:S(2)}) collective-permute-start(bf16[1024,256]{1,0:T(8,128)(2,1)S(1)} %get-tuple-element.118), channel_id=1, source_target_pairs={{0,4},{2,6},{4,0},{6,2},{8,12},{10,14},{12,8},{14,10},{1,5},{3,7},... | collective-permute-start | bytes 1572872 | tf_op jit(solution)/shard_map/ppermute | solution.py:539
  59.6 1.6 %collective-permute-start.15 = (bf16[512,256]{1,0:T(8,128)(2,1)S(1)}, bf16[512,256]{1,0:T(8,128)(2,1)S(1)}, u32[]{:S(2)}, u32[]{:S(2)}) collective-permute-start(bf16[512,256]{1,0:T(8,128)(2,1)S(1)} %get-tuple-element.127), channel_id=1, source_target_pairs={{0,1},{1,0},{2,3},{3,2},{4,5},{5,4},{6,7},{7,6},{8,9},{9,8},{10,11... | collective-permute-start | bytes 786440 | tf_op jit(solution)/shard_map/ppermute | solution.py:536
  65.4 1.6 %collective-permute-start.19 = (bf16[512,256]{1,0:T(8,128)(2,1)S(1)}, bf16[512,256]{1,0:T(8,128)(2,1)S(1)}, u32[]{:S(2)}, u32[]{:S(2)}) collective-permute-start(bf16[512,256]{1,0:T(8,128)(2,1)S(1)} %get-tuple-element.135), channel_id=1, source_target_pairs={{0,1},{1,0},{2,3},{3,2},{4,5},{5,4},{6,7},{7,6},{8,9},{9,8},{10,11... | collective-permute-start | bytes 786440 | tf_op jit(solution)/shard_map/ppermute | solution.py:536

commit v9 on v8

--- a/solution.py
+++ b/solution.py
@@ -554,7 +554,7 @@
     )
     (keys,) = call(keys_kernel, (k_own, k_came), [frame_one])
     values, kv = call(values_kernel, (keys, v_own, v_came), [frame_one, frame_two])
-    qg_send, _ = lax.optimization_barrier((qg_send, kv))
+    qg_send, _ = lax.optimization_barrier((qg_send, keys))
     y_k = swapped(keys, y_swap)
     z_k = swapped(keys, z_swap)
     a_kv = swapped(kv, near_swap)

time: 68.1 us -> 63.6 us (0.934)
  waiting for transfers between devices: 20.1 us -> 16.6 us
  starting transfers between devices: 23.1 us -> 22.2 us
    ppermute x15, waiting for transfers between devices: 17 us -> 13.5 us  [swapped(): return lax.ppermute(value, 'tm', swap.pairs)]
    ppermute x15, starting transfers between devices: 21.9 us -> 21 us  [swapped(): return lax.ppermute(value, 'tm', swap.pairs)]
  transfers between devices with their start and end apart: 20 -> 20, of which waited for: 6 -> 8; matrix products, arithmetic and copies ran while one was open for 0% -> 0% of each run, Pallas kernels for 34% -> 36%
where the time goes in v9:
time: 63.6 us; the launch traced here: 63.3 us
  Pallas kernels  23.7 us (37%)
  starting transfers between devices  22.2 us (35%)
  waiting for transfers between devices  16.6 us (26%)
  between operations  0.85 us (1%)
    pallas_call x21, Pallas kernels, call(): pl.pallas_call(kernel, out_shape=out_shape, in_specs=[scalars if a.dtype...  23.7 us
    ppermute x15, starting transfers between devices, swapped(): return lax.ppermute(value, 'tm', swap.pairs)  21 us
    ppermute x15, waiting for transfers between devices, swapped(): return lax.ppermute(value, 'tm', swap.pairs)  13.5 us
    ppermute x5, waiting for transfers between devices, across(): return lax.ppermute(value, 'space', [(0, 1), (1, 0)])  3.06 us
  transfers between devices with their start and end apart: 20, of which 8 were waited for; matrix products, arithmetic and copies ran while one was open for 0% of the time, Pallas kernels for 36%

profile of v9, /device:TPU:0, one launch (start us, length us, event | category | flops | bytes accessed | tf_op | source)
XLA Modules:
  0.0 63.3 jit_solution(16784649854873249937)
XLA Ops:
  1.2 1.3 %shard_map.84 = (bf16[512,128]{1,0:T(8,128)(2,1)S(1)}, bf16[512,128]{1,0:T(8,128)(2,1)S(1)}, bf16[512,256]{1,0:T(8,128)(2,1)S(1)}, bf16[512,256]{1,0:T(8,128)(2,1)S(1)}, s32[8,16]{1,0:T(8,128)S(1)}) custom-call(bf16[512,256]{1,0:T(8,128)(2,1)} %k.1, bf16[512,256]{1,0:T(8,128)(2,1)} %v.1, bf16[512,256]{1,0:T(8,128)(2,1)} %q.1, bf16[512,256]{1,0:T(8,128)(2,1)} %g.1, ...), custom_call_target="tpu_custom_call" | custom-call | flops 1024 | bytes 1024 | tf_op jit(solution)/shard_map/pallas_call | solution.py:38
  3.1 0.7 %collective-permute-start.1 = (bf16[1024,128]{1,0:T(8,128)(2,1)S(1)}, bf16[1024,128]{1,0:T(8,128)(2,1)S(1)}, u32[]{:S(2)}, u32[]{:S(2)}) collective-permute-start(bf16[1024,128]{1,0:T(8,128)(2,1)S(1)} %shard_map.85.keys), channel_id=1, source_target_pairs={{0,0},{2,2},{4,8},{6,10},{8,4},{10,6},{12,12},{14,14},{1,1},{3,3},... | collective-permute-start | bytes 786440 | tf_op jit(solution)/shard_map/ppermute | solution.py:539
  3.9 2.7 %collective-permute-start.7 = (bf16[1024,256]{1,0:T(8,128)(2,1)S(1)}, bf16[1024,256]{1,0:T(8,128)(2,1)S(1)}, u32[]{:S(2)}, u32[]{:S(2)}) collective-permute-start(bf16[1024,256]{1,0:T(8,128)(2,1)S(1)} %get-tuple-element.84.kv), channel_id=1, source_target_pairs={{0,2},{2,0},{4,6},{6,4},{8,10},{10,8},{12,14},{14,12},{1,3},{3,1},... | collective-permute-start | bytes 1572872 | tf_op jit(solution)/shard_map/ppermute | solution.py:539
  6.5 4.4 %collective-permute-start.6 = (bf16[1024,128]{1,0:T(8,128)(2,1)S(1)}, bf16[1024,128]{1,0:T(8,128)(2,1)S(1)}, u32[]{:S(2)}, u32[]{:S(2)}) collective-permute-start(bf16[1024,128]{1,0:T(8,128)(2,1)S(1)} %shard_map.85.keys), channel_id=1, source_target_pairs={{0,4},{2,6},{4,0},{6,2},{8,12},{10,14},{12,8},{14,10},{1,5},{3,7},... | collective-permute-start | bytes 786440 | tf_op jit(solution)/shard_map/ppermute | solution.py:539
  11.0 0.7 %collective-permute-start.4 = (bf16[1024,128]{1,0:T(8,128)(2,1)S(1)}, bf16[1024,128]{1,0:T(8,128)(2,1)S(1)}, u32[]{:S(2)}, u32[]{:S(2)}) collective-permute-start(bf16[1024,128]{1,0:T(8,128)(2,1)S(1)} %get-tuple-element.79), channel_id=1, source_target_pairs={{0,0},{2,2},{4,8},{6,10},{8,4},{10,6},{12,12},{14,14},{1,1},{3,3},... | collective-permute-start | bytes 786440 | tf_op jit(solution)/shard_map/ppermute | solution.py:539
  11.8 6.3 %collective-permute-done.6.z.z_k = bf16[1024,128]{1,0:T(8,128)(2,1)S(1)} collective-permute-done((bf16[1024,128]{1,0:T(8,128)(2,1)S(1)}, bf16[1024,128]{1,0:T(8,128)(2,1)S(1)}, u32[]{:S(2)}, u32[]{:S(2)}) %collective-permute-start.6) | collective-permute-done | bytes 262176 | tf_op jit(solution)/shard_map/ppermute | solution.py:539
  18.1 0.6 %shard_map.89 = bf16[512,256]{1,0:T(8,128)(2,1)S(1)} custom-call(s32[8,16]{1,0:T(8,128)S(1)} %get-tuple-element.77.lists.refs_0_, bf16[1024,256]{1,0:T(8,128)(2,1)S(1)} %get-tuple-element.84.kv), custom_call_target="tpu_custom_call" | custom-call | flops 1024 | bytes 1024 | tf_op jit(solution)/shard_map/pallas_call | solution.py:38
  18.7 0.6 collective-permute-start.8
  19.3 1.9 %collective-permute-start.9 = (bf16[512,256]{1,0:T(8,128)(2,1)S(1)}, bf16[512,256]{1,0:T(8,128)(2,1)S(1)}, u32[]{:S(2)}, u32[]{:S(2)}) collective-permute-start(bf16[512,256]{1,0:T(8,128)(2,1)S(1)} %shard_map.89), channel_id=1, source_target_pairs={{0,8},{2,10},{4,12},{6,14},{8,0},{10,2},{12,4},{14,6},{1,9},{3,11}... | collective-permute-start | bytes 786440 | tf_op jit(solution)/shard_map/ppermute | solution.py:539
  21.3 3.5 %shard_map.90 = (f32[8,1024]{1,0:T(8,128)S(1)}, f32[128,1024]{1,0:T(8,128)S(1)}) custom-call(s32[8,16]{1,0:T(8,128)S(1)} %get-tuple-element.77.lists.refs_0_, bf16[1024,256]{1,0:T(8,128)(2,1)S(1)} %get-tuple-element.76.qg.refs_1_, bf16[1024,256]{1,0:T(8,128)(2,1)S(1)} %get-tuple-element.84.kv, bf16[1024,256]{1,0:T(8,128)(2,1)S(1)} %collective-permute-done.7.a_kv), custom_call_target="tpu_custom_call" | custom-call | flops 1024 | bytes 1024 | tf_op jit(solution)/shard_map/pallas_call | solution.py:38
  25.3 1.3 %collective-permute-start.10 = (bf16[1024,128]{1,0:T(8,128)(2,1)S(1)}, bf16[1024,128]{1,0:T(8,128)(2,1)S(1)}, u32[]{:S(2)}, u32[]{:S(2)}) collective-permute-start(bf16[1024,128]{1,0:T(8,128)(2,1)S(1)} %shard_map.91), channel_id=1, source_target_pairs={{0,2},{2,0},{4,6},{6,4},{8,10},{10,8},{12,14},{14,12},{1,3},{3,1},... | collective-permute-start | bytes 786440 | tf_op jit(solution)/shard_map/ppermute | solution.py:539
  26.6 2.6 %shard_map.92 = (f32[8,1024]{1,0:T(8,128)S(1)}, f32[128,1024]{1,0:T(8,128)S(1)}, f32[2,512,512]{2,1,0:T(8,128)S(1)}) custom-call(s32[8,16]{1,0:T(8,128)S(1)} %get-tuple-element.77.lists.refs_0_, bf16[1024,256]{1,0:T(8,128)(2,1)S(1)} %get-tuple-element.76.qg.refs_1_, f32[8,1024]{1,0:T(8,128)S(1)} %get-tuple-element.93.stat, ...), custom_call_target="tpu_custom_call" | custom-call | flops 1024 | bytes 1024 | tf_op jit(solution)/shard_map/pallas_call | solution.py:38
  29.2 3.8 %collective-permute-done.9.refs_0_.refs_8_ = bf16[512,256]{1,0:T(8,128)(2,1)S(1)} collective-permute-done((bf16[512,256]{1,0:T(8,128)(2,1)S(1)}, bf16[512,256]{1,0:T(8,128)(2,1)S(1)}, u32[]{:S(2)}, u32[]{:S(2)}) %collective-permute-start.9) | collective-permute-done | bytes 262176 | tf_op jit(solution)/shard_map/ppermute | solution.py:539
  33.1 1.0 %shard_map.93 = (f32[8,1024]{1,0:T(8,128)S(1)}, f32[128,1024]{1,0:T(8,128)S(1)}, bf16[512,128]{1,0:T(8,128)(2,1)S(1)}) custom-call(bf16[1024,256]{1,0:T(8,128)(2,1)S(1)} %get-tuple-element.76.qg.refs_1_, f32[8,1024]{1,0:T(8,128)S(1)} %get-tuple-element.95.stat, f32[128,1024]{1,0:T(8,128)S(1)} %get-tuple-element.98.acc, ...), custom_call_target="tpu_custom_call" | custom-call | flops 1024 | bytes 1024 | tf_op jit(solution)/shard_map/pallas_call | solution.py:38
  34.1 1.1 %shard_map.94 = (bf16[1024,128]{1,0:T(8,128)(2,1)S(1)}, f32[2,512,512]{2,1,0:T(8,128)S(1)}) custom-call(s32[8,16]{1,0:T(8,128)S(1)} %get-tuple-element.77.lists.refs_0_, bf16[1024,256]{1,0:T(8,128)(2,1)S(1)} %get-tuple-element.76.qg.refs_1_, f32[8,1024]{1,0:T(8,128)S(1)} %get-tuple-element.100.lse_ref.refs_3_, f32[2,512,512]{2,1,0:T(8,128)S(1)} %get-tuple-element.102.s_ref), custom_call_target="tpu_custom_call" | custom-call | flops 1024 | bytes 1024 | tf_op jit(solution)/shard_map/pallas_call | solution.py:38
  35.2 1.1 %collective-permute-start.12 = (bf16[1024,128]{1,0:T(8,128)(2,1)S(1)}, bf16[1024,128]{1,0:T(8,128)(2,1)S(1)}, u32[]{:S(2)}, u32[]{:S(2)}) collective-permute-start(bf16[1024,128]{1,0:T(8,128)(2,1)S(1)} %get-tuple-element.109), channel_id=1, source_target_pairs={{0,2},{2,0},{4,6},{6,4},{8,10},{10,8},{12,14},{14,12},{1,3},{3,1},... | collective-permute-start | bytes 786440 | tf_op jit(solution)/shard_map/ppermute | solution.py:539
  36.3 2.3 %shard_map.95 = (bf16[128,1024]{1,0:T(8,128)(2,1)S(1)}, f32[8,1024]{1,0:T(8,128)S(1)}, bf16[1024,128]{1,0:T(8,128)(2,1)S(1)}, f32[128,1024]{1,0:T(8,128)S(1)}, bf16[512,128]{1,0:T(8,128)(2,1)S(1)}) custom-call(s32[8,16]{1,0:T(8,128)S(1)} %get-tuple-element.77.lists.refs_0_, bf16[1024,256]{1,0:T(8,128)(2,1)S(1)} %get-tuple-element.76.qg.refs_1_, ...), custom_call_target="tpu_custom_call" | custom-call | flops 1024 | bytes 1024 | tf_op jit(solution)/shard_map/pallas_call | solution.py:38
  38.6 1.1 %collective-permute-start.14 = (bf16[1024,128]{1,0:T(8,128)(2,1)S(1)}, bf16[1024,128]{1,0:T(8,128)(2,1)S(1)}, u32[]{:S(2)}, u32[]{:S(2)}) collective-permute-start(bf16[1024,128]{1,0:T(8,128)(2,1)S(1)} %get-tuple-element.116), channel_id=1, source_target_pairs={{0,2},{2,0},{4,6},{6,4},{8,10},{10,8},{12,14},{14,12},{1,3},{3,1},... | collective-permute-start | bytes 786440 | tf_op jit(solution)/shard_map/ppermute | solution.py:539
  39.6 2.9 %collective-permute-start.11 = (bf16[512,128]{1,0:T(8,128)(2,1)S(1)}, bf16[512,128]{1,0:T(8,128)(2,1)S(1)}, u32[]{:S(2)}, u32[]{:S(2)}) collective-permute-start(bf16[512,128]{1,0:T(8,128)(2,1)S(1)} %get-tuple-element.106), channel_id=1, source_target_pairs={{0,8},{2,10},{4,12},{6,14},{8,0},{10,2},{12,4},{14,6},{1,9},{3,11}... | collective-permute-start | bytes 393224 | tf_op jit(solution)/shard_map/ppermute | solution.py:539
  42.6 2.2 %shard_map.96 = (bf16[1024,256]{1,0:T(8,128)(2,1)S(1)}, f32[128,1024]{1,0:T(8,128)S(1)}) custom-call(s32[8,16]{1,0:T(8,128)S(1)} %get-tuple-element.77.lists.refs_0_, bf16[1024,256]{1,0:T(8,128)(2,1)S(1)} %get-tuple-element.76.qg.refs_1_, f32[8,1024]{1,0:T(8,128)S(1)} %get-tuple-element.100.lse_ref.refs_3_, f32[8,1024]{1,0:T(8,128)S(1)} %get-tuple-element.105.dot_ref, ...), custom_call_target="tpu_custom_call" | custom-call | flops 1024 | bytes 1024 | tf_op jit(solution)/shard_map/pallas_call | solution.py:38
  44.8 1.1 %collective-permute-done.13.refs_2_ = bf16[512,128]{1,0:T(8,128)(2,1)S(1)} collective-permute-done((bf16[512,128]{1,0:T(8,128)(2,1)S(1)}, bf16[512,128]{1,0:T(8,128)(2,1)S(1)}, u32[]{:S(2)}, u32[]{:S(2)}) %collective-permute-start.13) | collective-permute-done | bytes 131104 | tf_op jit(solution)/shard_map/ppermute | solution.py:539
  46.0 2.2 %shard_map.97 = (f32[1024,256]{1,0:T(8,128)S(1)}, f32[1024,256]{1,0:T(8,128)S(1)}, f32[128,1024]{1,0:T(8,128)S(1)}) custom-call(s32[8,16]{1,0:T(8,128)S(1)} %get-tuple-element.77.lists.refs_0_, bf16[1024,256]{1,0:T(8,128)(2,1)S(1)} %get-tuple-element.76.qg.refs_1_, f32[8,1024]{1,0:T(8,128)S(1)} %get-tuple-element.100.lse_ref.refs_3_, ...), custom_call_target="tpu_custom_call" | custom-call | flops 2684354560 | bytes 1024 | tf_op jit(solution)/shard_map/pallas_call | solution.py:38
  48.2 0.7 %collective-permute-start.16 = (bf16[1024,256]{1,0:T(8,128)(2,1)S(1)}, bf16[1024,256]{1,0:T(8,128)(2,1)S(1)}, u32[]{:S(2)}, u32[]{:S(2)}) collective-permute-start(bf16[1024,256]{1,0:T(8,128)(2,1)S(1)} %get-tuple-element.133), channel_id=1, source_target_pairs={{0,2},{2,0},{4,6},{6,4},{8,10},{10,8},{12,14},{14,12},{1,3},{3,1},... | collective-permute-start | bytes 1572872 | tf_op jit(solution)/shard_map/ppermute | solution.py:539
  49.1 0.7 %collective-permute-start.17 = (bf16[1024,256]{1,0:T(8,128)(2,1)S(1)}, bf16[1024,256]{1,0:T(8,128)(2,1)S(1)}, u32[]{:S(2)}, u32[]{:S(2)}) collective-permute-start(bf16[1024,256]{1,0:T(8,128)(2,1)S(1)} %get-tuple-element.119), channel_id=1, source_target_pairs={{0,0},{2,2},{4,8},{6,10},{8,4},{10,6},{12,12},{14,14},{1,1},{3,3},... | collective-permute-start | bytes 1572872 | tf_op jit(solution)/shard_map/ppermute | solution.py:539
  49.8 2.3 %collective-permute-start.18 = (bf16[1024,256]{1,0:T(8,128)(2,1)S(1)}, bf16[1024,256]{1,0:T(8,128)(2,1)S(1)}, u32[]{:S(2)}, u32[]{:S(2)}) collective-permute-start(bf16[1024,256]{1,0:T(8,128)(2,1)S(1)} %get-tuple-element.118), channel_id=1, source_target_pairs={{0,4},{2,6},{4,0},{6,2},{8,12},{10,14},{12,8},{14,10},{1,5},{3,7},... | collective-permute-start | bytes 1572872 | tf_op jit(solution)/shard_map/ppermute | solution.py:539
  52.1 0.7 %shard_map.99.placed = f32[1024,256]{1,0:T(8,128)S(1)} custom-call(s32[8,16]{1,0:T(8,128)S(1)} %get-tuple-element.77.lists.refs_0_, bf16[512,128]{1,0:T(8,128)(2,1)S(1)} %collective-permute-done.11.refs_1_, bf16[512,128]{1,0:T(8,128)(2,1)S(1)} %collective-permute-done.13.refs_2_), custom_call_target="tpu_custom_call" | custom-call | flops 1024 | bytes 1024 | tf_op jit(solution)/shard_map/pallas_call | solution.py:38
  52.9 3.2 %shard_map.100 = (f32[1024,256]{1,0:T(8,128)S(1)}, bf16[512,256]{1,0:T(8,128)(2,1)S(1)}, bf16[512,256]{1,0:T(8,128)(2,1)S(1)}) custom-call(bf16[1024,256]{1,0:T(8,128)(2,1)S(1)} %get-tuple-element.76.qg.refs_1_, f32[8,1024]{1,0:T(8,128)S(1)} %get-tuple-element.100.lse_ref.refs_3_, f32[8,1024]{1,0:T(8,128)S(1)} %get-tuple-element.105.dot_ref, ...), custom_call_target="tpu_custom_call" | custom-call | flops 2684354560 | bytes 1024 | tf_op jit(solution)/shard_map/pallas_call | solution.py:38
  56.1 1.5 %collective-permute-done.15.came = bf16[512,256]{1,0:T(8,128)(2,1)S(1)} collective-permute-done((bf16[512,256]{1,0:T(8,128)(2,1)S(1)}, bf16[512,256]{1,0:T(8,128)(2,1)S(1)}, u32[]{:S(2)}, u32[]{:S(2)}) %collective-permute-start.15) | collective-permute-done | bytes 262176 | tf_op jit(solution)/shard_map/ppermute | solution.py:536
  57.7 0.9 %shard_map.101 = (bf16[512,256]{1,0:T(8,128)(2,1)}, bf16[512,256]{1,0:T(8,128)(2,1)}) custom-call(bf16[512,256]{1,0:T(8,128)(2,1)S(1)} %get-tuple-element.126.keep, bf16[512,256]{1,0:T(8,128)(2,1)S(1)} %collective-permute-done.15.came), custom_call_target="tpu_custom_call" | custom-call | flops 1024 | bytes 1024 | tf_op jit(solution)/shard_map/pallas_call | solution.py:38
  59.3 1.4 %collective-permute-done.18.came = bf16[1024,256]{1,0:T(8,128)(2,1)S(1)} collective-permute-done((bf16[1024,256]{1,0:T(8,128)(2,1)S(1)}, bf16[1024,256]{1,0:T(8,128)(2,1)S(1)}, u32[]{:S(2)}, u32[]{:S(2)}) %collective-permute-start.18) | collective-permute-done | bytes 524320 | tf_op jit(solution)/shard_map/ppermute | solution.py:539
  60.9 1.5 %collective-permute-done.19.came = bf16[512,256]{1,0:T(8,128)(2,1)S(1)} collective-permute-done((bf16[512,256]{1,0:T(8,128)(2,1)S(1)}, bf16[512,256]{1,0:T(8,128)(2,1)S(1)}, u32[]{:S(2)}, u32[]{:S(2)}) %collective-permute-start.19) | collective-permute-done | bytes 262176 | tf_op jit(solution)/shard_map/ppermute | solution.py:536
  62.5 0.9 %shard_map.104 = (bf16[512,256]{1,0:T(8,128)(2,1)}, bf16[512,256]{1,0:T(8,128)(2,1)}) custom-call(bf16[512,256]{1,0:T(8,128)(2,1)S(1)} %get-tuple-element.134.keep, bf16[512,256]{1,0:T(8,128)(2,1)S(1)} %collective-permute-done.19.came), custom_call_target="tpu_custom_call" | custom-call | flops 1024 | bytes 1024 | tf_op jit(solution)/shard_map/pallas_call | solution.py:38
  (29 shorter events, 3.2 us)
Async XLA Ops:
  0.6 1.9 %collective-permute-start = (bf16[512,256]{1,0:T(8,128)(2,1)}, bf16[512,256]{1,0:T(8,128)(2,1)S(1)}, u32[]{:S(2)}, u32[]{:S(2)}) collective-permute-start(bf16[512,256]{1,0:T(8,128)(2,1)} %k.1), channel_id=1, source_target_pairs={{0,1},{1,0},{2,3},{3,2},{4,5},{5,4},{6,7},{7,6},{8,9},{9,8},{10,11... | collective-permute-start | bytes 786440 | tf_op jit(solution)/shard_map/ppermute | solution.py:536
  1.2 2.6 %collective-permute-start.3 = (bf16[512,256]{1,0:T(8,128)(2,1)}, bf16[512,256]{1,0:T(8,128)(2,1)S(1)}, u32[]{:S(2)}, u32[]{:S(2)}) collective-permute-start(bf16[512,256]{1,0:T(8,128)(2,1)} %v.1), channel_id=1, source_target_pairs={{0,1},{1,0},{2,3},{3,2},{4,5},{5,4},{6,7},{7,6},{8,9},{9,8},{10,11... | collective-permute-start | bytes 786440 | tf_op jit(solution)/shard_map/ppermute | solution.py:536
  2.6 8.4 %collective-permute-start.2 = (bf16[512,256]{1,0:T(8,128)(2,1)S(1)}, bf16[512,256]{1,0:T(8,128)(2,1)S(1)}, u32[]{:S(2)}, u32[]{:S(2)}) collective-permute-start(bf16[512,256]{1,0:T(8,128)(2,1)S(1)} %get-tuple-element.74), channel_id=1, source_target_pairs={{0,1},{1,0},{2,3},{3,2},{4,5},{5,4},{6,7},{7,6},{8,9},{9,8},{10,11... | collective-permute-start | bytes 786440 | tf_op jit(solution)/shard_map/ppermute | solution.py:536
  3.1 8.6 %collective-permute-start.1 = (bf16[1024,128]{1,0:T(8,128)(2,1)S(1)}, bf16[1024,128]{1,0:T(8,128)(2,1)S(1)}, u32[]{:S(2)}, u32[]{:S(2)}) collective-permute-start(bf16[1024,128]{1,0:T(8,128)(2,1)S(1)} %shard_map.85.keys), channel_id=1, source_target_pairs={{0,0},{2,2},{4,8},{6,10},{8,4},{10,6},{12,12},{14,14},{1,1},{3,3},... | collective-permute-start | bytes 786440 | tf_op jit(solution)/shard_map/ppermute | solution.py:539
  3.9 17.4 %collective-permute-start.7 = (bf16[1024,256]{1,0:T(8,128)(2,1)S(1)}, bf16[1024,256]{1,0:T(8,128)(2,1)S(1)}, u32[]{:S(2)}, u32[]{:S(2)}) collective-permute-start(bf16[1024,256]{1,0:T(8,128)(2,1)S(1)} %get-tuple-element.84.kv), channel_id=1, source_target_pairs={{0,2},{2,0},{4,6},{6,4},{8,10},{10,8},{12,14},{14,12},{1,3},{3,1},... | collective-permute-start | bytes 1572872 | tf_op jit(solution)/shard_map/ppermute | solution.py:539
  6.5 11.5 %collective-permute-start.6 = (bf16[1024,128]{1,0:T(8,128)(2,1)S(1)}, bf16[1024,128]{1,0:T(8,128)(2,1)S(1)}, u32[]{:S(2)}, u32[]{:S(2)}) collective-permute-start(bf16[1024,128]{1,0:T(8,128)(2,1)S(1)} %shard_map.85.keys), channel_id=1, source_target_pairs={{0,4},{2,6},{4,0},{6,2},{8,12},{10,14},{12,8},{14,10},{1,5},{3,7},... | collective-permute-start | bytes 786440 | tf_op jit(solution)/shard_map/ppermute | solution.py:539
  10.9 14.1 %collective-permute-start.5 = (bf16[1024,128]{1,0:T(8,128)(2,1)S(1)}, bf16[1024,128]{1,0:T(8,128)(2,1)S(1)}, u32[]{:S(2)}, u32[]{:S(2)}) collective-permute-start(bf16[1024,128]{1,0:T(8,128)(2,1)S(1)} %get-tuple-element.79), channel_id=1, source_target_pairs={{0,4},{2,6},{4,0},{6,2},{8,12},{10,14},{12,8},{14,10},{1,5},{3,7},... | collective-permute-start | bytes 786440 | tf_op jit(solution)/shard_map/ppermute | solution.py:539
  11.0 14.1 %collective-permute-start.4 = (bf16[1024,128]{1,0:T(8,128)(2,1)S(1)}, bf16[1024,128]{1,0:T(8,128)(2,1)S(1)}, u32[]{:S(2)}, u32[]{:S(2)}) collective-permute-start(bf16[1024,128]{1,0:T(8,128)(2,1)S(1)} %get-tuple-element.79), channel_id=1, source_target_pairs={{0,0},{2,2},{4,8},{6,10},{8,4},{10,6},{12,12},{14,14},{1,1},{3,3},... | collective-permute-start | bytes 786440 | tf_op jit(solution)/shard_map/ppermute | solution.py:539
  18.7 7.8 %collective-permute-start.8 = (bf16[1024,128]{1,0:T(8,128)(2,1)S(1)}, bf16[1024,128]{1,0:T(8,128)(2,1)S(1)}, u32[]{:S(2)}, u32[]{:S(2)}) collective-permute-start(bf16[1024,128]{1,0:T(8,128)(2,1)S(1)} %shard_map.88), channel_id=1, source_target_pairs={{0,2},{2,0},{4,6},{6,4},{8,10},{10,8},{12,14},{14,12},{1,3},{3,1},... | collective-permute-start | bytes 786440 | tf_op jit(solution)/shard_map/ppermute | solution.py:539
  19.3 13.7 %collective-permute-start.9 = (bf16[512,256]{1,0:T(8,128)(2,1)S(1)}, bf16[512,256]{1,0:T(8,128)(2,1)S(1)}, u32[]{:S(2)}, u32[]{:S(2)}) collective-permute-start(bf16[512,256]{1,0:T(8,128)(2,1)S(1)} %shard_map.89), channel_id=1, source_target_pairs={{0,8},{2,10},{4,12},{6,14},{8,0},{10,2},{12,4},{14,6},{1,9},{3,11}... | collective-permute-start | bytes 786440 | tf_op jit(solution)/shard_map/ppermute | solution.py:539
  25.3 11.0 %collective-permute-start.10 = (bf16[1024,128]{1,0:T(8,128)(2,1)S(1)}, bf16[1024,128]{1,0:T(8,128)(2,1)S(1)}, u32[]{:S(2)}, u32[]{:S(2)}) collective-permute-start(bf16[1024,128]{1,0:T(8,128)(2,1)S(1)} %shard_map.91), channel_id=1, source_target_pairs={{0,2},{2,0},{4,6},{6,4},{8,10},{10,8},{12,14},{14,12},{1,3},{3,1},... | collective-permute-start | bytes 786440 | tf_op jit(solution)/shard_map/ppermute | solution.py:539
  35.2 10.8 %collective-permute-start.12 = (bf16[1024,128]{1,0:T(8,128)(2,1)S(1)}, bf16[1024,128]{1,0:T(8,128)(2,1)S(1)}, u32[]{:S(2)}, u32[]{:S(2)}) collective-permute-start(bf16[1024,128]{1,0:T(8,128)(2,1)S(1)} %get-tuple-element.109), channel_id=1, source_target_pairs={{0,2},{2,0},{4,6},{6,4},{8,10},{10,8},{12,14},{14,12},{1,3},{3,1},... | collective-permute-start | bytes 786440 | tf_op jit(solution)/shard_map/ppermute | solution.py:539
  36.3 9.7 %collective-permute-start.13 = (bf16[512,128]{1,0:T(8,128)(2,1)S(1)}, bf16[512,128]{1,0:T(8,128)(2,1)S(1)}, u32[]{:S(2)}, u32[]{:S(2)}) collective-permute-start(bf16[512,128]{1,0:T(8,128)(2,1)S(1)} %get-tuple-element.110), channel_id=1, source_target_pairs={{0,8},{2,10},{4,12},{6,14},{8,0},{10,2},{12,4},{14,6},{1,9},{3,11}... | collective-permute-start | bytes 393224 | tf_op jit(solution)/shard_map/ppermute | solution.py:539
  38.6 9.6 %collective-permute-start.14 = (bf16[1024,128]{1,0:T(8,128)(2,1)S(1)}, bf16[1024,128]{1,0:T(8,128)(2,1)S(1)}, u32[]{:S(2)}, u32[]{:S(2)}) collective-permute-start(bf16[1024,128]{1,0:T(8,128)(2,1)S(1)} %get-tuple-element.116), channel_id=1, source_target_pairs={{0,2},{2,0},{4,6},{6,4},{8,10},{10,8},{12,14},{14,12},{1,3},{3,1},... | collective-permute-start | bytes 786440 | tf_op jit(solution)/shard_map/ppermute | solution.py:539
  39.6 12.5 %collective-permute-start.11 = (bf16[512,128]{1,0:T(8,128)(2,1)S(1)}, bf16[512,128]{1,0:T(8,128)(2,1)S(1)}, u32[]{:S(2)}, u32[]{:S(2)}) collective-permute-start(bf16[512,128]{1,0:T(8,128)(2,1)S(1)} %get-tuple-element.106), channel_id=1, source_target_pairs={{0,8},{2,10},{4,12},{6,14},{8,0},{10,2},{12,4},{14,6},{1,9},{3,11}... | collective-permute-start | bytes 393224 | tf_op jit(solution)/shard_map/ppermute | solution.py:539
  48.2 10.9 %collective-permute-start.16 = (bf16[1024,256]{1,0:T(8,128)(2,1)S(1)}, bf16[1024,256]{1,0:T(8,128)(2,1)S(1)}, u32[]{:S(2)}, u32[]{:S(2)}) collective-permute-start(bf16[1024,256]{1,0:T(8,128)(2,1)S(1)} %get-tuple-element.133), channel_id=1, source_target_pairs={{0,2},{2,0},{4,6},{6,4},{8,10},{10,8},{12,14},{14,12},{1,3},{3,1},... | collective-permute-start | bytes 1572872 | tf_op jit(solution)/shard_map/ppermute | solution.py:539
  49.1 10.0 %collective-permute-start.17 = (bf16[1024,256]{1,0:T(8,128)(2,1)S(1)}, bf16[1024,256]{1,0:T(8,128)(2,1)S(1)}, u32[]{:S(2)}, u32[]{:S(2)}) collective-permute-start(bf16[1024,256]{1,0:T(8,128)(2,1)S(1)} %get-tuple-element.119), channel_id=1, source_target_pairs={{0,0},{2,2},{4,8},{6,10},{8,4},{10,6},{12,12},{14,14},{1,1},{3,3},... | collective-permute-start | bytes 1572872 | tf_op jit(solution)/shard_map/ppermute | solution.py:539
  49.8 10.9 %collective-permute-start.18 = (bf16[1024,256]{1,0:T(8,128)(2,1)S(1)}, bf16[1024,256]{1,0:T(8,128)(2,1)S(1)}, u32[]{:S(2)}, u32[]{:S(2)}) collective-permute-start(bf16[1024,256]{1,0:T(8,128)(2,1)S(1)} %get-tuple-element.118), channel_id=1, source_target_pairs={{0,4},{2,6},{4,0},{6,2},{8,12},{10,14},{12,8},{14,10},{1,5},{3,7},... | collective-permute-start | bytes 1572872 | tf_op jit(solution)/shard_map/ppermute | solution.py:539
  56.1 1.6 %collective-permute-start.15 = (bf16[512,256]{1,0:T(8,128)(2,1)S(1)}, bf16[512,256]{1,0:T(8,128)(2,1)S(1)}, u32[]{:S(2)}, u32[]{:S(2)}) collective-permute-start(bf16[512,256]{1,0:T(8,128)(2,1)S(1)} %get-tuple-element.127), channel_id=1, source_target_pairs={{0,1},{1,0},{2,3},{3,2},{4,5},{5,4},{6,7},{7,6},{8,9},{9,8},{10,11... | collective-permute-start | bytes 786440 | tf_op jit(solution)/shard_map/ppermute | solution.py:536
  60.9 1.6 %collective-permute-start.19 = (bf16[512,256]{1,0:T(8,128)(2,1)S(1)}, bf16[512,256]{1,0:T(8,128)(2,1)S(1)}, u32[]{:S(2)}, u32[]{:S(2)}) collective-permute-start(bf16[512,256]{1,0:T(8,128)(2,1)S(1)} %get-tuple-element.135), channel_id=1, source_target_pairs={{0,1},{1,0},{2,3},{3,2},{4,5},{5,4},{6,7},{7,6},{8,9},{9,8},{10,11... | collective-permute-start | bytes 786440 | tf_op jit(solution)/shard_map/ppermute | solution.py:536

commit v10 on v9

--- a/solution.py
+++ b/solution.py
@@ -334,14 +334,17 @@
         late[slab] = s_ref[2 * block :, :]
 
 
-def close_kernel(block, far, qg, stat, acc, *refs):
+def close_kernel(block, relayed, far, lists_any, qg, stat, acc, late_s, *refs):
     n = len(far)
     far_kv = refs[:n]
-    lse_ref, part_ref = refs[n : n + 2]
-    far_dv = refs[n + 2 : 2 * n + 2]
-    s_ref = refs[2 * n + 2]
+    lse_ref, part_ref, dc_v, p_ref = refs[n : n + 4]
+    far_dv = refs[n + 4 : 2 * n + 4]
+    s_ref, grad, lists, sem = refs[2 * n + 4 :]
     half = qg.shape[0] // 2
     frame = lax.axis_index("tm")
+    copy = pltpu.make_async_copy(lists_any, lists, sem)
+    copy.start()
+    grad[...] = jnp.zeros_like(grad)
     for slab in range(2):
         rows = rows_of(slab, half)
         q, g = qg[rows, KEY], qg[rows, VALUE]
@@ -357,16 +360,11 @@
         for group, s in group_scores(groups, s_ref):
             p = raised(group, s, lse)
             store_grads(group, dot_nn(p.astype(BF16), g), "dv")
-
-
-def shares_kernel(block, relayed, lists, qg, lse_ref, s_ref, dc_v, p_ref, grad):
-    half = qg.shape[0] // 2
-    frame = lax.axis_index("tm")
-    grad[...] = jnp.zeros_like(grad)
+    copy.wait()
     for slab in range(2):
         rows = rows_of(slab, half)
         group = listed(relayed, lists, frame, slab, block, None, None, 2, dv=(grad, ALL))
-        p = raised(group, s_ref[slab], lse_ref[0:1, rows])
+        p = raised(group, late_s[slab], lse_ref[0:1, rows])
         p_ref[slab] = p
         store_grads(group, dot_nn(p.astype(BF16), qg[rows, VALUE]), "dv")
     dc_v[...] = grad[...].astype(BF16)
@@ -542,7 +540,7 @@
         return pltpu.VMEM((pieces * block, s_dev), F32)
 
 
-    k_came, v_came = across(key_rows), across(value_rows)
+    k_came = across(key_rows)
     sources = (key_rows, value_rows, queries, out_grad, block_lists.T)
     k_own, v_own, qg_own, qg_send, lists = call(
         pack_kernel,
@@ -553,6 +551,8 @@
         scalars=HBM,
     )
     (keys,) = call(keys_kernel, (k_own, k_came), [frame_one])
+    later_rows, _ = lax.optimization_barrier((value_rows, keys))
+    v_came = across(later_rows)
     values, kv = call(values_kernel, (keys, v_own, v_came), [frame_one, frame_two])
     qg_send, _ = lax.optimization_barrier((qg_send, keys))
     y_k = swapped(keys, y_swap)
@@ -563,9 +563,9 @@
     y_k, qg_came = lax.optimization_barrier((y_k, across(qg_send)))
     work = 4 * s_dev * s_dev * DH
     qg, turned = call(join_kernel, (qg_own, qg_came), [frame_two, turned_bf], flops=15 * work)
-    y_k, z_k, turned = lax.optimization_barrier((y_k, z_k, turned))
     kv, _ = lax.optimization_barrier((kv, turned))
     far_send = call(functools.partial(select_kernel, far, block), (lists, kv), [pair] * n)
+    y_k, z_k, far_send = lax.optimization_barrier((y_k, z_k, far_send))
     (relay_k,) = call(relay_kernel, (y_k, z_k), [frame_one])
     relay_k, far_send = lax.optimization_barrier((relay_k, far_send))
     a_kv, _ = lax.optimization_barrier((a_kv, relay_k))
@@ -589,17 +589,17 @@
         scratch=[scores(4)],
     )
     acc, far_kv = lax.optimization_barrier((acc, far_kv))
-    lse, part, *far_dv = call(
-        functools.partial(close_kernel, block, far),
-        (qg, stat, acc, *far_kv),
-        [stat_row, turned_sum] + [single] * n,
-        scratch=[scores(n)],
-    )
-    dc_v, probs = call(
-        functools.partial(shares_kernel, block, relayed),
-        (lists, qg, lse, late_scores),
-        [frame_one, score_two],
-        scratch=[grad_one],
+    lse, part, dc_v, probs, *far_dv = call(
+        functools.partial(close_kernel, block, relayed, far),
+        (lists, qg, stat, acc, late_scores, *far_kv),
+        [stat_row, turned_sum, frame_one, score_two] + [single] * n,
+        scratch=[
+            scores(n),
+            grad_one,
+            pltpu.SMEM(lists.shape, jnp.int32),
+            pltpu.SemaphoreType.DMA(()),
+        ],
+        scalars=pl.BlockSpec(memory_space=pl.ANY),
     )
     dc_v_came = swapped(dc_v, near_swap)
     far_dv_came = [swapped(value, swap) for value, swap in zip(far_dv, far)]

time: 63.6 us -> 63.7 us (level)
  waiting for transfers between devices: 16.6 us -> 18 us
    ppermute x15, waiting for transfers between devices: 13.5 us -> 14.3 us  [swapped(): return lax.ppermute(value, 'tm', swap.pairs)]
    ppermute x5, waiting for transfers between devices: 3.06 us -> 3.7 us  [across(): return lax.ppermute(value, 'space', [(0, 1), (1, 0)])]
    pallas_call x21 -> x20, Pallas kernels: 23.7 us -> 23.1 us  [call(): pl.pallas_call(kernel, out_shape=out_shape, in_specs=[scalars if a.dtype...]
  transfers between devices with their start and end apart: 20 -> 20, of which waited for: 8 -> 10; matrix products, arithmetic and copies ran while one was open for 0% -> 0% of each run, Pallas kernels for 36% -> 35%
where the time goes in v10:
time: 63.7 us; the launch traced here: 63.5 us
  Pallas kernels  23.1 us (36%)
  starting transfers between devices  21.7 us (34%)
  waiting for transfers between devices  18 us (28%)
  between operations  0.83 us (1%)
    pallas_call x20, Pallas kernels, call(): pl.pallas_call(kernel, out_shape=out_shape, in_specs=[scalars if a.dtype...  23.1 us
    ppermute x15, starting transfers between devices, swapped(): return lax.ppermute(value, 'tm', swap.pairs)  20.4 us
    ppermute x15, waiting for transfers between devices, swapped(): return lax.ppermute(value, 'tm', swap.pairs)  14.3 us
    ppermute x5, waiting for transfers between devices, across(): return lax.ppermute(value, 'space', [(0, 1), (1, 0)])  3.7 us
  transfers between devices with their start and end apart: 20, of which 10 were waited for; matrix products, arithmetic and copies ran while one was open for 0% of the time, Pallas kernels for 35%

profile of v10, /device:TPU:0, one launch (start us, length us, event | category | flops | bytes accessed | tf_op | source)
XLA Modules:
  0.0 63.5 jit_solution(12369122073139917721)
XLA Ops:
  1.1 1.3 %shard_map.84 = (bf16[512,128]{1,0:T(8,128)(2,1)S(1)}, bf16[512,128]{1,0:T(8,128)(2,1)S(1)}, bf16[512,256]{1,0:T(8,128)(2,1)S(1)}, bf16[512,256]{1,0:T(8,128)(2,1)S(1)}, s32[8,16]{1,0:T(8,128)S(1)}) custom-call(bf16[512,256]{1,0:T(8,128)(2,1)} %k.1, bf16[512,256]{1,0:T(8,128)(2,1)} %v.1, bf16[512,256]{1,0:T(8,128)(2,1)} %q.1, bf16[512,256]{1,0:T(8,128)(2,1)} %g.1, ...), custom_call_target="tpu_custom_call" | custom-call | flops 1024 | bytes 1024 | tf_op jit(solution)/shard_map/pallas_call | solution.py:38
  3.1 0.7 %collective-permute-start.1 = (bf16[1024,128]{1,0:T(8,128)(2,1)S(1)}, bf16[1024,128]{1,0:T(8,128)(2,1)S(1)}, u32[]{:S(2)}, u32[]{:S(2)}) collective-permute-start(bf16[1024,128]{1,0:T(8,128)(2,1)S(1)} %shard_map.85.keys), channel_id=1, source_target_pairs={{0,0},{2,2},{4,8},{6,10},{8,4},{10,6},{12,12},{14,14},{1,1},{3,3},... | collective-permute-start | bytes 786440 | tf_op jit(solution)/shard_map/ppermute | solution.py:537
  4.5 3.0 %collective-permute-start.6 = (bf16[1024,256]{1,0:T(8,128)(2,1)S(1)}, bf16[1024,256]{1,0:T(8,128)(2,1)S(1)}, u32[]{:S(2)}, u32[]{:S(2)}) collective-permute-start(bf16[1024,256]{1,0:T(8,128)(2,1)S(1)} %get-tuple-element.84.kv), channel_id=1, source_target_pairs={{0,2},{2,0},{4,6},{6,4},{8,10},{10,8},{12,14},{14,12},{1,3},{3,1},... | collective-permute-start | bytes 1572872 | tf_op jit(solution)/shard_map/ppermute | solution.py:537
  7.5 3.8 %collective-permute-start.7 = (bf16[1024,128]{1,0:T(8,128)(2,1)S(1)}, bf16[1024,128]{1,0:T(8,128)(2,1)S(1)}, u32[]{:S(2)}, u32[]{:S(2)}) collective-permute-start(bf16[1024,128]{1,0:T(8,128)(2,1)S(1)} %shard_map.85.keys), channel_id=1, source_target_pairs={{0,4},{2,6},{4,0},{6,2},{8,12},{10,14},{12,8},{14,10},{1,5},{3,7},... | collective-permute-start | bytes 786440 | tf_op jit(solution)/shard_map/ppermute | solution.py:537
  11.3 0.7 %collective-permute-start.4 = (bf16[1024,128]{1,0:T(8,128)(2,1)S(1)}, bf16[1024,128]{1,0:T(8,128)(2,1)S(1)}, u32[]{:S(2)}, u32[]{:S(2)}) collective-permute-start(bf16[1024,128]{1,0:T(8,128)(2,1)S(1)} %get-tuple-element.81), channel_id=1, source_target_pairs={{0,0},{2,2},{4,8},{6,10},{8,4},{10,6},{12,12},{14,14},{1,1},{3,3},... | collective-permute-start | bytes 786440 | tf_op jit(solution)/shard_map/ppermute | solution.py:537
  12.2 0.6 %shard_map.88 = bf16[512,256]{1,0:T(8,128)(2,1)S(1)} custom-call(s32[8,16]{1,0:T(8,128)S(1)} %get-tuple-element.78.lists.lists_any.refs_0_, bf16[1024,256]{1,0:T(8,128)(2,1)S(1)} %get-tuple-element.84.kv), custom_call_target="tpu_custom_call" | custom-call | flops 1024 | bytes 1024 | tf_op jit(solution)/shard_map/pallas_call | solution.py:38
  12.8 5.7 %collective-permute-done.7.z.z_k = bf16[1024,128]{1,0:T(8,128)(2,1)S(1)} collective-permute-done((bf16[1024,128]{1,0:T(8,128)(2,1)S(1)}, bf16[1024,128]{1,0:T(8,128)(2,1)S(1)}, u32[]{:S(2)}, u32[]{:S(2)}) %collective-permute-start.7) | collective-permute-done | bytes 262176 | tf_op jit(solution)/shard_map/ppermute | solution.py:537
  18.5 0.6 collective-permute-start.8
  19.1 1.9 %collective-permute-start.9 = (bf16[512,256]{1,0:T(8,128)(2,1)S(1)}, bf16[512,256]{1,0:T(8,128)(2,1)S(1)}, u32[]{:S(2)}, u32[]{:S(2)}) collective-permute-start(bf16[512,256]{1,0:T(8,128)(2,1)S(1)} %shard_map.88), channel_id=1, source_target_pairs={{0,8},{2,10},{4,12},{6,14},{8,0},{10,2},{12,4},{14,6},{1,9},{3,11}... | collective-permute-start | bytes 786440 | tf_op jit(solution)/shard_map/ppermute | solution.py:537
  21.0 3.5 %shard_map.90 = (f32[8,1024]{1,0:T(8,128)S(1)}, f32[128,1024]{1,0:T(8,128)S(1)}) custom-call(s32[8,16]{1,0:T(8,128)S(1)} %get-tuple-element.78.lists.lists_any.refs_0_, bf16[1024,256]{1,0:T(8,128)(2,1)S(1)} %get-tuple-element.77.qg.refs_1_, bf16[1024,256]{1,0:T(8,128)(2,1)S(1)} %get-tuple-element.84.kv, bf16[1024,256]{1,0:T(8,128)(2,1)S(1)} %collective-permute-done.6.a_kv), custom_call_target="tpu_custom_call" | custom-call | flops 1024 | bytes 1024 | tf_op jit(solution)/shard_map/pallas_call | solution.py:38
  24.9 1.4 %collective-permute-start.10 = (bf16[1024,128]{1,0:T(8,128)(2,1)S(1)}, bf16[1024,128]{1,0:T(8,128)(2,1)S(1)}, u32[]{:S(2)}, u32[]{:S(2)}) collective-permute-start(bf16[1024,128]{1,0:T(8,128)(2,1)S(1)} %shard_map.91), channel_id=1, source_target_pairs={{0,2},{2,0},{4,6},{6,4},{8,10},{10,8},{12,14},{14,12},{1,3},{3,1},... | collective-permute-start | bytes 786440 | tf_op jit(solution)/shard_map/ppermute | solution.py:537
  26.3 2.6 %shard_map.92 = (f32[8,1024]{1,0:T(8,128)S(1)}, f32[128,1024]{1,0:T(8,128)S(1)}, f32[2,512,512]{2,1,0:T(8,128)S(1)}) custom-call(s32[8,16]{1,0:T(8,128)S(1)} %get-tuple-element.78.lists.lists_any.refs_0_, bf16[1024,256]{1,0:T(8,128)(2,1)S(1)} %get-tuple-element.77.qg.refs_1_, f32[8,1024]{1,0:T(8,128)S(1)} %get-tuple-element.95.stat, ...), custom_call_target="tpu_custom_call" | custom-call | flops 1024 | bytes 1024 | tf_op jit(solution)/shard_map/pallas_call | solution.py:38
  29.0 4.1 %collective-permute-done.9.refs_0_.refs_8_ = bf16[512,256]{1,0:T(8,128)(2,1)S(1)} collective-permute-done((bf16[512,256]{1,0:T(8,128)(2,1)S(1)}, bf16[512,256]{1,0:T(8,128)(2,1)S(1)}, u32[]{:S(2)}, u32[]{:S(2)}) %collective-permute-start.9) | collective-permute-done | bytes 262176 | tf_op jit(solution)/shard_map/ppermute | solution.py:537
  33.1 1.5 %shard_map.93 = (f32[8,1024]{1,0:T(8,128)S(1)}, f32[128,1024]{1,0:T(8,128)S(1)}, bf16[1024,128]{1,0:T(8,128)(2,1)S(1)}, f32[2,512,512]{2,1,0:T(8,128)S(1)}, bf16[512,128]{1,0:T(8,128)(2,1)S(1)}) custom-call(s32[8,16]{1,0:T(8,128)S(1)} %get-tuple-element.78.lists.lists_any.refs_0_, bf16[1024,256]{1,0:T(8,128)(2,1)S(1)} %get-tuple-element.77.qg.refs_1_, ...), custom_call_target="tpu_custom_call" | custom-call | flops 1024 | bytes 1024 | tf_op jit(solution)/shard_map/pallas_call | solution.py:38
  34.6 1.1 %collective-permute-start.12 = (bf16[1024,128]{1,0:T(8,128)(2,1)S(1)}, bf16[1024,128]{1,0:T(8,128)(2,1)S(1)}, u32[]{:S(2)}, u32[]{:S(2)}) collective-permute-start(bf16[1024,128]{1,0:T(8,128)(2,1)S(1)} %get-tuple-element.111), channel_id=1, source_target_pairs={{0,2},{2,0},{4,6},{6,4},{8,10},{10,8},{12,14},{14,12},{1,3},{3,1},... | collective-permute-start | bytes 786440 | tf_op jit(solution)/shard_map/ppermute | solution.py:537
  35.7 2.3 %shard_map.94 = (bf16[128,1024]{1,0:T(8,128)(2,1)S(1)}, f32[8,1024]{1,0:T(8,128)S(1)}, bf16[1024,128]{1,0:T(8,128)(2,1)S(1)}, f32[128,1024]{1,0:T(8,128)S(1)}, bf16[512,128]{1,0:T(8,128)(2,1)S(1)}) custom-call(s32[8,16]{1,0:T(8,128)S(1)} %get-tuple-element.78.lists.lists_any.refs_0_, bf16[1024,256]{1,0:T(8,128)(2,1)S(1)} %get-tuple-element.77.qg.refs_1_, ...), custom_call_target="tpu_custom_call" | custom-call | flops 1024 | bytes 1024 | tf_op jit(solution)/shard_map/pallas_call | solution.py:38
  38.0 1.1 %collective-permute-start.14 = (bf16[1024,128]{1,0:T(8,128)(2,1)S(1)}, bf16[1024,128]{1,0:T(8,128)(2,1)S(1)}, u32[]{:S(2)}, u32[]{:S(2)}) collective-permute-start(bf16[1024,128]{1,0:T(8,128)(2,1)S(1)} %get-tuple-element.118), channel_id=1, source_target_pairs={{0,2},{2,0},{4,6},{6,4},{8,10},{10,8},{12,14},{14,12},{1,3},{3,1},... | collective-permute-start | bytes 786440 | tf_op jit(solution)/shard_map/ppermute | solution.py:537
  39.1 2.9 %collective-permute-start.11 = (bf16[512,128]{1,0:T(8,128)(2,1)S(1)}, bf16[512,128]{1,0:T(8,128)(2,1)S(1)}, u32[]{:S(2)}, u32[]{:S(2)}) collective-permute-start(bf16[512,128]{1,0:T(8,128)(2,1)S(1)} %get-tuple-element.108), channel_id=1, source_target_pairs={{0,8},{2,10},{4,12},{6,14},{8,0},{10,2},{12,4},{14,6},{1,9},{3,11}... | collective-permute-start | bytes 393224 | tf_op jit(solution)/shard_map/ppermute | solution.py:537
  42.0 2.2 %shard_map.95 = (bf16[1024,256]{1,0:T(8,128)(2,1)S(1)}, f32[128,1024]{1,0:T(8,128)S(1)}) custom-call(s32[8,16]{1,0:T(8,128)S(1)} %get-tuple-element.78.lists.lists_any.refs_0_, bf16[1024,256]{1,0:T(8,128)(2,1)S(1)} %get-tuple-element.77.qg.refs_1_, f32[8,1024]{1,0:T(8,128)S(1)} %get-tuple-element.103.refs_3_.lse_ref, ...), custom_call_target="tpu_custom_call" | custom-call | flops 1024 | bytes 1024 | tf_op jit(solution)/shard_map/pallas_call | solution.py:38
  44.3 1.1 %collective-permute-done.13.refs_2_ = bf16[512,128]{1,0:T(8,128)(2,1)S(1)} collective-permute-done((bf16[512,128]{1,0:T(8,128)(2,1)S(1)}, bf16[512,128]{1,0:T(8,128)(2,1)S(1)}, u32[]{:S(2)}, u32[]{:S(2)}) %collective-permute-start.13) | collective-permute-done | bytes 131104 | tf_op jit(solution)/shard_map/ppermute | solution.py:537
  45.4 2.2 %shard_map.96 = (f32[1024,256]{1,0:T(8,128)S(1)}, f32[1024,256]{1,0:T(8,128)S(1)}, f32[128,1024]{1,0:T(8,128)S(1)}) custom-call(s32[8,16]{1,0:T(8,128)S(1)} %get-tuple-element.78.lists.lists_any.refs_0_, bf16[1024,256]{1,0:T(8,128)(2,1)S(1)} %get-tuple-element.77.qg.refs_1_, f32[8,1024]{1,0:T(8,128)S(1)} %get-tuple-element.103.refs_3_.lse_ref, ...), custom_call_target="tpu_custom_call" | custom-call | flops 2684354560 | bytes 1024 | tf_op jit(solution)/shard_map/pallas_call | solution.py:38
  47.7 0.7 %collective-permute-start.16 = (bf16[1024,256]{1,0:T(8,128)(2,1)S(1)}, bf16[1024,256]{1,0:T(8,128)(2,1)S(1)}, u32[]{:S(2)}, u32[]{:S(2)}) collective-permute-start(bf16[1024,256]{1,0:T(8,128)(2,1)S(1)} %get-tuple-element.135), channel_id=1, source_target_pairs={{0,2},{2,0},{4,6},{6,4},{8,10},{10,8},{12,14},{14,12},{1,3},{3,1},... | collective-permute-start | bytes 1572872 | tf_op jit(solution)/shard_map/ppermute | solution.py:537
  48.6 0.7 %collective-permute-start.17 = (bf16[1024,256]{1,0:T(8,128)(2,1)S(1)}, bf16[1024,256]{1,0:T(8,128)(2,1)S(1)}, u32[]{:S(2)}, u32[]{:S(2)}) collective-permute-start(bf16[1024,256]{1,0:T(8,128)(2,1)S(1)} %get-tuple-element.121), channel_id=1, source_target_pairs={{0,0},{2,2},{4,8},{6,10},{8,4},{10,6},{12,12},{14,14},{1,1},{3,3},... | collective-permute-start | bytes 1572872 | tf_op jit(solution)/shard_map/ppermute | solution.py:537
  49.3 1.9 %collective-permute-start.18 = (bf16[1024,256]{1,0:T(8,128)(2,1)S(1)}, bf16[1024,256]{1,0:T(8,128)(2,1)S(1)}, u32[]{:S(2)}, u32[]{:S(2)}) collective-permute-start(bf16[1024,256]{1,0:T(8,128)(2,1)S(1)} %get-tuple-element.120), channel_id=1, source_target_pairs={{0,4},{2,6},{4,0},{6,2},{8,12},{10,14},{12,8},{14,10},{1,5},{3,7},... | collective-permute-start | bytes 1572872 | tf_op jit(solution)/shard_map/ppermute | solution.py:537
  51.2 0.7 %shard_map.98.placed = f32[1024,256]{1,0:T(8,128)S(1)} custom-call(s32[8,16]{1,0:T(8,128)S(1)} %get-tuple-element.78.lists.lists_any.refs_0_, bf16[512,128]{1,0:T(8,128)(2,1)S(1)} %collective-permute-done.11.refs_1_, bf16[512,128]{1,0:T(8,128)(2,1)S(1)} %collective-permute-done.13.refs_2_), custom_call_target="tpu_custom_call" | custom-call | flops 1024 | bytes 1024 | tf_op jit(solution)/shard_map/pallas_call | solution.py:38
  51.9 3.2 %shard_map.99 = (f32[1024,256]{1,0:T(8,128)S(1)}, bf16[512,256]{1,0:T(8,128)(2,1)S(1)}, bf16[512,256]{1,0:T(8,128)(2,1)S(1)}) custom-call(bf16[1024,256]{1,0:T(8,128)(2,1)S(1)} %get-tuple-element.77.qg.refs_1_, f32[8,1024]{1,0:T(8,128)S(1)} %get-tuple-element.103.refs_3_.lse_ref, f32[8,1024]{1,0:T(8,128)S(1)} %get-tuple-element.107.dot_ref, ...), custom_call_target="tpu_custom_call" | custom-call | flops 2684354560 | bytes 1024 | tf_op jit(solution)/shard_map/pallas_call | solution.py:38
  55.2 1.5 %collective-permute-done.15.came = bf16[512,256]{1,0:T(8,128)(2,1)S(1)} collective-permute-done((bf16[512,256]{1,0:T(8,128)(2,1)S(1)}, bf16[512,256]{1,0:T(8,128)(2,1)S(1)}, u32[]{:S(2)}, u32[]{:S(2)}) %collective-permute-start.15) | collective-permute-done | bytes 262176 | tf_op jit(solution)/shard_map/ppermute | solution.py:534
  56.7 0.9 %shard_map.100 = (bf16[512,256]{1,0:T(8,128)(2,1)}, bf16[512,256]{1,0:T(8,128)(2,1)}) custom-call(bf16[512,256]{1,0:T(8,128)(2,1)S(1)} %get-tuple-element.128.keep, bf16[512,256]{1,0:T(8,128)(2,1)S(1)} %collective-permute-done.15.came), custom_call_target="tpu_custom_call" | custom-call | flops 1024 | bytes 1024 | tf_op jit(solution)/shard_map/pallas_call | solution.py:38
  57.6 1.5 %collective-permute-done.16.refs_0_ = bf16[1024,256]{1,0:T(8,128)(2,1)S(1)} collective-permute-done((bf16[1024,256]{1,0:T(8,128)(2,1)S(1)}, bf16[1024,256]{1,0:T(8,128)(2,1)S(1)}, u32[]{:S(2)}, u32[]{:S(2)}) %collective-permute-start.16) | collective-permute-done | bytes 524320 | tf_op jit(solution)/shard_map/ppermute | solution.py:537
  59.3 1.5 %collective-permute-done.18.came = bf16[1024,256]{1,0:T(8,128)(2,1)S(1)} collective-permute-done((bf16[1024,256]{1,0:T(8,128)(2,1)S(1)}, bf16[1024,256]{1,0:T(8,128)(2,1)S(1)}, u32[]{:S(2)}, u32[]{:S(2)}) %collective-permute-start.18) | collective-permute-done | bytes 524320 | tf_op jit(solution)/shard_map/ppermute | solution.py:537
  61.1 1.5 %collective-permute-done.19.came = bf16[512,256]{1,0:T(8,128)(2,1)S(1)} collective-permute-done((bf16[512,256]{1,0:T(8,128)(2,1)S(1)}, bf16[512,256]{1,0:T(8,128)(2,1)S(1)}, u32[]{:S(2)}, u32[]{:S(2)}) %collective-permute-start.19) | collective-permute-done | bytes 262176 | tf_op jit(solution)/shard_map/ppermute | solution.py:534
  62.6 0.9 %shard_map.103 = (bf16[512,256]{1,0:T(8,128)(2,1)}, bf16[512,256]{1,0:T(8,128)(2,1)}) custom-call(bf16[512,256]{1,0:T(8,128)(2,1)S(1)} %get-tuple-element.136.keep, bf16[512,256]{1,0:T(8,128)(2,1)S(1)} %collective-permute-done.19.came), custom_call_target="tpu_custom_call" | custom-call | flops 1024 | bytes 1024 | tf_op jit(solution)/shard_map/pallas_call | solution.py:38
  (28 shorter events, 3.3 us)
Async XLA Ops:
  0.6 1.9 %collective-permute-start = (bf16[512,256]{1,0:T(8,128)(2,1)}, bf16[512,256]{1,0:T(8,128)(2,1)S(1)}, u32[]{:S(2)}, u32[]{:S(2)}) collective-permute-start(bf16[512,256]{1,0:T(8,128)(2,1)} %k.1), channel_id=1, source_target_pairs={{0,1},{1,0},{2,3},{3,2},{4,5},{5,4},{6,7},{7,6},{8,9},{9,8},{10,11... | collective-permute-start | bytes 786440 | tf_op jit(solution)/shard_map/ppermute | solution.py:534
  2.6 1.8 %collective-permute-start.3 = (bf16[512,256]{1,0:T(8,128)(2,1)}, bf16[512,256]{1,0:T(8,128)(2,1)S(1)}, u32[]{:S(2)}, u32[]{:S(2)}) collective-permute-start(bf16[512,256]{1,0:T(8,128)(2,1)} %v.1), channel_id=1, source_target_pairs={{0,1},{1,0},{2,3},{3,2},{4,5},{5,4},{6,7},{7,6},{8,9},{9,8},{10,11... | collective-permute-start | bytes 786440 | tf_op jit(solution)/shard_map/ppermute | solution.py:534
  3.0 8.3 %collective-permute-start.2 = (bf16[512,256]{1,0:T(8,128)(2,1)S(1)}, bf16[512,256]{1,0:T(8,128)(2,1)S(1)}, u32[]{:S(2)}, u32[]{:S(2)}) collective-permute-start(bf16[512,256]{1,0:T(8,128)(2,1)S(1)} %get-tuple-element.75), channel_id=1, source_target_pairs={{0,1},{1,0},{2,3},{3,2},{4,5},{5,4},{6,7},{7,6},{8,9},{9,8},{10,11... | collective-permute-start | bytes 786440 | tf_op jit(solution)/shard_map/ppermute | solution.py:534
  3.1 8.9 %collective-permute-start.1 = (bf16[1024,128]{1,0:T(8,128)(2,1)S(1)}, bf16[1024,128]{1,0:T(8,128)(2,1)S(1)}, u32[]{:S(2)}, u32[]{:S(2)}) collective-permute-start(bf16[1024,128]{1,0:T(8,128)(2,1)S(1)} %shard_map.85.keys), channel_id=1, source_target_pairs={{0,0},{2,2},{4,8},{6,10},{8,4},{10,6},{12,12},{14,14},{1,1},{3,3},... | collective-permute-start | bytes 786440 | tf_op jit(solution)/shard_map/ppermute | solution.py:537
  4.5 16.5 %collective-permute-start.6 = (bf16[1024,256]{1,0:T(8,128)(2,1)S(1)}, bf16[1024,256]{1,0:T(8,128)(2,1)S(1)}, u32[]{:S(2)}, u32[]{:S(2)}) collective-permute-start(bf16[1024,256]{1,0:T(8,128)(2,1)S(1)} %get-tuple-element.84.kv), channel_id=1, source_target_pairs={{0,2},{2,0},{4,6},{6,4},{8,10},{10,8},{12,14},{14,12},{1,3},{3,1},... | collective-permute-start | bytes 1572872 | tf_op jit(solution)/shard_map/ppermute | solution.py:537
  7.5 11.0 %collective-permute-start.7 = (bf16[1024,128]{1,0:T(8,128)(2,1)S(1)}, bf16[1024,128]{1,0:T(8,128)(2,1)S(1)}, u32[]{:S(2)}, u32[]{:S(2)}) collective-permute-start(bf16[1024,128]{1,0:T(8,128)(2,1)S(1)} %shard_map.85.keys), channel_id=1, source_target_pairs={{0,4},{2,6},{4,0},{6,2},{8,12},{10,14},{12,8},{14,10},{1,5},{3,7},... | collective-permute-start | bytes 786440 | tf_op jit(solution)/shard_map/ppermute | solution.py:537
  11.3 13.4 %collective-permute-start.5 = (bf16[1024,128]{1,0:T(8,128)(2,1)S(1)}, bf16[1024,128]{1,0:T(8,128)(2,1)S(1)}, u32[]{:S(2)}, u32[]{:S(2)}) collective-permute-start(bf16[1024,128]{1,0:T(8,128)(2,1)S(1)} %get-tuple-element.81), channel_id=1, source_target_pairs={{0,4},{2,6},{4,0},{6,2},{8,12},{10,14},{12,8},{14,10},{1,5},{3,7},... | collective-permute-start | bytes 786440 | tf_op jit(solution)/shard_map/ppermute | solution.py:537
  11.3 13.4 %collective-permute-start.4 = (bf16[1024,128]{1,0:T(8,128)(2,1)S(1)}, bf16[1024,128]{1,0:T(8,128)(2,1)S(1)}, u32[]{:S(2)}, u32[]{:S(2)}) collective-permute-start(bf16[1024,128]{1,0:T(8,128)(2,1)S(1)} %get-tuple-element.81), channel_id=1, source_target_pairs={{0,0},{2,2},{4,8},{6,10},{8,4},{10,6},{12,12},{14,14},{1,1},{3,3},... | collective-permute-start | bytes 786440 | tf_op jit(solution)/shard_map/ppermute | solution.py:537
  18.5 7.8 %collective-permute-start.8 = (bf16[1024,128]{1,0:T(8,128)(2,1)S(1)}, bf16[1024,128]{1,0:T(8,128)(2,1)S(1)}, u32[]{:S(2)}, u32[]{:S(2)}) collective-permute-start(bf16[1024,128]{1,0:T(8,128)(2,1)S(1)} %shard_map.89), channel_id=1, source_target_pairs={{0,2},{2,0},{4,6},{6,4},{8,10},{10,8},{12,14},{14,12},{1,3},{3,1},... | collective-permute-start | bytes 786440 | tf_op jit(solution)/shard_map/ppermute | solution.py:537
  19.1 14.0 %collective-permute-start.9 = (bf16[512,256]{1,0:T(8,128)(2,1)S(1)}, bf16[512,256]{1,0:T(8,128)(2,1)S(1)}, u32[]{:S(2)}, u32[]{:S(2)}) collective-permute-start(bf16[512,256]{1,0:T(8,128)(2,1)S(1)} %shard_map.88), channel_id=1, source_target_pairs={{0,8},{2,10},{4,12},{6,14},{8,0},{10,2},{12,4},{14,6},{1,9},{3,11}... | collective-permute-start | bytes 786440 | tf_op jit(solution)/shard_map/ppermute | solution.py:537
  24.9 10.8 %collective-permute-start.10 = (bf16[1024,128]{1,0:T(8,128)(2,1)S(1)}, bf16[1024,128]{1,0:T(8,128)(2,1)S(1)}, u32[]{:S(2)}, u32[]{:S(2)}) collective-permute-start(bf16[1024,128]{1,0:T(8,128)(2,1)S(1)} %shard_map.91), channel_id=1, source_target_pairs={{0,2},{2,0},{4,6},{6,4},{8,10},{10,8},{12,14},{14,12},{1,3},{3,1},... | collective-permute-start | bytes 786440 | tf_op jit(solution)/shard_map/ppermute | solution.py:537
  34.6 10.8 %collective-permute-start.12 = (bf16[1024,128]{1,0:T(8,128)(2,1)S(1)}, bf16[1024,128]{1,0:T(8,128)(2,1)S(1)}, u32[]{:S(2)}, u32[]{:S(2)}) collective-permute-start(bf16[1024,128]{1,0:T(8,128)(2,1)S(1)} %get-tuple-element.111), channel_id=1, source_target_pairs={{0,2},{2,0},{4,6},{6,4},{8,10},{10,8},{12,14},{14,12},{1,3},{3,1},... | collective-permute-start | bytes 786440 | tf_op jit(solution)/shard_map/ppermute | solution.py:537
  35.7 9.7 %collective-permute-start.13 = (bf16[512,128]{1,0:T(8,128)(2,1)S(1)}, bf16[512,128]{1,0:T(8,128)(2,1)S(1)}, u32[]{:S(2)}, u32[]{:S(2)}) collective-permute-start(bf16[512,128]{1,0:T(8,128)(2,1)S(1)} %get-tuple-element.112), channel_id=1, source_target_pairs={{0,8},{2,10},{4,12},{6,14},{8,0},{10,2},{12,4},{14,6},{1,9},{3,11}... | collective-permute-start | bytes 393224 | tf_op jit(solution)/shard_map/ppermute | solution.py:537
  38.0 9.7 %collective-permute-start.14 = (bf16[1024,128]{1,0:T(8,128)(2,1)S(1)}, bf16[1024,128]{1,0:T(8,128)(2,1)S(1)}, u32[]{:S(2)}, u32[]{:S(2)}) collective-permute-start(bf16[1024,128]{1,0:T(8,128)(2,1)S(1)} %get-tuple-element.118), channel_id=1, source_target_pairs={{0,2},{2,0},{4,6},{6,4},{8,10},{10,8},{12,14},{14,12},{1,3},{3,1},... | collective-permute-start | bytes 786440 | tf_op jit(solution)/shard_map/ppermute | solution.py:537
  39.1 12.1 %collective-permute-start.11 = (bf16[512,128]{1,0:T(8,128)(2,1)S(1)}, bf16[512,128]{1,0:T(8,128)(2,1)S(1)}, u32[]{:S(2)}, u32[]{:S(2)}) collective-permute-start(bf16[512,128]{1,0:T(8,128)(2,1)S(1)} %get-tuple-element.108), channel_id=1, source_target_pairs={{0,8},{2,10},{4,12},{6,14},{8,0},{10,2},{12,4},{14,6},{1,9},{3,11}... | collective-permute-start | bytes 393224 | tf_op jit(solution)/shard_map/ppermute | solution.py:537
  47.7 11.4 %collective-permute-start.16 = (bf16[1024,256]{1,0:T(8,128)(2,1)S(1)}, bf16[1024,256]{1,0:T(8,128)(2,1)S(1)}, u32[]{:S(2)}, u32[]{:S(2)}) collective-permute-start(bf16[1024,256]{1,0:T(8,128)(2,1)S(1)} %get-tuple-element.135), channel_id=1, source_target_pairs={{0,2},{2,0},{4,6},{6,4},{8,10},{10,8},{12,14},{14,12},{1,3},{3,1},... | collective-permute-start | bytes 1572872 | tf_op jit(solution)/shard_map/ppermute | solution.py:537
  48.6 10.5 %collective-permute-start.17 = (bf16[1024,256]{1,0:T(8,128)(2,1)S(1)}, bf16[1024,256]{1,0:T(8,128)(2,1)S(1)}, u32[]{:S(2)}, u32[]{:S(2)}) collective-permute-start(bf16[1024,256]{1,0:T(8,128)(2,1)S(1)} %get-tuple-element.121), channel_id=1, source_target_pairs={{0,0},{2,2},{4,8},{6,10},{8,4},{10,6},{12,12},{14,14},{1,1},{3,3},... | collective-permute-start | bytes 1572872 | tf_op jit(solution)/shard_map/ppermute | solution.py:537
  49.3 11.6 %collective-permute-start.18 = (bf16[1024,256]{1,0:T(8,128)(2,1)S(1)}, bf16[1024,256]{1,0:T(8,128)(2,1)S(1)}, u32[]{:S(2)}, u32[]{:S(2)}) collective-permute-start(bf16[1024,256]{1,0:T(8,128)(2,1)S(1)} %get-tuple-element.120), channel_id=1, source_target_pairs={{0,4},{2,6},{4,0},{6,2},{8,12},{10,14},{12,8},{14,10},{1,5},{3,7},... | collective-permute-start | bytes 1572872 | tf_op jit(solution)/shard_map/ppermute | solution.py:537
  55.1 1.6 %collective-permute-start.15 = (bf16[512,256]{1,0:T(8,128)(2,1)S(1)}, bf16[512,256]{1,0:T(8,128)(2,1)S(1)}, u32[]{:S(2)}, u32[]{:S(2)}) collective-permute-start(bf16[512,256]{1,0:T(8,128)(2,1)S(1)} %get-tuple-element.129), channel_id=1, source_target_pairs={{0,1},{1,0},{2,3},{3,2},{4,5},{5,4},{6,7},{7,6},{8,9},{9,8},{10,11... | collective-permute-start | bytes 786440 | tf_op jit(solution)/shard_map/ppermute | solution.py:534
  61.0 1.6 %collective-permute-start.19 = (bf16[512,256]{1,0:T(8,128)(2,1)S(1)}, bf16[512,256]{1,0:T(8,128)(2,1)S(1)}, u32[]{:S(2)}, u32[]{:S(2)}) collective-permute-start(bf16[512,256]{1,0:T(8,128)(2,1)S(1)} %get-tuple-element.137), channel_id=1, source_target_pairs={{0,1},{1,0},{2,3},{3,2},{4,5},{5,4},{6,7},{7,6},{8,9},{9,8},{10,11... | collective-permute-start | bytes 786440 | tf_op jit(solution)/shard_map/ppermute | solution.py:534

commit v11 on v10

--- a/solution.py
+++ b/solution.py
@@ -51,7 +51,11 @@
     for frame in range(count):
         up = ((frame // distance) % 2 == 0) != second
         target = frame + distance if up else frame - distance
-        pairs.append((frame, target if 0 <= target < count else frame))
+        for core in range(2):
+            if 0 <= target < count:
+                pairs.append((frame * 2 + core, target * 2 + core))
+            else:
+                pairs.append((frame * 2 + core, frame * 2 + 1 - core))
     return pairs
 
 
@@ -60,7 +64,7 @@
         self.count, self.level, self.second = count, level, second
         self.levels = count.bit_length() - 1
         self.pairs = swap_pairs(count, 1 << level, second)
-        self.moves = any(source != target for source, target in self.pairs)
+        self.moves = any(source // 2 != target // 2 for source, target in self.pairs)
 
     def partner(self, frame):
         odd = lax.rem(lax.shift_right_logical(frame, self.level), 2)
@@ -534,13 +538,13 @@
         return lax.ppermute(value, "space", [(0, 1), (1, 0)])
 
     def swapped(value, swap):
-        return lax.ppermute(value, "tm", swap.pairs)
+        return lax.ppermute(value, ("tm", "space"), swap.pairs)
 
     def scores(pieces):
         return pltpu.VMEM((pieces * block, s_dev), F32)
 
 
-    k_came = across(key_rows)
+    k_came, v_came = across(key_rows), across(value_rows)
     sources = (key_rows, value_rows, queries, out_grad, block_lists.T)
     k_own, v_own, qg_own, qg_send, lists = call(
         pack_kernel,
@@ -551,8 +555,6 @@
         scalars=HBM,
     )
     (keys,) = call(keys_kernel, (k_own, k_came), [frame_one])
-    later_rows, _ = lax.optimization_barrier((value_rows, keys))
-    v_came = across(later_rows)
     values, kv = call(values_kernel, (keys, v_own, v_came), [frame_one, frame_two])
     qg_send, _ = lax.optimization_barrier((qg_send, keys))
     y_k = swapped(keys, y_swap)

time: 63.7 us -> 64 us (level)
  waiting for transfers between devices: 18 us -> 23.4 us
  starting transfers between devices: 21.7 us -> 16.5 us
    ppermute x15, waiting for transfers between devices: 14.3 us -> 20.3 us  [swapped(): return lax.ppermute(value, ('tm', 'space'), swap.pairs)]
    ppermute x15, starting transfers between devices: 20.4 us -> 15.3 us  [swapped(): return lax.ppermute(value, ('tm', 'space'), swap.pairs)]
where the time goes in v11:
time: 64 us; the launch traced here: 63.8 us
  waiting for transfers between devices  23.4 us (37%)
  Pallas kernels  23.1 us (36%)
  starting transfers between devices  16.5 us (26%)
  between operations  0.81 us (1%)
    pallas_call x20, Pallas kernels, call(): pl.pallas_call(kernel, out_shape=out_shape, in_specs=[scalars if a.dtype...  23.1 us
    ppermute x15, waiting for transfers between devices, swapped(): return lax.ppermute(value, ('tm', 'space'), swap.pairs)  20.3 us
    ppermute x15, starting transfers between devices, swapped(): return lax.ppermute(value, ('tm', 'space'), swap.pairs)  15.3 us
    ppermute x5, waiting for transfers between devices, across(): return lax.ppermute(value, 'space', [(0, 1), (1, 0)])  3.06 us
  transfers between devices with their start and end apart: 20, of which 10 were waited for; matrix products, arithmetic and copies ran while one was open for 0% of the time, Pallas kernels for 35%

profile of v11, /device:TPU:0, one launch (start us, length us, event | category | flops | bytes accessed | tf_op | source)
XLA Modules:
  0.0 63.8 jit_solution(12943162879547411894)
XLA Ops:
  0.6 0.5 collective-permute-start
  1.2 1.3 %shard_map.84 = (bf16[512,128]{1,0:T(8,128)(2,1)S(1)}, bf16[512,128]{1,0:T(8,128)(2,1)S(1)}, bf16[512,256]{1,0:T(8,128)(2,1)S(1)}, bf16[512,256]{1,0:T(8,128)(2,1)S(1)}, s32[8,16]{1,0:T(8,128)S(1)}) custom-call(bf16[512,256]{1,0:T(8,128)(2,1)} %k.1, bf16[512,256]{1,0:T(8,128)(2,1)} %v.1, bf16[512,256]{1,0:T(8,128)(2,1)} %q.1, bf16[512,256]{1,0:T(8,128)(2,1)} %g.1, ...), custom_call_target="tpu_custom_call" | custom-call | flops 1024 | bytes 1024 | tf_op jit(solution)/shard_map/pallas_call | solution.py:38
  2.6 0.5 collective-permute-start.2
  3.3 3.0 %collective-permute-start.6 = (bf16[1024,256]{1,0:T(8,128)(2,1)S(1)}, bf16[1024,256]{1,0:T(8,128)(2,1)S(1)}, u32[]{:S(2)}, u32[]{:S(2)}) collective-permute-start(bf16[1024,256]{1,0:T(8,128)(2,1)S(1)} %get-tuple-element.82.kv), channel_id=1, source_target_pairs={{0,2},{1,3},{2,0},{3,1},{4,6},{5,7},{6,4},{7,5},{8,10},{9,11},{10,... | collective-permute-start | bytes 1572872 | tf_op jit(solution)/shard_map/ppermute | solution.py:541
  6.3 2.7 %collective-permute-start.7 = (bf16[1024,128]{1,0:T(8,128)(2,1)S(1)}, bf16[1024,128]{1,0:T(8,128)(2,1)S(1)}, u32[]{:S(2)}, u32[]{:S(2)}) collective-permute-start(bf16[1024,128]{1,0:T(8,128)(2,1)S(1)} %shard_map.85.keys), channel_id=1, source_target_pairs={{0,4},{1,5},{2,6},{3,7},{4,0},{5,1},{6,2},{7,3},{8,12},{9,13},{10,... | collective-permute-start | bytes 786440 | tf_op jit(solution)/shard_map/ppermute | solution.py:541
  9.2 0.6 %shard_map.88 = bf16[512,256]{1,0:T(8,128)(2,1)S(1)} custom-call(s32[8,16]{1,0:T(8,128)S(1)} %get-tuple-element.77.lists.lists_any.refs_0_, bf16[1024,256]{1,0:T(8,128)(2,1)S(1)} %get-tuple-element.82.kv), custom_call_target="tpu_custom_call" | custom-call | flops 1024 | bytes 1024 | tf_op jit(solution)/shard_map/pallas_call | solution.py:38
  9.8 6.3 %collective-permute-done.7.z.z_k = bf16[1024,128]{1,0:T(8,128)(2,1)S(1)} collective-permute-done((bf16[1024,128]{1,0:T(8,128)(2,1)S(1)}, bf16[1024,128]{1,0:T(8,128)(2,1)S(1)}, u32[]{:S(2)}, u32[]{:S(2)}) %collective-permute-start.7) | collective-permute-done | bytes 262176 | tf_op jit(solution)/shard_map/ppermute | solution.py:541
  16.2 0.6 collective-permute-start.8
  16.7 1.9 %collective-permute-start.9 = (bf16[512,256]{1,0:T(8,128)(2,1)S(1)}, bf16[512,256]{1,0:T(8,128)(2,1)S(1)}, u32[]{:S(2)}, u32[]{:S(2)}) collective-permute-start(bf16[512,256]{1,0:T(8,128)(2,1)S(1)} %shard_map.88), channel_id=1, source_target_pairs={{0,8},{1,9},{2,10},{3,11},{4,12},{5,13},{6,14},{7,15},{8,0},{9,1},... | collective-permute-start | bytes 786440 | tf_op jit(solution)/shard_map/ppermute | solution.py:541
  19.0 3.5 %shard_map.90 = (f32[8,1024]{1,0:T(8,128)S(1)}, f32[128,1024]{1,0:T(8,128)S(1)}) custom-call(s32[8,16]{1,0:T(8,128)S(1)} %get-tuple-element.77.lists.lists_any.refs_0_, bf16[1024,256]{1,0:T(8,128)(2,1)S(1)} %get-tuple-element.76.qg.refs_1_, bf16[1024,256]{1,0:T(8,128)(2,1)S(1)} %get-tuple-element.82.kv, bf16[1024,256]{1,0:T(8,128)(2,1)S(1)} %collective-permute-done.6.a_kv), custom_call_target="tpu_custom_call" | custom-call | flops 1024 | bytes 1024 | tf_op jit(solution)/shard_map/pallas_call | solution.py:38
  22.5 1.2 %collective-permute-done.5.z.z_v = bf16[1024,128]{1,0:T(8,128)(2,1)S(1)} collective-permute-done((bf16[1024,128]{1,0:T(8,128)(2,1)S(1)}, bf16[1024,128]{1,0:T(8,128)(2,1)S(1)}, u32[]{:S(2)}, u32[]{:S(2)}) %collective-permute-start.5) | collective-permute-done | bytes 262176 | tf_op jit(solution)/shard_map/ppermute | solution.py:541
  23.9 1.0 %collective-permute-start.10 = (bf16[1024,128]{1,0:T(8,128)(2,1)S(1)}, bf16[1024,128]{1,0:T(8,128)(2,1)S(1)}, u32[]{:S(2)}, u32[]{:S(2)}) collective-permute-start(bf16[1024,128]{1,0:T(8,128)(2,1)S(1)} %shard_map.91), channel_id=1, source_target_pairs={{0,2},{1,3},{2,0},{3,1},{4,6},{5,7},{6,4},{7,5},{8,10},{9,11},{10,... | collective-permute-start | bytes 786440 | tf_op jit(solution)/shard_map/ppermute | solution.py:541
  24.9 2.6 %shard_map.92 = (f32[8,1024]{1,0:T(8,128)S(1)}, f32[128,1024]{1,0:T(8,128)S(1)}, f32[2,512,512]{2,1,0:T(8,128)S(1)}) custom-call(s32[8,16]{1,0:T(8,128)S(1)} %get-tuple-element.77.lists.lists_any.refs_0_, bf16[1024,256]{1,0:T(8,128)(2,1)S(1)} %get-tuple-element.76.qg.refs_1_, f32[8,1024]{1,0:T(8,128)S(1)} %get-tuple-element.93.stat, ...), custom_call_target="tpu_custom_call" | custom-call | flops 1024 | bytes 1024 | tf_op jit(solution)/shard_map/pallas_call | solution.py:38
  27.5 3.2 %collective-permute-done.9.refs_0_.refs_8_ = bf16[512,256]{1,0:T(8,128)(2,1)S(1)} collective-permute-done((bf16[512,256]{1,0:T(8,128)(2,1)S(1)}, bf16[512,256]{1,0:T(8,128)(2,1)S(1)}, u32[]{:S(2)}, u32[]{:S(2)}) %collective-permute-start.9) | collective-permute-done | bytes 262176 | tf_op jit(solution)/shard_map/ppermute | solution.py:541
  30.7 1.5 %shard_map.93 = (f32[8,1024]{1,0:T(8,128)S(1)}, f32[128,1024]{1,0:T(8,128)S(1)}, bf16[1024,128]{1,0:T(8,128)(2,1)S(1)}, f32[2,512,512]{2,1,0:T(8,128)S(1)}, bf16[512,128]{1,0:T(8,128)(2,1)S(1)}) custom-call(s32[8,16]{1,0:T(8,128)S(1)} %get-tuple-element.77.lists.lists_any.refs_0_, bf16[1024,256]{1,0:T(8,128)(2,1)S(1)} %get-tuple-element.76.qg.refs_1_, ...), custom_call_target="tpu_custom_call" | custom-call | flops 1024 | bytes 1024 | tf_op jit(solution)/shard_map/pallas_call | solution.py:38
  32.2 1.5 %collective-permute-start.12 = (bf16[1024,128]{1,0:T(8,128)(2,1)S(1)}, bf16[1024,128]{1,0:T(8,128)(2,1)S(1)}, u32[]{:S(2)}, u32[]{:S(2)}) collective-permute-start(bf16[1024,128]{1,0:T(8,128)(2,1)S(1)} %get-tuple-element.109), channel_id=1, source_target_pairs={{0,2},{1,3},{2,0},{3,1},{4,6},{5,7},{6,4},{7,5},{8,10},{9,11},{10,... | collective-permute-start | bytes 786440 | tf_op jit(solution)/shard_map/ppermute | solution.py:541
  33.8 2.3 %shard_map.94 = (bf16[128,1024]{1,0:T(8,128)(2,1)S(1)}, f32[8,1024]{1,0:T(8,128)S(1)}, bf16[1024,128]{1,0:T(8,128)(2,1)S(1)}, f32[128,1024]{1,0:T(8,128)S(1)}, bf16[512,128]{1,0:T(8,128)(2,1)S(1)}) custom-call(s32[8,16]{1,0:T(8,128)S(1)} %get-tuple-element.77.lists.lists_any.refs_0_, bf16[1024,256]{1,0:T(8,128)(2,1)S(1)} %get-tuple-element.76.qg.refs_1_, ...), custom_call_target="tpu_custom_call" | custom-call | flops 1024 | bytes 1024 | tf_op jit(solution)/shard_map/pallas_call | solution.py:38
  36.1 0.6 collective-permute-start.14
  36.7 2.9 %collective-permute-start.11 = (bf16[512,128]{1,0:T(8,128)(2,1)S(1)}, bf16[512,128]{1,0:T(8,128)(2,1)S(1)}, u32[]{:S(2)}, u32[]{:S(2)}) collective-permute-start(bf16[512,128]{1,0:T(8,128)(2,1)S(1)} %get-tuple-element.106), channel_id=1, source_target_pairs={{0,8},{1,9},{2,10},{3,11},{4,12},{5,13},{6,14},{7,15},{8,0},{9,1},... | collective-permute-start | bytes 393224 | tf_op jit(solution)/shard_map/ppermute | solution.py:541
  39.6 2.2 %shard_map.95 = (bf16[1024,256]{1,0:T(8,128)(2,1)S(1)}, f32[128,1024]{1,0:T(8,128)S(1)}) custom-call(s32[8,16]{1,0:T(8,128)S(1)} %get-tuple-element.77.lists.lists_any.refs_0_, bf16[1024,256]{1,0:T(8,128)(2,1)S(1)} %get-tuple-element.76.qg.refs_1_, f32[8,1024]{1,0:T(8,128)S(1)} %get-tuple-element.101.refs_3_.lse_ref, ...), custom_call_target="tpu_custom_call" | custom-call | flops 1024 | bytes 1024 | tf_op jit(solution)/shard_map/pallas_call | solution.py:38
  41.9 1.7 %collective-permute-done.13.refs_2_ = bf16[512,128]{1,0:T(8,128)(2,1)S(1)} collective-permute-done((bf16[512,128]{1,0:T(8,128)(2,1)S(1)}, bf16[512,128]{1,0:T(8,128)(2,1)S(1)}, u32[]{:S(2)}, u32[]{:S(2)}) %collective-permute-start.13) | collective-permute-done | bytes 131104 | tf_op jit(solution)/shard_map/ppermute | solution.py:541
  43.6 2.2 %shard_map.96 = (f32[1024,256]{1,0:T(8,128)S(1)}, f32[1024,256]{1,0:T(8,128)S(1)}, f32[128,1024]{1,0:T(8,128)S(1)}) custom-call(s32[8,16]{1,0:T(8,128)S(1)} %get-tuple-element.77.lists.lists_any.refs_0_, bf16[1024,256]{1,0:T(8,128)(2,1)S(1)} %get-tuple-element.76.qg.refs_1_, f32[8,1024]{1,0:T(8,128)S(1)} %get-tuple-element.101.refs_3_.lse_ref, ...), custom_call_target="tpu_custom_call" | custom-call | flops 2684354560 | bytes 1024 | tf_op jit(solution)/shard_map/pallas_call | solution.py:38
  45.8 0.7 %collective-permute-start.16 = (bf16[1024,256]{1,0:T(8,128)(2,1)S(1)}, bf16[1024,256]{1,0:T(8,128)(2,1)S(1)}, u32[]{:S(2)}, u32[]{:S(2)}) collective-permute-start(bf16[1024,256]{1,0:T(8,128)(2,1)S(1)} %get-tuple-element.133), channel_id=1, source_target_pairs={{0,2},{1,3},{2,0},{3,1},{4,6},{5,7},{6,4},{7,5},{8,10},{9,11},{10,... | collective-permute-start | bytes 1572872 | tf_op jit(solution)/shard_map/ppermute | solution.py:541
  46.9 0.8 %collective-permute-done.11.refs_1_ = bf16[512,128]{1,0:T(8,128)(2,1)S(1)} collective-permute-done((bf16[512,128]{1,0:T(8,128)(2,1)S(1)}, bf16[512,128]{1,0:T(8,128)(2,1)S(1)}, u32[]{:S(2)}, u32[]{:S(2)}) %collective-permute-start.11) | collective-permute-done | bytes 131104 | tf_op jit(solution)/shard_map/ppermute | solution.py:541
  47.7 0.7 %shard_map.98.placed = f32[1024,256]{1,0:T(8,128)S(1)} custom-call(s32[8,16]{1,0:T(8,128)S(1)} %get-tuple-element.77.lists.lists_any.refs_0_, bf16[512,128]{1,0:T(8,128)(2,1)S(1)} %collective-permute-done.11.refs_1_, bf16[512,128]{1,0:T(8,128)(2,1)S(1)} %collective-permute-done.13.refs_2_), custom_call_target="tpu_custom_call" | custom-call | flops 1024 | bytes 1024 | tf_op jit(solution)/shard_map/pallas_call | solution.py:38
  48.5 3.2 %shard_map.99 = (f32[1024,256]{1,0:T(8,128)S(1)}, bf16[512,256]{1,0:T(8,128)(2,1)S(1)}, bf16[512,256]{1,0:T(8,128)(2,1)S(1)}) custom-call(bf16[1024,256]{1,0:T(8,128)(2,1)S(1)} %get-tuple-element.76.qg.refs_1_, f32[8,1024]{1,0:T(8,128)S(1)} %get-tuple-element.101.refs_3_.lse_ref, f32[8,1024]{1,0:T(8,128)S(1)} %get-tuple-element.105.dot_ref, ...), custom_call_target="tpu_custom_call" | custom-call | flops 2684354560 | bytes 1024 | tf_op jit(solution)/shard_map/pallas_call | solution.py:38
  51.7 1.5 %collective-permute-done.15.came = bf16[512,256]{1,0:T(8,128)(2,1)S(1)} collective-permute-done((bf16[512,256]{1,0:T(8,128)(2,1)S(1)}, bf16[512,256]{1,0:T(8,128)(2,1)S(1)}, u32[]{:S(2)}, u32[]{:S(2)}) %collective-permute-start.15) | collective-permute-done | bytes 262176 | tf_op jit(solution)/shard_map/ppermute | solution.py:538
  53.2 0.9 %shard_map.100 = (bf16[512,256]{1,0:T(8,128)(2,1)}, bf16[512,256]{1,0:T(8,128)(2,1)}) custom-call(bf16[512,256]{1,0:T(8,128)(2,1)S(1)} %get-tuple-element.126.keep, bf16[512,256]{1,0:T(8,128)(2,1)S(1)} %collective-permute-done.15.came), custom_call_target="tpu_custom_call" | custom-call | flops 1024 | bytes 1024 | tf_op jit(solution)/shard_map/pallas_call | solution.py:38
  54.1 2.9 %collective-permute-done.16.refs_0_ = bf16[1024,256]{1,0:T(8,128)(2,1)S(1)} collective-permute-done((bf16[1024,256]{1,0:T(8,128)(2,1)S(1)}, bf16[1024,256]{1,0:T(8,128)(2,1)S(1)}, u32[]{:S(2)}, u32[]{:S(2)}) %collective-permute-start.16) | collective-permute-done | bytes 524320 | tf_op jit(solution)/shard_map/ppermute | solution.py:541
  57.2 3.9 %collective-permute-done.18.came = bf16[1024,256]{1,0:T(8,128)(2,1)S(1)} collective-permute-done((bf16[1024,256]{1,0:T(8,128)(2,1)S(1)}, bf16[1024,256]{1,0:T(8,128)(2,1)S(1)}, u32[]{:S(2)}, u32[]{:S(2)}) %collective-permute-start.18) | collective-permute-done | bytes 524320 | tf_op jit(solution)/shard_map/ppermute | solution.py:541
  61.4 1.5 %collective-permute-done.19.came = bf16[512,256]{1,0:T(8,128)(2,1)S(1)} collective-permute-done((bf16[512,256]{1,0:T(8,128)(2,1)S(1)}, bf16[512,256]{1,0:T(8,128)(2,1)S(1)}, u32[]{:S(2)}, u32[]{:S(2)}) %collective-permute-start.19) | collective-permute-done | bytes 262176 | tf_op jit(solution)/shard_map/ppermute | solution.py:538
  62.9 0.9 %shard_map.103 = (bf16[512,256]{1,0:T(8,128)(2,1)}, bf16[512,256]{1,0:T(8,128)(2,1)}) custom-call(bf16[512,256]{1,0:T(8,128)(2,1)S(1)} %get-tuple-element.134.keep, bf16[512,256]{1,0:T(8,128)(2,1)S(1)} %collective-permute-done.19.came), custom_call_target="tpu_custom_call" | custom-call | flops 1024 | bytes 1024 | tf_op jit(solution)/shard_map/pallas_call | solution.py:38
  (28 shorter events, 2.0 us)
Async XLA Ops:
  0.6 1.9 %collective-permute-start = (bf16[512,256]{1,0:T(8,128)(2,1)}, bf16[512,256]{1,0:T(8,128)(2,1)S(1)}, u32[]{:S(2)}, u32[]{:S(2)}) collective-permute-start(bf16[512,256]{1,0:T(8,128)(2,1)} %k.1), channel_id=1, source_target_pairs={{0,1},{1,0},{2,3},{3,2},{4,5},{5,4},{6,7},{7,6},{8,9},{9,8},{10,11... | collective-permute-start | bytes 786440 | tf_op jit(solution)/shard_map/ppermute | solution.py:538
  1.2 2.0 %collective-permute-start.3 = (bf16[512,256]{1,0:T(8,128)(2,1)}, bf16[512,256]{1,0:T(8,128)(2,1)S(1)}, u32[]{:S(2)}, u32[]{:S(2)}) collective-permute-start(bf16[512,256]{1,0:T(8,128)(2,1)} %v.1), channel_id=1, source_target_pairs={{0,1},{1,0},{2,3},{3,2},{4,5},{5,4},{6,7},{7,6},{8,9},{9,8},{10,11... | collective-permute-start | bytes 786440 | tf_op jit(solution)/shard_map/ppermute | solution.py:538
  2.6 6.5 %collective-permute-start.2 = (bf16[512,256]{1,0:T(8,128)(2,1)S(1)}, bf16[512,256]{1,0:T(8,128)(2,1)S(1)}, u32[]{:S(2)}, u32[]{:S(2)}) collective-permute-start(bf16[512,256]{1,0:T(8,128)(2,1)S(1)} %get-tuple-element.74), channel_id=1, source_target_pairs={{0,1},{1,0},{2,3},{3,2},{4,5},{5,4},{6,7},{7,6},{8,9},{9,8},{10,11... | collective-permute-start | bytes 786440 | tf_op jit(solution)/shard_map/ppermute | solution.py:538
  3.1 6.0 %collective-permute-start.1 = (bf16[1024,128]{1,0:T(8,128)(2,1)S(1)}, bf16[1024,128]{1,0:T(8,128)(2,1)S(1)}, u32[]{:S(2)}, u32[]{:S(2)}) collective-permute-start(bf16[1024,128]{1,0:T(8,128)(2,1)S(1)} %shard_map.85.keys), channel_id=1, source_target_pairs={{0,1},{1,0},{2,3},{3,2},{4,8},{5,9},{6,10},{7,11},{8,4},{9,5},{10,... | collective-permute-start | bytes 786440 | tf_op jit(solution)/shard_map/ppermute | solution.py:541
  3.3 15.7 %collective-permute-start.6 = (bf16[1024,256]{1,0:T(8,128)(2,1)S(1)}, bf16[1024,256]{1,0:T(8,128)(2,1)S(1)}, u32[]{:S(2)}, u32[]{:S(2)}) collective-permute-start(bf16[1024,256]{1,0:T(8,128)(2,1)S(1)} %get-tuple-element.82.kv), channel_id=1, source_target_pairs={{0,2},{1,3},{2,0},{3,1},{4,6},{5,7},{6,4},{7,5},{8,10},{9,11},{10,... | collective-permute-start | bytes 1572872 | tf_op jit(solution)/shard_map/ppermute | solution.py:541
  6.3 9.8 %collective-permute-start.7 = (bf16[1024,128]{1,0:T(8,128)(2,1)S(1)}, bf16[1024,128]{1,0:T(8,128)(2,1)S(1)}, u32[]{:S(2)}, u32[]{:S(2)}) collective-permute-start(bf16[1024,128]{1,0:T(8,128)(2,1)S(1)} %shard_map.85.keys), channel_id=1, source_target_pairs={{0,4},{1,5},{2,6},{3,7},{4,0},{5,1},{6,2},{7,3},{8,12},{9,13},{10,... | collective-permute-start | bytes 786440 | tf_op jit(solution)/shard_map/ppermute | solution.py:541
  9.0 14.6 %collective-permute-start.5 = (bf16[1024,128]{1,0:T(8,128)(2,1)S(1)}, bf16[1024,128]{1,0:T(8,128)(2,1)S(1)}, u32[]{:S(2)}, u32[]{:S(2)}) collective-permute-start(bf16[1024,128]{1,0:T(8,128)(2,1)S(1)} %get-tuple-element.79), channel_id=1, source_target_pairs={{0,4},{1,5},{2,6},{3,7},{4,0},{5,1},{6,2},{7,3},{8,12},{9,13},{10,... | collective-permute-start | bytes 786440 | tf_op jit(solution)/shard_map/ppermute | solution.py:541
  9.0 14.6 %collective-permute-start.4 = (bf16[1024,128]{1,0:T(8,128)(2,1)S(1)}, bf16[1024,128]{1,0:T(8,128)(2,1)S(1)}, u32[]{:S(2)}, u32[]{:S(2)}) collective-permute-start(bf16[1024,128]{1,0:T(8,128)(2,1)S(1)} %get-tuple-element.79), channel_id=1, source_target_pairs={{0,1},{1,0},{2,3},{3,2},{4,8},{5,9},{6,10},{7,11},{8,4},{9,5},{10,... | collective-permute-start | bytes 786440 | tf_op jit(solution)/shard_map/ppermute | solution.py:541
  16.2 8.7 %collective-permute-start.8 = (bf16[1024,128]{1,0:T(8,128)(2,1)S(1)}, bf16[1024,128]{1,0:T(8,128)(2,1)S(1)}, u32[]{:S(2)}, u32[]{:S(2)}) collective-permute-start(bf16[1024,128]{1,0:T(8,128)(2,1)S(1)} %shard_map.89), channel_id=1, source_target_pairs={{0,2},{1,3},{2,0},{3,1},{4,6},{5,7},{6,4},{7,5},{8,10},{9,11},{10,... | collective-permute-start | bytes 786440 | tf_op jit(solution)/shard_map/ppermute | solution.py:541
  16.7 14.0 %collective-permute-start.9 = (bf16[512,256]{1,0:T(8,128)(2,1)S(1)}, bf16[512,256]{1,0:T(8,128)(2,1)S(1)}, u32[]{:S(2)}, u32[]{:S(2)}) collective-permute-start(bf16[512,256]{1,0:T(8,128)(2,1)S(1)} %shard_map.88), channel_id=1, source_target_pairs={{0,8},{1,9},{2,10},{3,11},{4,12},{5,13},{6,14},{7,15},{8,0},{9,1},... | collective-permute-start | bytes 786440 | tf_op jit(solution)/shard_map/ppermute | solution.py:541
  23.9 9.9 %collective-permute-start.10 = (bf16[1024,128]{1,0:T(8,128)(2,1)S(1)}, bf16[1024,128]{1,0:T(8,128)(2,1)S(1)}, u32[]{:S(2)}, u32[]{:S(2)}) collective-permute-start(bf16[1024,128]{1,0:T(8,128)(2,1)S(1)} %shard_map.91), channel_id=1, source_target_pairs={{0,2},{1,3},{2,0},{3,1},{4,6},{5,7},{6,4},{7,5},{8,10},{9,11},{10,... | collective-permute-start | bytes 786440 | tf_op jit(solution)/shard_map/ppermute | solution.py:541
  32.2 11.3 %collective-permute-start.12 = (bf16[1024,128]{1,0:T(8,128)(2,1)S(1)}, bf16[1024,128]{1,0:T(8,128)(2,1)S(1)}, u32[]{:S(2)}, u32[]{:S(2)}) collective-permute-start(bf16[1024,128]{1,0:T(8,128)(2,1)S(1)} %get-tuple-element.109), channel_id=1, source_target_pairs={{0,2},{1,3},{2,0},{3,1},{4,6},{5,7},{6,4},{7,5},{8,10},{9,11},{10,... | collective-permute-start | bytes 786440 | tf_op jit(solution)/shard_map/ppermute | solution.py:541
  33.8 9.8 %collective-permute-start.13 = (bf16[512,128]{1,0:T(8,128)(2,1)S(1)}, bf16[512,128]{1,0:T(8,128)(2,1)S(1)}, u32[]{:S(2)}, u32[]{:S(2)}) collective-permute-start(bf16[512,128]{1,0:T(8,128)(2,1)S(1)} %get-tuple-element.110), channel_id=1, source_target_pairs={{0,8},{1,9},{2,10},{3,11},{4,12},{5,13},{6,14},{7,15},{8,0},{9,1},... | collective-permute-start | bytes 393224 | tf_op jit(solution)/shard_map/ppermute | solution.py:541
  36.1 9.8 %collective-permute-start.14 = (bf16[1024,128]{1,0:T(8,128)(2,1)S(1)}, bf16[1024,128]{1,0:T(8,128)(2,1)S(1)}, u32[]{:S(2)}, u32[]{:S(2)}) collective-permute-start(bf16[1024,128]{1,0:T(8,128)(2,1)S(1)} %get-tuple-element.116), channel_id=1, source_target_pairs={{0,2},{1,3},{2,0},{3,1},{4,6},{5,7},{6,4},{7,5},{8,10},{9,11},{10,... | collective-permute-start | bytes 786440 | tf_op jit(solution)/shard_map/ppermute | solution.py:541
  36.7 11.0 %collective-permute-start.11 = (bf16[512,128]{1,0:T(8,128)(2,1)S(1)}, bf16[512,128]{1,0:T(8,128)(2,1)S(1)}, u32[]{:S(2)}, u32[]{:S(2)}) collective-permute-start(bf16[512,128]{1,0:T(8,128)(2,1)S(1)} %get-tuple-element.106), channel_id=1, source_target_pairs={{0,8},{1,9},{2,10},{3,11},{4,12},{5,13},{6,14},{7,15},{8,0},{9,1},... | collective-permute-start | bytes 393224 | tf_op jit(solution)/shard_map/ppermute | solution.py:541
  45.8 11.2 %collective-permute-start.16 = (bf16[1024,256]{1,0:T(8,128)(2,1)S(1)}, bf16[1024,256]{1,0:T(8,128)(2,1)S(1)}, u32[]{:S(2)}, u32[]{:S(2)}) collective-permute-start(bf16[1024,256]{1,0:T(8,128)(2,1)S(1)} %get-tuple-element.133), channel_id=1, source_target_pairs={{0,2},{1,3},{2,0},{3,1},{4,6},{5,7},{6,4},{7,5},{8,10},{9,11},{10,... | collective-permute-start | bytes 1572872 | tf_op jit(solution)/shard_map/ppermute | solution.py:541
  46.7 10.3 %collective-permute-start.17 = (bf16[1024,256]{1,0:T(8,128)(2,1)S(1)}, bf16[1024,256]{1,0:T(8,128)(2,1)S(1)}, u32[]{:S(2)}, u32[]{:S(2)}) collective-permute-start(bf16[1024,256]{1,0:T(8,128)(2,1)S(1)} %get-tuple-element.119), channel_id=1, source_target_pairs={{0,1},{1,0},{2,3},{3,2},{4,8},{5,9},{6,10},{7,11},{8,4},{9,5},{10,... | collective-permute-start | bytes 1572872 | tf_op jit(solution)/shard_map/ppermute | solution.py:541
  46.8 14.3 %collective-permute-start.18 = (bf16[1024,256]{1,0:T(8,128)(2,1)S(1)}, bf16[1024,256]{1,0:T(8,128)(2,1)S(1)}, u32[]{:S(2)}, u32[]{:S(2)}) collective-permute-start(bf16[1024,256]{1,0:T(8,128)(2,1)S(1)} %get-tuple-element.118), channel_id=1, source_target_pairs={{0,4},{1,5},{2,6},{3,7},{4,0},{5,1},{6,2},{7,3},{8,12},{9,13},{10,... | collective-permute-start | bytes 1572872 | tf_op jit(solution)/shard_map/ppermute | solution.py:541
  51.6 1.6 %collective-permute-start.15 = (bf16[512,256]{1,0:T(8,128)(2,1)S(1)}, bf16[512,256]{1,0:T(8,128)(2,1)S(1)}, u32[]{:S(2)}, u32[]{:S(2)}) collective-permute-start(bf16[512,256]{1,0:T(8,128)(2,1)S(1)} %get-tuple-element.127), channel_id=1, source_target_pairs={{0,1},{1,0},{2,3},{3,2},{4,5},{5,4},{6,7},{7,6},{8,9},{9,8},{10,11... | collective-permute-start | bytes 786440 | tf_op jit(solution)/shard_map/ppermute | solution.py:538
  61.3 1.6 %collective-permute-start.19 = (bf16[512,256]{1,0:T(8,128)(2,1)S(1)}, bf16[512,256]{1,0:T(8,128)(2,1)S(1)}, u32[]{:S(2)}, u32[]{:S(2)}) collective-permute-start(bf16[512,256]{1,0:T(8,128)(2,1)S(1)} %get-tuple-element.135), channel_id=1, source_target_pairs={{0,1},{1,0},{2,3},{3,2},{4,5},{5,4},{6,7},{7,6},{8,9},{9,8},{10,11... | collective-permute-start | bytes 786440 | tf_op jit(solution)/shard_map/ppermute | solution.py:538

commit v12 on v11

--- a/solution.py
+++ b/solution.py
@@ -341,9 +341,7 @@
 def close_kernel(block, relayed, far, lists_any, qg, stat, acc, late_s, *refs):
     n = len(far)
     far_kv = refs[:n]
-    lse_ref, part_ref, dc_v, p_ref = refs[n : n + 4]
-    far_dv = refs[n + 4 : 2 * n + 4]
-    s_ref, grad, lists, sem = refs[2 * n + 4 :]
+    lse_ref, part_ref, dc_v, p_ref, s_ref, grad, lists, sem = refs[n:]
     half = qg.shape[0] // 2
     frame = lax.axis_index("tm")
     copy = pltpu.make_async_copy(lists_any, lists, sem)
@@ -351,19 +349,13 @@
     grad[...] = jnp.zeros_like(grad)
     for slab in range(2):
         rows = rows_of(slab, half)
-        q, g = qg[rows, KEY], qg[rows, VALUE]
-        groups = [
-            [arrived(swap, frame, slab, block, kv, dv=(out, ALL))]
-            for swap, kv, out in zip(far, far_kv, far_dv)
-        ]
+        q = qg[rows, KEY]
+        groups = [[arrived(swap, frame, slab, block, kv)] for swap, kv in zip(far, far_kv)]
         old = load_state((stat, acc), rows)
         peak, total, out = forward_slab(q, groups, n, s_ref, old)
         part_ref[:, rows] = out / total
         lse = peak * EXP_SCALE + jnp.log2(total)
         lse_ref[0:1, rows] = lse
-        for group, s in group_scores(groups, s_ref):
-            p = raised(group, s, lse)
-            store_grads(group, dot_nn(p.astype(BF16), g), "dv")
     copy.wait()
     for slab in range(2):
         rows = rows_of(slab, half)
@@ -398,7 +390,7 @@
         dot_ref[0:1, rows] = row_dot
         dq = backward_group(q, g, lse, row_dot, group, p)
         for swap, kv, out in zip(far, far_kv, far_grad):
-            group = [arrived(swap, frame, slab, block, kv, dk=(out, ALL))]
+            group = [arrived(swap, frame, slab, block, kv, dk=(out, KEY), dv=(out, VALUE))]
             dq = dq + backward_group(q, g, lse, row_dot, group)
         dq_ref[:, rows] = dq
     dc_k[...] = grad[...].astype(BF16)
@@ -470,17 +462,15 @@
 
 
 def place_kernel(block, far, *refs):
-    n = len(far)
     lists, total = refs[0], refs[-1]
     frame = lax.axis_index("tm")
     total[...] = jnp.zeros_like(total)
-    for swap, came_k, came_v in zip(far, refs[1 : 1 + n], refs[1 + n : -1]):
+    for swap, came in zip(far, refs[1:-1]):
         for slab in range(2):
             b, exists = swap.block_of_theirs(lists, frame, slab, 0)
             rows = pl.ds(pl.multiple_of(b * block, block), block)
-            for came, cols in ((came_k, KEY), (came_v, VALUE)):
-                part = came[rows_of(slab, block), :].astype(F32)
-                total[rows, cols] += jnp.where(exists, part, 0.0)
+            part = came[rows_of(slab, block), :].astype(F32)
+            total[rows, :] += jnp.where(exists, part, 0.0)
 
 
 def add_kernel(swaps, near, *refs):
@@ -591,10 +581,10 @@
         scratch=[scores(4)],
     )
     acc, far_kv = lax.optimization_barrier((acc, far_kv))
-    lse, part, dc_v, probs, *far_dv = call(
+    lse, part, dc_v, probs = call(
         functools.partial(close_kernel, block, relayed, far),
         (lists, qg, stat, acc, late_scores, *far_kv),
-        [stat_row, turned_sum, frame_one, score_two] + [single] * n,
+        [stat_row, turned_sum, frame_one, score_two],
         scratch=[
             scores(n),
             grad_one,
@@ -604,14 +594,13 @@
         scalars=pl.BlockSpec(memory_space=pl.ANY),
     )
     dc_v_came = swapped(dc_v, near_swap)
-    far_dv_came = [swapped(value, swap) for value, swap in zip(far_dv, far)]
     o, row_dot, dc_k, dq, *far_grad = call(
         functools.partial(late_kernel, block, relayed, far),
         (lists, qg, turned, lse, part, probs, c_k, c_v, *far_kv),
-        [turned_bf, stat_row, frame_one, turned_sum] + [single] * n,
+        [turned_bf, stat_row, frame_one, turned_sum] + [pair] * n,
         scratch=[grad_one],
     )
-    far_dk_came = [swapped(value, swap) for value, swap in zip(far_grad, far)]
+    far_came = [swapped(value, swap) for value, swap in zip(far_grad, far)]
     dc_k_came = swapped(dc_k, near_swap)
     da, dq = call(
         functools.partial(first_kernel, block, near_swap),
@@ -621,7 +610,6 @@
     )
     da, dc_k_came = lax.optimization_barrier((da, dc_k_came))
     da_came = swapped(da, near_swap)
-    dc_v_came, far_dv_came = lax.optimization_barrier((dc_v_came, far_dv_came))
     dz, dy, dq = call(
         functools.partial(second_kernel, block, (z_swap, y_swap)),
         (lists, qg, lse, row_dot, dq, dc_v_came, y_k, z_k, y_v, z_v),
@@ -632,8 +620,8 @@
     dy_came = swapped(dy, y_swap)
     dz_came = swapped(dz, z_swap)
     dq, dz, dy = lax.optimization_barrier((dq, dz, dy))
-    far_dk_came, dq = lax.optimization_barrier((far_dk_came, dq))
-    (placed,) = call(functools.partial(place_kernel, block, far), (lists, *far_dk_came, *far_dv_came), [frame_sum])
+    far_came, dq = lax.optimization_barrier((far_came, dq))
+    (placed,) = call(functools.partial(place_kernel, block, far), (lists, *far_came), [frame_sum])
     near, q_keep, q_send = call(
         own_kernel,
         (qg, lse, row_dot, dq, o, kv, placed),

time: 64 us -> 63.8 us (level)
  starting transfers between devices: 16.5 us -> 14.7 us
  waiting for transfers between devices: 23.4 us -> 25 us
    ppermute x15 -> x14, starting transfers between devices: 15.3 us -> 13.5 us  [swapped(): return lax.ppermute(value, ('tm', 'space'), swap.pairs)]
    ppermute x15 -> x14, waiting for transfers between devices: 20.3 us -> 22 us  [swapped(): return lax.ppermute(value, ('tm', 'space'), swap.pairs)]
  transfers between devices with their start and end apart: 20 -> 19, of which waited for: 10 -> 11; matrix products, arithmetic and copies ran while one was open for 0% -> 0% of each run, Pallas kernels for 35% -> 35%
where the time goes in v12:
time: 63.8 us; the launch traced here: 63.6 us
  waiting for transfers between devices  25 us (39%)
  Pallas kernels  23.1 us (36%)
  starting transfers between devices  14.7 us (23%)
  between operations  0.8 us (1%)
    pallas_call x20, Pallas kernels, call(): pl.pallas_call(kernel, out_shape=out_shape, in_specs=[scalars if a.dtype...  23.1 us
    ppermute x14, waiting for transfers between devices, swapped(): return lax.ppermute(value, ('tm', 'space'), swap.pairs)  22 us
    ppermute x14, starting transfers between devices, swapped(): return lax.ppermute(value, ('tm', 'space'), swap.pairs)  13.5 us
    ppermute x5, waiting for transfers between devices, across(): return lax.ppermute(value, 'space', [(0, 1), (1, 0)])  3.06 us
  transfers between devices with their start and end apart: 19, of which 11 were waited for; matrix products, arithmetic and copies ran while one was open for 0% of the time, Pallas kernels for 35%

profile of v12, /device:TPU:0, one launch (start us, length us, event | category | flops | bytes accessed | tf_op | source)
XLA Modules:
  0.0 63.6 jit_solution(5662909013412914245)
XLA Ops:
  0.6 0.5 collective-permute-start
  1.2 1.3 %shard_map.84 = (bf16[512,128]{1,0:T(8,128)(2,1)S(1)}, bf16[512,128]{1,0:T(8,128)(2,1)S(1)}, bf16[512,256]{1,0:T(8,128)(2,1)S(1)}, bf16[512,256]{1,0:T(8,128)(2,1)S(1)}, s32[8,16]{1,0:T(8,128)S(1)}) custom-call(bf16[512,256]{1,0:T(8,128)(2,1)} %k.1, bf16[512,256]{1,0:T(8,128)(2,1)} %v.1, bf16[512,256]{1,0:T(8,128)(2,1)} %q.1, bf16[512,256]{1,0:T(8,128)(2,1)} %g.1, ...), custom_call_target="tpu_custom_call" | custom-call | flops 1024 | bytes 1024 | tf_op jit(solution)/shard_map/pallas_call | solution.py:38
  2.6 0.5 collective-permute-start.2
  3.3 3.0 %collective-permute-start.6 = (bf16[1024,256]{1,0:T(8,128)(2,1)S(1)}, bf16[1024,256]{1,0:T(8,128)(2,1)S(1)}, u32[]{:S(2)}, u32[]{:S(2)}) collective-permute-start(bf16[1024,256]{1,0:T(8,128)(2,1)S(1)} %get-tuple-element.79.kv), channel_id=1, source_target_pairs={{0,2},{1,3},{2,0},{3,1},{4,6},{5,7},{6,4},{7,5},{8,10},{9,11},{10,... | collective-permute-start | bytes 1572872 | tf_op jit(solution)/shard_map/ppermute | solution.py:531
  6.3 2.7 %collective-permute-start.7 = (bf16[1024,128]{1,0:T(8,128)(2,1)S(1)}, bf16[1024,128]{1,0:T(8,128)(2,1)S(1)}, u32[]{:S(2)}, u32[]{:S(2)}) collective-permute-start(bf16[1024,128]{1,0:T(8,128)(2,1)S(1)} %shard_map.85.keys), channel_id=1, source_target_pairs={{0,4},{1,5},{2,6},{3,7},{4,0},{5,1},{6,2},{7,3},{8,12},{9,13},{10,... | collective-permute-start | bytes 786440 | tf_op jit(solution)/shard_map/ppermute | solution.py:531
  9.2 0.6 %shard_map.88 = bf16[512,256]{1,0:T(8,128)(2,1)S(1)} custom-call(s32[8,16]{1,0:T(8,128)S(1)} %get-tuple-element.74.lists.lists_any.refs_0_, bf16[1024,256]{1,0:T(8,128)(2,1)S(1)} %get-tuple-element.79.kv), custom_call_target="tpu_custom_call" | custom-call | flops 1024 | bytes 1024 | tf_op jit(solution)/shard_map/pallas_call | solution.py:38
  9.8 6.3 %collective-permute-done.7.z.z_k = bf16[1024,128]{1,0:T(8,128)(2,1)S(1)} collective-permute-done((bf16[1024,128]{1,0:T(8,128)(2,1)S(1)}, bf16[1024,128]{1,0:T(8,128)(2,1)S(1)}, u32[]{:S(2)}, u32[]{:S(2)}) %collective-permute-start.7) | collective-permute-done | bytes 262176 | tf_op jit(solution)/shard_map/ppermute | solution.py:531
  16.2 0.6 collective-permute-start.8
  16.7 1.9 %collective-permute-start.9 = (bf16[512,256]{1,0:T(8,128)(2,1)S(1)}, bf16[512,256]{1,0:T(8,128)(2,1)S(1)}, u32[]{:S(2)}, u32[]{:S(2)}) collective-permute-start(bf16[512,256]{1,0:T(8,128)(2,1)S(1)} %shard_map.88), channel_id=1, source_target_pairs={{0,8},{1,9},{2,10},{3,11},{4,12},{5,13},{6,14},{7,15},{8,0},{9,1},... | collective-permute-start | bytes 786440 | tf_op jit(solution)/shard_map/ppermute | solution.py:531
  19.0 3.5 %shard_map.90 = (f32[8,1024]{1,0:T(8,128)S(1)}, f32[128,1024]{1,0:T(8,128)S(1)}) custom-call(s32[8,16]{1,0:T(8,128)S(1)} %get-tuple-element.74.lists.lists_any.refs_0_, bf16[1024,256]{1,0:T(8,128)(2,1)S(1)} %get-tuple-element.73.qg.refs_1_, bf16[1024,256]{1,0:T(8,128)(2,1)S(1)} %get-tuple-element.79.kv, bf16[1024,256]{1,0:T(8,128)(2,1)S(1)} %collective-permute-done.6.a_kv), custom_call_target="tpu_custom_call" | custom-call | flops 1024 | bytes 1024 | tf_op jit(solution)/shard_map/pallas_call | solution.py:38
  22.5 1.2 %collective-permute-done.5.z.z_v = bf16[1024,128]{1,0:T(8,128)(2,1)S(1)} collective-permute-done((bf16[1024,128]{1,0:T(8,128)(2,1)S(1)}, bf16[1024,128]{1,0:T(8,128)(2,1)S(1)}, u32[]{:S(2)}, u32[]{:S(2)}) %collective-permute-start.5) | collective-permute-done | bytes 262176 | tf_op jit(solution)/shard_map/ppermute | solution.py:531
  23.9 1.0 %collective-permute-start.10 = (bf16[1024,128]{1,0:T(8,128)(2,1)S(1)}, bf16[1024,128]{1,0:T(8,128)(2,1)S(1)}, u32[]{:S(2)}, u32[]{:S(2)}) collective-permute-start(bf16[1024,128]{1,0:T(8,128)(2,1)S(1)} %shard_map.91), channel_id=1, source_target_pairs={{0,2},{1,3},{2,0},{3,1},{4,6},{5,7},{6,4},{7,5},{8,10},{9,11},{10,... | collective-permute-start | bytes 786440 | tf_op jit(solution)/shard_map/ppermute | solution.py:531
  24.9 2.6 %shard_map.92 = (f32[8,1024]{1,0:T(8,128)S(1)}, f32[128,1024]{1,0:T(8,128)S(1)}, f32[2,512,512]{2,1,0:T(8,128)S(1)}) custom-call(s32[8,16]{1,0:T(8,128)S(1)} %get-tuple-element.74.lists.lists_any.refs_0_, bf16[1024,256]{1,0:T(8,128)(2,1)S(1)} %get-tuple-element.73.qg.refs_1_, f32[8,1024]{1,0:T(8,128)S(1)} %get-tuple-element.90.stat, ...), custom_call_target="tpu_custom_call" | custom-call | flops 1024 | bytes 1024 | tf_op jit(solution)/shard_map/pallas_call | solution.py:38
  27.5 3.2 %collective-permute-done.9.refs_0_.refs_8_ = bf16[512,256]{1,0:T(8,128)(2,1)S(1)} collective-permute-done((bf16[512,256]{1,0:T(8,128)(2,1)S(1)}, bf16[512,256]{1,0:T(8,128)(2,1)S(1)}, u32[]{:S(2)}, u32[]{:S(2)}) %collective-permute-start.9) | collective-permute-done | bytes 262176 | tf_op jit(solution)/shard_map/ppermute | solution.py:531
  30.7 1.4 %shard_map.93 = (f32[8,1024]{1,0:T(8,128)S(1)}, f32[128,1024]{1,0:T(8,128)S(1)}, bf16[1024,128]{1,0:T(8,128)(2,1)S(1)}, f32[2,512,512]{2,1,0:T(8,128)S(1)}) custom-call(s32[8,16]{1,0:T(8,128)S(1)} %get-tuple-element.74.lists.lists_any.refs_0_, bf16[1024,256]{1,0:T(8,128)(2,1)S(1)} %get-tuple-element.73.qg.refs_1_, f32[8,1024]{1,0:T(8,128)S(1)} %get-tuple-element.92.stat, ...), custom_call_target="tpu_custom_call" | custom-call | flops 1024 | bytes 1024 | tf_op jit(solution)/shard_map/pallas_call | solution.py:38
  32.1 1.5 %collective-permute-start.12 = (bf16[1024,128]{1,0:T(8,128)(2,1)S(1)}, bf16[1024,128]{1,0:T(8,128)(2,1)S(1)}, u32[]{:S(2)}, u32[]{:S(2)}) collective-permute-start(bf16[1024,128]{1,0:T(8,128)(2,1)S(1)} %get-tuple-element.106), channel_id=1, source_target_pairs={{0,2},{1,3},{2,0},{3,1},{4,6},{5,7},{6,4},{7,5},{8,10},{9,11},{10,... | collective-permute-start | bytes 786440 | tf_op jit(solution)/shard_map/ppermute | solution.py:531
  33.7 2.5 %shard_map.94 = (bf16[128,1024]{1,0:T(8,128)(2,1)S(1)}, f32[8,1024]{1,0:T(8,128)S(1)}, bf16[1024,128]{1,0:T(8,128)(2,1)S(1)}, f32[128,1024]{1,0:T(8,128)S(1)}, bf16[512,256]{1,0:T(8,128)(2,1)S(1)}) custom-call(s32[8,16]{1,0:T(8,128)S(1)} %get-tuple-element.74.lists.lists_any.refs_0_, bf16[1024,256]{1,0:T(8,128)(2,1)S(1)} %get-tuple-element.73.qg.refs_1_, ...), custom_call_target="tpu_custom_call" | custom-call | flops 1024 | bytes 1024 | tf_op jit(solution)/shard_map/pallas_call | solution.py:38
  36.1 0.6 collective-permute-start.13
  36.8 2.2 %shard_map.95 = (bf16[1024,256]{1,0:T(8,128)(2,1)S(1)}, f32[128,1024]{1,0:T(8,128)S(1)}) custom-call(s32[8,16]{1,0:T(8,128)S(1)} %get-tuple-element.74.lists.lists_any.refs_0_, bf16[1024,256]{1,0:T(8,128)(2,1)S(1)} %get-tuple-element.73.qg.refs_1_, f32[8,1024]{1,0:T(8,128)S(1)} %get-tuple-element.98.refs_3_.lse_ref, ...), custom_call_target="tpu_custom_call" | custom-call | flops 1024 | bytes 1024 | tf_op jit(solution)/shard_map/pallas_call | solution.py:38
  39.0 1.5 %collective-permute-done.12.came = bf16[1024,128]{1,0:T(8,128)(2,1)S(1)} collective-permute-done((bf16[1024,128]{1,0:T(8,128)(2,1)S(1)}, bf16[1024,128]{1,0:T(8,128)(2,1)S(1)}, u32[]{:S(2)}, u32[]{:S(2)}) %collective-permute-start.12) | collective-permute-done | bytes 262176 | tf_op jit(solution)/shard_map/ppermute | solution.py:531
  40.6 2.2 %shard_map.96 = (f32[1024,256]{1,0:T(8,128)S(1)}, f32[1024,256]{1,0:T(8,128)S(1)}, f32[128,1024]{1,0:T(8,128)S(1)}) custom-call(s32[8,16]{1,0:T(8,128)S(1)} %get-tuple-element.74.lists.lists_any.refs_0_, bf16[1024,256]{1,0:T(8,128)(2,1)S(1)} %get-tuple-element.73.qg.refs_1_, f32[8,1024]{1,0:T(8,128)S(1)} %get-tuple-element.98.refs_3_.lse_ref, ...), custom_call_target="tpu_custom_call" | custom-call | flops 2684354560 | bytes 1024 | tf_op jit(solution)/shard_map/pallas_call | solution.py:38
  42.8 1.8 %collective-permute-done.13.came = bf16[1024,128]{1,0:T(8,128)(2,1)S(1)} collective-permute-done((bf16[1024,128]{1,0:T(8,128)(2,1)S(1)}, bf16[1024,128]{1,0:T(8,128)(2,1)S(1)}, u32[]{:S(2)}, u32[]{:S(2)}) %collective-permute-start.13) | collective-permute-done | bytes 262176 | tf_op jit(solution)/shard_map/ppermute | solution.py:531
  44.7 1.7 %collective-permute-start.15 = (bf16[1024,256]{1,0:T(8,128)(2,1)S(1)}, bf16[1024,256]{1,0:T(8,128)(2,1)S(1)}, u32[]{:S(2)}, u32[]{:S(2)}) collective-permute-start(bf16[1024,256]{1,0:T(8,128)(2,1)S(1)} %get-tuple-element.127), channel_id=1, source_target_pairs={{0,2},{1,3},{2,0},{3,1},{4,6},{5,7},{6,4},{7,5},{8,10},{9,11},{10,... | collective-permute-start | bytes 1572872 | tf_op jit(solution)/shard_map/ppermute | solution.py:531
  46.8 2.6 %collective-permute-done.11.refs_1_ = bf16[512,256]{1,0:T(8,128)(2,1)S(1)} collective-permute-done((bf16[512,256]{1,0:T(8,128)(2,1)S(1)}, bf16[512,256]{1,0:T(8,128)(2,1)S(1)}, u32[]{:S(2)}, u32[]{:S(2)}) %collective-permute-start.11) | collective-permute-done | bytes 262176 | tf_op jit(solution)/shard_map/ppermute | solution.py:531
  49.3 0.7 %shard_map.98.placed = f32[1024,256]{1,0:T(8,128)S(1)} custom-call(s32[8,16]{1,0:T(8,128)S(1)} %get-tuple-element.74.lists.lists_any.refs_0_, bf16[512,256]{1,0:T(8,128)(2,1)S(1)} %collective-permute-done.11.refs_1_), custom_call_target="tpu_custom_call" | custom-call | flops 1024 | bytes 1024 | tf_op jit(solution)/shard_map/pallas_call | solution.py:38
  50.1 3.2 %shard_map.99 = (f32[1024,256]{1,0:T(8,128)S(1)}, bf16[512,256]{1,0:T(8,128)(2,1)S(1)}, bf16[512,256]{1,0:T(8,128)(2,1)S(1)}) custom-call(bf16[1024,256]{1,0:T(8,128)(2,1)S(1)} %get-tuple-element.73.qg.refs_1_, f32[8,1024]{1,0:T(8,128)S(1)} %get-tuple-element.98.refs_3_.lse_ref, f32[8,1024]{1,0:T(8,128)S(1)} %get-tuple-element.102.dot_ref, ...), custom_call_target="tpu_custom_call" | custom-call | flops 2684354560 | bytes 1024 | tf_op jit(solution)/shard_map/pallas_call | solution.py:38
  53.3 1.5 %collective-permute-done.14.came = bf16[512,256]{1,0:T(8,128)(2,1)S(1)} collective-permute-done((bf16[512,256]{1,0:T(8,128)(2,1)S(1)}, bf16[512,256]{1,0:T(8,128)(2,1)S(1)}, u32[]{:S(2)}, u32[]{:S(2)}) %collective-permute-start.14) | collective-permute-done | bytes 262176 | tf_op jit(solution)/shard_map/ppermute | solution.py:528
  54.9 0.9 %shard_map.100 = (bf16[512,256]{1,0:T(8,128)(2,1)}, bf16[512,256]{1,0:T(8,128)(2,1)}) custom-call(bf16[512,256]{1,0:T(8,128)(2,1)S(1)} %get-tuple-element.120.keep, bf16[512,256]{1,0:T(8,128)(2,1)S(1)} %collective-permute-done.14.came), custom_call_target="tpu_custom_call" | custom-call | flops 1024 | bytes 1024 | tf_op jit(solution)/shard_map/pallas_call | solution.py:38
  55.7 1.3 %collective-permute-done.15.refs_0_ = bf16[1024,256]{1,0:T(8,128)(2,1)S(1)} collective-permute-done((bf16[1024,256]{1,0:T(8,128)(2,1)S(1)}, bf16[1024,256]{1,0:T(8,128)(2,1)S(1)}, u32[]{:S(2)}, u32[]{:S(2)}) %collective-permute-start.15) | collective-permute-done | bytes 524320 | tf_op jit(solution)/shard_map/ppermute | solution.py:531
  57.3 3.7 %collective-permute-done.17.came = bf16[1024,256]{1,0:T(8,128)(2,1)S(1)} collective-permute-done((bf16[1024,256]{1,0:T(8,128)(2,1)S(1)}, bf16[1024,256]{1,0:T(8,128)(2,1)S(1)}, u32[]{:S(2)}, u32[]{:S(2)}) %collective-permute-start.17) | collective-permute-done | bytes 524320 | tf_op jit(solution)/shard_map/ppermute | solution.py:531
  61.2 1.5 %collective-permute-done.18.came = bf16[512,256]{1,0:T(8,128)(2,1)S(1)} collective-permute-done((bf16[512,256]{1,0:T(8,128)(2,1)S(1)}, bf16[512,256]{1,0:T(8,128)(2,1)S(1)}, u32[]{:S(2)}, u32[]{:S(2)}) %collective-permute-start.18) | collective-permute-done | bytes 262176 | tf_op jit(solution)/shard_map/ppermute | solution.py:528
  62.8 0.9 %shard_map.103 = (bf16[512,256]{1,0:T(8,128)(2,1)}, bf16[512,256]{1,0:T(8,128)(2,1)}) custom-call(bf16[512,256]{1,0:T(8,128)(2,1)S(1)} %get-tuple-element.128.keep, bf16[512,256]{1,0:T(8,128)(2,1)S(1)} %collective-permute-done.18.came), custom_call_target="tpu_custom_call" | custom-call | flops 1024 | bytes 1024 | tf_op jit(solution)/shard_map/pallas_call | solution.py:38
  (26 shorter events, 2.0 us)
Async XLA Ops:
  0.6 1.9 %collective-permute-start = (bf16[512,256]{1,0:T(8,128)(2,1)}, bf16[512,256]{1,0:T(8,128)(2,1)S(1)}, u32[]{:S(2)}, u32[]{:S(2)}) collective-permute-start(bf16[512,256]{1,0:T(8,128)(2,1)} %k.1), channel_id=1, source_target_pairs={{0,1},{1,0},{2,3},{3,2},{4,5},{5,4},{6,7},{7,6},{8,9},{9,8},{10,11... | collective-permute-start | bytes 786440 | tf_op jit(solution)/shard_map/ppermute | solution.py:528
  1.2 2.0 %collective-permute-start.3 = (bf16[512,256]{1,0:T(8,128)(2,1)}, bf16[512,256]{1,0:T(8,128)(2,1)S(1)}, u32[]{:S(2)}, u32[]{:S(2)}) collective-permute-start(bf16[512,256]{1,0:T(8,128)(2,1)} %v.1), channel_id=1, source_target_pairs={{0,1},{1,0},{2,3},{3,2},{4,5},{5,4},{6,7},{7,6},{8,9},{9,8},{10,11... | collective-permute-start | bytes 786440 | tf_op jit(solution)/shard_map/ppermute | solution.py:528
  2.6 6.5 %collective-permute-start.2 = (bf16[512,256]{1,0:T(8,128)(2,1)S(1)}, bf16[512,256]{1,0:T(8,128)(2,1)S(1)}, u32[]{:S(2)}, u32[]{:S(2)}) collective-permute-start(bf16[512,256]{1,0:T(8,128)(2,1)S(1)} %get-tuple-element.71), channel_id=1, source_target_pairs={{0,1},{1,0},{2,3},{3,2},{4,5},{5,4},{6,7},{7,6},{8,9},{9,8},{10,11... | collective-permute-start | bytes 786440 | tf_op jit(solution)/shard_map/ppermute | solution.py:528
  3.1 6.0 %collective-permute-start.1 = (bf16[1024,128]{1,0:T(8,128)(2,1)S(1)}, bf16[1024,128]{1,0:T(8,128)(2,1)S(1)}, u32[]{:S(2)}, u32[]{:S(2)}) collective-permute-start(bf16[1024,128]{1,0:T(8,128)(2,1)S(1)} %shard_map.85.keys), channel_id=1, source_target_pairs={{0,1},{1,0},{2,3},{3,2},{4,8},{5,9},{6,10},{7,11},{8,4},{9,5},{10,... | collective-permute-start | bytes 786440 | tf_op jit(solution)/shard_map/ppermute | solution.py:531
  3.3 15.7 %collective-permute-start.6 = (bf16[1024,256]{1,0:T(8,128)(2,1)S(1)}, bf16[1024,256]{1,0:T(8,128)(2,1)S(1)}, u32[]{:S(2)}, u32[]{:S(2)}) collective-permute-start(bf16[1024,256]{1,0:T(8,128)(2,1)S(1)} %get-tuple-element.79.kv), channel_id=1, source_target_pairs={{0,2},{1,3},{2,0},{3,1},{4,6},{5,7},{6,4},{7,5},{8,10},{9,11},{10,... | collective-permute-start | bytes 1572872 | tf_op jit(solution)/shard_map/ppermute | solution.py:531
  6.3 9.8 %collective-permute-start.7 = (bf16[1024,128]{1,0:T(8,128)(2,1)S(1)}, bf16[1024,128]{1,0:T(8,128)(2,1)S(1)}, u32[]{:S(2)}, u32[]{:S(2)}) collective-permute-start(bf16[1024,128]{1,0:T(8,128)(2,1)S(1)} %shard_map.85.keys), channel_id=1, source_target_pairs={{0,4},{1,5},{2,6},{3,7},{4,0},{5,1},{6,2},{7,3},{8,12},{9,13},{10,... | collective-permute-start | bytes 786440 | tf_op jit(solution)/shard_map/ppermute | solution.py:531
  9.0 14.6 %collective-permute-start.5 = (bf16[1024,128]{1,0:T(8,128)(2,1)S(1)}, bf16[1024,128]{1,0:T(8,128)(2,1)S(1)}, u32[]{:S(2)}, u32[]{:S(2)}) collective-permute-start(bf16[1024,128]{1,0:T(8,128)(2,1)S(1)} %get-tuple-element.76), channel_id=1, source_target_pairs={{0,4},{1,5},{2,6},{3,7},{4,0},{5,1},{6,2},{7,3},{8,12},{9,13},{10,... | collective-permute-start | bytes 786440 | tf_op jit(solution)/shard_map/ppermute | solution.py:531
  9.0 14.6 %collective-permute-start.4 = (bf16[1024,128]{1,0:T(8,128)(2,1)S(1)}, bf16[1024,128]{1,0:T(8,128)(2,1)S(1)}, u32[]{:S(2)}, u32[]{:S(2)}) collective-permute-start(bf16[1024,128]{1,0:T(8,128)(2,1)S(1)} %get-tuple-element.76), channel_id=1, source_target_pairs={{0,1},{1,0},{2,3},{3,2},{4,8},{5,9},{6,10},{7,11},{8,4},{9,5},{10,... | collective-permute-start | bytes 786440 | tf_op jit(solution)/shard_map/ppermute | solution.py:531
  16.2 8.7 %collective-permute-start.8 = (bf16[1024,128]{1,0:T(8,128)(2,1)S(1)}, bf16[1024,128]{1,0:T(8,128)(2,1)S(1)}, u32[]{:S(2)}, u32[]{:S(2)}) collective-permute-start(bf16[1024,128]{1,0:T(8,128)(2,1)S(1)} %shard_map.89), channel_id=1, source_target_pairs={{0,2},{1,3},{2,0},{3,1},{4,6},{5,7},{6,4},{7,5},{8,10},{9,11},{10,... | collective-permute-start | bytes 786440 | tf_op jit(solution)/shard_map/ppermute | solution.py:531
  16.7 14.0 %collective-permute-start.9 = (bf16[512,256]{1,0:T(8,128)(2,1)S(1)}, bf16[512,256]{1,0:T(8,128)(2,1)S(1)}, u32[]{:S(2)}, u32[]{:S(2)}) collective-permute-start(bf16[512,256]{1,0:T(8,128)(2,1)S(1)} %shard_map.88), channel_id=1, source_target_pairs={{0,8},{1,9},{2,10},{3,11},{4,12},{5,13},{6,14},{7,15},{8,0},{9,1},... | collective-permute-start | bytes 786440 | tf_op jit(solution)/shard_map/ppermute | solution.py:531
  23.9 9.8 %collective-permute-start.10 = (bf16[1024,128]{1,0:T(8,128)(2,1)S(1)}, bf16[1024,128]{1,0:T(8,128)(2,1)S(1)}, u32[]{:S(2)}, u32[]{:S(2)}) collective-permute-start(bf16[1024,128]{1,0:T(8,128)(2,1)S(1)} %shard_map.91), channel_id=1, source_target_pairs={{0,2},{1,3},{2,0},{3,1},{4,6},{5,7},{6,4},{7,5},{8,10},{9,11},{10,... | collective-permute-start | bytes 786440 | tf_op jit(solution)/shard_map/ppermute | solution.py:531
  32.1 8.5 %collective-permute-start.12 = (bf16[1024,128]{1,0:T(8,128)(2,1)S(1)}, bf16[1024,128]{1,0:T(8,128)(2,1)S(1)}, u32[]{:S(2)}, u32[]{:S(2)}) collective-permute-start(bf16[1024,128]{1,0:T(8,128)(2,1)S(1)} %get-tuple-element.106), channel_id=1, source_target_pairs={{0,2},{1,3},{2,0},{3,1},{4,6},{5,7},{6,4},{7,5},{8,10},{9,11},{10,... | collective-permute-start | bytes 786440 | tf_op jit(solution)/shard_map/ppermute | solution.py:531
  36.1 8.5 %collective-permute-start.13 = (bf16[1024,128]{1,0:T(8,128)(2,1)S(1)}, bf16[1024,128]{1,0:T(8,128)(2,1)S(1)}, u32[]{:S(2)}, u32[]{:S(2)}) collective-permute-start(bf16[1024,128]{1,0:T(8,128)(2,1)S(1)} %get-tuple-element.111), channel_id=1, source_target_pairs={{0,2},{1,3},{2,0},{3,1},{4,6},{5,7},{6,4},{7,5},{8,10},{9,11},{10,... | collective-permute-start | bytes 786440 | tf_op jit(solution)/shard_map/ppermute | solution.py:531
  36.7 12.6 %collective-permute-start.11 = (bf16[512,256]{1,0:T(8,128)(2,1)S(1)}, bf16[512,256]{1,0:T(8,128)(2,1)S(1)}, u32[]{:S(2)}, u32[]{:S(2)}) collective-permute-start(bf16[512,256]{1,0:T(8,128)(2,1)S(1)} %get-tuple-element.103), channel_id=1, source_target_pairs={{0,8},{1,9},{2,10},{3,11},{4,12},{5,13},{6,14},{7,15},{8,0},{9,1},... | collective-permute-start | bytes 786440 | tf_op jit(solution)/shard_map/ppermute | solution.py:531
  44.7 12.4 %collective-permute-start.15 = (bf16[1024,256]{1,0:T(8,128)(2,1)S(1)}, bf16[1024,256]{1,0:T(8,128)(2,1)S(1)}, u32[]{:S(2)}, u32[]{:S(2)}) collective-permute-start(bf16[1024,256]{1,0:T(8,128)(2,1)S(1)} %get-tuple-element.127), channel_id=1, source_target_pairs={{0,2},{1,3},{2,0},{3,1},{4,6},{5,7},{6,4},{7,5},{8,10},{9,11},{10,... | collective-permute-start | bytes 1572872 | tf_op jit(solution)/shard_map/ppermute | solution.py:531
  46.6 10.5 %collective-permute-start.16 = (bf16[1024,256]{1,0:T(8,128)(2,1)S(1)}, bf16[1024,256]{1,0:T(8,128)(2,1)S(1)}, u32[]{:S(2)}, u32[]{:S(2)}) collective-permute-start(bf16[1024,256]{1,0:T(8,128)(2,1)S(1)} %get-tuple-element.114), channel_id=1, source_target_pairs={{0,1},{1,0},{2,3},{3,2},{4,8},{5,9},{6,10},{7,11},{8,4},{9,5},{10,... | collective-permute-start | bytes 1572872 | tf_op jit(solution)/shard_map/ppermute | solution.py:531
  46.7 14.3 %collective-permute-start.17 = (bf16[1024,256]{1,0:T(8,128)(2,1)S(1)}, bf16[1024,256]{1,0:T(8,128)(2,1)S(1)}, u32[]{:S(2)}, u32[]{:S(2)}) collective-permute-start(bf16[1024,256]{1,0:T(8,128)(2,1)S(1)} %get-tuple-element.113), channel_id=1, source_target_pairs={{0,4},{1,5},{2,6},{3,7},{4,0},{5,1},{6,2},{7,3},{8,12},{9,13},{10,... | collective-permute-start | bytes 1572872 | tf_op jit(solution)/shard_map/ppermute | solution.py:531
  53.3 1.6 %collective-permute-start.14 = (bf16[512,256]{1,0:T(8,128)(2,1)S(1)}, bf16[512,256]{1,0:T(8,128)(2,1)S(1)}, u32[]{:S(2)}, u32[]{:S(2)}) collective-permute-start(bf16[512,256]{1,0:T(8,128)(2,1)S(1)} %get-tuple-element.121), channel_id=1, source_target_pairs={{0,1},{1,0},{2,3},{3,2},{4,5},{5,4},{6,7},{7,6},{8,9},{9,8},{10,11... | collective-permute-start | bytes 786440 | tf_op jit(solution)/shard_map/ppermute | solution.py:528
  61.2 1.6 %collective-permute-start.18 = (bf16[512,256]{1,0:T(8,128)(2,1)S(1)}, bf16[512,256]{1,0:T(8,128)(2,1)S(1)}, u32[]{:S(2)}, u32[]{:S(2)}) collective-permute-start(bf16[512,256]{1,0:T(8,128)(2,1)S(1)} %get-tuple-element.129), channel_id=1, source_target_pairs={{0,1},{1,0},{2,3},{3,2},{4,5},{5,4},{6,7},{7,6},{8,9},{9,8},{10,11... | collective-permute-start | bytes 786440 | tf_op jit(solution)/shard_map/ppermute | solution.py:528

commit v13 on v12

--- a/solution.py
+++ b/solution.py
@@ -608,7 +608,6 @@
         [frame_two, turned_sum],
         scratch=[pltpu.VMEM((2 * s_dev, 2 * DH), F32)],
     )
-    da, dc_k_came = lax.optimization_barrier((da, dc_k_came))
     da_came = swapped(da, near_swap)
     dz, dy, dq = call(
         functools.partial(second_kernel, block, (z_swap, y_swap)),

time: 63.8 us -> 63.6 us (level)
  transfers between devices with their start and end apart: 19 -> 19, of which waited for: 11 -> 10; matrix products, arithmetic and copies ran while one was open for 0% -> 0% of each run, Pallas kernels for 35% -> 35%
where the time goes in v13:
time: 63.6 us; the launch traced here: 63.4 us
  waiting for transfers between devices  24.9 us (39%)
  Pallas kernels  23.1 us (36%)
  starting transfers between devices  14.6 us (23%)
  between operations  0.81 us (1%)
    pallas_call x20, Pallas kernels, call(): pl.pallas_call(kernel, out_shape=out_shape, in_specs=[scalars if a.dtype...  23.1 us
    ppermute x14, waiting for transfers between devices, swapped(): return lax.ppermute(value, ('tm', 'space'), swap.pairs)  21.9 us
    ppermute x14, starting transfers between devices, swapped(): return lax.ppermute(value, ('tm', 'space'), swap.pairs)  13.4 us
    ppermute x5, waiting for transfers between devices, across(): return lax.ppermute(value, 'space', [(0, 1), (1, 0)])  3.06 us
  transfers between devices with their start and end apart: 19, of which 10 were waited for; matrix products, arithmetic and copies ran while one was open for 0% of the time, Pallas kernels for 35%

profile of v13, /device:TPU:0, one launch (start us, length us, event | category | flops | bytes accessed | tf_op | source)
XLA Modules:
  0.0 63.4 jit_solution(15528082350352771594)
XLA Ops:
  0.6 0.5 collective-permute-start
  1.2 1.3 %shard_map.84 = (bf16[512,128]{1,0:T(8,128)(2,1)S(1)}, bf16[512,128]{1,0:T(8,128)(2,1)S(1)}, bf16[512,256]{1,0:T(8,128)(2,1)S(1)}, bf16[512,256]{1,0:T(8,128)(2,1)S(1)}, s32[8,16]{1,0:T(8,128)S(1)}) custom-call(bf16[512,256]{1,0:T(8,128)(2,1)} %k.1, bf16[512,256]{1,0:T(8,128)(2,1)} %v.1, bf16[512,256]{1,0:T(8,128)(2,1)} %q.1, bf16[512,256]{1,0:T(8,128)(2,1)} %g.1, ...), custom_call_target="tpu_custom_call" | custom-call | flops 1024 | bytes 1024 | tf_op jit(solution)/shard_map/pallas_call | solution.py:38
  2.6 0.5 collective-permute-start.2
  3.3 3.0 %collective-permute-start.6 = (bf16[1024,256]{1,0:T(8,128)(2,1)S(1)}, bf16[1024,256]{1,0:T(8,128)(2,1)S(1)}, u32[]{:S(2)}, u32[]{:S(2)}) collective-permute-start(bf16[1024,256]{1,0:T(8,128)(2,1)S(1)} %get-tuple-element.77.kv), channel_id=1, source_target_pairs={{0,2},{1,3},{2,0},{3,1},{4,6},{5,7},{6,4},{7,5},{8,10},{9,11},{10,... | collective-permute-start | bytes 1572872 | tf_op jit(solution)/shard_map/ppermute | solution.py:531
  6.3 2.7 %collective-permute-start.7 = (bf16[1024,128]{1,0:T(8,128)(2,1)S(1)}, bf16[1024,128]{1,0:T(8,128)(2,1)S(1)}, u32[]{:S(2)}, u32[]{:S(2)}) collective-permute-start(bf16[1024,128]{1,0:T(8,128)(2,1)S(1)} %shard_map.85.keys), channel_id=1, source_target_pairs={{0,4},{1,5},{2,6},{3,7},{4,0},{5,1},{6,2},{7,3},{8,12},{9,13},{10,... | collective-permute-start | bytes 786440 | tf_op jit(solution)/shard_map/ppermute | solution.py:531
  9.2 0.6 %shard_map.88 = bf16[512,256]{1,0:T(8,128)(2,1)S(1)} custom-call(s32[8,16]{1,0:T(8,128)S(1)} %get-tuple-element.72.lists.lists_any.refs_0_, bf16[1024,256]{1,0:T(8,128)(2,1)S(1)} %get-tuple-element.77.kv), custom_call_target="tpu_custom_call" | custom-call | flops 1024 | bytes 1024 | tf_op jit(solution)/shard_map/pallas_call | solution.py:38
  9.8 6.3 %collective-permute-done.7.z.z_k = bf16[1024,128]{1,0:T(8,128)(2,1)S(1)} collective-permute-done((bf16[1024,128]{1,0:T(8,128)(2,1)S(1)}, bf16[1024,128]{1,0:T(8,128)(2,1)S(1)}, u32[]{:S(2)}, u32[]{:S(2)}) %collective-permute-start.7) | collective-permute-done | bytes 262176 | tf_op jit(solution)/shard_map/ppermute | solution.py:531
  16.2 0.6 collective-permute-start.8
  16.7 1.9 %collective-permute-start.9 = (bf16[512,256]{1,0:T(8,128)(2,1)S(1)}, bf16[512,256]{1,0:T(8,128)(2,1)S(1)}, u32[]{:S(2)}, u32[]{:S(2)}) collective-permute-start(bf16[512,256]{1,0:T(8,128)(2,1)S(1)} %shard_map.88), channel_id=1, source_target_pairs={{0,8},{1,9},{2,10},{3,11},{4,12},{5,13},{6,14},{7,15},{8,0},{9,1},... | collective-permute-start | bytes 786440 | tf_op jit(solution)/shard_map/ppermute | solution.py:531
  18.7 0.3 collective-permute-done.6.a_kv
  19.0 3.5 %shard_map.90 = (f32[8,1024]{1,0:T(8,128)S(1)}, f32[128,1024]{1,0:T(8,128)S(1)}) custom-call(s32[8,16]{1,0:T(8,128)S(1)} %get-tuple-element.72.lists.lists_any.refs_0_, bf16[1024,256]{1,0:T(8,128)(2,1)S(1)} %get-tuple-element.71.qg.refs_1_, bf16[1024,256]{1,0:T(8,128)(2,1)S(1)} %get-tuple-element.77.kv, bf16[1024,256]{1,0:T(8,128)(2,1)S(1)} %collective-permute-done.6.a_kv), custom_call_target="tpu_custom_call" | custom-call | flops 1024 | bytes 1024 | tf_op jit(solution)/shard_map/pallas_call | solution.py:38
  22.5 1.2 %collective-permute-done.5.z.z_v = bf16[1024,128]{1,0:T(8,128)(2,1)S(1)} collective-permute-done((bf16[1024,128]{1,0:T(8,128)(2,1)S(1)}, bf16[1024,128]{1,0:T(8,128)(2,1)S(1)}, u32[]{:S(2)}, u32[]{:S(2)}) %collective-permute-start.5) | collective-permute-done | bytes 262176 | tf_op jit(solution)/shard_map/ppermute | solution.py:531
  23.9 1.0 %collective-permute-start.10 = (bf16[1024,128]{1,0:T(8,128)(2,1)S(1)}, bf16[1024,128]{1,0:T(8,128)(2,1)S(1)}, u32[]{:S(2)}, u32[]{:S(2)}) collective-permute-start(bf16[1024,128]{1,0:T(8,128)(2,1)S(1)} %shard_map.91), channel_id=1, source_target_pairs={{0,2},{1,3},{2,0},{3,1},{4,6},{5,7},{6,4},{7,5},{8,10},{9,11},{10,... | collective-permute-start | bytes 786440 | tf_op jit(solution)/shard_map/ppermute | solution.py:531
  24.9 2.6 %shard_map.92 = (f32[8,1024]{1,0:T(8,128)S(1)}, f32[128,1024]{1,0:T(8,128)S(1)}, f32[2,512,512]{2,1,0:T(8,128)S(1)}) custom-call(s32[8,16]{1,0:T(8,128)S(1)} %get-tuple-element.72.lists.lists_any.refs_0_, bf16[1024,256]{1,0:T(8,128)(2,1)S(1)} %get-tuple-element.71.qg.refs_1_, f32[8,1024]{1,0:T(8,128)S(1)} %get-tuple-element.88.stat, ...), custom_call_target="tpu_custom_call" | custom-call | flops 1024 | bytes 1024 | tf_op jit(solution)/shard_map/pallas_call | solution.py:38
  27.5 3.2 %collective-permute-done.9.refs_0_.refs_8_ = bf16[512,256]{1,0:T(8,128)(2,1)S(1)} collective-permute-done((bf16[512,256]{1,0:T(8,128)(2,1)S(1)}, bf16[512,256]{1,0:T(8,128)(2,1)S(1)}, u32[]{:S(2)}, u32[]{:S(2)}) %collective-permute-start.9) | collective-permute-done | bytes 262176 | tf_op jit(solution)/shard_map/ppermute | solution.py:531
  30.7 1.4 %shard_map.93 = (f32[8,1024]{1,0:T(8,128)S(1)}, f32[128,1024]{1,0:T(8,128)S(1)}, bf16[1024,128]{1,0:T(8,128)(2,1)S(1)}, f32[2,512,512]{2,1,0:T(8,128)S(1)}) custom-call(s32[8,16]{1,0:T(8,128)S(1)} %get-tuple-element.72.lists.lists_any.refs_0_, bf16[1024,256]{1,0:T(8,128)(2,1)S(1)} %get-tuple-element.71.qg.refs_1_, f32[8,1024]{1,0:T(8,128)S(1)} %get-tuple-element.90.stat, ...), custom_call_target="tpu_custom_call" | custom-call | flops 1024 | bytes 1024 | tf_op jit(solution)/shard_map/pallas_call | solution.py:38
  32.1 1.5 %collective-permute-start.12 = (bf16[1024,128]{1,0:T(8,128)(2,1)S(1)}, bf16[1024,128]{1,0:T(8,128)(2,1)S(1)}, u32[]{:S(2)}, u32[]{:S(2)}) collective-permute-start(bf16[1024,128]{1,0:T(8,128)(2,1)S(1)} %get-tuple-element.104), channel_id=1, source_target_pairs={{0,2},{1,3},{2,0},{3,1},{4,6},{5,7},{6,4},{7,5},{8,10},{9,11},{10,... | collective-permute-start | bytes 786440 | tf_op jit(solution)/shard_map/ppermute | solution.py:531
  33.7 2.5 %shard_map.94 = (bf16[128,1024]{1,0:T(8,128)(2,1)S(1)}, f32[8,1024]{1,0:T(8,128)S(1)}, bf16[1024,128]{1,0:T(8,128)(2,1)S(1)}, f32[128,1024]{1,0:T(8,128)S(1)}, bf16[512,256]{1,0:T(8,128)(2,1)S(1)}) custom-call(s32[8,16]{1,0:T(8,128)S(1)} %get-tuple-element.72.lists.lists_any.refs_0_, bf16[1024,256]{1,0:T(8,128)(2,1)S(1)} %get-tuple-element.71.qg.refs_1_, ...), custom_call_target="tpu_custom_call" | custom-call | flops 1024 | bytes 1024 | tf_op jit(solution)/shard_map/pallas_call | solution.py:38
  36.1 0.6 collective-permute-start.13
  36.8 2.2 %shard_map.95 = (bf16[1024,256]{1,0:T(8,128)(2,1)S(1)}, f32[128,1024]{1,0:T(8,128)S(1)}) custom-call(s32[8,16]{1,0:T(8,128)S(1)} %get-tuple-element.72.lists.lists_any.refs_0_, bf16[1024,256]{1,0:T(8,128)(2,1)S(1)} %get-tuple-element.71.qg.refs_1_, f32[8,1024]{1,0:T(8,128)S(1)} %get-tuple-element.96.refs_3_.lse_ref, ...), custom_call_target="tpu_custom_call" | custom-call | flops 1024 | bytes 1024 | tf_op jit(solution)/shard_map/pallas_call | solution.py:38
  39.0 1.5 %collective-permute-start.15 = (bf16[1024,256]{1,0:T(8,128)(2,1)S(1)}, bf16[1024,256]{1,0:T(8,128)(2,1)S(1)}, u32[]{:S(2)}, u32[]{:S(2)}) collective-permute-start(bf16[1024,256]{1,0:T(8,128)(2,1)S(1)} %get-tuple-element.123), channel_id=1, source_target_pairs={{0,2},{1,3},{2,0},{3,1},{4,6},{5,7},{6,4},{7,5},{8,10},{9,11},{10,... | collective-permute-start | bytes 1572872 | tf_op jit(solution)/shard_map/ppermute | solution.py:531
  40.6 2.2 %shard_map.96 = (f32[1024,256]{1,0:T(8,128)S(1)}, f32[1024,256]{1,0:T(8,128)S(1)}, f32[128,1024]{1,0:T(8,128)S(1)}) custom-call(s32[8,16]{1,0:T(8,128)S(1)} %get-tuple-element.72.lists.lists_any.refs_0_, bf16[1024,256]{1,0:T(8,128)(2,1)S(1)} %get-tuple-element.71.qg.refs_1_, f32[8,1024]{1,0:T(8,128)S(1)} %get-tuple-element.96.refs_3_.lse_ref, ...), custom_call_target="tpu_custom_call" | custom-call | flops 2684354560 | bytes 1024 | tf_op jit(solution)/shard_map/pallas_call | solution.py:38
  42.8 3.4 %collective-permute-done.13.came = bf16[1024,128]{1,0:T(8,128)(2,1)S(1)} collective-permute-done((bf16[1024,128]{1,0:T(8,128)(2,1)S(1)}, bf16[1024,128]{1,0:T(8,128)(2,1)S(1)}, u32[]{:S(2)}, u32[]{:S(2)}) %collective-permute-start.13) | collective-permute-done | bytes 262176 | tf_op jit(solution)/shard_map/ppermute | solution.py:531
  46.7 2.6 %collective-permute-done.11.refs_1_ = bf16[512,256]{1,0:T(8,128)(2,1)S(1)} collective-permute-done((bf16[512,256]{1,0:T(8,128)(2,1)S(1)}, bf16[512,256]{1,0:T(8,128)(2,1)S(1)}, u32[]{:S(2)}, u32[]{:S(2)}) %collective-permute-start.11) | collective-permute-done | bytes 262176 | tf_op jit(solution)/shard_map/ppermute | solution.py:531
  49.3 0.7 %shard_map.98.placed = f32[1024,256]{1,0:T(8,128)S(1)} custom-call(s32[8,16]{1,0:T(8,128)S(1)} %get-tuple-element.72.lists.lists_any.refs_0_, bf16[512,256]{1,0:T(8,128)(2,1)S(1)} %collective-permute-done.11.refs_1_), custom_call_target="tpu_custom_call" | custom-call | flops 1024 | bytes 1024 | tf_op jit(solution)/shard_map/pallas_call | solution.py:38
  50.1 3.2 %shard_map.99 = (f32[1024,256]{1,0:T(8,128)S(1)}, bf16[512,256]{1,0:T(8,128)(2,1)S(1)}, bf16[512,256]{1,0:T(8,128)(2,1)S(1)}) custom-call(bf16[1024,256]{1,0:T(8,128)(2,1)S(1)} %get-tuple-element.71.qg.refs_1_, f32[8,1024]{1,0:T(8,128)S(1)} %get-tuple-element.96.refs_3_.lse_ref, f32[8,1024]{1,0:T(8,128)S(1)} %get-tuple-element.100.dot_ref, ...), custom_call_target="tpu_custom_call" | custom-call | flops 2684354560 | bytes 1024 | tf_op jit(solution)/shard_map/pallas_call | solution.py:38
  53.3 1.5 %collective-permute-done.14.came = bf16[512,256]{1,0:T(8,128)(2,1)S(1)} collective-permute-done((bf16[512,256]{1,0:T(8,128)(2,1)S(1)}, bf16[512,256]{1,0:T(8,128)(2,1)S(1)}, u32[]{:S(2)}, u32[]{:S(2)}) %collective-permute-start.14) | collective-permute-done | bytes 262176 | tf_op jit(solution)/shard_map/ppermute | solution.py:528
  54.9 0.9 %shard_map.100 = (bf16[512,256]{1,0:T(8,128)(2,1)}, bf16[512,256]{1,0:T(8,128)(2,1)}) custom-call(bf16[512,256]{1,0:T(8,128)(2,1)S(1)} %get-tuple-element.116.keep, bf16[512,256]{1,0:T(8,128)(2,1)S(1)} %collective-permute-done.14.came), custom_call_target="tpu_custom_call" | custom-call | flops 1024 | bytes 1024 | tf_op jit(solution)/shard_map/pallas_call | solution.py:38
  55.9 0.2 shard_map.101.near
  56.1 4.7 %collective-permute-done.17.came = bf16[1024,256]{1,0:T(8,128)(2,1)S(1)} collective-permute-done((bf16[1024,256]{1,0:T(8,128)(2,1)S(1)}, bf16[1024,256]{1,0:T(8,128)(2,1)S(1)}, u32[]{:S(2)}, u32[]{:S(2)}) %collective-permute-start.17) | collective-permute-done | bytes 524320 | tf_op jit(solution)/shard_map/ppermute | solution.py:531
  61.0 1.5 %collective-permute-done.18.came = bf16[512,256]{1,0:T(8,128)(2,1)S(1)} collective-permute-done((bf16[512,256]{1,0:T(8,128)(2,1)S(1)}, bf16[512,256]{1,0:T(8,128)(2,1)S(1)}, u32[]{:S(2)}, u32[]{:S(2)}) %collective-permute-start.18) | collective-permute-done | bytes 262176 | tf_op jit(solution)/shard_map/ppermute | solution.py:528
  62.6 0.9 %shard_map.103 = (bf16[512,256]{1,0:T(8,128)(2,1)}, bf16[512,256]{1,0:T(8,128)(2,1)}) custom-call(bf16[512,256]{1,0:T(8,128)(2,1)S(1)} %get-tuple-element.124.keep, bf16[512,256]{1,0:T(8,128)(2,1)S(1)} %collective-permute-done.18.came), custom_call_target="tpu_custom_call" | custom-call | flops 1024 | bytes 1024 | tf_op jit(solution)/shard_map/pallas_call | solution.py:38
  (26 shorter events, 1.7 us)
Async XLA Ops:
  0.6 1.9 %collective-permute-start = (bf16[512,256]{1,0:T(8,128)(2,1)}, bf16[512,256]{1,0:T(8,128)(2,1)S(1)}, u32[]{:S(2)}, u32[]{:S(2)}) collective-permute-start(bf16[512,256]{1,0:T(8,128)(2,1)} %k.1), channel_id=1, source_target_pairs={{0,1},{1,0},{2,3},{3,2},{4,5},{5,4},{6,7},{7,6},{8,9},{9,8},{10,11... | collective-permute-start | bytes 786440 | tf_op jit(solution)/shard_map/ppermute | solution.py:528
  1.2 2.0 %collective-permute-start.3 = (bf16[512,256]{1,0:T(8,128)(2,1)}, bf16[512,256]{1,0:T(8,128)(2,1)S(1)}, u32[]{:S(2)}, u32[]{:S(2)}) collective-permute-start(bf16[512,256]{1,0:T(8,128)(2,1)} %v.1), channel_id=1, source_target_pairs={{0,1},{1,0},{2,3},{3,2},{4,5},{5,4},{6,7},{7,6},{8,9},{9,8},{10,11... | collective-permute-start | bytes 786440 | tf_op jit(solution)/shard_map/ppermute | solution.py:528
  2.6 6.5 %collective-permute-start.2 = (bf16[512,256]{1,0:T(8,128)(2,1)S(1)}, bf16[512,256]{1,0:T(8,128)(2,1)S(1)}, u32[]{:S(2)}, u32[]{:S(2)}) collective-permute-start(bf16[512,256]{1,0:T(8,128)(2,1)S(1)} %get-tuple-element.69), channel_id=1, source_target_pairs={{0,1},{1,0},{2,3},{3,2},{4,5},{5,4},{6,7},{7,6},{8,9},{9,8},{10,11... | collective-permute-start | bytes 786440 | tf_op jit(solution)/shard_map/ppermute | solution.py:528
  3.1 6.0 %collective-permute-start.1 = (bf16[1024,128]{1,0:T(8,128)(2,1)S(1)}, bf16[1024,128]{1,0:T(8,128)(2,1)S(1)}, u32[]{:S(2)}, u32[]{:S(2)}) collective-permute-start(bf16[1024,128]{1,0:T(8,128)(2,1)S(1)} %shard_map.85.keys), channel_id=1, source_target_pairs={{0,1},{1,0},{2,3},{3,2},{4,8},{5,9},{6,10},{7,11},{8,4},{9,5},{10,... | collective-permute-start | bytes 786440 | tf_op jit(solution)/shard_map/ppermute | solution.py:531
  3.3 15.7 %collective-permute-start.6 = (bf16[1024,256]{1,0:T(8,128)(2,1)S(1)}, bf16[1024,256]{1,0:T(8,128)(2,1)S(1)}, u32[]{:S(2)}, u32[]{:S(2)}) collective-permute-start(bf16[1024,256]{1,0:T(8,128)(2,1)S(1)} %get-tuple-element.77.kv), channel_id=1, source_target_pairs={{0,2},{1,3},{2,0},{3,1},{4,6},{5,7},{6,4},{7,5},{8,10},{9,11},{10,... | collective-permute-start | bytes 1572872 | tf_op jit(solution)/shard_map/ppermute | solution.py:531
  6.3 9.8 %collective-permute-start.7 = (bf16[1024,128]{1,0:T(8,128)(2,1)S(1)}, bf16[1024,128]{1,0:T(8,128)(2,1)S(1)}, u32[]{:S(2)}, u32[]{:S(2)}) collective-permute-start(bf16[1024,128]{1,0:T(8,128)(2,1)S(1)} %shard_map.85.keys), channel_id=1, source_target_pairs={{0,4},{1,5},{2,6},{3,7},{4,0},{5,1},{6,2},{7,3},{8,12},{9,13},{10,... | collective-permute-start | bytes 786440 | tf_op jit(solution)/shard_map/ppermute | solution.py:531
  9.0 14.6 %collective-permute-start.5 = (bf16[1024,128]{1,0:T(8,128)(2,1)S(1)}, bf16[1024,128]{1,0:T(8,128)(2,1)S(1)}, u32[]{:S(2)}, u32[]{:S(2)}) collective-permute-start(bf16[1024,128]{1,0:T(8,128)(2,1)S(1)} %get-tuple-element.74), channel_id=1, source_target_pairs={{0,4},{1,5},{2,6},{3,7},{4,0},{5,1},{6,2},{7,3},{8,12},{9,13},{10,... | collective-permute-start | bytes 786440 | tf_op jit(solution)/shard_map/ppermute | solution.py:531
  9.0 14.6 %collective-permute-start.4 = (bf16[1024,128]{1,0:T(8,128)(2,1)S(1)}, bf16[1024,128]{1,0:T(8,128)(2,1)S(1)}, u32[]{:S(2)}, u32[]{:S(2)}) collective-permute-start(bf16[1024,128]{1,0:T(8,128)(2,1)S(1)} %get-tuple-element.74), channel_id=1, source_target_pairs={{0,1},{1,0},{2,3},{3,2},{4,8},{5,9},{6,10},{7,11},{8,4},{9,5},{10,... | collective-permute-start | bytes 786440 | tf_op jit(solution)/shard_map/ppermute | solution.py:531
  16.2 8.7 %collective-permute-start.8 = (bf16[1024,128]{1,0:T(8,128)(2,1)S(1)}, bf16[1024,128]{1,0:T(8,128)(2,1)S(1)}, u32[]{:S(2)}, u32[]{:S(2)}) collective-permute-start(bf16[1024,128]{1,0:T(8,128)(2,1)S(1)} %shard_map.89), channel_id=1, source_target_pairs={{0,2},{1,3},{2,0},{3,1},{4,6},{5,7},{6,4},{7,5},{8,10},{9,11},{10,... | collective-permute-start | bytes 786440 | tf_op jit(solution)/shard_map/ppermute | solution.py:531
  16.7 14.0 %collective-permute-start.9 = (bf16[512,256]{1,0:T(8,128)(2,1)S(1)}, bf16[512,256]{1,0:T(8,128)(2,1)S(1)}, u32[]{:S(2)}, u32[]{:S(2)}) collective-permute-start(bf16[512,256]{1,0:T(8,128)(2,1)S(1)} %shard_map.88), channel_id=1, source_target_pairs={{0,8},{1,9},{2,10},{3,11},{4,12},{5,13},{6,14},{7,15},{8,0},{9,1},... | collective-permute-start | bytes 786440 | tf_op jit(solution)/shard_map/ppermute | solution.py:531
  23.9 9.8 %collective-permute-start.10 = (bf16[1024,128]{1,0:T(8,128)(2,1)S(1)}, bf16[1024,128]{1,0:T(8,128)(2,1)S(1)}, u32[]{:S(2)}, u32[]{:S(2)}) collective-permute-start(bf16[1024,128]{1,0:T(8,128)(2,1)S(1)} %shard_map.91), channel_id=1, source_target_pairs={{0,2},{1,3},{2,0},{3,1},{4,6},{5,7},{6,4},{7,5},{8,10},{9,11},{10,... | collective-permute-start | bytes 786440 | tf_op jit(solution)/shard_map/ppermute | solution.py:531
  32.1 8.5 %collective-permute-start.12 = (bf16[1024,128]{1,0:T(8,128)(2,1)S(1)}, bf16[1024,128]{1,0:T(8,128)(2,1)S(1)}, u32[]{:S(2)}, u32[]{:S(2)}) collective-permute-start(bf16[1024,128]{1,0:T(8,128)(2,1)S(1)} %get-tuple-element.104), channel_id=1, source_target_pairs={{0,2},{1,3},{2,0},{3,1},{4,6},{5,7},{6,4},{7,5},{8,10},{9,11},{10,... | collective-permute-start | bytes 786440 | tf_op jit(solution)/shard_map/ppermute | solution.py:531
  36.1 10.0 %collective-permute-start.13 = (bf16[1024,128]{1,0:T(8,128)(2,1)S(1)}, bf16[1024,128]{1,0:T(8,128)(2,1)S(1)}, u32[]{:S(2)}, u32[]{:S(2)}) collective-permute-start(bf16[1024,128]{1,0:T(8,128)(2,1)S(1)} %get-tuple-element.108), channel_id=1, source_target_pairs={{0,2},{1,3},{2,0},{3,1},{4,6},{5,7},{6,4},{7,5},{8,10},{9,11},{10,... | collective-permute-start | bytes 786440 | tf_op jit(solution)/shard_map/ppermute | solution.py:531
  36.7 12.6 %collective-permute-start.11 = (bf16[512,256]{1,0:T(8,128)(2,1)S(1)}, bf16[512,256]{1,0:T(8,128)(2,1)S(1)}, u32[]{:S(2)}, u32[]{:S(2)}) collective-permute-start(bf16[512,256]{1,0:T(8,128)(2,1)S(1)} %get-tuple-element.101), channel_id=1, source_target_pairs={{0,8},{1,9},{2,10},{3,11},{4,12},{5,13},{6,14},{7,15},{8,0},{9,1},... | collective-permute-start | bytes 786440 | tf_op jit(solution)/shard_map/ppermute | solution.py:531
  39.0 16.9 %collective-permute-start.15 = (bf16[1024,256]{1,0:T(8,128)(2,1)S(1)}, bf16[1024,256]{1,0:T(8,128)(2,1)S(1)}, u32[]{:S(2)}, u32[]{:S(2)}) collective-permute-start(bf16[1024,256]{1,0:T(8,128)(2,1)S(1)} %get-tuple-element.123), channel_id=1, source_target_pairs={{0,2},{1,3},{2,0},{3,1},{4,6},{5,7},{6,4},{7,5},{8,10},{9,11},{10,... | collective-permute-start | bytes 1572872 | tf_op jit(solution)/shard_map/ppermute | solution.py:531
  46.4 9.5 %collective-permute-start.16 = (bf16[1024,256]{1,0:T(8,128)(2,1)S(1)}, bf16[1024,256]{1,0:T(8,128)(2,1)S(1)}, u32[]{:S(2)}, u32[]{:S(2)}) collective-permute-start(bf16[1024,256]{1,0:T(8,128)(2,1)S(1)} %get-tuple-element.110), channel_id=1, source_target_pairs={{0,1},{1,0},{2,3},{3,2},{4,8},{5,9},{6,10},{7,11},{8,4},{9,5},{10,... | collective-permute-start | bytes 1572872 | tf_op jit(solution)/shard_map/ppermute | solution.py:531
  46.5 14.3 %collective-permute-start.17 = (bf16[1024,256]{1,0:T(8,128)(2,1)S(1)}, bf16[1024,256]{1,0:T(8,128)(2,1)S(1)}, u32[]{:S(2)}, u32[]{:S(2)}) collective-permute-start(bf16[1024,256]{1,0:T(8,128)(2,1)S(1)} %get-tuple-element.109), channel_id=1, source_target_pairs={{0,4},{1,5},{2,6},{3,7},{4,0},{5,1},{6,2},{7,3},{8,12},{9,13},{10,... | collective-permute-start | bytes 1572872 | tf_op jit(solution)/shard_map/ppermute | solution.py:531
  53.3 1.6 %collective-permute-start.14 = (bf16[512,256]{1,0:T(8,128)(2,1)S(1)}, bf16[512,256]{1,0:T(8,128)(2,1)S(1)}, u32[]{:S(2)}, u32[]{:S(2)}) collective-permute-start(bf16[512,256]{1,0:T(8,128)(2,1)S(1)} %get-tuple-element.117), channel_id=1, source_target_pairs={{0,1},{1,0},{2,3},{3,2},{4,5},{5,4},{6,7},{7,6},{8,9},{9,8},{10,11... | collective-permute-start | bytes 786440 | tf_op jit(solution)/shard_map/ppermute | solution.py:528
  61.0 1.6 %collective-permute-start.18 = (bf16[512,256]{1,0:T(8,128)(2,1)S(1)}, bf16[512,256]{1,0:T(8,128)(2,1)S(1)}, u32[]{:S(2)}, u32[]{:S(2)}) collective-permute-start(bf16[512,256]{1,0:T(8,128)(2,1)S(1)} %get-tuple-element.125), channel_id=1, source_target_pairs={{0,1},{1,0},{2,3},{3,2},{4,5},{5,4},{6,7},{7,6},{8,9},{9,8},{10,11... | collective-permute-start | bytes 786440 | tf_op jit(solution)/shard_map/ppermute | solution.py:528

commit v14 on v13

--- a/solution.py
+++ b/solution.py
@@ -412,23 +412,26 @@
 
 
 def second_kernel(
-    block, swaps, lists, qg, lse_ref, dot_ref, dq_old, came, y_k, z_k, y_v, z_v, dz, dy, dq_ref
+    block, swaps, lists, qg, lse_ref, dot_ref, dq_old, came, y_k, z_k, y_v, z_v,
+    dz_k, dy_k, dz_v, dy_v, dq_ref, z_sum, y_sum,
 ):
     half = qg.shape[0] // 2
     frame = lax.axis_index("tm")
     z, y = swaps
     relays = forwards_first(frame)
     more = came[...].astype(F32)
-    for ref, takes in ((dz, relays), (dy, jnp.logical_not(relays))):
-        ref[:, KEY] = jnp.zeros_like(more)
-        ref[:, VALUE] = jnp.where(takes, more, 0.0)
+    for k, v, takes in ((dz_k, z_sum, relays), (dy_k, y_sum, jnp.logical_not(relays))):
+        k[...] = jnp.zeros_like(more)
+        v[...] = jnp.where(takes, more, 0.0)
     for slab in range(2):
         rows = rows_of(slab, half)
         q, g, lse, row_dot = qg[rows, KEY], qg[rows, VALUE], lse_ref[0:1, rows], dot_ref[0:1, rows]
         at = (lists, frame, slab, block)
-        group = listed(z, *at, (z_k, ALL), (z_v, ALL), dk=(dz, KEY), dv=(dz, VALUE))
-        group += listed(y, *at, (y_k, ALL), (y_v, ALL), dk=(dy, KEY), dv=(dy, VALUE))
+        group = listed(z, *at, (z_k, ALL), (z_v, ALL), dk=(dz_k, ALL), dv=(z_sum, ALL))
+        group += listed(y, *at, (y_k, ALL), (y_v, ALL), dk=(dy_k, ALL), dv=(y_sum, ALL))
         dq_ref[:, rows] = dq_old[:, rows] + backward_group(q, g, lse, row_dot, group)
+    dz_v[...] = z_sum[...].astype(BF16)
+    dy_v[...] = y_sum[...].astype(BF16)
 
 
 def own_kernel(qg, lse_ref, dot_ref, dq_old, o, kv, placed, near, keep, send):
@@ -455,17 +458,19 @@
 def merge_kernel(dz, dy, came, z_out, y_out):
     first = forwards_first(lax.axis_index("tm"))
     more = came[...].astype(F32)
-    z_out[:, KEY] = (dz[:, KEY] + jnp.where(first, more, 0.0)).astype(BF16)
-    y_out[:, KEY] = (dy[:, KEY] + jnp.where(first, 0.0, more)).astype(BF16)
-    z_out[:, VALUE] = dz[:, VALUE].astype(BF16)
-    y_out[:, VALUE] = dy[:, VALUE].astype(BF16)
-
-
-def place_kernel(block, far, *refs):
-    lists, total = refs[0], refs[-1]
-    frame = lax.axis_index("tm")
-    total[...] = jnp.zeros_like(total)
-    for swap, came in zip(far, refs[1:-1]):
+    z_out[...] = (dz[...] + jnp.where(first, more, 0.0)).astype(BF16)
+    y_out[...] = (dy[...] + jnp.where(first, 0.0, more)).astype(BF16)
+
+
+def place_kernel(block, swaps, far, *refs):
+    lists, z_came, y_came, total = refs[0], refs[1], refs[2], refs[-1]
+    frame = lax.axis_index("tm")
+    values = 0.0
+    for swap, came in zip(swaps, (z_came, y_came)):
+        values = values + jnp.where(swap.partner(frame)[2], came[...].astype(F32), 0.0)
+    total[:, KEY] = jnp.zeros_like(values)
+    total[:, VALUE] = values
+    for swap, came in zip(far, refs[3:-1]):
         for slab in range(2):
             b, exists = swap.block_of_theirs(lists, frame, slab, 0)
             rows = pl.ds(pl.multiple_of(b * block, block), block)
@@ -473,13 +478,12 @@
             total[rows, :] += jnp.where(exists, part, 0.0)
 
 
-def add_kernel(swaps, near, *refs):
-    frame = lax.axis_index("tm")
-    total = near[...]
-    for swap, came in zip(swaps, refs[:-1]):
-        _, _, exists = swap.partner(frame)
-        total = total + jnp.where(exists, came[...].astype(F32), 0.0)
-    refs[-1][...] = total
+def add_kernel(swaps, near, da, dy, total):
+    frame = lax.axis_index("tm")
+    by_a, by_y = (swap.partner(frame)[2] for swap in swaps)
+    total[:, VALUE] = near[:, VALUE] + jnp.where(by_a, da[:, VALUE].astype(F32), 0.0)
+    keys = near[:, KEY] + jnp.where(by_a, da[:, KEY].astype(F32), 0.0)
+    total[:, KEY] = keys + jnp.where(by_y, dy[...].astype(F32), 0.0)
 
 
 def gather_kernel(swap, near, came, keep, send):
@@ -490,7 +494,8 @@
         for slab, out in ((1 - mine, send), (mine, keep)):
             rows = rows_of(slab, half)
             part = jnp.where(exists, came[rows, :].astype(F32), 0.0)
-            out[...] = (near[rows, :] + part).astype(BF16)
+            out[:, KEY] = (near[rows, KEY] + part).astype(BF16)
+            out[:, VALUE] = near[rows, VALUE].astype(BF16)
 
     each_core(body)
 
@@ -602,6 +607,16 @@
     )
     far_came = [swapped(value, swap) for value, swap in zip(far_grad, far)]
     dc_k_came = swapped(dc_k, near_swap)
+    key_sum = sds((2 * s_dev, DH), F32)
+    dz_k, dy_k, dz_v, dy_v, dq = call(
+        functools.partial(second_kernel, block, (z_swap, y_swap)),
+        (lists, qg, lse, row_dot, dq, dc_v_came, y_k, z_k, y_v, z_v),
+        [key_sum, key_sum, frame_one, frame_one, turned_sum],
+        scratch=[grad_one, grad_one],
+        flops=20 * work,
+    )
+    dy_v_came = swapped(dy_v, y_swap)
+    dz_v_came = swapped(dz_v, z_swap)
     da, dq = call(
         functools.partial(first_kernel, block, near_swap),
         (lists, qg, lse, row_dot, dq, a_kv),
@@ -609,35 +624,32 @@
         scratch=[pltpu.VMEM((2 * s_dev, 2 * DH), F32)],
     )
     da_came = swapped(da, near_swap)
-    dz, dy, dq = call(
-        functools.partial(second_kernel, block, (z_swap, y_swap)),
-        (lists, qg, lse, row_dot, dq, dc_v_came, y_k, z_k, y_v, z_v),
-        [frame_sum, frame_sum, turned_sum],
-        flops=20 * work,
-    )
-    dz, dy = call(merge_kernel, (dz, dy, dc_k_came), [frame_two, frame_two])
-    dy_came = swapped(dy, y_swap)
-    dz_came = swapped(dz, z_swap)
-    dq, dz, dy = lax.optimization_barrier((dq, dz, dy))
+    dz_k, dy_k = call(merge_kernel, (dz_k, dy_k, dc_k_came), [frame_one, frame_one])
+    dy_k_came = swapped(dy_k, y_swap)
+    dz_k_came = swapped(dz_k, z_swap)
+    dq, dz_k, dy_k = lax.optimization_barrier((dq, dz_k, dy_k))
     far_came, dq = lax.optimization_barrier((far_came, dq))
-    (placed,) = call(functools.partial(place_kernel, block, far), (lists, *far_came), [frame_sum])
+    (placed,) = call(
+        functools.partial(place_kernel, block, (z_swap, y_swap), far),
+        (lists, dz_v_came, dy_v_came, *far_came),
+        [frame_sum],
+    )
     near, q_keep, q_send = call(
         own_kernel,
         (qg, lse, row_dot, dq, o, kv, placed),
         [frame_sum, pair, pair],
-        flops=20 * work,
+        flops=28 * work,
     )
     outputs = [sds((s_dev, width), BF16)] * 2
     attn_out, grad_q = call(finish_kernel, (q_keep, across(q_send)), outputs)
-    near, attn_out, grad_q = lax.optimization_barrier((near, attn_out, grad_q))
     (near,) = call(
         functools.partial(add_kernel, (near_swap, y_swap)),
-        (near, da_came, dy_came),
+        (near, da_came, dy_k_came),
         [frame_sum],
-        flops=20 * work,
+        flops=5 * work,
     )
     k_keep, k_send = call(
-        functools.partial(gather_kernel, z_swap), (near, dz_came), [pair, pair]
+        functools.partial(gather_kernel, z_swap), (near, dz_k_came), [pair, pair]
     )
     grad_k, grad_v = call(finish_kernel, (k_keep, across(k_send)), outputs)
     return attn_out, grad_q, grad_k, grad_v

time: 63.6 us -> 63.2 us (level)
  waiting for transfers between devices: 24.9 us -> 20.1 us
  starting transfers between devices: 14.6 us -> 19 us
    ppermute x14 -> x16, starting transfers between devices: 13.4 us -> 17.8 us  [swapped(): return lax.ppermute(value, ('tm', 'space'), swap.pairs)]
    ppermute x14 -> x16, waiting for transfers between devices: 21.9 us -> 19.4 us  [swapped(): return lax.ppermute(value, ('tm', 'space'), swap.pairs)]
    ppermute x5, waiting for transfers between devices: 3.06 us -> 0.64 us  [across(): return lax.ppermute(value, 'space', [(0, 1), (1, 0)])]
  transfers between devices with their start and end apart: 19 -> 21, of which waited for: 10 -> 8; matrix products, arithmetic and copies ran while one was open for 0% -> 0% of each run, Pallas kernels for 35% -> 35%
where the time goes in v14:
time: 63.2 us; the launch traced here: 63 us
  Pallas kernels  23.1 us (37%)
  waiting for transfers between devices  20.1 us (32%)
  starting transfers between devices  19 us (30%)
  between operations  0.83 us (1%)
    pallas_call x20, Pallas kernels, call(): pl.pallas_call(kernel, out_shape=out_shape, in_specs=[scalars if a.dtype...  23.1 us
    ppermute x16, waiting for transfers between devices, swapped(): return lax.ppermute(value, ('tm', 'space'), swap.pairs)  19.4 us
    ppermute x16, starting transfers between devices, swapped(): return lax.ppermute(value, ('tm', 'space'), swap.pairs)  17.8 us
  transfers between devices with their start and end apart: 21, of which 8 were waited for; matrix products, arithmetic and copies ran while one was open for 0% of the time, Pallas kernels for 35%

profile of v14, /device:TPU:0, one launch (start us, length us, event | category | flops | bytes accessed | tf_op | source)
XLA Modules:
  0.0 63.0 jit_solution(7209497292253187807)
XLA Ops:
  0.6 0.5 collective-permute-start
  1.2 1.3 %shard_map.84 = (bf16[512,128]{1,0:T(8,128)(2,1)S(1)}, bf16[512,128]{1,0:T(8,128)(2,1)S(1)}, bf16[512,256]{1,0:T(8,128)(2,1)S(1)}, bf16[512,256]{1,0:T(8,128)(2,1)S(1)}, s32[8,16]{1,0:T(8,128)S(1)}) custom-call(bf16[512,256]{1,0:T(8,128)(2,1)} %k.1, bf16[512,256]{1,0:T(8,128)(2,1)} %v.1, bf16[512,256]{1,0:T(8,128)(2,1)} %q.1, bf16[512,256]{1,0:T(8,128)(2,1)} %g.1, ...), custom_call_target="tpu_custom_call" | custom-call | flops 1024 | bytes 1024 | tf_op jit(solution)/shard_map/pallas_call | solution.py:38
  2.6 0.5 collective-permute-start.2
  3.3 3.0 %collective-permute-start.6 = (bf16[1024,256]{1,0:T(8,128)(2,1)S(1)}, bf16[1024,256]{1,0:T(8,128)(2,1)S(1)}, u32[]{:S(2)}, u32[]{:S(2)}) collective-permute-start(bf16[1024,256]{1,0:T(8,128)(2,1)S(1)} %get-tuple-element.76.kv), channel_id=1, source_target_pairs={{0,2},{1,3},{2,0},{3,1},{4,6},{5,7},{6,4},{7,5},{8,10},{9,11},{10,... | collective-permute-start | bytes 1572872 | tf_op jit(solution)/shard_map/ppermute | solution.py:536
  6.3 2.7 %collective-permute-start.7 = (bf16[1024,128]{1,0:T(8,128)(2,1)S(1)}, bf16[1024,128]{1,0:T(8,128)(2,1)S(1)}, u32[]{:S(2)}, u32[]{:S(2)}) collective-permute-start(bf16[1024,128]{1,0:T(8,128)(2,1)S(1)} %shard_map.85.keys), channel_id=1, source_target_pairs={{0,4},{1,5},{2,6},{3,7},{4,0},{5,1},{6,2},{7,3},{8,12},{9,13},{10,... | collective-permute-start | bytes 786440 | tf_op jit(solution)/shard_map/ppermute | solution.py:536
  9.2 0.6 %shard_map.88 = bf16[512,256]{1,0:T(8,128)(2,1)S(1)} custom-call(s32[8,16]{1,0:T(8,128)S(1)} %get-tuple-element.71.lists.lists_any.refs_0_, bf16[1024,256]{1,0:T(8,128)(2,1)S(1)} %get-tuple-element.76.kv), custom_call_target="tpu_custom_call" | custom-call | flops 1024 | bytes 1024 | tf_op jit(solution)/shard_map/pallas_call | solution.py:38
  9.8 6.3 %collective-permute-done.7.z.z_k = bf16[1024,128]{1,0:T(8,128)(2,1)S(1)} collective-permute-done((bf16[1024,128]{1,0:T(8,128)(2,1)S(1)}, bf16[1024,128]{1,0:T(8,128)(2,1)S(1)}, u32[]{:S(2)}, u32[]{:S(2)}) %collective-permute-start.7) | collective-permute-done | bytes 262176 | tf_op jit(solution)/shard_map/ppermute | solution.py:536
  16.2 0.6 collective-permute-start.8
  16.7 1.9 %collective-permute-start.9 = (bf16[512,256]{1,0:T(8,128)(2,1)S(1)}, bf16[512,256]{1,0:T(8,128)(2,1)S(1)}, u32[]{:S(2)}, u32[]{:S(2)}) collective-permute-start(bf16[512,256]{1,0:T(8,128)(2,1)S(1)} %shard_map.88), channel_id=1, source_target_pairs={{0,8},{1,9},{2,10},{3,11},{4,12},{5,13},{6,14},{7,15},{8,0},{9,1},... | collective-permute-start | bytes 786440 | tf_op jit(solution)/shard_map/ppermute | solution.py:536
  18.7 0.3 collective-permute-done.6.a_kv
  19.0 3.5 %shard_map.90 = (f32[8,1024]{1,0:T(8,128)S(1)}, f32[128,1024]{1,0:T(8,128)S(1)}) custom-call(s32[8,16]{1,0:T(8,128)S(1)} %get-tuple-element.71.lists.lists_any.refs_0_, bf16[1024,256]{1,0:T(8,128)(2,1)S(1)} %get-tuple-element.70.qg.refs_1_, bf16[1024,256]{1,0:T(8,128)(2,1)S(1)} %get-tuple-element.76.kv, bf16[1024,256]{1,0:T(8,128)(2,1)S(1)} %collective-permute-done.6.a_kv), custom_call_target="tpu_custom_call" | custom-call | flops 1024 | bytes 1024 | tf_op jit(solution)/shard_map/pallas_call | solution.py:38
  22.5 1.2 %collective-permute-done.5.z.z_v = bf16[1024,128]{1,0:T(8,128)(2,1)S(1)} collective-permute-done((bf16[1024,128]{1,0:T(8,128)(2,1)S(1)}, bf16[1024,128]{1,0:T(8,128)(2,1)S(1)}, u32[]{:S(2)}, u32[]{:S(2)}) %collective-permute-start.5) | collective-permute-done | bytes 262176 | tf_op jit(solution)/shard_map/ppermute | solution.py:536
  23.6 0.2 shard_map.91
  23.9 1.0 %collective-permute-start.10 = (bf16[1024,128]{1,0:T(8,128)(2,1)S(1)}, bf16[1024,128]{1,0:T(8,128)(2,1)S(1)}, u32[]{:S(2)}, u32[]{:S(2)}) collective-permute-start(bf16[1024,128]{1,0:T(8,128)(2,1)S(1)} %shard_map.91), channel_id=1, source_target_pairs={{0,2},{1,3},{2,0},{3,1},{4,6},{5,7},{6,4},{7,5},{8,10},{9,11},{10,... | collective-permute-start | bytes 786440 | tf_op jit(solution)/shard_map/ppermute | solution.py:536
  24.9 2.6 %shard_map.92 = (f32[8,1024]{1,0:T(8,128)S(1)}, f32[128,1024]{1,0:T(8,128)S(1)}, f32[2,512,512]{2,1,0:T(8,128)S(1)}) custom-call(s32[8,16]{1,0:T(8,128)S(1)} %get-tuple-element.71.lists.lists_any.refs_0_, bf16[1024,256]{1,0:T(8,128)(2,1)S(1)} %get-tuple-element.70.qg.refs_1_, f32[8,1024]{1,0:T(8,128)S(1)} %get-tuple-element.87.stat, ...), custom_call_target="tpu_custom_call" | custom-call | flops 1024 | bytes 1024 | tf_op jit(solution)/shard_map/pallas_call | solution.py:38
  27.5 3.2 %collective-permute-done.9.refs_0_.refs_8_ = bf16[512,256]{1,0:T(8,128)(2,1)S(1)} collective-permute-done((bf16[512,256]{1,0:T(8,128)(2,1)S(1)}, bf16[512,256]{1,0:T(8,128)(2,1)S(1)}, u32[]{:S(2)}, u32[]{:S(2)}) %collective-permute-start.9) | collective-permute-done | bytes 262176 | tf_op jit(solution)/shard_map/ppermute | solution.py:536
  30.7 1.4 %shard_map.93 = (f32[8,1024]{1,0:T(8,128)S(1)}, f32[128,1024]{1,0:T(8,128)S(1)}, bf16[1024,128]{1,0:T(8,128)(2,1)S(1)}, f32[2,512,512]{2,1,0:T(8,128)S(1)}) custom-call(s32[8,16]{1,0:T(8,128)S(1)} %get-tuple-element.71.lists.lists_any.refs_0_, bf16[1024,256]{1,0:T(8,128)(2,1)S(1)} %get-tuple-element.70.qg.refs_1_, f32[8,1024]{1,0:T(8,128)S(1)} %get-tuple-element.89.stat, ...), custom_call_target="tpu_custom_call" | custom-call | flops 1024 | bytes 1024 | tf_op jit(solution)/shard_map/pallas_call | solution.py:38
  32.1 1.5 %collective-permute-start.12 = (bf16[1024,128]{1,0:T(8,128)(2,1)S(1)}, bf16[1024,128]{1,0:T(8,128)(2,1)S(1)}, u32[]{:S(2)}, u32[]{:S(2)}) collective-permute-start(bf16[1024,128]{1,0:T(8,128)(2,1)S(1)} %get-tuple-element.102), channel_id=1, source_target_pairs={{0,2},{1,3},{2,0},{3,1},{4,6},{5,7},{6,4},{7,5},{8,10},{9,11},{10,... | collective-permute-start | bytes 786440 | tf_op jit(solution)/shard_map/ppermute | solution.py:536
  33.7 2.5 %shard_map.94 = (bf16[128,1024]{1,0:T(8,128)(2,1)S(1)}, f32[8,1024]{1,0:T(8,128)S(1)}, bf16[1024,128]{1,0:T(8,128)(2,1)S(1)}, f32[128,1024]{1,0:T(8,128)S(1)}, bf16[512,256]{1,0:T(8,128)(2,1)S(1)}) custom-call(s32[8,16]{1,0:T(8,128)S(1)} %get-tuple-element.71.lists.lists_any.refs_0_, bf16[1024,256]{1,0:T(8,128)(2,1)S(1)} %get-tuple-element.70.qg.refs_1_, ...), custom_call_target="tpu_custom_call" | custom-call | flops 1024 | bytes 1024 | tf_op jit(solution)/shard_map/pallas_call | solution.py:38
  36.2 0.6 collective-permute-start.13
  36.8 3.7 %collective-permute-done.12.came = bf16[1024,128]{1,0:T(8,128)(2,1)S(1)} collective-permute-done((bf16[1024,128]{1,0:T(8,128)(2,1)S(1)}, bf16[1024,128]{1,0:T(8,128)(2,1)S(1)}, u32[]{:S(2)}, u32[]{:S(2)}) %collective-permute-start.12) | collective-permute-done | bytes 262176 | tf_op jit(solution)/shard_map/ppermute | solution.py:536
  40.5 2.2 %shard_map.95 = (f32[1024,128]{1,0:T(8,128)S(1)}, f32[1024,128]{1,0:T(8,128)S(1)}, bf16[1024,128]{1,0:T(8,128)(2,1)S(1)}, bf16[1024,128]{1,0:T(8,128)(2,1)S(1)}, f32[128,1024]{1,0:T(8,128)S(1)}) custom-call(s32[8,16]{1,0:T(8,128)S(1)} %get-tuple-element.71.lists.lists_any.refs_0_, bf16[1024,256]{1,0:T(8,128)(2,1)S(1)} %get-tuple-element.70.qg.refs_1_, ...), custom_call_target="tpu_custom_call" | custom-call | flops 2684354560 | bytes 1024 | tf_op jit(solution)/shard_map/pallas_call | solution.py:38
  42.9 2.2 %shard_map.96 = (bf16[1024,256]{1,0:T(8,128)(2,1)S(1)}, f32[128,1024]{1,0:T(8,128)S(1)}) custom-call(s32[8,16]{1,0:T(8,128)S(1)} %get-tuple-element.71.lists.lists_any.refs_0_, bf16[1024,256]{1,0:T(8,128)(2,1)S(1)} %get-tuple-element.70.qg.refs_1_, f32[8,1024]{1,0:T(8,128)S(1)} %get-tuple-element.95.refs_3_.lse_ref, ...), custom_call_target="tpu_custom_call" | custom-call | flops 1024 | bytes 1024 | tf_op jit(solution)/shard_map/pallas_call | solution.py:38
  45.1 2.5 %collective-permute-start.17 = (bf16[1024,256]{1,0:T(8,128)(2,1)S(1)}, bf16[1024,256]{1,0:T(8,128)(2,1)S(1)}, u32[]{:S(2)}, u32[]{:S(2)}) collective-permute-start(bf16[1024,256]{1,0:T(8,128)(2,1)S(1)} %get-tuple-element.121), channel_id=1, source_target_pairs={{0,2},{1,3},{2,0},{3,1},{4,6},{5,7},{6,4},{7,5},{8,10},{9,11},{10,... | collective-permute-start | bytes 1572872 | tf_op jit(solution)/shard_map/ppermute | solution.py:536
  47.7 3.6 %collective-permute-start.19 = (bf16[1024,128]{1,0:T(8,128)(2,1)S(1)}, bf16[1024,128]{1,0:T(8,128)(2,1)S(1)}, u32[]{:S(2)}, u32[]{:S(2)}) collective-permute-start(bf16[1024,128]{1,0:T(8,128)(2,1)S(1)} %get-tuple-element.108), channel_id=1, source_target_pairs={{0,4},{1,5},{2,6},{3,7},{4,0},{5,1},{6,2},{7,3},{8,12},{9,13},{10,... | collective-permute-start | bytes 786440 | tf_op jit(solution)/shard_map/ppermute | solution.py:536
  51.3 3.7 %collective-permute-done.14.refs_1_ = bf16[1024,128]{1,0:T(8,128)(2,1)S(1)} collective-permute-done((bf16[1024,128]{1,0:T(8,128)(2,1)S(1)}, bf16[1024,128]{1,0:T(8,128)(2,1)S(1)}, u32[]{:S(2)}, u32[]{:S(2)}) %collective-permute-start.14) | collective-permute-done | bytes 262176 | tf_op jit(solution)/shard_map/ppermute | solution.py:536
  55.0 0.8 %shard_map.98.placed = f32[1024,256]{1,0:T(8,128)S(1)} custom-call(s32[8,16]{1,0:T(8,128)S(1)} %get-tuple-element.71.lists.lists_any.refs_0_, bf16[1024,128]{1,0:T(8,128)(2,1)S(1)} %collective-permute-done.14.refs_1_, bf16[1024,128]{1,0:T(8,128)(2,1)S(1)} %collective-permute-done.15.refs_2_, bf16[512,256]{1,0:T(8,128)(2,1)S(1)} %collective-permute-done.11.refs_3_), custom_call_target="tpu_custom_call" | custom-call | flops 1024 | bytes 1024 | tf_op jit(solution)/shard_map/pallas_call | solution.py:38
  55.8 3.2 %shard_map.99 = (f32[1024,256]{1,0:T(8,128)S(1)}, bf16[512,256]{1,0:T(8,128)(2,1)S(1)}, bf16[512,256]{1,0:T(8,128)(2,1)S(1)}) custom-call(bf16[1024,256]{1,0:T(8,128)(2,1)S(1)} %get-tuple-element.70.qg.refs_1_, f32[8,1024]{1,0:T(8,128)S(1)} %get-tuple-element.95.refs_3_.lse_ref, f32[8,1024]{1,0:T(8,128)S(1)} %get-tuple-element.99.dot_ref, ...), custom_call_target="tpu_custom_call" | custom-call | flops 3758096384 | bytes 1024 | tf_op jit(solution)/shard_map/pallas_call | solution.py:38
  59.1 1.1 %collective-permute-done.17.da = bf16[1024,256]{1,0:T(8,128)(2,1)S(1)} collective-permute-done((bf16[1024,256]{1,0:T(8,128)(2,1)S(1)}, bf16[1024,256]{1,0:T(8,128)(2,1)S(1)}, u32[]{:S(2)}, u32[]{:S(2)}) %collective-permute-start.17) | collective-permute-done | bytes 524320 | tf_op jit(solution)/shard_map/ppermute | solution.py:536
  60.6 0.9 %shard_map.100 = (bf16[512,256]{1,0:T(8,128)(2,1)}, bf16[512,256]{1,0:T(8,128)(2,1)}) custom-call(bf16[512,256]{1,0:T(8,128)(2,1)S(1)} %get-tuple-element.116.keep, bf16[512,256]{1,0:T(8,128)(2,1)S(1)} %collective-permute-done.16.came), custom_call_target="tpu_custom_call" | custom-call | flops 1024 | bytes 1024 | tf_op jit(solution)/shard_map/pallas_call | solution.py:38
  61.5 0.6 collective-permute-done.20.came
  62.1 0.9 %shard_map.103 = (bf16[512,256]{1,0:T(8,128)(2,1)}, bf16[512,256]{1,0:T(8,128)(2,1)}) custom-call(bf16[512,256]{1,0:T(8,128)(2,1)S(1)} %get-tuple-element.122.keep, bf16[512,256]{1,0:T(8,128)(2,1)S(1)} %collective-permute-done.20.came), custom_call_target="tpu_custom_call" | custom-call | flops 1024 | bytes 1024 | tf_op jit(solution)/shard_map/pallas_call | solution.py:38
  (30 shorter events, 1.4 us)
Async XLA Ops:
  0.6 1.9 %collective-permute-start = (bf16[512,256]{1,0:T(8,128)(2,1)}, bf16[512,256]{1,0:T(8,128)(2,1)S(1)}, u32[]{:S(2)}, u32[]{:S(2)}) collective-permute-start(bf16[512,256]{1,0:T(8,128)(2,1)} %k.1), channel_id=1, source_target_pairs={{0,1},{1,0},{2,3},{3,2},{4,5},{5,4},{6,7},{7,6},{8,9},{9,8},{10,11... | collective-permute-start | bytes 786440 | tf_op jit(solution)/shard_map/ppermute | solution.py:533
  1.2 2.0 %collective-permute-start.3 = (bf16[512,256]{1,0:T(8,128)(2,1)}, bf16[512,256]{1,0:T(8,128)(2,1)S(1)}, u32[]{:S(2)}, u32[]{:S(2)}) collective-permute-start(bf16[512,256]{1,0:T(8,128)(2,1)} %v.1), channel_id=1, source_target_pairs={{0,1},{1,0},{2,3},{3,2},{4,5},{5,4},{6,7},{7,6},{8,9},{9,8},{10,11... | collective-permute-start | bytes 786440 | tf_op jit(solution)/shard_map/ppermute | solution.py:533
  2.6 6.5 %collective-permute-start.2 = (bf16[512,256]{1,0:T(8,128)(2,1)S(1)}, bf16[512,256]{1,0:T(8,128)(2,1)S(1)}, u32[]{:S(2)}, u32[]{:S(2)}) collective-permute-start(bf16[512,256]{1,0:T(8,128)(2,1)S(1)} %get-tuple-element.68), channel_id=1, source_target_pairs={{0,1},{1,0},{2,3},{3,2},{4,5},{5,4},{6,7},{7,6},{8,9},{9,8},{10,11... | collective-permute-start | bytes 786440 | tf_op jit(solution)/shard_map/ppermute | solution.py:533
  3.1 6.0 %collective-permute-start.1 = (bf16[1024,128]{1,0:T(8,128)(2,1)S(1)}, bf16[1024,128]{1,0:T(8,128)(2,1)S(1)}, u32[]{:S(2)}, u32[]{:S(2)}) collective-permute-start(bf16[1024,128]{1,0:T(8,128)(2,1)S(1)} %shard_map.85.keys), channel_id=1, source_target_pairs={{0,1},{1,0},{2,3},{3,2},{4,8},{5,9},{6,10},{7,11},{8,4},{9,5},{10,... | collective-permute-start | bytes 786440 | tf_op jit(solution)/shard_map/ppermute | solution.py:536
  3.3 15.7 %collective-permute-start.6 = (bf16[1024,256]{1,0:T(8,128)(2,1)S(1)}, bf16[1024,256]{1,0:T(8,128)(2,1)S(1)}, u32[]{:S(2)}, u32[]{:S(2)}) collective-permute-start(bf16[1024,256]{1,0:T(8,128)(2,1)S(1)} %get-tuple-element.76.kv), channel_id=1, source_target_pairs={{0,2},{1,3},{2,0},{3,1},{4,6},{5,7},{6,4},{7,5},{8,10},{9,11},{10,... | collective-permute-start | bytes 1572872 | tf_op jit(solution)/shard_map/ppermute | solution.py:536
  6.3 9.8 %collective-permute-start.7 = (bf16[1024,128]{1,0:T(8,128)(2,1)S(1)}, bf16[1024,128]{1,0:T(8,128)(2,1)S(1)}, u32[]{:S(2)}, u32[]{:S(2)}) collective-permute-start(bf16[1024,128]{1,0:T(8,128)(2,1)S(1)} %shard_map.85.keys), channel_id=1, source_target_pairs={{0,4},{1,5},{2,6},{3,7},{4,0},{5,1},{6,2},{7,3},{8,12},{9,13},{10,... | collective-permute-start | bytes 786440 | tf_op jit(solution)/shard_map/ppermute | solution.py:536
  9.0 14.6 %collective-permute-start.5 = (bf16[1024,128]{1,0:T(8,128)(2,1)S(1)}, bf16[1024,128]{1,0:T(8,128)(2,1)S(1)}, u32[]{:S(2)}, u32[]{:S(2)}) collective-permute-start(bf16[1024,128]{1,0:T(8,128)(2,1)S(1)} %get-tuple-element.73), channel_id=1, source_target_pairs={{0,4},{1,5},{2,6},{3,7},{4,0},{5,1},{6,2},{7,3},{8,12},{9,13},{10,... | collective-permute-start | bytes 786440 | tf_op jit(solution)/shard_map/ppermute | solution.py:536
  9.0 14.6 %collective-permute-start.4 = (bf16[1024,128]{1,0:T(8,128)(2,1)S(1)}, bf16[1024,128]{1,0:T(8,128)(2,1)S(1)}, u32[]{:S(2)}, u32[]{:S(2)}) collective-permute-start(bf16[1024,128]{1,0:T(8,128)(2,1)S(1)} %get-tuple-element.73), channel_id=1, source_target_pairs={{0,1},{1,0},{2,3},{3,2},{4,8},{5,9},{6,10},{7,11},{8,4},{9,5},{10,... | collective-permute-start | bytes 786440 | tf_op jit(solution)/shard_map/ppermute | solution.py:536
  16.2 8.7 %collective-permute-start.8 = (bf16[1024,128]{1,0:T(8,128)(2,1)S(1)}, bf16[1024,128]{1,0:T(8,128)(2,1)S(1)}, u32[]{:S(2)}, u32[]{:S(2)}) collective-permute-start(bf16[1024,128]{1,0:T(8,128)(2,1)S(1)} %shard_map.89), channel_id=1, source_target_pairs={{0,2},{1,3},{2,0},{3,1},{4,6},{5,7},{6,4},{7,5},{8,10},{9,11},{10,... | collective-permute-start | bytes 786440 | tf_op jit(solution)/shard_map/ppermute | solution.py:536
  16.7 14.0 %collective-permute-start.9 = (bf16[512,256]{1,0:T(8,128)(2,1)S(1)}, bf16[512,256]{1,0:T(8,128)(2,1)S(1)}, u32[]{:S(2)}, u32[]{:S(2)}) collective-permute-start(bf16[512,256]{1,0:T(8,128)(2,1)S(1)} %shard_map.88), channel_id=1, source_target_pairs={{0,8},{1,9},{2,10},{3,11},{4,12},{5,13},{6,14},{7,15},{8,0},{9,1},... | collective-permute-start | bytes 786440 | tf_op jit(solution)/shard_map/ppermute | solution.py:536
  23.9 9.8 %collective-permute-start.10 = (bf16[1024,128]{1,0:T(8,128)(2,1)S(1)}, bf16[1024,128]{1,0:T(8,128)(2,1)S(1)}, u32[]{:S(2)}, u32[]{:S(2)}) collective-permute-start(bf16[1024,128]{1,0:T(8,128)(2,1)S(1)} %shard_map.91), channel_id=1, source_target_pairs={{0,2},{1,3},{2,0},{3,1},{4,6},{5,7},{6,4},{7,5},{8,10},{9,11},{10,... | collective-permute-start | bytes 786440 | tf_op jit(solution)/shard_map/ppermute | solution.py:536
  32.1 8.4 %collective-permute-start.12 = (bf16[1024,128]{1,0:T(8,128)(2,1)S(1)}, bf16[1024,128]{1,0:T(8,128)(2,1)S(1)}, u32[]{:S(2)}, u32[]{:S(2)}) collective-permute-start(bf16[1024,128]{1,0:T(8,128)(2,1)S(1)} %get-tuple-element.102), channel_id=1, source_target_pairs={{0,2},{1,3},{2,0},{3,1},{4,6},{5,7},{6,4},{7,5},{8,10},{9,11},{10,... | collective-permute-start | bytes 786440 | tf_op jit(solution)/shard_map/ppermute | solution.py:536
  36.1 15.2 %collective-permute-start.11 = (bf16[512,256]{1,0:T(8,128)(2,1)S(1)}, bf16[512,256]{1,0:T(8,128)(2,1)S(1)}, u32[]{:S(2)}, u32[]{:S(2)}) collective-permute-start(bf16[512,256]{1,0:T(8,128)(2,1)S(1)} %get-tuple-element.100), channel_id=1, source_target_pairs={{0,8},{1,9},{2,10},{3,11},{4,12},{5,13},{6,14},{7,15},{8,0},{9,1},... | collective-permute-start | bytes 786440 | tf_op jit(solution)/shard_map/ppermute | solution.py:536
  36.2 11.4 %collective-permute-start.13 = (bf16[1024,128]{1,0:T(8,128)(2,1)S(1)}, bf16[1024,128]{1,0:T(8,128)(2,1)S(1)}, u32[]{:S(2)}, u32[]{:S(2)}) collective-permute-start(bf16[1024,128]{1,0:T(8,128)(2,1)S(1)} %get-tuple-element.107), channel_id=1, source_target_pairs={{0,2},{1,3},{2,0},{3,1},{4,6},{5,7},{6,4},{7,5},{8,10},{9,11},{10,... | collective-permute-start | bytes 786440 | tf_op jit(solution)/shard_map/ppermute | solution.py:536
  42.7 12.3 %collective-permute-start.14 = (bf16[1024,128]{1,0:T(8,128)(2,1)S(1)}, bf16[1024,128]{1,0:T(8,128)(2,1)S(1)}, u32[]{:S(2)}, u32[]{:S(2)}) collective-permute-start(bf16[1024,128]{1,0:T(8,128)(2,1)S(1)} %get-tuple-element.113), channel_id=1, source_target_pairs={{0,4},{1,5},{2,6},{3,7},{4,0},{5,1},{6,2},{7,3},{8,12},{9,13},{10,... | collective-permute-start | bytes 786440 | tf_op jit(solution)/shard_map/ppermute | solution.py:536
  42.8 12.2 %collective-permute-start.15 = (bf16[1024,128]{1,0:T(8,128)(2,1)S(1)}, bf16[1024,128]{1,0:T(8,128)(2,1)S(1)}, u32[]{:S(2)}, u32[]{:S(2)}) collective-permute-start(bf16[1024,128]{1,0:T(8,128)(2,1)S(1)} %get-tuple-element.114), channel_id=1, source_target_pairs={{0,1},{1,0},{2,3},{3,2},{4,8},{5,9},{6,10},{7,11},{8,4},{9,5},{10,... | collective-permute-start | bytes 786440 | tf_op jit(solution)/shard_map/ppermute | solution.py:536
  45.1 15.0 %collective-permute-start.17 = (bf16[1024,256]{1,0:T(8,128)(2,1)S(1)}, bf16[1024,256]{1,0:T(8,128)(2,1)S(1)}, u32[]{:S(2)}, u32[]{:S(2)}) collective-permute-start(bf16[1024,256]{1,0:T(8,128)(2,1)S(1)} %get-tuple-element.121), channel_id=1, source_target_pairs={{0,2},{1,3},{2,0},{3,1},{4,6},{5,7},{6,4},{7,5},{8,10},{9,11},{10,... | collective-permute-start | bytes 1572872 | tf_op jit(solution)/shard_map/ppermute | solution.py:536
  47.7 12.6 %collective-permute-start.19 = (bf16[1024,128]{1,0:T(8,128)(2,1)S(1)}, bf16[1024,128]{1,0:T(8,128)(2,1)S(1)}, u32[]{:S(2)}, u32[]{:S(2)}) collective-permute-start(bf16[1024,128]{1,0:T(8,128)(2,1)S(1)} %get-tuple-element.108), channel_id=1, source_target_pairs={{0,4},{1,5},{2,6},{3,7},{4,0},{5,1},{6,2},{7,3},{8,12},{9,13},{10,... | collective-permute-start | bytes 786440 | tf_op jit(solution)/shard_map/ppermute | solution.py:536
  51.3 8.9 %collective-permute-start.18 = (bf16[1024,128]{1,0:T(8,128)(2,1)S(1)}, bf16[1024,128]{1,0:T(8,128)(2,1)S(1)}, u32[]{:S(2)}, u32[]{:S(2)}) collective-permute-start(bf16[1024,128]{1,0:T(8,128)(2,1)S(1)} %get-tuple-element.109), channel_id=1, source_target_pairs={{0,1},{1,0},{2,3},{3,2},{4,8},{5,9},{6,10},{7,11},{8,4},{9,5},{10,... | collective-permute-start | bytes 786440 | tf_op jit(solution)/shard_map/ppermute | solution.py:536
  59.0 1.6 %collective-permute-start.16 = (bf16[512,256]{1,0:T(8,128)(2,1)S(1)}, bf16[512,256]{1,0:T(8,128)(2,1)S(1)}, u32[]{:S(2)}, u32[]{:S(2)}) collective-permute-start(bf16[512,256]{1,0:T(8,128)(2,1)S(1)} %get-tuple-element.117), channel_id=1, source_target_pairs={{0,1},{1,0},{2,3},{3,2},{4,5},{5,4},{6,7},{7,6},{8,9},{9,8},{10,11... | collective-permute-start | bytes 786440 | tf_op jit(solution)/shard_map/ppermute | solution.py:533
  60.5 1.6 %collective-permute-start.20 = (bf16[512,256]{1,0:T(8,128)(2,1)S(1)}, bf16[512,256]{1,0:T(8,128)(2,1)S(1)}, u32[]{:S(2)}, u32[]{:S(2)}) collective-permute-start(bf16[512,256]{1,0:T(8,128)(2,1)S(1)} %get-tuple-element.123), channel_id=1, source_target_pairs={{0,1},{1,0},{2,3},{3,2},{4,5},{5,4},{6,7},{7,6},{8,9},{9,8},{10,11... | collective-permute-start | bytes 786440 | tf_op jit(solution)/shard_map/ppermute | solution.py:533

commit v15 on v14

--- a/solution.py
+++ b/solution.py
@@ -624,7 +624,7 @@
         scratch=[pltpu.VMEM((2 * s_dev, 2 * DH), F32)],
     )
     da_came = swapped(da, near_swap)
-    dz_k, dy_k = call(merge_kernel, (dz_k, dy_k, dc_k_came), [frame_one, frame_one])
+    dz_k, dy_k = call(merge_kernel, (dz_k, dy_k, dc_k_came), [frame_one, frame_one], flops=20 * work)
     dy_k_came = swapped(dy_k, y_swap)
     dz_k_came = swapped(dz_k, z_swap)
     dq, dz_k, dy_k = lax.optimization_barrier((dq, dz_k, dy_k))

time: 63.2 us -> 63.2 us (level)
  no operation moved by 1% of the time
where the time goes in v15:
time: 63.2 us; the launch traced here: 63 us
  Pallas kernels  23.1 us (37%)
  waiting for transfers between devices  20.2 us (32%)
  starting transfers between devices  18.9 us (30%)
  between operations  0.83 us (1%)
    pallas_call x20, Pallas kernels, call(): pl.pallas_call(kernel, out_shape=out_shape, in_specs=[scalars if a.dtype...  23.1 us
    ppermute x16, waiting for transfers between devices, swapped(): return lax.ppermute(value, ('tm', 'space'), swap.pairs)  19.5 us
    ppermute x16, starting transfers between devices, swapped(): return lax.ppermute(value, ('tm', 'space'), swap.pairs)  17.7 us
  transfers between devices with their start and end apart: 21, of which 8 were waited for; matrix products, arithmetic and copies ran while one was open for 0% of the time, Pallas kernels for 35%

profile of v15, /device:TPU:0, one launch (start us, length us, event | category | flops | bytes accessed | tf_op | source)
XLA Modules:
  0.0 63.0 jit_solution(8788831522451191306)
XLA Ops:
  0.6 0.5 collective-permute-start
  1.2 1.3 %shard_map.84 = (bf16[512,128]{1,0:T(8,128)(2,1)S(1)}, bf16[512,128]{1,0:T(8,128)(2,1)S(1)}, bf16[512,256]{1,0:T(8,128)(2,1)S(1)}, bf16[512,256]{1,0:T(8,128)(2,1)S(1)}, s32[8,16]{1,0:T(8,128)S(1)}) custom-call(bf16[512,256]{1,0:T(8,128)(2,1)} %k.1, bf16[512,256]{1,0:T(8,128)(2,1)} %v.1, bf16[512,256]{1,0:T(8,128)(2,1)} %q.1, bf16[512,256]{1,0:T(8,128)(2,1)} %g.1, ...), custom_call_target="tpu_custom_call" | custom-call | flops 1024 | bytes 1024 | tf_op jit(solution)/shard_map/pallas_call | solution.py:38
  2.6 0.5 collective-permute-start.2
  3.3 3.0 %collective-permute-start.6 = (bf16[1024,256]{1,0:T(8,128)(2,1)S(1)}, bf16[1024,256]{1,0:T(8,128)(2,1)S(1)}, u32[]{:S(2)}, u32[]{:S(2)}) collective-permute-start(bf16[1024,256]{1,0:T(8,128)(2,1)S(1)} %get-tuple-element.76.kv), channel_id=1, source_target_pairs={{0,2},{1,3},{2,0},{3,1},{4,6},{5,7},{6,4},{7,5},{8,10},{9,11},{10,... | collective-permute-start | bytes 1572872 | tf_op jit(solution)/shard_map/ppermute | solution.py:536
  6.3 2.7 %collective-permute-start.7 = (bf16[1024,128]{1,0:T(8,128)(2,1)S(1)}, bf16[1024,128]{1,0:T(8,128)(2,1)S(1)}, u32[]{:S(2)}, u32[]{:S(2)}) collective-permute-start(bf16[1024,128]{1,0:T(8,128)(2,1)S(1)} %shard_map.85.keys), channel_id=1, source_target_pairs={{0,4},{1,5},{2,6},{3,7},{4,0},{5,1},{6,2},{7,3},{8,12},{9,13},{10,... | collective-permute-start | bytes 786440 | tf_op jit(solution)/shard_map/ppermute | solution.py:536
  9.2 0.6 %shard_map.88 = bf16[512,256]{1,0:T(8,128)(2,1)S(1)} custom-call(s32[8,16]{1,0:T(8,128)S(1)} %get-tuple-element.71.lists.lists_any.refs_0_, bf16[1024,256]{1,0:T(8,128)(2,1)S(1)} %get-tuple-element.76.kv), custom_call_target="tpu_custom_call" | custom-call | flops 1024 | bytes 1024 | tf_op jit(solution)/shard_map/pallas_call | solution.py:38
  9.8 6.3 %collective-permute-done.7.z.z_k = bf16[1024,128]{1,0:T(8,128)(2,1)S(1)} collective-permute-done((bf16[1024,128]{1,0:T(8,128)(2,1)S(1)}, bf16[1024,128]{1,0:T(8,128)(2,1)S(1)}, u32[]{:S(2)}, u32[]{:S(2)}) %collective-permute-start.7) | collective-permute-done | bytes 262176 | tf_op jit(solution)/shard_map/ppermute | solution.py:536
  16.2 0.6 collective-permute-start.8
  16.7 1.9 %collective-permute-start.9 = (bf16[512,256]{1,0:T(8,128)(2,1)S(1)}, bf16[512,256]{1,0:T(8,128)(2,1)S(1)}, u32[]{:S(2)}, u32[]{:S(2)}) collective-permute-start(bf16[512,256]{1,0:T(8,128)(2,1)S(1)} %shard_map.88), channel_id=1, source_target_pairs={{0,8},{1,9},{2,10},{3,11},{4,12},{5,13},{6,14},{7,15},{8,0},{9,1},... | collective-permute-start | bytes 786440 | tf_op jit(solution)/shard_map/ppermute | solution.py:536
  18.7 0.3 collective-permute-done.6.a_kv
  19.0 3.5 %shard_map.90 = (f32[8,1024]{1,0:T(8,128)S(1)}, f32[128,1024]{1,0:T(8,128)S(1)}) custom-call(s32[8,16]{1,0:T(8,128)S(1)} %get-tuple-element.71.lists.lists_any.refs_0_, bf16[1024,256]{1,0:T(8,128)(2,1)S(1)} %get-tuple-element.70.qg.refs_1_, bf16[1024,256]{1,0:T(8,128)(2,1)S(1)} %get-tuple-element.76.kv, bf16[1024,256]{1,0:T(8,128)(2,1)S(1)} %collective-permute-done.6.a_kv), custom_call_target="tpu_custom_call" | custom-call | flops 1024 | bytes 1024 | tf_op jit(solution)/shard_map/pallas_call | solution.py:38
  22.5 1.2 %collective-permute-done.5.z.z_v = bf16[1024,128]{1,0:T(8,128)(2,1)S(1)} collective-permute-done((bf16[1024,128]{1,0:T(8,128)(2,1)S(1)}, bf16[1024,128]{1,0:T(8,128)(2,1)S(1)}, u32[]{:S(2)}, u32[]{:S(2)}) %collective-permute-start.5) | collective-permute-done | bytes 262176 | tf_op jit(solution)/shard_map/ppermute | solution.py:536
  23.6 0.2 shard_map.91
  23.9 1.0 %collective-permute-start.10 = (bf16[1024,128]{1,0:T(8,128)(2,1)S(1)}, bf16[1024,128]{1,0:T(8,128)(2,1)S(1)}, u32[]{:S(2)}, u32[]{:S(2)}) collective-permute-start(bf16[1024,128]{1,0:T(8,128)(2,1)S(1)} %shard_map.91), channel_id=1, source_target_pairs={{0,2},{1,3},{2,0},{3,1},{4,6},{5,7},{6,4},{7,5},{8,10},{9,11},{10,... | collective-permute-start | bytes 786440 | tf_op jit(solution)/shard_map/ppermute | solution.py:536
  24.9 2.6 %shard_map.92 = (f32[8,1024]{1,0:T(8,128)S(1)}, f32[128,1024]{1,0:T(8,128)S(1)}, f32[2,512,512]{2,1,0:T(8,128)S(1)}) custom-call(s32[8,16]{1,0:T(8,128)S(1)} %get-tuple-element.71.lists.lists_any.refs_0_, bf16[1024,256]{1,0:T(8,128)(2,1)S(1)} %get-tuple-element.70.qg.refs_1_, f32[8,1024]{1,0:T(8,128)S(1)} %get-tuple-element.87.stat, ...), custom_call_target="tpu_custom_call" | custom-call | flops 1024 | bytes 1024 | tf_op jit(solution)/shard_map/pallas_call | solution.py:38
  27.5 3.2 %collective-permute-done.9.refs_0_.refs_8_ = bf16[512,256]{1,0:T(8,128)(2,1)S(1)} collective-permute-done((bf16[512,256]{1,0:T(8,128)(2,1)S(1)}, bf16[512,256]{1,0:T(8,128)(2,1)S(1)}, u32[]{:S(2)}, u32[]{:S(2)}) %collective-permute-start.9) | collective-permute-done | bytes 262176 | tf_op jit(solution)/shard_map/ppermute | solution.py:536
  30.7 1.4 %shard_map.93 = (f32[8,1024]{1,0:T(8,128)S(1)}, f32[128,1024]{1,0:T(8,128)S(1)}, bf16[1024,128]{1,0:T(8,128)(2,1)S(1)}, f32[2,512,512]{2,1,0:T(8,128)S(1)}) custom-call(s32[8,16]{1,0:T(8,128)S(1)} %get-tuple-element.71.lists.lists_any.refs_0_, bf16[1024,256]{1,0:T(8,128)(2,1)S(1)} %get-tuple-element.70.qg.refs_1_, f32[8,1024]{1,0:T(8,128)S(1)} %get-tuple-element.89.stat, ...), custom_call_target="tpu_custom_call" | custom-call | flops 1024 | bytes 1024 | tf_op jit(solution)/shard_map/pallas_call | solution.py:38
  32.1 1.5 %collective-permute-start.12 = (bf16[1024,128]{1,0:T(8,128)(2,1)S(1)}, bf16[1024,128]{1,0:T(8,128)(2,1)S(1)}, u32[]{:S(2)}, u32[]{:S(2)}) collective-permute-start(bf16[1024,128]{1,0:T(8,128)(2,1)S(1)} %get-tuple-element.102), channel_id=1, source_target_pairs={{0,2},{1,3},{2,0},{3,1},{4,6},{5,7},{6,4},{7,5},{8,10},{9,11},{10,... | collective-permute-start | bytes 786440 | tf_op jit(solution)/shard_map/ppermute | solution.py:536
  33.7 2.5 %shard_map.94 = (bf16[128,1024]{1,0:T(8,128)(2,1)S(1)}, f32[8,1024]{1,0:T(8,128)S(1)}, bf16[1024,128]{1,0:T(8,128)(2,1)S(1)}, f32[128,1024]{1,0:T(8,128)S(1)}, bf16[512,256]{1,0:T(8,128)(2,1)S(1)}) custom-call(s32[8,16]{1,0:T(8,128)S(1)} %get-tuple-element.71.lists.lists_any.refs_0_, bf16[1024,256]{1,0:T(8,128)(2,1)S(1)} %get-tuple-element.70.qg.refs_1_, ...), custom_call_target="tpu_custom_call" | custom-call | flops 1024 | bytes 1024 | tf_op jit(solution)/shard_map/pallas_call | solution.py:38
  36.1 0.6 collective-permute-start.13
  36.8 3.8 %collective-permute-done.12.came = bf16[1024,128]{1,0:T(8,128)(2,1)S(1)} collective-permute-done((bf16[1024,128]{1,0:T(8,128)(2,1)S(1)}, bf16[1024,128]{1,0:T(8,128)(2,1)S(1)}, u32[]{:S(2)}, u32[]{:S(2)}) %collective-permute-start.12) | collective-permute-done | bytes 262176 | tf_op jit(solution)/shard_map/ppermute | solution.py:536
  40.6 2.2 %shard_map.95 = (f32[1024,128]{1,0:T(8,128)S(1)}, f32[1024,128]{1,0:T(8,128)S(1)}, bf16[1024,128]{1,0:T(8,128)(2,1)S(1)}, bf16[1024,128]{1,0:T(8,128)(2,1)S(1)}, f32[128,1024]{1,0:T(8,128)S(1)}) custom-call(s32[8,16]{1,0:T(8,128)S(1)} %get-tuple-element.71.lists.lists_any.refs_0_, bf16[1024,256]{1,0:T(8,128)(2,1)S(1)} %get-tuple-element.70.qg.refs_1_, ...), custom_call_target="tpu_custom_call" | custom-call | flops 2684354560 | bytes 1024 | tf_op jit(solution)/shard_map/pallas_call | solution.py:38
  42.9 2.2 %shard_map.96 = (bf16[1024,256]{1,0:T(8,128)(2,1)S(1)}, f32[128,1024]{1,0:T(8,128)S(1)}) custom-call(s32[8,16]{1,0:T(8,128)S(1)} %get-tuple-element.71.lists.lists_any.refs_0_, bf16[1024,256]{1,0:T(8,128)(2,1)S(1)} %get-tuple-element.70.qg.refs_1_, f32[8,1024]{1,0:T(8,128)S(1)} %get-tuple-element.95.refs_3_.lse_ref, ...), custom_call_target="tpu_custom_call" | custom-call | flops 1024 | bytes 1024 | tf_op jit(solution)/shard_map/pallas_call | solution.py:38
  45.2 2.4 %collective-permute-start.17 = (bf16[1024,256]{1,0:T(8,128)(2,1)S(1)}, bf16[1024,256]{1,0:T(8,128)(2,1)S(1)}, u32[]{:S(2)}, u32[]{:S(2)}) collective-permute-start(bf16[1024,256]{1,0:T(8,128)(2,1)S(1)} %get-tuple-element.121), channel_id=1, source_target_pairs={{0,2},{1,3},{2,0},{3,1},{4,6},{5,7},{6,4},{7,5},{8,10},{9,11},{10,... | collective-permute-start | bytes 1572872 | tf_op jit(solution)/shard_map/ppermute | solution.py:536
  47.7 3.6 %collective-permute-start.19 = (bf16[1024,128]{1,0:T(8,128)(2,1)S(1)}, bf16[1024,128]{1,0:T(8,128)(2,1)S(1)}, u32[]{:S(2)}, u32[]{:S(2)}) collective-permute-start(bf16[1024,128]{1,0:T(8,128)(2,1)S(1)} %get-tuple-element.108), channel_id=1, source_target_pairs={{0,4},{1,5},{2,6},{3,7},{4,0},{5,1},{6,2},{7,3},{8,12},{9,13},{10,... | collective-permute-start | bytes 786440 | tf_op jit(solution)/shard_map/ppermute | solution.py:536
  51.3 3.6 %collective-permute-done.14.refs_1_ = bf16[1024,128]{1,0:T(8,128)(2,1)S(1)} collective-permute-done((bf16[1024,128]{1,0:T(8,128)(2,1)S(1)}, bf16[1024,128]{1,0:T(8,128)(2,1)S(1)}, u32[]{:S(2)}, u32[]{:S(2)}) %collective-permute-start.14) | collective-permute-done | bytes 262176 | tf_op jit(solution)/shard_map/ppermute | solution.py:536
  54.9 0.8 %shard_map.98.placed = f32[1024,256]{1,0:T(8,128)S(1)} custom-call(s32[8,16]{1,0:T(8,128)S(1)} %get-tuple-element.71.lists.lists_any.refs_0_, bf16[1024,128]{1,0:T(8,128)(2,1)S(1)} %collective-permute-done.14.refs_1_, bf16[1024,128]{1,0:T(8,128)(2,1)S(1)} %collective-permute-done.15.refs_2_, bf16[512,256]{1,0:T(8,128)(2,1)S(1)} %collective-permute-done.11.refs_3_), custom_call_target="tpu_custom_call" | custom-call | flops 1024 | bytes 1024 | tf_op jit(solution)/shard_map/pallas_call | solution.py:38
  55.8 3.2 %shard_map.99 = (f32[1024,256]{1,0:T(8,128)S(1)}, bf16[512,256]{1,0:T(8,128)(2,1)S(1)}, bf16[512,256]{1,0:T(8,128)(2,1)S(1)}) custom-call(bf16[1024,256]{1,0:T(8,128)(2,1)S(1)} %get-tuple-element.70.qg.refs_1_, f32[8,1024]{1,0:T(8,128)S(1)} %get-tuple-element.95.refs_3_.lse_ref, f32[8,1024]{1,0:T(8,128)S(1)} %get-tuple-element.99.dot_ref, ...), custom_call_target="tpu_custom_call" | custom-call | flops 3758096384 | bytes 1024 | tf_op jit(solution)/shard_map/pallas_call | solution.py:38
  59.0 1.2 %collective-permute-done.17.da = bf16[1024,256]{1,0:T(8,128)(2,1)S(1)} collective-permute-done((bf16[1024,256]{1,0:T(8,128)(2,1)S(1)}, bf16[1024,256]{1,0:T(8,128)(2,1)S(1)}, u32[]{:S(2)}, u32[]{:S(2)}) %collective-permute-start.17) | collective-permute-done | bytes 524320 | tf_op jit(solution)/shard_map/ppermute | solution.py:536
  60.6 0.9 %shard_map.100 = (bf16[512,256]{1,0:T(8,128)(2,1)}, bf16[512,256]{1,0:T(8,128)(2,1)}) custom-call(bf16[512,256]{1,0:T(8,128)(2,1)S(1)} %get-tuple-element.116.keep, bf16[512,256]{1,0:T(8,128)(2,1)S(1)} %collective-permute-done.16.came), custom_call_target="tpu_custom_call" | custom-call | flops 1024 | bytes 1024 | tf_op jit(solution)/shard_map/pallas_call | solution.py:38
  61.5 0.6 collective-permute-done.20.came
  62.1 0.9 %shard_map.103 = (bf16[512,256]{1,0:T(8,128)(2,1)}, bf16[512,256]{1,0:T(8,128)(2,1)}) custom-call(bf16[512,256]{1,0:T(8,128)(2,1)S(1)} %get-tuple-element.122.keep, bf16[512,256]{1,0:T(8,128)(2,1)S(1)} %collective-permute-done.20.came), custom_call_target="tpu_custom_call" | custom-call | flops 1024 | bytes 1024 | tf_op jit(solution)/shard_map/pallas_call | solution.py:38
  (30 shorter events, 1.3 us)
Async XLA Ops:
  0.6 1.9 %collective-permute-start = (bf16[512,256]{1,0:T(8,128)(2,1)}, bf16[512,256]{1,0:T(8,128)(2,1)S(1)}, u32[]{:S(2)}, u32[]{:S(2)}) collective-permute-start(bf16[512,256]{1,0:T(8,128)(2,1)} %k.1), channel_id=1, source_target_pairs={{0,1},{1,0},{2,3},{3,2},{4,5},{5,4},{6,7},{7,6},{8,9},{9,8},{10,11... | collective-permute-start | bytes 786440 | tf_op jit(solution)/shard_map/ppermute | solution.py:533
  1.2 2.0 %collective-permute-start.3 = (bf16[512,256]{1,0:T(8,128)(2,1)}, bf16[512,256]{1,0:T(8,128)(2,1)S(1)}, u32[]{:S(2)}, u32[]{:S(2)}) collective-permute-start(bf16[512,256]{1,0:T(8,128)(2,1)} %v.1), channel_id=1, source_target_pairs={{0,1},{1,0},{2,3},{3,2},{4,5},{5,4},{6,7},{7,6},{8,9},{9,8},{10,11... | collective-permute-start | bytes 786440 | tf_op jit(solution)/shard_map/ppermute | solution.py:533
  2.6 6.5 %collective-permute-start.2 = (bf16[512,256]{1,0:T(8,128)(2,1)S(1)}, bf16[512,256]{1,0:T(8,128)(2,1)S(1)}, u32[]{:S(2)}, u32[]{:S(2)}) collective-permute-start(bf16[512,256]{1,0:T(8,128)(2,1)S(1)} %get-tuple-element.68), channel_id=1, source_target_pairs={{0,1},{1,0},{2,3},{3,2},{4,5},{5,4},{6,7},{7,6},{8,9},{9,8},{10,11... | collective-permute-start | bytes 786440 | tf_op jit(solution)/shard_map/ppermute | solution.py:533
  3.1 6.0 %collective-permute-start.1 = (bf16[1024,128]{1,0:T(8,128)(2,1)S(1)}, bf16[1024,128]{1,0:T(8,128)(2,1)S(1)}, u32[]{:S(2)}, u32[]{:S(2)}) collective-permute-start(bf16[1024,128]{1,0:T(8,128)(2,1)S(1)} %shard_map.85.keys), channel_id=1, source_target_pairs={{0,1},{1,0},{2,3},{3,2},{4,8},{5,9},{6,10},{7,11},{8,4},{9,5},{10,... | collective-permute-start | bytes 786440 | tf_op jit(solution)/shard_map/ppermute | solution.py:536
  3.3 15.7 %collective-permute-start.6 = (bf16[1024,256]{1,0:T(8,128)(2,1)S(1)}, bf16[1024,256]{1,0:T(8,128)(2,1)S(1)}, u32[]{:S(2)}, u32[]{:S(2)}) collective-permute-start(bf16[1024,256]{1,0:T(8,128)(2,1)S(1)} %get-tuple-element.76.kv), channel_id=1, source_target_pairs={{0,2},{1,3},{2,0},{3,1},{4,6},{5,7},{6,4},{7,5},{8,10},{9,11},{10,... | collective-permute-start | bytes 1572872 | tf_op jit(solution)/shard_map/ppermute | solution.py:536
  6.3 9.8 %collective-permute-start.7 = (bf16[1024,128]{1,0:T(8,128)(2,1)S(1)}, bf16[1024,128]{1,0:T(8,128)(2,1)S(1)}, u32[]{:S(2)}, u32[]{:S(2)}) collective-permute-start(bf16[1024,128]{1,0:T(8,128)(2,1)S(1)} %shard_map.85.keys), channel_id=1, source_target_pairs={{0,4},{1,5},{2,6},{3,7},{4,0},{5,1},{6,2},{7,3},{8,12},{9,13},{10,... | collective-permute-start | bytes 786440 | tf_op jit(solution)/shard_map/ppermute | solution.py:536
  9.0 14.6 %collective-permute-start.5 = (bf16[1024,128]{1,0:T(8,128)(2,1)S(1)}, bf16[1024,128]{1,0:T(8,128)(2,1)S(1)}, u32[]{:S(2)}, u32[]{:S(2)}) collective-permute-start(bf16[1024,128]{1,0:T(8,128)(2,1)S(1)} %get-tuple-element.73), channel_id=1, source_target_pairs={{0,4},{1,5},{2,6},{3,7},{4,0},{5,1},{6,2},{7,3},{8,12},{9,13},{10,... | collective-permute-start | bytes 786440 | tf_op jit(solution)/shard_map/ppermute | solution.py:536
  9.0 14.6 %collective-permute-start.4 = (bf16[1024,128]{1,0:T(8,128)(2,1)S(1)}, bf16[1024,128]{1,0:T(8,128)(2,1)S(1)}, u32[]{:S(2)}, u32[]{:S(2)}) collective-permute-start(bf16[1024,128]{1,0:T(8,128)(2,1)S(1)} %get-tuple-element.73), channel_id=1, source_target_pairs={{0,1},{1,0},{2,3},{3,2},{4,8},{5,9},{6,10},{7,11},{8,4},{9,5},{10,... | collective-permute-start | bytes 786440 | tf_op jit(solution)/shard_map/ppermute | solution.py:536
  16.2 8.7 %collective-permute-start.8 = (bf16[1024,128]{1,0:T(8,128)(2,1)S(1)}, bf16[1024,128]{1,0:T(8,128)(2,1)S(1)}, u32[]{:S(2)}, u32[]{:S(2)}) collective-permute-start(bf16[1024,128]{1,0:T(8,128)(2,1)S(1)} %shard_map.89), channel_id=1, source_target_pairs={{0,2},{1,3},{2,0},{3,1},{4,6},{5,7},{6,4},{7,5},{8,10},{9,11},{10,... | collective-permute-start | bytes 786440 | tf_op jit(solution)/shard_map/ppermute | solution.py:536
  16.7 14.0 %collective-permute-start.9 = (bf16[512,256]{1,0:T(8,128)(2,1)S(1)}, bf16[512,256]{1,0:T(8,128)(2,1)S(1)}, u32[]{:S(2)}, u32[]{:S(2)}) collective-permute-start(bf16[512,256]{1,0:T(8,128)(2,1)S(1)} %shard_map.88), channel_id=1, source_target_pairs={{0,8},{1,9},{2,10},{3,11},{4,12},{5,13},{6,14},{7,15},{8,0},{9,1},... | collective-permute-start | bytes 786440 | tf_op jit(solution)/shard_map/ppermute | solution.py:536
  23.9 9.8 %collective-permute-start.10 = (bf16[1024,128]{1,0:T(8,128)(2,1)S(1)}, bf16[1024,128]{1,0:T(8,128)(2,1)S(1)}, u32[]{:S(2)}, u32[]{:S(2)}) collective-permute-start(bf16[1024,128]{1,0:T(8,128)(2,1)S(1)} %shard_map.91), channel_id=1, source_target_pairs={{0,2},{1,3},{2,0},{3,1},{4,6},{5,7},{6,4},{7,5},{8,10},{9,11},{10,... | collective-permute-start | bytes 786440 | tf_op jit(solution)/shard_map/ppermute | solution.py:536
  32.1 8.5 %collective-permute-start.12 = (bf16[1024,128]{1,0:T(8,128)(2,1)S(1)}, bf16[1024,128]{1,0:T(8,128)(2,1)S(1)}, u32[]{:S(2)}, u32[]{:S(2)}) collective-permute-start(bf16[1024,128]{1,0:T(8,128)(2,1)S(1)} %get-tuple-element.102), channel_id=1, source_target_pairs={{0,2},{1,3},{2,0},{3,1},{4,6},{5,7},{6,4},{7,5},{8,10},{9,11},{10,... | collective-permute-start | bytes 786440 | tf_op jit(solution)/shard_map/ppermute | solution.py:536
  36.1 11.4 %collective-permute-start.13 = (bf16[1024,128]{1,0:T(8,128)(2,1)S(1)}, bf16[1024,128]{1,0:T(8,128)(2,1)S(1)}, u32[]{:S(2)}, u32[]{:S(2)}) collective-permute-start(bf16[1024,128]{1,0:T(8,128)(2,1)S(1)} %get-tuple-element.107), channel_id=1, source_target_pairs={{0,2},{1,3},{2,0},{3,1},{4,6},{5,7},{6,4},{7,5},{8,10},{9,11},{10,... | collective-permute-start | bytes 786440 | tf_op jit(solution)/shard_map/ppermute | solution.py:536
  36.7 14.6 %collective-permute-start.11 = (bf16[512,256]{1,0:T(8,128)(2,1)S(1)}, bf16[512,256]{1,0:T(8,128)(2,1)S(1)}, u32[]{:S(2)}, u32[]{:S(2)}) collective-permute-start(bf16[512,256]{1,0:T(8,128)(2,1)S(1)} %get-tuple-element.100), channel_id=1, source_target_pairs={{0,8},{1,9},{2,10},{3,11},{4,12},{5,13},{6,14},{7,15},{8,0},{9,1},... | collective-permute-start | bytes 786440 | tf_op jit(solution)/shard_map/ppermute | solution.py:536
  42.8 12.1 %collective-permute-start.14 = (bf16[1024,128]{1,0:T(8,128)(2,1)S(1)}, bf16[1024,128]{1,0:T(8,128)(2,1)S(1)}, u32[]{:S(2)}, u32[]{:S(2)}) collective-permute-start(bf16[1024,128]{1,0:T(8,128)(2,1)S(1)} %get-tuple-element.113), channel_id=1, source_target_pairs={{0,4},{1,5},{2,6},{3,7},{4,0},{5,1},{6,2},{7,3},{8,12},{9,13},{10,... | collective-permute-start | bytes 786440 | tf_op jit(solution)/shard_map/ppermute | solution.py:536
  42.8 12.0 %collective-permute-start.15 = (bf16[1024,128]{1,0:T(8,128)(2,1)S(1)}, bf16[1024,128]{1,0:T(8,128)(2,1)S(1)}, u32[]{:S(2)}, u32[]{:S(2)}) collective-permute-start(bf16[1024,128]{1,0:T(8,128)(2,1)S(1)} %get-tuple-element.114), channel_id=1, source_target_pairs={{0,1},{1,0},{2,3},{3,2},{4,8},{5,9},{6,10},{7,11},{8,4},{9,5},{10,... | collective-permute-start | bytes 786440 | tf_op jit(solution)/shard_map/ppermute | solution.py:536
  45.2 15.0 %collective-permute-start.17 = (bf16[1024,256]{1,0:T(8,128)(2,1)S(1)}, bf16[1024,256]{1,0:T(8,128)(2,1)S(1)}, u32[]{:S(2)}, u32[]{:S(2)}) collective-permute-start(bf16[1024,256]{1,0:T(8,128)(2,1)S(1)} %get-tuple-element.121), channel_id=1, source_target_pairs={{0,2},{1,3},{2,0},{3,1},{4,6},{5,7},{6,4},{7,5},{8,10},{9,11},{10,... | collective-permute-start | bytes 1572872 | tf_op jit(solution)/shard_map/ppermute | solution.py:536
  47.7 12.6 %collective-permute-start.19 = (bf16[1024,128]{1,0:T(8,128)(2,1)S(1)}, bf16[1024,128]{1,0:T(8,128)(2,1)S(1)}, u32[]{:S(2)}, u32[]{:S(2)}) collective-permute-start(bf16[1024,128]{1,0:T(8,128)(2,1)S(1)} %get-tuple-element.108), channel_id=1, source_target_pairs={{0,4},{1,5},{2,6},{3,7},{4,0},{5,1},{6,2},{7,3},{8,12},{9,13},{10,... | collective-permute-start | bytes 786440 | tf_op jit(solution)/shard_map/ppermute | solution.py:536
  51.3 8.9 %collective-permute-start.18 = (bf16[1024,128]{1,0:T(8,128)(2,1)S(1)}, bf16[1024,128]{1,0:T(8,128)(2,1)S(1)}, u32[]{:S(2)}, u32[]{:S(2)}) collective-permute-start(bf16[1024,128]{1,0:T(8,128)(2,1)S(1)} %get-tuple-element.109), channel_id=1, source_target_pairs={{0,1},{1,0},{2,3},{3,2},{4,8},{5,9},{6,10},{7,11},{8,4},{9,5},{10,... | collective-permute-start | bytes 786440 | tf_op jit(solution)/shard_map/ppermute | solution.py:536
  58.9 1.6 %collective-permute-start.16 = (bf16[512,256]{1,0:T(8,128)(2,1)S(1)}, bf16[512,256]{1,0:T(8,128)(2,1)S(1)}, u32[]{:S(2)}, u32[]{:S(2)}) collective-permute-start(bf16[512,256]{1,0:T(8,128)(2,1)S(1)} %get-tuple-element.117), channel_id=1, source_target_pairs={{0,1},{1,0},{2,3},{3,2},{4,5},{5,4},{6,7},{7,6},{8,9},{9,8},{10,11... | collective-permute-start | bytes 786440 | tf_op jit(solution)/shard_map/ppermute | solution.py:533
  60.5 1.6 %collective-permute-start.20 = (bf16[512,256]{1,0:T(8,128)(2,1)S(1)}, bf16[512,256]{1,0:T(8,128)(2,1)S(1)}, u32[]{:S(2)}, u32[]{:S(2)}) collective-permute-start(bf16[512,256]{1,0:T(8,128)(2,1)S(1)} %get-tuple-element.123), channel_id=1, source_target_pairs={{0,1},{1,0},{2,3},{3,2},{4,5},{5,4},{6,7},{7,6},{8,9},{9,8},{10,11... | collective-permute-start | bytes 786440 | tf_op jit(solution)/shard_map/ppermute | solution.py:533

commit v16 on v14

--- a/solution.py
+++ b/solution.py
@@ -368,14 +368,17 @@
 
 def late_kernel(block, relayed, far, *refs):
     n = len(far)
-    lists, qg, turned, lse_ref, part_ref, p_ref, c_k, c_v = refs[:8]
+    lists_any, qg, turned, lse_ref, part_ref, p_ref, c_k, c_v = refs[:8]
     far_kv = refs[8 : 8 + n]
     o_ref, dot_ref, dc_k, dq_ref = refs[8 + n : 12 + n]
     far_grad = refs[12 + n : 12 + 2 * n]
-    grad = refs[12 + 2 * n]
+    grad, lists, sem = refs[12 + 2 * n :]
+    copy = pltpu.make_async_copy(lists_any, lists, sem)
+    copy.start()
     half = qg.shape[0] // 2
     frame = lax.axis_index("tm")
     grad[...] = jnp.zeros_like(grad)
+    copy.wait()
     for slab in range(2):
         rows = rows_of(slab, half)
         q, g, lse = qg[rows, KEY], qg[rows, VALUE], lse_ref[0:1, rows]
@@ -603,7 +606,12 @@
         functools.partial(late_kernel, block, relayed, far),
         (lists, qg, turned, lse, part, probs, c_k, c_v, *far_kv),
         [turned_bf, stat_row, frame_one, turned_sum] + [pair] * n,
-        scratch=[grad_one],
+        scratch=[
+            grad_one,
+            pltpu.SMEM(lists.shape, jnp.int32),
+            pltpu.SemaphoreType.DMA(()),
+        ],
+        scalars=pl.BlockSpec(memory_space=pl.ANY),
     )
     far_came = [swapped(value, swap) for value, swap in zip(far_grad, far)]
     dc_k_came = swapped(dc_k, near_swap)

time: 63.2 us -> 63.2 us (level)
  no operation moved by 1% of the time
where the time goes in v16:
time: 63.2 us; the launch traced here: 63 us
  Pallas kernels  23 us (36%)
  waiting for transfers between devices  20.1 us (32%)
  starting transfers between devices  19 us (30%)
  between operations  0.84 us (1%)
    pallas_call x20, Pallas kernels, call(): pl.pallas_call(kernel, out_shape=out_shape, in_specs=[scalars if a.dtype...  23 us
    ppermute x16, waiting for transfers between devices, swapped(): return lax.ppermute(value, ('tm', 'space'), swap.pairs)  19.5 us
    ppermute x16, starting transfers between devices, swapped(): return lax.ppermute(value, ('tm', 'space'), swap.pairs)  17.7 us
  transfers between devices with their start and end apart: 21, of which 8 were waited for; matrix products, arithmetic and copies ran while one was open for 0% of the time, Pallas kernels for 35%

profile of v16, /device:TPU:0, one launch (start us, length us, event | category | flops | bytes accessed | tf_op | source)
XLA Modules:
  0.0 63.0 jit_solution(571339785255707621)
XLA Ops:
  0.6 0.5 collective-permute-start
  1.2 1.3 %shard_map.84 = (bf16[512,128]{1,0:T(8,128)(2,1)S(1)}, bf16[512,128]{1,0:T(8,128)(2,1)S(1)}, bf16[512,256]{1,0:T(8,128)(2,1)S(1)}, bf16[512,256]{1,0:T(8,128)(2,1)S(1)}, s32[8,16]{1,0:T(8,128)S(1)}) custom-call(bf16[512,256]{1,0:T(8,128)(2,1)} %k.1, bf16[512,256]{1,0:T(8,128)(2,1)} %v.1, bf16[512,256]{1,0:T(8,128)(2,1)} %q.1, bf16[512,256]{1,0:T(8,128)(2,1)} %g.1, ...), custom_call_target="tpu_custom_call" | custom-call | flops 1024 | bytes 1024 | tf_op jit(solution)/shard_map/pallas_call | solution.py:38
  2.6 0.5 collective-permute-start.2
  3.3 3.0 %collective-permute-start.6 = (bf16[1024,256]{1,0:T(8,128)(2,1)S(1)}, bf16[1024,256]{1,0:T(8,128)(2,1)S(1)}, u32[]{:S(2)}, u32[]{:S(2)}) collective-permute-start(bf16[1024,256]{1,0:T(8,128)(2,1)S(1)} %get-tuple-element.76.kv), channel_id=1, source_target_pairs={{0,2},{1,3},{2,0},{3,1},{4,6},{5,7},{6,4},{7,5},{8,10},{9,11},{10,... | collective-permute-start | bytes 1572872 | tf_op jit(solution)/shard_map/ppermute | solution.py:539
  6.3 2.7 %collective-permute-start.7 = (bf16[1024,128]{1,0:T(8,128)(2,1)S(1)}, bf16[1024,128]{1,0:T(8,128)(2,1)S(1)}, u32[]{:S(2)}, u32[]{:S(2)}) collective-permute-start(bf16[1024,128]{1,0:T(8,128)(2,1)S(1)} %shard_map.85.keys), channel_id=1, source_target_pairs={{0,4},{1,5},{2,6},{3,7},{4,0},{5,1},{6,2},{7,3},{8,12},{9,13},{10,... | collective-permute-start | bytes 786440 | tf_op jit(solution)/shard_map/ppermute | solution.py:539
  9.2 0.6 %shard_map.88 = bf16[512,256]{1,0:T(8,128)(2,1)S(1)} custom-call(s32[8,16]{1,0:T(8,128)S(1)} %get-tuple-element.71.lists.lists_any.refs_0_, bf16[1024,256]{1,0:T(8,128)(2,1)S(1)} %get-tuple-element.76.kv), custom_call_target="tpu_custom_call" | custom-call | flops 1024 | bytes 1024 | tf_op jit(solution)/shard_map/pallas_call | solution.py:38
  9.8 6.3 %collective-permute-done.7.z.z_k = bf16[1024,128]{1,0:T(8,128)(2,1)S(1)} collective-permute-done((bf16[1024,128]{1,0:T(8,128)(2,1)S(1)}, bf16[1024,128]{1,0:T(8,128)(2,1)S(1)}, u32[]{:S(2)}, u32[]{:S(2)}) %collective-permute-start.7) | collective-permute-done | bytes 262176 | tf_op jit(solution)/shard_map/ppermute | solution.py:539
  16.2 0.6 collective-permute-start.8
  16.7 1.9 %collective-permute-start.9 = (bf16[512,256]{1,0:T(8,128)(2,1)S(1)}, bf16[512,256]{1,0:T(8,128)(2,1)S(1)}, u32[]{:S(2)}, u32[]{:S(2)}) collective-permute-start(bf16[512,256]{1,0:T(8,128)(2,1)S(1)} %shard_map.88), channel_id=1, source_target_pairs={{0,8},{1,9},{2,10},{3,11},{4,12},{5,13},{6,14},{7,15},{8,0},{9,1},... | collective-permute-start | bytes 786440 | tf_op jit(solution)/shard_map/ppermute | solution.py:539
  18.7 0.3 collective-permute-done.6.a_kv
  19.0 3.5 %shard_map.90 = (f32[8,1024]{1,0:T(8,128)S(1)}, f32[128,1024]{1,0:T(8,128)S(1)}) custom-call(s32[8,16]{1,0:T(8,128)S(1)} %get-tuple-element.71.lists.lists_any.refs_0_, bf16[1024,256]{1,0:T(8,128)(2,1)S(1)} %get-tuple-element.70.qg.refs_1_, bf16[1024,256]{1,0:T(8,128)(2,1)S(1)} %get-tuple-element.76.kv, bf16[1024,256]{1,0:T(8,128)(2,1)S(1)} %collective-permute-done.6.a_kv), custom_call_target="tpu_custom_call" | custom-call | flops 1024 | bytes 1024 | tf_op jit(solution)/shard_map/pallas_call | solution.py:38
  22.5 1.2 %collective-permute-done.5.z.z_v = bf16[1024,128]{1,0:T(8,128)(2,1)S(1)} collective-permute-done((bf16[1024,128]{1,0:T(8,128)(2,1)S(1)}, bf16[1024,128]{1,0:T(8,128)(2,1)S(1)}, u32[]{:S(2)}, u32[]{:S(2)}) %collective-permute-start.5) | collective-permute-done | bytes 262176 | tf_op jit(solution)/shard_map/ppermute | solution.py:539
  23.6 0.2 shard_map.91
  23.9 1.0 %collective-permute-start.10 = (bf16[1024,128]{1,0:T(8,128)(2,1)S(1)}, bf16[1024,128]{1,0:T(8,128)(2,1)S(1)}, u32[]{:S(2)}, u32[]{:S(2)}) collective-permute-start(bf16[1024,128]{1,0:T(8,128)(2,1)S(1)} %shard_map.91), channel_id=1, source_target_pairs={{0,2},{1,3},{2,0},{3,1},{4,6},{5,7},{6,4},{7,5},{8,10},{9,11},{10,... | collective-permute-start | bytes 786440 | tf_op jit(solution)/shard_map/ppermute | solution.py:539
  24.9 2.6 %shard_map.92 = (f32[8,1024]{1,0:T(8,128)S(1)}, f32[128,1024]{1,0:T(8,128)S(1)}, f32[2,512,512]{2,1,0:T(8,128)S(1)}) custom-call(s32[8,16]{1,0:T(8,128)S(1)} %get-tuple-element.71.lists.lists_any.refs_0_, bf16[1024,256]{1,0:T(8,128)(2,1)S(1)} %get-tuple-element.70.qg.refs_1_, f32[8,1024]{1,0:T(8,128)S(1)} %get-tuple-element.87.stat, ...), custom_call_target="tpu_custom_call" | custom-call | flops 1024 | bytes 1024 | tf_op jit(solution)/shard_map/pallas_call | solution.py:38
  27.5 3.2 %collective-permute-done.9.refs_0_.refs_8_ = bf16[512,256]{1,0:T(8,128)(2,1)S(1)} collective-permute-done((bf16[512,256]{1,0:T(8,128)(2,1)S(1)}, bf16[512,256]{1,0:T(8,128)(2,1)S(1)}, u32[]{:S(2)}, u32[]{:S(2)}) %collective-permute-start.9) | collective-permute-done | bytes 262176 | tf_op jit(solution)/shard_map/ppermute | solution.py:539
  30.7 1.4 %shard_map.93 = (f32[8,1024]{1,0:T(8,128)S(1)}, f32[128,1024]{1,0:T(8,128)S(1)}, bf16[1024,128]{1,0:T(8,128)(2,1)S(1)}, f32[2,512,512]{2,1,0:T(8,128)S(1)}) custom-call(s32[8,16]{1,0:T(8,128)S(1)} %get-tuple-element.71.lists.lists_any.refs_0_, bf16[1024,256]{1,0:T(8,128)(2,1)S(1)} %get-tuple-element.70.qg.refs_1_, f32[8,1024]{1,0:T(8,128)S(1)} %get-tuple-element.89.stat, ...), custom_call_target="tpu_custom_call" | custom-call | flops 1024 | bytes 1024 | tf_op jit(solution)/shard_map/pallas_call | solution.py:38
  32.1 1.5 %collective-permute-start.12 = (bf16[1024,128]{1,0:T(8,128)(2,1)S(1)}, bf16[1024,128]{1,0:T(8,128)(2,1)S(1)}, u32[]{:S(2)}, u32[]{:S(2)}) collective-permute-start(bf16[1024,128]{1,0:T(8,128)(2,1)S(1)} %get-tuple-element.102), channel_id=1, source_target_pairs={{0,2},{1,3},{2,0},{3,1},{4,6},{5,7},{6,4},{7,5},{8,10},{9,11},{10,... | collective-permute-start | bytes 786440 | tf_op jit(solution)/shard_map/ppermute | solution.py:539
  33.7 2.5 %shard_map.94 = (bf16[128,1024]{1,0:T(8,128)(2,1)S(1)}, f32[8,1024]{1,0:T(8,128)S(1)}, bf16[1024,128]{1,0:T(8,128)(2,1)S(1)}, f32[128,1024]{1,0:T(8,128)S(1)}, bf16[512,256]{1,0:T(8,128)(2,1)S(1)}) custom-call(s32[8,16]{1,0:T(8,128)S(1)} %get-tuple-element.71.lists.lists_any.refs_0_, bf16[1024,256]{1,0:T(8,128)(2,1)S(1)} %get-tuple-element.70.qg.refs_1_, ...), custom_call_target="tpu_custom_call" | custom-call | flops 1024 | bytes 1024 | tf_op jit(solution)/shard_map/pallas_call | solution.py:38
  36.2 0.6 collective-permute-start.13
  36.8 3.7 %collective-permute-done.12.came = bf16[1024,128]{1,0:T(8,128)(2,1)S(1)} collective-permute-done((bf16[1024,128]{1,0:T(8,128)(2,1)S(1)}, bf16[1024,128]{1,0:T(8,128)(2,1)S(1)}, u32[]{:S(2)}, u32[]{:S(2)}) %collective-permute-start.12) | collective-permute-done | bytes 262176 | tf_op jit(solution)/shard_map/ppermute | solution.py:539
  40.5 2.2 %shard_map.95 = (f32[1024,128]{1,0:T(8,128)S(1)}, f32[1024,128]{1,0:T(8,128)S(1)}, bf16[1024,128]{1,0:T(8,128)(2,1)S(1)}, bf16[1024,128]{1,0:T(8,128)(2,1)S(1)}, f32[128,1024]{1,0:T(8,128)S(1)}) custom-call(s32[8,16]{1,0:T(8,128)S(1)} %get-tuple-element.71.lists.lists_any.refs_0_, bf16[1024,256]{1,0:T(8,128)(2,1)S(1)} %get-tuple-element.70.qg.refs_1_, ...), custom_call_target="tpu_custom_call" | custom-call | flops 2684354560 | bytes 1024 | tf_op jit(solution)/shard_map/pallas_call | solution.py:38
  42.9 2.2 %shard_map.96 = (bf16[1024,256]{1,0:T(8,128)(2,1)S(1)}, f32[128,1024]{1,0:T(8,128)S(1)}) custom-call(s32[8,16]{1,0:T(8,128)S(1)} %get-tuple-element.71.lists.lists_any.refs_0_, bf16[1024,256]{1,0:T(8,128)(2,1)S(1)} %get-tuple-element.70.qg.refs_1_, f32[8,1024]{1,0:T(8,128)S(1)} %get-tuple-element.95.refs_3_.lse_ref, ...), custom_call_target="tpu_custom_call" | custom-call | flops 1024 | bytes 1024 | tf_op jit(solution)/shard_map/pallas_call | solution.py:38
  45.1 2.4 %collective-permute-start.17 = (bf16[1024,256]{1,0:T(8,128)(2,1)S(1)}, bf16[1024,256]{1,0:T(8,128)(2,1)S(1)}, u32[]{:S(2)}, u32[]{:S(2)}) collective-permute-start(bf16[1024,256]{1,0:T(8,128)(2,1)S(1)} %get-tuple-element.121), channel_id=1, source_target_pairs={{0,2},{1,3},{2,0},{3,1},{4,6},{5,7},{6,4},{7,5},{8,10},{9,11},{10,... | collective-permute-start | bytes 1572872 | tf_op jit(solution)/shard_map/ppermute | solution.py:539
  47.7 3.6 %collective-permute-start.19 = (bf16[1024,128]{1,0:T(8,128)(2,1)S(1)}, bf16[1024,128]{1,0:T(8,128)(2,1)S(1)}, u32[]{:S(2)}, u32[]{:S(2)}) collective-permute-start(bf16[1024,128]{1,0:T(8,128)(2,1)S(1)} %get-tuple-element.108), channel_id=1, source_target_pairs={{0,4},{1,5},{2,6},{3,7},{4,0},{5,1},{6,2},{7,3},{8,12},{9,13},{10,... | collective-permute-start | bytes 786440 | tf_op jit(solution)/shard_map/ppermute | solution.py:539
  51.3 3.6 %collective-permute-done.14.refs_1_ = bf16[1024,128]{1,0:T(8,128)(2,1)S(1)} collective-permute-done((bf16[1024,128]{1,0:T(8,128)(2,1)S(1)}, bf16[1024,128]{1,0:T(8,128)(2,1)S(1)}, u32[]{:S(2)}, u32[]{:S(2)}) %collective-permute-start.14) | collective-permute-done | bytes 262176 | tf_op jit(solution)/shard_map/ppermute | solution.py:539
  54.9 0.8 %shard_map.98.placed = f32[1024,256]{1,0:T(8,128)S(1)} custom-call(s32[8,16]{1,0:T(8,128)S(1)} %get-tuple-element.71.lists.lists_any.refs_0_, bf16[1024,128]{1,0:T(8,128)(2,1)S(1)} %collective-permute-done.14.refs_1_, bf16[1024,128]{1,0:T(8,128)(2,1)S(1)} %collective-permute-done.15.refs_2_, bf16[512,256]{1,0:T(8,128)(2,1)S(1)} %collective-permute-done.11.refs_3_), custom_call_target="tpu_custom_call" | custom-call | flops 1024 | bytes 1024 | tf_op jit(solution)/shard_map/pallas_call | solution.py:38
  55.8 3.2 %shard_map.99 = (f32[1024,256]{1,0:T(8,128)S(1)}, bf16[512,256]{1,0:T(8,128)(2,1)S(1)}, bf16[512,256]{1,0:T(8,128)(2,1)S(1)}) custom-call(bf16[1024,256]{1,0:T(8,128)(2,1)S(1)} %get-tuple-element.70.qg.refs_1_, f32[8,1024]{1,0:T(8,128)S(1)} %get-tuple-element.95.refs_3_.lse_ref, f32[8,1024]{1,0:T(8,128)S(1)} %get-tuple-element.99.dot_ref, ...), custom_call_target="tpu_custom_call" | custom-call | flops 3758096384 | bytes 1024 | tf_op jit(solution)/shard_map/pallas_call | solution.py:38
  59.0 1.1 %collective-permute-done.17.da = bf16[1024,256]{1,0:T(8,128)(2,1)S(1)} collective-permute-done((bf16[1024,256]{1,0:T(8,128)(2,1)S(1)}, bf16[1024,256]{1,0:T(8,128)(2,1)S(1)}, u32[]{:S(2)}, u32[]{:S(2)}) %collective-permute-start.17) | collective-permute-done | bytes 524320 | tf_op jit(solution)/shard_map/ppermute | solution.py:539
  60.6 0.9 %shard_map.100 = (bf16[512,256]{1,0:T(8,128)(2,1)}, bf16[512,256]{1,0:T(8,128)(2,1)}) custom-call(bf16[512,256]{1,0:T(8,128)(2,1)S(1)} %get-tuple-element.116.keep, bf16[512,256]{1,0:T(8,128)(2,1)S(1)} %collective-permute-done.16.came), custom_call_target="tpu_custom_call" | custom-call | flops 1024 | bytes 1024 | tf_op jit(solution)/shard_map/pallas_call | solution.py:38
  61.5 0.6 collective-permute-done.20.came
  62.1 0.9 %shard_map.103 = (bf16[512,256]{1,0:T(8,128)(2,1)}, bf16[512,256]{1,0:T(8,128)(2,1)}) custom-call(bf16[512,256]{1,0:T(8,128)(2,1)S(1)} %get-tuple-element.122.keep, bf16[512,256]{1,0:T(8,128)(2,1)S(1)} %collective-permute-done.20.came), custom_call_target="tpu_custom_call" | custom-call | flops 1024 | bytes 1024 | tf_op jit(solution)/shard_map/pallas_call | solution.py:38
  (30 shorter events, 1.4 us)
Async XLA Ops:
  0.6 1.9 %collective-permute-start = (bf16[512,256]{1,0:T(8,128)(2,1)}, bf16[512,256]{1,0:T(8,128)(2,1)S(1)}, u32[]{:S(2)}, u32[]{:S(2)}) collective-permute-start(bf16[512,256]{1,0:T(8,128)(2,1)} %k.1), channel_id=1, source_target_pairs={{0,1},{1,0},{2,3},{3,2},{4,5},{5,4},{6,7},{7,6},{8,9},{9,8},{10,11... | collective-permute-start | bytes 786440 | tf_op jit(solution)/shard_map/ppermute | solution.py:536
  1.2 2.0 %collective-permute-start.3 = (bf16[512,256]{1,0:T(8,128)(2,1)}, bf16[512,256]{1,0:T(8,128)(2,1)S(1)}, u32[]{:S(2)}, u32[]{:S(2)}) collective-permute-start(bf16[512,256]{1,0:T(8,128)(2,1)} %v.1), channel_id=1, source_target_pairs={{0,1},{1,0},{2,3},{3,2},{4,5},{5,4},{6,7},{7,6},{8,9},{9,8},{10,11... | collective-permute-start | bytes 786440 | tf_op jit(solution)/shard_map/ppermute | solution.py:536
  2.6 6.5 %collective-permute-start.2 = (bf16[512,256]{1,0:T(8,128)(2,1)S(1)}, bf16[512,256]{1,0:T(8,128)(2,1)S(1)}, u32[]{:S(2)}, u32[]{:S(2)}) collective-permute-start(bf16[512,256]{1,0:T(8,128)(2,1)S(1)} %get-tuple-element.68), channel_id=1, source_target_pairs={{0,1},{1,0},{2,3},{3,2},{4,5},{5,4},{6,7},{7,6},{8,9},{9,8},{10,11... | collective-permute-start | bytes 786440 | tf_op jit(solution)/shard_map/ppermute | solution.py:536
  3.1 6.0 %collective-permute-start.1 = (bf16[1024,128]{1,0:T(8,128)(2,1)S(1)}, bf16[1024,128]{1,0:T(8,128)(2,1)S(1)}, u32[]{:S(2)}, u32[]{:S(2)}) collective-permute-start(bf16[1024,128]{1,0:T(8,128)(2,1)S(1)} %shard_map.85.keys), channel_id=1, source_target_pairs={{0,1},{1,0},{2,3},{3,2},{4,8},{5,9},{6,10},{7,11},{8,4},{9,5},{10,... | collective-permute-start | bytes 786440 | tf_op jit(solution)/shard_map/ppermute | solution.py:539
  3.3 15.7 %collective-permute-start.6 = (bf16[1024,256]{1,0:T(8,128)(2,1)S(1)}, bf16[1024,256]{1,0:T(8,128)(2,1)S(1)}, u32[]{:S(2)}, u32[]{:S(2)}) collective-permute-start(bf16[1024,256]{1,0:T(8,128)(2,1)S(1)} %get-tuple-element.76.kv), channel_id=1, source_target_pairs={{0,2},{1,3},{2,0},{3,1},{4,6},{5,7},{6,4},{7,5},{8,10},{9,11},{10,... | collective-permute-start | bytes 1572872 | tf_op jit(solution)/shard_map/ppermute | solution.py:539
  6.3 9.8 %collective-permute-start.7 = (bf16[1024,128]{1,0:T(8,128)(2,1)S(1)}, bf16[1024,128]{1,0:T(8,128)(2,1)S(1)}, u32[]{:S(2)}, u32[]{:S(2)}) collective-permute-start(bf16[1024,128]{1,0:T(8,128)(2,1)S(1)} %shard_map.85.keys), channel_id=1, source_target_pairs={{0,4},{1,5},{2,6},{3,7},{4,0},{5,1},{6,2},{7,3},{8,12},{9,13},{10,... | collective-permute-start | bytes 786440 | tf_op jit(solution)/shard_map/ppermute | solution.py:539
  9.0 14.6 %collective-permute-start.5 = (bf16[1024,128]{1,0:T(8,128)(2,1)S(1)}, bf16[1024,128]{1,0:T(8,128)(2,1)S(1)}, u32[]{:S(2)}, u32[]{:S(2)}) collective-permute-start(bf16[1024,128]{1,0:T(8,128)(2,1)S(1)} %get-tuple-element.73), channel_id=1, source_target_pairs={{0,4},{1,5},{2,6},{3,7},{4,0},{5,1},{6,2},{7,3},{8,12},{9,13},{10,... | collective-permute-start | bytes 786440 | tf_op jit(solution)/shard_map/ppermute | solution.py:539
  9.0 14.6 %collective-permute-start.4 = (bf16[1024,128]{1,0:T(8,128)(2,1)S(1)}, bf16[1024,128]{1,0:T(8,128)(2,1)S(1)}, u32[]{:S(2)}, u32[]{:S(2)}) collective-permute-start(bf16[1024,128]{1,0:T(8,128)(2,1)S(1)} %get-tuple-element.73), channel_id=1, source_target_pairs={{0,1},{1,0},{2,3},{3,2},{4,8},{5,9},{6,10},{7,11},{8,4},{9,5},{10,... | collective-permute-start | bytes 786440 | tf_op jit(solution)/shard_map/ppermute | solution.py:539
  16.2 8.7 %collective-permute-start.8 = (bf16[1024,128]{1,0:T(8,128)(2,1)S(1)}, bf16[1024,128]{1,0:T(8,128)(2,1)S(1)}, u32[]{:S(2)}, u32[]{:S(2)}) collective-permute-start(bf16[1024,128]{1,0:T(8,128)(2,1)S(1)} %shard_map.89), channel_id=1, source_target_pairs={{0,2},{1,3},{2,0},{3,1},{4,6},{5,7},{6,4},{7,5},{8,10},{9,11},{10,... | collective-permute-start | bytes 786440 | tf_op jit(solution)/shard_map/ppermute | solution.py:539
  16.7 14.0 %collective-permute-start.9 = (bf16[512,256]{1,0:T(8,128)(2,1)S(1)}, bf16[512,256]{1,0:T(8,128)(2,1)S(1)}, u32[]{:S(2)}, u32[]{:S(2)}) collective-permute-start(bf16[512,256]{1,0:T(8,128)(2,1)S(1)} %shard_map.88), channel_id=1, source_target_pairs={{0,8},{1,9},{2,10},{3,11},{4,12},{5,13},{6,14},{7,15},{8,0},{9,1},... | collective-permute-start | bytes 786440 | tf_op jit(solution)/shard_map/ppermute | solution.py:539
  23.9 9.8 %collective-permute-start.10 = (bf16[1024,128]{1,0:T(8,128)(2,1)S(1)}, bf16[1024,128]{1,0:T(8,128)(2,1)S(1)}, u32[]{:S(2)}, u32[]{:S(2)}) collective-permute-start(bf16[1024,128]{1,0:T(8,128)(2,1)S(1)} %shard_map.91), channel_id=1, source_target_pairs={{0,2},{1,3},{2,0},{3,1},{4,6},{5,7},{6,4},{7,5},{8,10},{9,11},{10,... | collective-permute-start | bytes 786440 | tf_op jit(solution)/shard_map/ppermute | solution.py:539
  32.1 8.4 %collective-permute-start.12 = (bf16[1024,128]{1,0:T(8,128)(2,1)S(1)}, bf16[1024,128]{1,0:T(8,128)(2,1)S(1)}, u32[]{:S(2)}, u32[]{:S(2)}) collective-permute-start(bf16[1024,128]{1,0:T(8,128)(2,1)S(1)} %get-tuple-element.102), channel_id=1, source_target_pairs={{0,2},{1,3},{2,0},{3,1},{4,6},{5,7},{6,4},{7,5},{8,10},{9,11},{10,... | collective-permute-start | bytes 786440 | tf_op jit(solution)/shard_map/ppermute | solution.py:539
  36.1 15.2 %collective-permute-start.11 = (bf16[512,256]{1,0:T(8,128)(2,1)S(1)}, bf16[512,256]{1,0:T(8,128)(2,1)S(1)}, u32[]{:S(2)}, u32[]{:S(2)}) collective-permute-start(bf16[512,256]{1,0:T(8,128)(2,1)S(1)} %get-tuple-element.100), channel_id=1, source_target_pairs={{0,8},{1,9},{2,10},{3,11},{4,12},{5,13},{6,14},{7,15},{8,0},{9,1},... | collective-permute-start | bytes 786440 | tf_op jit(solution)/shard_map/ppermute | solution.py:539
  36.2 11.4 %collective-permute-start.13 = (bf16[1024,128]{1,0:T(8,128)(2,1)S(1)}, bf16[1024,128]{1,0:T(8,128)(2,1)S(1)}, u32[]{:S(2)}, u32[]{:S(2)}) collective-permute-start(bf16[1024,128]{1,0:T(8,128)(2,1)S(1)} %get-tuple-element.107), channel_id=1, source_target_pairs={{0,2},{1,3},{2,0},{3,1},{4,6},{5,7},{6,4},{7,5},{8,10},{9,11},{10,... | collective-permute-start | bytes 786440 | tf_op jit(solution)/shard_map/ppermute | solution.py:539
  42.7 12.2 %collective-permute-start.14 = (bf16[1024,128]{1,0:T(8,128)(2,1)S(1)}, bf16[1024,128]{1,0:T(8,128)(2,1)S(1)}, u32[]{:S(2)}, u32[]{:S(2)}) collective-permute-start(bf16[1024,128]{1,0:T(8,128)(2,1)S(1)} %get-tuple-element.113), channel_id=1, source_target_pairs={{0,4},{1,5},{2,6},{3,7},{4,0},{5,1},{6,2},{7,3},{8,12},{9,13},{10,... | collective-permute-start | bytes 786440 | tf_op jit(solution)/shard_map/ppermute | solution.py:539
  42.8 12.1 %collective-permute-start.15 = (bf16[1024,128]{1,0:T(8,128)(2,1)S(1)}, bf16[1024,128]{1,0:T(8,128)(2,1)S(1)}, u32[]{:S(2)}, u32[]{:S(2)}) collective-permute-start(bf16[1024,128]{1,0:T(8,128)(2,1)S(1)} %get-tuple-element.114), channel_id=1, source_target_pairs={{0,1},{1,0},{2,3},{3,2},{4,8},{5,9},{6,10},{7,11},{8,4},{9,5},{10,... | collective-permute-start | bytes 786440 | tf_op jit(solution)/shard_map/ppermute | solution.py:539
  45.1 15.0 %collective-permute-start.17 = (bf16[1024,256]{1,0:T(8,128)(2,1)S(1)}, bf16[1024,256]{1,0:T(8,128)(2,1)S(1)}, u32[]{:S(2)}, u32[]{:S(2)}) collective-permute-start(bf16[1024,256]{1,0:T(8,128)(2,1)S(1)} %get-tuple-element.121), channel_id=1, source_target_pairs={{0,2},{1,3},{2,0},{3,1},{4,6},{5,7},{6,4},{7,5},{8,10},{9,11},{10,... | collective-permute-start | bytes 1572872 | tf_op jit(solution)/shard_map/ppermute | solution.py:539
  47.7 12.6 %collective-permute-start.19 = (bf16[1024,128]{1,0:T(8,128)(2,1)S(1)}, bf16[1024,128]{1,0:T(8,128)(2,1)S(1)}, u32[]{:S(2)}, u32[]{:S(2)}) collective-permute-start(bf16[1024,128]{1,0:T(8,128)(2,1)S(1)} %get-tuple-element.108), channel_id=1, source_target_pairs={{0,4},{1,5},{2,6},{3,7},{4,0},{5,1},{6,2},{7,3},{8,12},{9,13},{10,... | collective-permute-start | bytes 786440 | tf_op jit(solution)/shard_map/ppermute | solution.py:539
  51.3 8.9 %collective-permute-start.18 = (bf16[1024,128]{1,0:T(8,128)(2,1)S(1)}, bf16[1024,128]{1,0:T(8,128)(2,1)S(1)}, u32[]{:S(2)}, u32[]{:S(2)}) collective-permute-start(bf16[1024,128]{1,0:T(8,128)(2,1)S(1)} %get-tuple-element.109), channel_id=1, source_target_pairs={{0,1},{1,0},{2,3},{3,2},{4,8},{5,9},{6,10},{7,11},{8,4},{9,5},{10,... | collective-permute-start | bytes 786440 | tf_op jit(solution)/shard_map/ppermute | solution.py:539
  58.9 1.6 %collective-permute-start.16 = (bf16[512,256]{1,0:T(8,128)(2,1)S(1)}, bf16[512,256]{1,0:T(8,128)(2,1)S(1)}, u32[]{:S(2)}, u32[]{:S(2)}) collective-permute-start(bf16[512,256]{1,0:T(8,128)(2,1)S(1)} %get-tuple-element.117), channel_id=1, source_target_pairs={{0,1},{1,0},{2,3},{3,2},{4,5},{5,4},{6,7},{7,6},{8,9},{9,8},{10,11... | collective-permute-start | bytes 786440 | tf_op jit(solution)/shard_map/ppermute | solution.py:536
  60.5 1.6 %collective-permute-start.20 = (bf16[512,256]{1,0:T(8,128)(2,1)S(1)}, bf16[512,256]{1,0:T(8,128)(2,1)S(1)}, u32[]{:S(2)}, u32[]{:S(2)}) collective-permute-start(bf16[512,256]{1,0:T(8,128)(2,1)S(1)} %get-tuple-element.123), channel_id=1, source_target_pairs={{0,1},{1,0},{2,3},{3,2},{4,5},{5,4},{6,7},{7,6},{8,9},{9,8},{10,11... | collective-permute-start | bytes 786440 | tf_op jit(solution)/shard_map/ppermute | solution.py:536
